TPU v7x, 512 devices: a whole 4x8x8 slice. The times are simulated.
512 devices in a mesh: row: 16 (over x, y_lo), col: 32 (over y_hi, z, core).
Axes of the slice: x: 4, y: 8 (y_hi: 2, y_lo: 4; y = y_hi * 4 + y_lo), z: 8, core: 2. Of those that a mesh axis runs over, the one named last changes fastest.
Arguments:
- source_map: float32 [8192, 8192], P('row', 'col'), may hold values from -6 to 6
- observed: float32 [8192, 8192], P('row', 'col'), may hold values from -6 to 6
- factor_x: float32 [32, 3, 256, 256], P('row'), may hold values from -0.21875 to 0.21875
- band_x: int32 [32, 3], P('row'), may hold values 0 or 1
- factor_y: float32 [32, 3, 256, 256], P('col'), may hold values from -0.21875 to 0.21875
- band_y: int32 [32, 3], P('col'), may hold values 0 or 1
- step_size: float32 [1], replicated, may hold values from 0.03 to 0.08
- threshold: float32 [1], replicated, may hold values from 0.1 to 0.4
Outputs:
- estimate: float32 [8192, 8192], P('row', 'col')
All inputs are finite; a program needn't handle non-finite values. No bound on the sum of `band_x` or of `band_y` on one device may be relied on, other than what follows from the above.
Results may differ from a plain program's by a relative error of at most 0.0003.
Values sent between devices are 32-bit elements; how exact they have to be, the bound alone decides.
No kernel may reach another device: no remote copies, remote signals or barrier semaphores. Data moves between devices by JAX's collectives and lax.ppermute only.
A program may use at most 64 MiB of HBM per device.

v0:
```python
import jax
import jax.numpy as jnp
from jax import lax
from jax.sharding import PartitionSpec as P

ITERS = 2


highest = lax.Precision.HIGHEST


def with_halo(x, sides, width):
    for axis, dim in sides:
        devices, length = (lax.axis_size(axis), x.shape[dim])
        up = [(i, (i + 1) % devices) for i in range(devices - 1)]
        down = [(j, i) for i, j in up]
        last = lax.slice_in_dim(x, length - width, length, axis=dim)
        leading = lax.slice_in_dim(x, 0, width, axis=dim)
        before = lax.ppermute(last, axis, up)
        after = lax.ppermute(leading, axis, down)
        x = jnp.concatenate([before, x, after], axis=dim)
    return x


def shrink(values, amount):
    return jnp.sign(values) * jnp.maximum(jnp.abs(values) - amount, 0.0)


def row_rim(values, block_size):
    return with_halo(values, (("row", 0),), block_size)


def col_rim(values, block_size):
    return with_halo(values, (("col", 1),), block_size)


def apply_left(masked, padded_rows, block_count):
    block_size = masked.shape[2]
    width = padded_rows.shape[1]
    blocks = padded_rows.reshape(block_count + 2, block_size, width)
    accumulated = jnp.zeros((block_count, block_size, width), jnp.float32)
    for slot_index in range(3):
        accumulated = accumulated + jnp.einsum(
            "rij,rjn->rin",
            masked[:, slot_index],
            blocks[slot_index : slot_index + block_count],
            precision=highest,
        )
    return accumulated.reshape(block_count * block_size, width)


def apply_right(masked, padded_cols, block_count):
    block_size = masked.shape[2]
    height = padded_cols.shape[0]
    blocks = padded_cols.reshape(height, block_count + 2, block_size)
    accumulated = jnp.zeros((height, block_count, block_size), jnp.float32)
    for slot_index in range(3):
        accumulated = accumulated + jnp.einsum(
            "njb,jab->nja",
            blocks[:, slot_index : slot_index + block_count],
            masked[:, slot_index],
            precision=highest,
        )
    return accumulated.reshape(height, block_count * block_size)


def adjoint_left(padded_factor, padded_rows, block_count):
    block_size = padded_factor.shape[2]
    width = padded_rows.shape[1]
    blocks = padded_rows.reshape(block_count + 2, block_size, width)
    accumulated = jnp.zeros((block_count, block_size, width), jnp.float32)
    for slot_index in range(3):
        first = 2 - slot_index
        accumulated = accumulated + jnp.einsum(
            "cij,cin->cjn",
            padded_factor[first : first + block_count, slot_index],
            blocks[first : first + block_count],
            precision=highest,
        )
    return accumulated.reshape(block_count * block_size, width)


def adjoint_right(padded_factor, padded_cols, block_count):
    block_size = padded_factor.shape[2]
    height = padded_cols.shape[0]
    blocks = padded_cols.reshape(height, block_count + 2, block_size)
    accumulated = jnp.zeros((height, block_count, block_size), jnp.float32)
    for slot_index in range(3):
        first = 2 - slot_index
        accumulated = accumulated + jnp.einsum(
            "nca,cab->ncb",
            blocks[:, first : first + block_count],
            padded_factor[first : first + block_count, slot_index],
            precision=highest,
        )
    return accumulated.reshape(height, block_count * block_size)


def per_device(source_map, observed, factor_x, band_x, factor_y, band_y, step_size, threshold):
    block_size = factor_x.shape[2]
    row_blocks = factor_x.shape[0]
    col_blocks = factor_y.shape[0]
    masked_x = factor_x * band_x.astype(jnp.float32)[:, :, None, None]
    masked_y = factor_y * band_y.astype(jnp.float32)[:, :, None, None]
    padded_fx = with_halo(masked_x, (("row", 0),), 1)
    padded_fy = with_halo(masked_y, (("col", 0),), 1)
    current = source_map
    for iteration in range(ITERS):
        left_product = col_rim(
            apply_left(masked_x, row_rim(current, block_size), row_blocks), block_size
        )
        forward = apply_right(masked_y, left_product, col_blocks)
        misfit = forward - observed
        adjoint_rows = col_rim(
            adjoint_left(padded_fx, row_rim(misfit, block_size), row_blocks), block_size
        )
        gradient = adjoint_right(padded_fy, adjoint_rows, col_blocks)
        current = shrink(current - step_size[0] * gradient, threshold[0])
    return current


def solution(mesh):
    in_specs = (
        P("row", "col"),
        P("row", "col"),
        P("row", None, None, None),
        P("row", None),
        P("col", None, None, None),
        P("col", None),
        P(),
        P(),
    )
    out_specs = P("row", "col")
    return jax.shard_map(
        per_device, mesh=mesh, in_specs=in_specs, out_specs=out_specs, check_vma=False
    )
```

profile of v0, /device:TPU:48, one launch (start us, length us, event | category | flops | bytes accessed | tf_op | source)
XLA Modules:
  0.0 252.3 jit_solution(13688070491049294652)
XLA Ops:
  1.1 2.6 %collective-permute-start.2 = (f32[256,256]{1,0:T(8,128)S(1)}, f32[256,256]{1,0:T(8,128)S(1)}, u32[]{:S(2)}, u32[]{:S(2)}) collective-permute-start(f32[256,256]{1,0:T(8,128)S(1)} %get-tuple-element.23), channel_id=1, source_target_pairs={{0,32},{32,64},{64,96},{96,128},{128,160},{160,192},{192,224},{224... | collective-permute-start | bytes 786440 | tf_op jit(solution)/shard_map/ppermute | solution.py:19
  3.7 3.3 %collective-permute-start.3 = (f32[256,256]{1,0:T(8,128)S(1)}, f32[256,256]{1,0:T(8,128)}, u32[]{:S(2)}, u32[]{:S(2)}) collective-permute-start(f32[256,256]{1,0:T(8,128)S(1)} %get-tuple-element.24), channel_id=1, source_target_pairs={{32,0},{64,32},{96,64},{128,96},{160,128},{192,160},{224,192},{256... | collective-permute-start | bytes 786440 | tf_op jit(solution)/shard_map/ppermute | solution.py:20
  10.7 3.3 %collective-permute-start.1 = (f32[1,3,256,256]{3,2,0,1:T(8,128)}, f32[1,3,256,256]{3,2,0,1:T(8,128)}, u32[]{:S(2)}, u32[]{:S(2)}) collective-permute-start(f32[1,3,256,256]{3,2,0,1:T(8,128)} %get-tuple-element.7), channel_id=1, source_target_pairs={{32,0},{64,32},{96,64},{128,96},{160,128},{192,160},{224,192},{256... | collective-permute-start | bytes 2359304 | tf_op jit(solution)/shard_map/ppermute | solution.py:20
  13.9 3.1 %collective-permute-start.7 = (f32[1,3,256,256]{3,2,0,1:T(8,128)}, f32[1,3,256,256]{3,2,0,1:T(8,128)}, u32[]{:S(2)}, u32[]{:S(2)}) collective-permute-start(f32[1,3,256,256]{3,2,0,1:T(8,128)} %get-tuple-element.8), channel_id=1, source_target_pairs={{0,32},{32,64},{64,96},{96,128},{128,160},{160,192},{192,224},{224... | collective-permute-start | bytes 2359304 | tf_op jit(solution)/shard_map/ppermute | solution.py:19
  17.7 2.7 %collective-permute-done.3 = f32[256,256]{1,0:T(8,128)} collective-permute-done((f32[256,256]{1,0:T(8,128)S(1)}, f32[256,256]{1,0:T(8,128)}, u32[]{:S(2)}, u32[]{:S(2)}) %collective-permute-start.3) | collective-permute-done | bytes 262176 | tf_op jit(solution)/shard_map/ppermute | solution.py:20
  22.8 8.0 %collective-permute-start.5 = (f32[512,256]{1,0:T(8,128)S(1)}, f32[512,256]{1,0:T(8,128)}, u32[]{:S(2)}, u32[]{:S(2)}) collective-permute-start(f32[512,256]{1,0:T(8,128)S(1)} %bitcast.129), channel_id=1, source_target_pairs={{1,0},{2,1},{3,2},{4,3},{5,4},{6,5},{7,6},{8,7},{9,8},{10,9},{11,1... | collective-permute-start | bytes 1572872 | tf_op jit(solution)/shard_map/ppermute | solution.py:20
  37.4 7.5 %collective-permute-done.5 = f32[512,256]{1,0:T(8,128)} collective-permute-done((f32[512,256]{1,0:T(8,128)S(1)}, f32[512,256]{1,0:T(8,128)}, u32[]{:S(2)}, u32[]{:S(2)}) %collective-permute-start.5) | collective-permute-done | bytes 524320 | tf_op jit(solution)/shard_map/ppermute | solution.py:20
  46.6 19.5 %collective-permute-done.4 = f32[512,256]{1,0:T(8,128)} collective-permute-done((f32[512,256]{1,0:T(8,128)S(1)}, f32[512,256]{1,0:T(8,128)}, u32[]{:S(2)}, u32[]{:S(2)}) %collective-permute-start.4) | collective-permute-done | bytes 524320 | tf_op jit(solution)/shard_map/ppermute | solution.py:19
  68.8 26.3 %collective-permute-start.6 = (f32[256,256]{0,1:T(8,128)S(1)}, f32[256,256]{0,1:T(8,128)S(1)}, u32[]{:S(2)}, u32[]{:S(2)}) collective-permute-start(f32[256,256]{0,1:T(8,128)S(1)} %get-tuple-element.19), channel_id=1, source_target_pairs={{32,0},{64,32},{96,64},{128,96},{160,128},{192,160},{224,192},{256... | collective-permute-start | bytes 786440 | tf_op jit(solution)/shard_map/ppermute | solution.py:20
  97.1 2.9 %fusion.22 = f32[2,256,256]{2,1,0:T(8,128)} fusion(f32[2,256,256]{2,1,0:T(8,128)} %bitcast.135, f32[2,3,256,256]{3,2,0,1:T(8,128)S(1)} %copy_multiply_fusion), kind=kOutput, calls=%fused_computation.47 | convolution fusion | flops 402653184 | bytes 1572864 | tf_op jit(solution)/shard_map/cij,cin->cjn/dot_general | solution.py:74
  101.9 2.1 fusion.18
  107.1 2.1 copy.36
  109.2 2.3 fusion.37
  113.5 2.4 collective-permute-start.11
  115.9 9.4 %collective-permute-start.9 = (f32[512,256]{1,0:T(8,128)}, f32[512,256]{1,0:T(8,128)}, u32[]{:S(2)}, u32[]{:S(2)}) collective-permute-start(f32[512,256]{1,0:T(8,128)} %bitcast.21), channel_id=1, source_target_pairs={{1,0},{2,1},{3,2},{4,3},{5,4},{6,5},{7,6},{8,7},{9,8},{10,9},{11,1... | collective-permute-start | bytes 1572872 | tf_op jit(solution)/shard_map/ppermute | solution.py:20
  126.7 2.1 fusion.30
  128.8 8.5 %collective-permute-done.11 = f32[512,256]{1,0:T(8,128)} collective-permute-done((f32[512,256]{1,0:T(8,128)}, f32[512,256]{1,0:T(8,128)}, u32[]{:S(2)}, u32[]{:S(2)}) %collective-permute-start.11) | collective-permute-done | bytes 524320 | tf_op jit(solution)/shard_map/ppermute | solution.py:19
  137.4 2.2 fusion.27
  140.5 2.4 maximum_multiply_fusion.1
  145.8 7.3 %collective-permute-start.13 = (f32[256,256]{0,1:T(8,128)}, f32[256,256]{0,1:T(8,128)S(1)}, u32[]{:S(2)}, u32[]{:S(2)}) collective-permute-start(f32[256,256]{0,1:T(8,128)} %get-tuple-element.15), channel_id=1, source_target_pairs={{32,0},{64,32},{96,64},{128,96},{160,128},{192,160},{224,192},{256... | collective-permute-start | bytes 786440 | tf_op jit(solution)/shard_map/ppermute | solution.py:20
  158.5 2.1 copy.39
  165.1 9.1 %collective-permute-start.15 = (f32[512,256]{1,0:T(8,128)S(1)}, f32[512,256]{1,0:T(8,128)S(1)}, u32[]{:S(2)}, u32[]{:S(2)}) collective-permute-start(f32[512,256]{1,0:T(8,128)S(1)} %bitcast.144), channel_id=1, source_target_pairs={{1,0},{2,1},{3,2},{4,3},{5,4},{6,5},{7,6},{8,7},{9,8},{10,9},{11,1... | collective-permute-start | bytes 1572872 | tf_op jit(solution)/shard_map/ppermute | solution.py:20
  176.8 9.7 %collective-permute-done.15 = f32[512,256]{1,0:T(8,128)S(1)} collective-permute-done((f32[512,256]{1,0:T(8,128)S(1)}, f32[512,256]{1,0:T(8,128)S(1)}, u32[]{:S(2)}, u32[]{:S(2)}) %collective-permute-start.15) | collective-permute-done | bytes 524320 | tf_op jit(solution)/shard_map/ppermute | solution.py:20
  187.1 12.0 %collective-permute-done.14 = f32[512,256]{1,0:T(8,128)S(1)} collective-permute-done((f32[512,256]{1,0:T(8,128)S(1)}, f32[512,256]{1,0:T(8,128)S(1)}, u32[]{:S(2)}, u32[]{:S(2)}) %collective-permute-start.14) | collective-permute-done | bytes 524320 | tf_op jit(solution)/shard_map/ppermute | solution.py:19
  201.6 6.8 %collective-permute-start.16 = (f32[256,256]{0,1:T(8,128)}, f32[256,256]{0,1:T(8,128)S(1)}, u32[]{:S(2)}, u32[]{:S(2)}) collective-permute-start(f32[256,256]{0,1:T(8,128)} %get-tuple-element.11), channel_id=1, source_target_pairs={{32,0},{64,32},{96,64},{128,96},{160,128},{192,160},{224,192},{256... | collective-permute-start | bytes 786440 | tf_op jit(solution)/shard_map/ppermute | solution.py:20
  210.4 2.9 %fusion.20 = f32[2,256,256]{2,1,0:T(8,128)} fusion(f32[2,256,256]{2,1,0:T(8,128)} %bitcast.136, f32[2,3,256,256]{3,2,0,1:T(8,128)S(1)} %copy_multiply_fusion), kind=kOutput, calls=%fused_computation.45 | convolution fusion | flops 402653184 | bytes 1572864 | tf_op jit(solution)/shard_map/cij,cin->cjn/dot_general | solution.py:74
  214.8 2.2 collective-permute-done.17
  218.8 2.2 fusion.38
  223.1 2.1 fusion
  227.1 9.9 %collective-permute-start.18 = (f32[512,256]{1,0:T(8,128)S(1)}, f32[512,256]{1,0:T(8,128)S(1)}, u32[]{:S(2)}, u32[]{:S(2)}) collective-permute-start(f32[512,256]{1,0:T(8,128)S(1)} %bitcast.133), channel_id=1, source_target_pairs={{1,0},{2,1},{3,2},{4,3},{5,4},{6,5},{7,6},{8,7},{9,8},{10,9},{11,1... | collective-permute-start | bytes 1572872 | tf_op jit(solution)/shard_map/ppermute | solution.py:20
  238.0 9.1 %collective-permute-done.19 = f32[512,256]{1,0:T(8,128)S(1)} collective-permute-done((f32[512,256]{1,0:T(8,128)S(1)}, f32[512,256]{1,0:T(8,128)S(1)}, u32[]{:S(2)}, u32[]{:S(2)}) %collective-permute-start.19) | collective-permute-done | bytes 524320 | tf_op jit(solution)/shard_map/ppermute | solution.py:19
  249.1 2.2 maximum_multiply_fusion
  (85 shorter events, 60.5 us)
Async XLA Ops:
  1.1 16.6 %collective-permute-start.2 = (f32[256,256]{1,0:T(8,128)S(1)}, f32[256,256]{1,0:T(8,128)S(1)}, u32[]{:S(2)}, u32[]{:S(2)}) collective-permute-start(f32[256,256]{1,0:T(8,128)S(1)} %get-tuple-element.23), channel_id=1, source_target_pairs={{0,32},{32,64},{64,96},{96,128},{128,160},{160,192},{192,224},{224... | collective-permute-start | bytes 786440 | tf_op jit(solution)/shard_map/ppermute | solution.py:19
  3.7 16.7 %collective-permute-start.3 = (f32[256,256]{1,0:T(8,128)S(1)}, f32[256,256]{1,0:T(8,128)}, u32[]{:S(2)}, u32[]{:S(2)}) collective-permute-start(f32[256,256]{1,0:T(8,128)S(1)} %get-tuple-element.24), channel_id=1, source_target_pairs={{32,0},{64,32},{96,64},{128,96},{160,128},{192,160},{224,192},{256... | collective-permute-start | bytes 786440 | tf_op jit(solution)/shard_map/ppermute | solution.py:20
  9.3 7.7 %copy-start = (f32[512,256]{1,0:T(8,128)S(1)}, f32[512,256]{1,0:T(8,128)}, u32[]{:S(2)}) copy-start(f32[512,256]{1,0:T(8,128)} %param.8) | copy-start | bytes 1572868
  10.7 89.3 %collective-permute-start.1 = (f32[1,3,256,256]{3,2,0,1:T(8,128)}, f32[1,3,256,256]{3,2,0,1:T(8,128)}, u32[]{:S(2)}, u32[]{:S(2)}) collective-permute-start(f32[1,3,256,256]{3,2,0,1:T(8,128)} %get-tuple-element.7), channel_id=1, source_target_pairs={{32,0},{64,32},{96,64},{128,96},{160,128},{192,160},{224,192},{256... | collective-permute-start | bytes 2359304 | tf_op jit(solution)/shard_map/ppermute | solution.py:20
  13.9 88.0 %collective-permute-start.7 = (f32[1,3,256,256]{3,2,0,1:T(8,128)}, f32[1,3,256,256]{3,2,0,1:T(8,128)}, u32[]{:S(2)}, u32[]{:S(2)}) collective-permute-start(f32[1,3,256,256]{3,2,0,1:T(8,128)} %get-tuple-element.8), channel_id=1, source_target_pairs={{0,32},{32,64},{64,96},{96,128},{128,160},{160,192},{192,224},{224... | collective-permute-start | bytes 2359304 | tf_op jit(solution)/shard_map/ppermute | solution.py:19
  22.1 8.7 %copy-start.12 = (s32[1,3]{1,0:T(1,128)S(1)}, s32[1,3]{1,0:T(1,128)}, u32[]{:S(2)}) copy-start(s32[1,3]{1,0:T(1,128)} %param.13) | copy-start | bytes 40
  22.1 10.6 %copy-start.11 = (f32[1,3,256,256]{3,2,1,0:T(8,128)S(1)}, f32[1,3,256,256]{3,2,1,0:T(8,128)}, u32[]{:S(2)}) copy-start(f32[1,3,256,256]{3,2,1,0:T(8,128)} %param.12) | copy-start | bytes 2359300
  22.8 22.2 %collective-permute-start.5 = (f32[512,256]{1,0:T(8,128)S(1)}, f32[512,256]{1,0:T(8,128)}, u32[]{:S(2)}, u32[]{:S(2)}) collective-permute-start(f32[512,256]{1,0:T(8,128)S(1)} %bitcast.129), channel_id=1, source_target_pairs={{1,0},{2,1},{3,2},{4,3},{5,4},{6,5},{7,6},{8,7},{9,8},{10,9},{11,1... | collective-permute-start | bytes 1572872 | tf_op jit(solution)/shard_map/ppermute | solution.py:20
  30.7 35.3 %collective-permute-start.4 = (f32[512,256]{1,0:T(8,128)S(1)}, f32[512,256]{1,0:T(8,128)}, u32[]{:S(2)}, u32[]{:S(2)}) collective-permute-start(f32[512,256]{1,0:T(8,128)S(1)} %bitcast.130), channel_id=1, source_target_pairs={{0,1},{1,2},{2,3},{3,4},{4,5},{5,6},{6,7},{7,8},{8,9},{9,10},{10,1... | collective-permute-start | bytes 1572872 | tf_op jit(solution)/shard_map/ppermute | solution.py:19
  32.8 96.0 %collective-permute-start.10 = (f32[1,3,256,256]{3,2,1,0:T(8,128)S(1)}, f32[1,3,256,256]{3,2,1,0:T(8,128)}, u32[]{:S(2)}, u32[]{:S(2)}) collective-permute-start(f32[1,3,256,256]{3,2,1,0:T(8,128)S(1)} %broadcast_multiply_fusion), channel_id=1, source_target_pairs={{0,1},{1,2},{2,3},{3,4},{4,5},{5,6},{6,7},{7,8},{8,9},{9,10},{10,1... | collective-permute-start | bytes 2359304 | tf_op jit(solution)/shard_map/ppermute | solution.py:19
  36.8 29.3 %copy-start.4 = (f32[512,256]{0,1:T(8,128)S(1)}, f32[512,256]{0,1:T(8,128)}, u32[]{:S(2)}) copy-start(f32[512,256]{0,1:T(8,128)} %copy.11) | copy-start | bytes 1572868
  68.8 35.2 %collective-permute-start.6 = (f32[256,256]{0,1:T(8,128)S(1)}, f32[256,256]{0,1:T(8,128)S(1)}, u32[]{:S(2)}, u32[]{:S(2)}) collective-permute-start(f32[256,256]{0,1:T(8,128)S(1)} %get-tuple-element.19), channel_id=1, source_target_pairs={{32,0},{64,32},{96,64},{128,96},{160,128},{192,160},{224,192},{256... | collective-permute-start | bytes 786440 | tf_op jit(solution)/shard_map/ppermute | solution.py:20
  95.2 8.8 %collective-permute-start.8 = (f32[256,256]{0,1:T(8,128)S(1)}, f32[256,256]{0,1:T(8,128)S(1)}, u32[]{:S(2)}, u32[]{:S(2)}) collective-permute-start(f32[256,256]{0,1:T(8,128)S(1)} %get-tuple-element.20), channel_id=1, source_target_pairs={{0,32},{32,64},{64,96},{96,128},{128,160},{160,192},{192,224},{224... | collective-permute-start | bytes 786440 | tf_op jit(solution)/shard_map/ppermute | solution.py:19
  100.0 39.6 %collective-permute-start = (f32[1,3,256,256]{3,2,1,0:T(8,128)S(1)}, f32[1,3,256,256]{3,2,1,0:T(8,128)}, u32[]{:S(2)}, u32[]{:S(2)}) collective-permute-start(f32[1,3,256,256]{3,2,1,0:T(8,128)S(1)} %broadcast_multiply_fusion), channel_id=1, source_target_pairs={{1,0},{2,1},{3,2},{4,3},{5,4},{6,5},{7,6},{8,7},{9,8},{10,9},{11,1... | collective-permute-start | bytes 2359304 | tf_op jit(solution)/shard_map/ppermute | solution.py:20
  107.1 4.5 %copy-start.1 = (f32[2,256,256]{2,1,0:T(8,128)S(1)}, f32[2,256,256]{2,1,0:T(8,128)}, u32[]{:S(2)}) copy-start(f32[2,256,256]{2,1,0:T(8,128)} %get-tuple-element.5) | copy-start | bytes 1572868
  109.2 2.4 copy-start.6
  109.2 2.4 copy-start.8
  113.5 23.9 %collective-permute-start.11 = (f32[512,256]{1,0:T(8,128)}, f32[512,256]{1,0:T(8,128)}, u32[]{:S(2)}, u32[]{:S(2)}) collective-permute-start(f32[512,256]{1,0:T(8,128)} %bitcast.21), channel_id=1, source_target_pairs={{0,1},{1,2},{2,3},{3,4},{4,5},{5,6},{6,7},{7,8},{8,9},{9,10},{10,1... | collective-permute-start | bytes 1572872 | tf_op jit(solution)/shard_map/ppermute | solution.py:19
  115.9 24.6 %collective-permute-start.9 = (f32[512,256]{1,0:T(8,128)}, f32[512,256]{1,0:T(8,128)}, u32[]{:S(2)}, u32[]{:S(2)}) collective-permute-start(f32[512,256]{1,0:T(8,128)} %bitcast.21), channel_id=1, source_target_pairs={{1,0},{2,1},{3,2},{4,3},{5,4},{6,5},{7,6},{8,7},{9,8},{10,9},{11,1... | collective-permute-start | bytes 1572872 | tf_op jit(solution)/shard_map/ppermute | solution.py:20
  143.9 11.9 %collective-permute-start.12 = (f32[256,256]{0,1:T(8,128)}, f32[256,256]{0,1:T(8,128)S(1)}, u32[]{:S(2)}, u32[]{:S(2)}) collective-permute-start(f32[256,256]{0,1:T(8,128)} %get-tuple-element.16), channel_id=1, source_target_pairs={{0,32},{32,64},{64,96},{96,128},{128,160},{160,192},{192,224},{224... | collective-permute-start | bytes 786440 | tf_op jit(solution)/shard_map/ppermute | solution.py:19
  145.8 11.5 %collective-permute-start.13 = (f32[256,256]{0,1:T(8,128)}, f32[256,256]{0,1:T(8,128)S(1)}, u32[]{:S(2)}, u32[]{:S(2)}) collective-permute-start(f32[256,256]{0,1:T(8,128)} %get-tuple-element.15), channel_id=1, source_target_pairs={{32,0},{64,32},{96,64},{128,96},{160,128},{192,160},{224,192},{256... | collective-permute-start | bytes 786440 | tf_op jit(solution)/shard_map/ppermute | solution.py:20
  158.5 4.2 %copy-start.9 = (f32[2,256,256]{2,1,0:T(8,128)S(1)}, f32[2,256,256]{2,1,0:T(8,128)}, u32[]{:S(2)}) copy-start(f32[2,256,256]{2,1,0:T(8,128)} %fusion.21) | copy-start | bytes 1572868
  165.1 34.0 %copy-start.5 = (f32[512,256]{0,1:T(8,128)S(1)}, f32[512,256]{0,1:T(8,128)}, u32[]{:S(2)}) copy-start(f32[512,256]{0,1:T(8,128)} %copy.11) | copy-start | bytes 1572868
  165.1 21.4 %collective-permute-start.15 = (f32[512,256]{1,0:T(8,128)S(1)}, f32[512,256]{1,0:T(8,128)S(1)}, u32[]{:S(2)}, u32[]{:S(2)}) collective-permute-start(f32[512,256]{1,0:T(8,128)S(1)} %bitcast.144), channel_id=1, source_target_pairs={{1,0},{2,1},{3,2},{4,3},{5,4},{6,5},{7,6},{8,7},{9,8},{10,9},{11,1... | collective-permute-start | bytes 1572872 | tf_op jit(solution)/shard_map/ppermute | solution.py:20
  174.2 24.9 %collective-permute-start.14 = (f32[512,256]{1,0:T(8,128)S(1)}, f32[512,256]{1,0:T(8,128)S(1)}, u32[]{:S(2)}, u32[]{:S(2)}) collective-permute-start(f32[512,256]{1,0:T(8,128)S(1)} %bitcast.145), channel_id=1, source_target_pairs={{0,1},{1,2},{2,3},{3,4},{4,5},{5,6},{6,7},{7,8},{8,9},{9,10},{10,1... | collective-permute-start | bytes 1572872 | tf_op jit(solution)/shard_map/ppermute | solution.py:19
  201.6 13.2 %collective-permute-start.16 = (f32[256,256]{0,1:T(8,128)}, f32[256,256]{0,1:T(8,128)S(1)}, u32[]{:S(2)}, u32[]{:S(2)}) collective-permute-start(f32[256,256]{0,1:T(8,128)} %get-tuple-element.11), channel_id=1, source_target_pairs={{32,0},{64,32},{96,64},{128,96},{160,128},{192,160},{224,192},{256... | collective-permute-start | bytes 786440 | tf_op jit(solution)/shard_map/ppermute | solution.py:20
  208.4 8.5 %collective-permute-start.17 = (f32[256,256]{0,1:T(8,128)}, f32[256,256]{0,1:T(8,128)S(1)}, u32[]{:S(2)}, u32[]{:S(2)}) collective-permute-start(f32[256,256]{0,1:T(8,128)} %get-tuple-element.12), channel_id=1, source_target_pairs={{0,32},{32,64},{64,96},{96,128},{128,160},{160,192},{192,224},{224... | collective-permute-start | bytes 786440 | tf_op jit(solution)/shard_map/ppermute | solution.py:19
  213.3 5.6 %copy-start.3 = (f32[2,256,256]{2,1,0:T(8,128)S(1)}, f32[2,256,256]{2,1,0:T(8,128)}, u32[]{:S(2)}) copy-start(f32[2,256,256]{2,1,0:T(8,128)} %get-tuple-element.6) | copy-start | bytes 1572868
  218.8 4.2 %copy-start.2 = (f32[2,256,256]{2,1,0:T(8,128)S(1)}, f32[2,256,256]{2,1,0:T(8,128)}, u32[]{:S(2)}) copy-start(f32[2,256,256]{2,1,0:T(8,128)} %get-tuple-element.5) | copy-start | bytes 1572868
  218.8 4.2 %copy-start.7 = (f32[2,256,256]{2,1,0:T(8,128)S(1)}, f32[2,256,256]{2,1,0:T(8,128)}, u32[]{:S(2)}) copy-start(f32[2,256,256]{2,1,0:T(8,128)} %fusion.20) | copy-start | bytes 1572868
  225.2 21.9 %collective-permute-start.19 = (f32[512,256]{1,0:T(8,128)S(1)}, f32[512,256]{1,0:T(8,128)S(1)}, u32[]{:S(2)}, u32[]{:S(2)}) collective-permute-start(f32[512,256]{1,0:T(8,128)S(1)} %bitcast.132), channel_id=1, source_target_pairs={{0,1},{1,2},{2,3},{3,4},{4,5},{5,6},{6,7},{7,8},{8,9},{9,10},{10,1... | collective-permute-start | bytes 1572872 | tf_op jit(solution)/shard_map/ppermute | solution.py:19
  227.1 22.0 %collective-permute-start.18 = (f32[512,256]{1,0:T(8,128)S(1)}, f32[512,256]{1,0:T(8,128)S(1)}, u32[]{:S(2)}, u32[]{:S(2)}) collective-permute-start(f32[512,256]{1,0:T(8,128)S(1)} %bitcast.133), channel_id=1, source_target_pairs={{1,0},{2,1},{3,2},{4,3},{5,4},{6,5},{7,6},{8,7},{9,8},{10,9},{11,1... | collective-permute-start | bytes 1572872 | tf_op jit(solution)/shard_map/ppermute | solution.py:20
  (1 other events, 1.8 us)
where the time goes:
time: 254 us; the launch traced here: 252 us
  starting transfers between devices  107 us (42%)
  waiting for transfers between devices  76.2 us (30%)
  matrix products  37.8 us (15%)
  local copies, waits for them, and re-layouts  21.1 us (8%)
  other arithmetic  8.65 us (3%)
    ppermute x10, starting transfers between devices, with_halo(): after = lax.ppermute(leading, axis, down)  85.3 us
    ppermute x10, waiting for transfers between devices, with_halo(): before = lax.ppermute(last, axis, up)  52.3 us
    ppermute x10, waiting for transfers between devices, with_halo(): after = lax.ppermute(leading, axis, down)  23.9 us
    ppermute x10, starting transfers between devices, with_halo(): before = lax.ppermute(last, axis, up)  21.5 us
    dot_general x6, matrix products, adjoint_left(): jnp.einsum('cij,cin->cjn', padded_factor[first:first + block_count, slot_...  14.2 us
    dot_general x6, matrix products, adjoint_right(): jnp.einsum('nca,cab->ncb', blocks[:, first:first + block_count], padded_f...  11.9 us
    slice x6, local copies, waits for them, and re-layouts, adjoint_left(): blocks[first:first + block_count]  9.21 us
    dot_general x6, matrix products, apply_right(): jnp.einsum('njb,jab->nja', blocks[:, slot_index:slot_index + block_count]...  5.86 us
  transfers between devices with their start and end apart: 20, of which 12 were waited for; matrix products, arithmetic and copies ran while one was open for 16% of the time, Pallas kernels for 0%

commit v1 on v0

v1 whole, which is shorter than its diff:
```python
import jax
import jax.numpy as jnp
from jax import lax
from jax.experimental import pallas as pl
from jax.experimental.pallas import tpu as pltpu
from jax.sharding import PartitionSpec as P

f32 = jnp.float32
bf16 = jnp.bfloat16
VMEM = pl.BlockSpec(memory_space=pltpu.VMEM)
SMEM = pl.BlockSpec(memory_space=pltpu.SMEM)


def split(x):
    hi = x.astype(bf16)
    return hi, (x - hi.astype(f32)).astype(bf16)


def dot3(xh, xl, yh, yl):
    mm = lambda a, b: jnp.dot(a, b, preferred_element_type=f32)
    return mm(xh, yh) + (mm(xh, yl) + mm(xl, yh))


def soft(v, h):
    return v - jnp.minimum(jnp.maximum(v, -h), h)


def call(body, ins, outs, flops, scratch=(), limit=24 << 20):
    size = lambda a: a.size * a.dtype.itemsize
    return pl.pallas_call(
        body,
        out_shape=[jax.ShapeDtypeStruct(s, d) for s, d in outs],
        in_specs=[SMEM if a.size < 64 else VMEM for a in ins],
        out_specs=[VMEM for _ in outs],
        scratch_shapes=list(scratch),
        compiler_params=pltpu.CompilerParams(vmem_limit_bytes=limit),
        cost_estimate=pl.CostEstimate(
            flops=flops, bytes_accessed=sum(size(a) for a in ins), transcendentals=0
        ),
    )(*ins)


def prepare(fx, bx, fy, by, pos):
    blk = fx.shape[2]

    def body(fx, bx, fy, by, pos, axh, axl, atxh, atxl, byh, byl, byth, bytl):
        row, rows, col, cols = pos[0], pos[1], pos[2], pos[3]

        def put(v, k, plain, trans):
            s = slice(k * blk, (k + 1) * blk)
            plain[0][:, s], plain[1][:, s] = split(v)
            trans[0][s, :], trans[1][s, :] = split(v.T)

        for r in range(2):
            for s in range(3):
                m = bx[r, s].astype(f32)
                if (r, s) == (0, 0):
                    m = jnp.where(row == 0, 0.0, m)
                if (r, s) == (1, 2):
                    m = jnp.where(row == rows - 1, 0.0, m)
                put(fx[r, s] * m, s, (axh.at[r], axl.at[r]), (atxh.at[r], atxl.at[r]))
        first = jnp.where(col % 2 == 0, 2, 0)
        for k, s in enumerate((first, 1, 2 - first)):
            m = by[0, s].astype(f32)
            m = jnp.where((s == 0) & (col == 0), 0.0, m)
            m = jnp.where((s == 2) & (col == cols - 1), 0.0, m)
            put(fy[0, s] * m, k, (byh, byl), (byth, bytl))

    outs = [((2, blk, 3 * blk), bf16)] * 2 + [((2, 3 * blk, blk), bf16)] * 2
    outs += [((blk, 3 * blk), bf16)] * 2 + [((3 * blk, blk), bf16)] * 2
    o = call(body, (fx, bx, fy, by, pos), outs, 1 << 24)
    return o[0:2], o[2:4], o[4:6], o[6:8]


def left(ax, xs, u):
    blk = xs[0].shape[0] // 4
    for r in range(2):
        s = slice(r * blk, (r + 3) * blk)
        u[r * blk : (r + 1) * blk, :] = dot3(ax[0][r], ax[1][r], xs[0][s, :], xs[1][s, :])


def apply_left(x, up, down, ax):
    blk, n = up.shape

    def body(x, up, down, axh, axl, u, xh, xl):
        for t, v in enumerate((up[...], x[:blk, :], x[blk:, :], down[...])):
            s = slice(t * blk, (t + 1) * blk)
            xh[s, :], xl[s, :] = split(v)
        left((axh, axl), (xh, xl), u)

    scratch = [pltpu.VMEM((4 * blk, n), bf16)] * 2
    return call(body, (x, up, down, *ax), [(x.shape, f32)], 36 * blk * blk * n, scratch)[0]


def right(ua, u, ub, observed, byt, by):
    m, blk = u.shape
    chunk = 256

    def body(ua, u, ub, obs, byth, bytl, byh, byl, qa, q, qb):
        for i in range(m // chunk):
            r = slice(i * chunk, (i + 1) * chunk)
            acc = -obs[r, :]
            for k, v in enumerate((ua, u, ub)):
                s = slice(k * blk, (k + 1) * blk)
                vh, vl = split(v[r, :])
                acc = acc + dot3(vh, vl, byth[s, :], bytl[s, :])
            mh, ml = split(acc)
            for k, o in enumerate((qa, q, qb)):
                s = slice(k * blk, (k + 1) * blk)
                o[r, :] = dot3(mh, ml, byh[:, s], byl[:, s])

    return call(body, (ua, u, ub, observed, *byt, *by), [(u.shape, f32)] * 3, 72 * m * blk * blk)


def back_left(q, ra, rb, atx, merged):
    m, n = q.shape
    blk = m // 2

    def body(q, ra, rb, ah, al, *outs):
        p = []
        for r in range(2):
            s = slice(r * blk, (r + 1) * blk)
            vh, vl = split(q[s, :] + ra[s, :] + rb[s, :])
            p.append(dot3(ah[r], al[r], vh, vl))
        p0 = p[0][:blk]
        p1 = p[0][blk : 2 * blk] + p[1][:blk]
        p2 = p[0][2 * blk :] + p[1][blk : 2 * blk]
        p3 = p[1][2 * blk :]
        if merged:
            top, bottom = outs
            top[:blk, :], top[blk:, :] = p0, p1
            bottom[:blk, :], bottom[blk:, :] = p2, p3
        else:
            top, mid, bottom = outs
            top[...], bottom[...] = p0, p3
            mid[:blk, :], mid[blk:, :] = p1, p2

    outs = [((m, n), f32)] * 2 if merged else [((blk, n), f32), ((m, n), f32), ((blk, n), f32)]
    return call(body, (q, ra, rb, *atx), outs, 36 * blk * blk * n)


def update_left(top, bottom, rtop, rbottom, x, up, down, sc, ax):
    blk, n = up.shape

    def body(top, bottom, rtop, rbottom, x, up, down, sc, axh, axl, xn, u, xh, xl):
        step, h = sc[0], sc[1]
        lo, hi = slice(0, blk), slice(blk, 2 * blk)
        parts = ((up[...], top, rtop, lo), (x[lo, :], top, rtop, hi))
        parts += ((x[hi, :], bottom, rbottom, lo), (down[...], bottom, rbottom, hi))
        for t, (v, a, b, s) in enumerate(parts):
            new = soft(v - step * (a[s, :] + b[s, :]), h)
            if t in (1, 2):
                xn[(t - 1) * blk : t * blk, :] = new
            d = slice(t * blk, (t + 1) * blk)
            xh[d, :], xl[d, :] = split(new)
        left((axh, axl), (xh, xl), u)

    scratch = [pltpu.VMEM((4 * blk, n), bf16)] * 2
    ins = (top, bottom, rtop, rbottom, x, up, down, sc, *ax)
    return call(body, ins, [(x.shape, f32)] * 2, 36 * blk * blk * n, scratch)


def update(mid, rup, rdown, x, sc):
    blk, n = rup.shape

    def body(mid, rup, rdown, x, sc, o):
        step, h = sc[0], sc[1]
        lo, hi = slice(0, blk), slice(blk, 2 * blk)
        for s, r in ((lo, rup), (hi, rdown)):
            o[s, :] = soft(x[s, :] - step * (mid[s, :] + r[...]), h)

    return call(body, (mid, rup, rdown, x, sc), [(x.shape, f32)], 1 << 20)[0]


def per_device(x, observed, fx, bx, fy, by, step_size, threshold):
    blk = fx.shape[2]
    rows, cols = lax.axis_size("row"), lax.axis_size("col")
    downward = [(i, i + 1) for i in range(rows - 1)]
    upward = [(i + 1, i) for i in range(rows - 1)]
    pairs = []
    for first in (0, 1):
        forth = [(i, i + 1) for i in range(first, cols - 1, 2)]
        pairs.append(forth + [(j, i) for i, j in forth])

    def row_swap(to_up, to_down):
        from_up = lax.ppermute(to_down, "row", downward)
        from_down = lax.ppermute(to_up, "row", upward)
        return from_up, from_down

    def col_swap(a, b):
        rb = lax.ppermute(b, "col", pairs[1])
        ra = lax.ppermute(a, "col", pairs[0])
        return ra, rb

    pos = jnp.stack([lax.axis_index("row"), rows, lax.axis_index("col"), cols]).astype(jnp.int32)
    sc = jnp.concatenate([step_size, threshold])
    up, down = row_swap(x[:blk], x[blk:])
    ax, atx, byf, byt = prepare(fx, bx, fy, by, pos)
    u = apply_left(x, up, down, ax)
    ua, ub = col_swap(u, u)
    qa, q, qb = right(ua, u, ub, observed, byt, byf)
    ra, rb = col_swap(qa, qb)
    top, bottom = back_left(q, ra, rb, atx, True)
    rtop, rbottom = row_swap(top, bottom)
    x, u = update_left(top, bottom, rtop, rbottom, x, up, down, sc, ax)
    ua, ub = col_swap(u, u)
    qa, q, qb = right(ua, u, ub, observed, byt, byf)
    ra, rb = col_swap(qa, qb)
    top, mid, bottom = back_left(q, ra, rb, atx, False)
    rup, rdown = row_swap(top, bottom)
    return update(mid, rup, rdown, x, sc)


def solution(mesh):
    in_specs = (
        P("row", "col"),
        P("row", "col"),
        P("row", None, None, None),
        P("row", None),
        P("col", None, None, None),
        P("col", None),
        P(),
        P(),
    )
    return jax.shard_map(
        per_device, mesh=mesh, in_specs=in_specs, out_specs=P("row", "col"), check_vma=False
    )
```

time: 254 us -> 164 us (0.65)
  the two profiles are of different devices: /device:TPU:48 before, /device:TPU:56 now
where the time goes in v1:
time: 164 us
  starting transfers between devices  83.2 us (51%)
  waiting for transfers between devices  62.8 us (38%)
  Pallas kernels  10.8 us (7%)
  local copies, waits for them, and re-layouts  5 us (3%)
    ppermute x4, starting transfers between devices, col_swap(): rb = lax.ppermute(b, 'col', pairs[1])  40.1 us
    ppermute x3, waiting for transfers between devices, row_swap(): from_down = lax.ppermute(to_up, 'row', upward)  27.9 us
    ppermute x4, waiting for transfers between devices, col_swap(): rb = lax.ppermute(b, 'col', pairs[1])  24.2 us
    ppermute x3, starting transfers between devices, row_swap(): from_up = lax.ppermute(to_down, 'row', downward)  19.6 us
    ppermute x3, starting transfers between devices, row_swap(): from_down = lax.ppermute(to_up, 'row', upward)  15.9 us
    pallas_call x8, Pallas kernels, call(): pl.pallas_call(body, out_shape=[jax.ShapeDtypeStruct(s, d) for s, d in ou...  10.8 us
    ppermute x3, waiting for transfers between devices, row_swap(): from_up = lax.ppermute(to_down, 'row', downward)  10.7 us
    ppermute x4, starting transfers between devices, col_swap(): ra = lax.ppermute(a, 'col', pairs[0])  7.68 us
  transfers between devices with their start and end apart: 14, of which 9 were waited for; matrix products, arithmetic and copies ran while one was open for 0% of the time, Pallas kernels for 1%

profile of v1, /device:TPU:56, one launch (start us, length us, event | category | flops | bytes accessed | tf_op | source)
XLA Modules:
  0.0 163.6 jit_solution(8027068841591932973)
XLA Ops:
  0.0 1.1 fusion
  1.1 3.3 %collective-permute-start.1 = (f32[256,256]{1,0:T(8,128)S(1)}, f32[256,256]{1,0:T(8,128)S(1)}, u32[]{:S(2)}, u32[]{:S(2)}) collective-permute-start(f32[256,256]{1,0:T(8,128)S(1)} %get-tuple-element.47), channel_id=1, source_target_pairs={{32,0},{64,32},{96,64},{128,96},{160,128},{192,160},{224,192},{256... | collective-permute-start | bytes 786440 | tf_op jit(solution)/shard_map/ppermute | solution.py:187
  4.4 5.3 %collective-permute-start = (f32[256,256]{1,0:T(8,128)S(1)}, f32[256,256]{1,0:T(8,128)S(1)}, u32[]{:S(2)}, u32[]{:S(2)}) collective-permute-start(f32[256,256]{1,0:T(8,128)S(1)} %get-tuple-element.48), channel_id=1, source_target_pairs={{0,32},{32,64},{64,96},{96,128},{128,160},{160,192},{192,224},{224... | collective-permute-start | bytes 786440 | tf_op jit(solution)/shard_map/ppermute | solution.py:186
  9.8 1.4 copy-done.1
  11.2 1.1 copy-done.2
  13.6 1.3 shard_map.82
  16.4 11.5 %collective-permute-start.3 = (f32[512,256]{1,0:T(8,128)S(1)}, f32[512,256]{1,0:T(8,128)S(1)}, u32[]{:S(2)}, u32[]{:S(2)}) collective-permute-start(f32[512,256]{1,0:T(8,128)S(1)} %shard_map.83.u), channel_id=1, source_target_pairs={{1,2},{3,4},{5,6},{7,8},{9,10},{11,12},{13,14},{15,16},{17,18},{19... | collective-permute-start | bytes 1572872 | tf_op jit(solution)/shard_map/ppermute | solution.py:191
  27.9 1.9 %collective-permute-start.2 = (f32[512,256]{1,0:T(8,128)S(1)}, f32[512,256]{1,0:T(8,128)S(1)}, u32[]{:S(2)}, u32[]{:S(2)}) collective-permute-start(f32[512,256]{1,0:T(8,128)S(1)} %shard_map.83.u), channel_id=1, source_target_pairs={{0,1},{2,3},{4,5},{6,7},{8,9},{10,11},{12,13},{14,15},{16,17},{18,... | collective-permute-start | bytes 1572872 | tf_op jit(solution)/shard_map/ppermute | solution.py:192
  29.8 5.0 %collective-permute-done.3.ub = f32[512,256]{1,0:T(8,128)S(1)} collective-permute-done((f32[512,256]{1,0:T(8,128)S(1)}, f32[512,256]{1,0:T(8,128)S(1)}, u32[]{:S(2)}, u32[]{:S(2)}) %collective-permute-start.3) | collective-permute-done | bytes 524320 | tf_op jit(solution)/shard_map/ppermute | solution.py:191
  34.8 2.0 %shard_map.84 = (f32[512,256]{1,0:T(8,128)S(1)}, f32[512,256]{1,0:T(8,128)S(1)}, f32[512,256]{1,0:T(8,128)S(1)}) custom-call(f32[512,256]{1,0:T(8,128)S(1)} %collective-permute-done.2.ua, f32[512,256]{1,0:T(8,128)S(1)} %shard_map.83.u, f32[512,256]{1,0:T(8,128)S(1)} %collective-permute-done.3.ub, f32[512,256]{1,0:T(8,128)S(1)} %copy-done.5, ...), custom_call_target="tpu_custom_call" | custom-call | flops 2415919104 | bytes 3670016 | tf_op jit(solution)/shard_map/pallas_call | solution.py:30
  36.9 1.9 %collective-permute-start.4 = (f32[512,256]{1,0:T(8,128)S(1)}, f32[512,256]{1,0:T(8,128)S(1)}, u32[]{:S(2)}, u32[]{:S(2)}) collective-permute-start(f32[512,256]{1,0:T(8,128)S(1)} %get-tuple-element.33), channel_id=1, source_target_pairs={{0,1},{2,3},{4,5},{6,7},{8,9},{10,11},{12,13},{14,15},{16,17},{18,... | collective-permute-start | bytes 1572872 | tf_op jit(solution)/shard_map/ppermute | solution.py:192
  38.8 9.7 %collective-permute-start.5 = (f32[512,256]{1,0:T(8,128)S(1)}, f32[512,256]{1,0:T(8,128)S(1)}, u32[]{:S(2)}, u32[]{:S(2)}) collective-permute-start(f32[512,256]{1,0:T(8,128)S(1)} %get-tuple-element.34), channel_id=1, source_target_pairs={{1,2},{3,4},{5,6},{7,8},{9,10},{11,12},{13,14},{15,16},{17,18},{19... | collective-permute-start | bytes 1572872 | tf_op jit(solution)/shard_map/ppermute | solution.py:191
  48.5 6.9 %collective-permute-done.5.rb = f32[512,256]{1,0:T(8,128)S(1)} collective-permute-done((f32[512,256]{1,0:T(8,128)S(1)}, f32[512,256]{1,0:T(8,128)S(1)}, u32[]{:S(2)}, u32[]{:S(2)}) %collective-permute-start.5) | collective-permute-done | bytes 524320 | tf_op jit(solution)/shard_map/ppermute | solution.py:191
  55.4 0.8 shard_map.85
  56.3 5.4 %collective-permute-start.7 = (f32[512,256]{1,0:T(8,128)S(1)}, f32[512,256]{1,0:T(8,128)S(1)}, u32[]{:S(2)}, u32[]{:S(2)}) collective-permute-start(f32[512,256]{1,0:T(8,128)S(1)} %get-tuple-element.37.top), channel_id=1, source_target_pairs={{32,0},{64,32},{96,64},{128,96},{160,128},{192,160},{224,192},{256... | collective-permute-start | bytes 1572872 | tf_op jit(solution)/shard_map/ppermute | solution.py:187
  61.7 4.5 %collective-permute-start.6 = (f32[512,256]{1,0:T(8,128)S(1)}, f32[512,256]{1,0:T(8,128)S(1)}, u32[]{:S(2)}, u32[]{:S(2)}) collective-permute-start(f32[512,256]{1,0:T(8,128)S(1)} %get-tuple-element.38.bottom), channel_id=1, source_target_pairs={{0,32},{32,64},{64,96},{96,128},{128,160},{160,192},{192,224},{224... | collective-permute-start | bytes 1572872 | tf_op jit(solution)/shard_map/ppermute | solution.py:186
  67.6 8.2 %collective-permute-done.7.rbottom = f32[512,256]{1,0:T(8,128)S(1)} collective-permute-done((f32[512,256]{1,0:T(8,128)S(1)}, f32[512,256]{1,0:T(8,128)S(1)}, u32[]{:S(2)}, u32[]{:S(2)}) %collective-permute-start.7) | collective-permute-done | bytes 524320 | tf_op jit(solution)/shard_map/ppermute | solution.py:187
  75.8 7.7 %collective-permute-done.6.rtop = f32[512,256]{1,0:T(8,128)S(1)} collective-permute-done((f32[512,256]{1,0:T(8,128)S(1)}, f32[512,256]{1,0:T(8,128)S(1)}, u32[]{:S(2)}, u32[]{:S(2)}) %collective-permute-start.6) | collective-permute-done | bytes 524320 | tf_op jit(solution)/shard_map/ppermute | solution.py:186
  83.5 1.5 shard_map.86
  85.0 9.5 %collective-permute-start.9 = (f32[512,256]{1,0:T(8,128)S(1)}, f32[512,256]{1,0:T(8,128)S(1)}, u32[]{:S(2)}, u32[]{:S(2)}) collective-permute-start(f32[512,256]{1,0:T(8,128)S(1)} %get-tuple-element.39.u), channel_id=1, source_target_pairs={{1,2},{3,4},{5,6},{7,8},{9,10},{11,12},{13,14},{15,16},{17,18},{19... | collective-permute-start | bytes 1572872 | tf_op jit(solution)/shard_map/ppermute | solution.py:191
  94.5 1.9 %collective-permute-start.8 = (f32[512,256]{1,0:T(8,128)S(1)}, f32[512,256]{1,0:T(8,128)S(1)}, u32[]{:S(2)}, u32[]{:S(2)}) collective-permute-start(f32[512,256]{1,0:T(8,128)S(1)} %get-tuple-element.39.u), channel_id=1, source_target_pairs={{0,1},{2,3},{4,5},{6,7},{8,9},{10,11},{12,13},{14,15},{16,17},{18,... | collective-permute-start | bytes 1572872 | tf_op jit(solution)/shard_map/ppermute | solution.py:192
  96.4 5.2 %collective-permute-done.9.ub = f32[512,256]{1,0:T(8,128)S(1)} collective-permute-done((f32[512,256]{1,0:T(8,128)S(1)}, f32[512,256]{1,0:T(8,128)S(1)}, u32[]{:S(2)}, u32[]{:S(2)}) %collective-permute-start.9) | collective-permute-done | bytes 524320 | tf_op jit(solution)/shard_map/ppermute | solution.py:191
  101.6 2.0 %shard_map.87 = (f32[512,256]{1,0:T(8,128)S(1)}, f32[512,256]{1,0:T(8,128)S(1)}, f32[512,256]{1,0:T(8,128)S(1)}) custom-call(f32[512,256]{1,0:T(8,128)S(1)} %collective-permute-done.8.ua, f32[512,256]{1,0:T(8,128)S(1)} %get-tuple-element.39.u, f32[512,256]{1,0:T(8,128)S(1)} %collective-permute-done.9.ub, f32[512,256]{1,0:T(8,128)S(1)} %copy-done.5, ...), custom_call_target="tpu_custom_call" | custom-call | flops 2415919104 | bytes 3670016 | tf_op jit(solution)/shard_map/pallas_call | solution.py:30
  103.7 1.9 %collective-permute-start.10 = (f32[512,256]{1,0:T(8,128)S(1)}, f32[512,256]{1,0:T(8,128)S(1)}, u32[]{:S(2)}, u32[]{:S(2)}) collective-permute-start(f32[512,256]{1,0:T(8,128)S(1)} %get-tuple-element.41), channel_id=1, source_target_pairs={{0,1},{2,3},{4,5},{6,7},{8,9},{10,11},{12,13},{14,15},{16,17},{18,... | collective-permute-start | bytes 1572872 | tf_op jit(solution)/shard_map/ppermute | solution.py:192
  105.6 9.5 %collective-permute-start.11 = (f32[512,256]{1,0:T(8,128)S(1)}, f32[512,256]{1,0:T(8,128)S(1)}, u32[]{:S(2)}, u32[]{:S(2)}) collective-permute-start(f32[512,256]{1,0:T(8,128)S(1)} %get-tuple-element.42), channel_id=1, source_target_pairs={{1,2},{3,4},{5,6},{7,8},{9,10},{11,12},{13,14},{15,16},{17,18},{19... | collective-permute-start | bytes 1572872 | tf_op jit(solution)/shard_map/ppermute | solution.py:191
  115.1 7.0 %collective-permute-done.11.rb = f32[512,256]{1,0:T(8,128)S(1)} collective-permute-done((f32[512,256]{1,0:T(8,128)S(1)}, f32[512,256]{1,0:T(8,128)S(1)}, u32[]{:S(2)}, u32[]{:S(2)}) %collective-permute-start.11) | collective-permute-done | bytes 524320 | tf_op jit(solution)/shard_map/ppermute | solution.py:191
  122.1 0.8 shard_map.88
  123.0 9.8 %collective-permute-start.12 = (f32[256,256]{1,0:T(8,128)S(1)}, f32[256,256]{1,0:T(8,128)S(1)}, u32[]{:S(2)}, u32[]{:S(2)}) collective-permute-start(f32[256,256]{1,0:T(8,128)S(1)} %get-tuple-element.44), channel_id=1, source_target_pairs={{0,32},{32,64},{64,96},{96,128},{128,160},{160,192},{192,224},{224... | collective-permute-start | bytes 786440 | tf_op jit(solution)/shard_map/ppermute | solution.py:186
  132.8 7.2 %collective-permute-start.13 = (f32[256,256]{1,0:T(8,128)S(1)}, f32[256,256]{1,0:T(8,128)S(1)}, u32[]{:S(2)}, u32[]{:S(2)}) collective-permute-start(f32[256,256]{1,0:T(8,128)S(1)} %get-tuple-element.45), channel_id=1, source_target_pairs={{32,0},{64,32},{96,64},{128,96},{160,128},{192,160},{224,192},{256... | collective-permute-start | bytes 786440 | tf_op jit(solution)/shard_map/ppermute | solution.py:187
  140.0 2.4 %collective-permute-done.12.rup = f32[256,256]{1,0:T(8,128)S(1)} collective-permute-done((f32[256,256]{1,0:T(8,128)S(1)}, f32[256,256]{1,0:T(8,128)S(1)}, u32[]{:S(2)}, u32[]{:S(2)}) %collective-permute-start.12) | collective-permute-done | bytes 262176 | tf_op jit(solution)/shard_map/ppermute | solution.py:186
  142.4 19.7 %collective-permute-done.13.rdown = f32[256,256]{1,0:T(8,128)S(1)} collective-permute-done((f32[256,256]{1,0:T(8,128)S(1)}, f32[256,256]{1,0:T(8,128)S(1)}, u32[]{:S(2)}, u32[]{:S(2)}) %collective-permute-start.13) | collective-permute-done | bytes 262176 | tf_op jit(solution)/shard_map/ppermute | solution.py:187
  162.1 1.5 shard_map.89
  (19 shorter events, 2.9 us)
Async XLA Ops:
  0.0 15.6 %copy-start = (f32[512,256]{1,0:T(8,128)S(1)}, f32[512,256]{1,0:T(8,128)}, u32[]{:S(2)}) copy-start(f32[512,256]{1,0:T(8,128)} %x.3) | copy-start | bytes 1572868
  1.1 13.8 %collective-permute-start.1 = (f32[256,256]{1,0:T(8,128)S(1)}, f32[256,256]{1,0:T(8,128)S(1)}, u32[]{:S(2)}, u32[]{:S(2)}) collective-permute-start(f32[256,256]{1,0:T(8,128)S(1)} %get-tuple-element.47), channel_id=1, source_target_pairs={{32,0},{64,32},{96,64},{128,96},{160,128},{192,160},{224,192},{256... | collective-permute-start | bytes 786440 | tf_op jit(solution)/shard_map/ppermute | solution.py:187
  4.4 11.2 %collective-permute-start = (f32[256,256]{1,0:T(8,128)S(1)}, f32[256,256]{1,0:T(8,128)S(1)}, u32[]{:S(2)}, u32[]{:S(2)}) collective-permute-start(f32[256,256]{1,0:T(8,128)S(1)} %get-tuple-element.48), channel_id=1, source_target_pairs={{0,32},{32,64},{64,96},{96,128},{128,160},{160,192},{192,224},{224... | collective-permute-start | bytes 786440 | tf_op jit(solution)/shard_map/ppermute | solution.py:186
  9.8 1.4 copy-start.1
  11.2 1.1 copy-start.2
  12.3 0.7 copy-start.3
  13.0 0.7 copy-start.4
  15.6 19.3 %copy-start.5 = (f32[512,256]{1,0:T(8,128)S(1)}, f32[512,256]{1,0:T(8,128)}, u32[]{:S(2)}) copy-start(f32[512,256]{1,0:T(8,128)} %obs.3) | copy-start | bytes 1572868
  16.4 18.4 %collective-permute-start.3 = (f32[512,256]{1,0:T(8,128)S(1)}, f32[512,256]{1,0:T(8,128)S(1)}, u32[]{:S(2)}, u32[]{:S(2)}) collective-permute-start(f32[512,256]{1,0:T(8,128)S(1)} %shard_map.83.u), channel_id=1, source_target_pairs={{1,2},{3,4},{5,6},{7,8},{9,10},{11,12},{13,14},{15,16},{17,18},{19... | collective-permute-start | bytes 1572872 | tf_op jit(solution)/shard_map/ppermute | solution.py:191
  27.9 7.0 %collective-permute-start.2 = (f32[512,256]{1,0:T(8,128)S(1)}, f32[512,256]{1,0:T(8,128)S(1)}, u32[]{:S(2)}, u32[]{:S(2)}) collective-permute-start(f32[512,256]{1,0:T(8,128)S(1)} %shard_map.83.u), channel_id=1, source_target_pairs={{0,1},{2,3},{4,5},{6,7},{8,9},{10,11},{12,13},{14,15},{16,17},{18,... | collective-permute-start | bytes 1572872 | tf_op jit(solution)/shard_map/ppermute | solution.py:192
  36.9 11.6 %collective-permute-start.4 = (f32[512,256]{1,0:T(8,128)S(1)}, f32[512,256]{1,0:T(8,128)S(1)}, u32[]{:S(2)}, u32[]{:S(2)}) collective-permute-start(f32[512,256]{1,0:T(8,128)S(1)} %get-tuple-element.33), channel_id=1, source_target_pairs={{0,1},{2,3},{4,5},{6,7},{8,9},{10,11},{12,13},{14,15},{16,17},{18,... | collective-permute-start | bytes 1572872 | tf_op jit(solution)/shard_map/ppermute | solution.py:192
  38.8 16.6 %collective-permute-start.5 = (f32[512,256]{1,0:T(8,128)S(1)}, f32[512,256]{1,0:T(8,128)S(1)}, u32[]{:S(2)}, u32[]{:S(2)}) collective-permute-start(f32[512,256]{1,0:T(8,128)S(1)} %get-tuple-element.34), channel_id=1, source_target_pairs={{1,2},{3,4},{5,6},{7,8},{9,10},{11,12},{13,14},{15,16},{17,18},{19... | collective-permute-start | bytes 1572872 | tf_op jit(solution)/shard_map/ppermute | solution.py:191
  56.3 19.5 %collective-permute-start.7 = (f32[512,256]{1,0:T(8,128)S(1)}, f32[512,256]{1,0:T(8,128)S(1)}, u32[]{:S(2)}, u32[]{:S(2)}) collective-permute-start(f32[512,256]{1,0:T(8,128)S(1)} %get-tuple-element.37.top), channel_id=1, source_target_pairs={{32,0},{64,32},{96,64},{128,96},{160,128},{192,160},{224,192},{256... | collective-permute-start | bytes 1572872 | tf_op jit(solution)/shard_map/ppermute | solution.py:187
  61.7 21.8 %collective-permute-start.6 = (f32[512,256]{1,0:T(8,128)S(1)}, f32[512,256]{1,0:T(8,128)S(1)}, u32[]{:S(2)}, u32[]{:S(2)}) collective-permute-start(f32[512,256]{1,0:T(8,128)S(1)} %get-tuple-element.38.bottom), channel_id=1, source_target_pairs={{0,32},{32,64},{64,96},{96,128},{128,160},{160,192},{192,224},{224... | collective-permute-start | bytes 1572872 | tf_op jit(solution)/shard_map/ppermute | solution.py:186
  85.0 16.6 %collective-permute-start.9 = (f32[512,256]{1,0:T(8,128)S(1)}, f32[512,256]{1,0:T(8,128)S(1)}, u32[]{:S(2)}, u32[]{:S(2)}) collective-permute-start(f32[512,256]{1,0:T(8,128)S(1)} %get-tuple-element.39.u), channel_id=1, source_target_pairs={{1,2},{3,4},{5,6},{7,8},{9,10},{11,12},{13,14},{15,16},{17,18},{19... | collective-permute-start | bytes 1572872 | tf_op jit(solution)/shard_map/ppermute | solution.py:191
  94.5 7.1 %collective-permute-start.8 = (f32[512,256]{1,0:T(8,128)S(1)}, f32[512,256]{1,0:T(8,128)S(1)}, u32[]{:S(2)}, u32[]{:S(2)}) collective-permute-start(f32[512,256]{1,0:T(8,128)S(1)} %get-tuple-element.39.u), channel_id=1, source_target_pairs={{0,1},{2,3},{4,5},{6,7},{8,9},{10,11},{12,13},{14,15},{16,17},{18,... | collective-permute-start | bytes 1572872 | tf_op jit(solution)/shard_map/ppermute | solution.py:192
  103.7 11.4 %collective-permute-start.10 = (f32[512,256]{1,0:T(8,128)S(1)}, f32[512,256]{1,0:T(8,128)S(1)}, u32[]{:S(2)}, u32[]{:S(2)}) collective-permute-start(f32[512,256]{1,0:T(8,128)S(1)} %get-tuple-element.41), channel_id=1, source_target_pairs={{0,1},{2,3},{4,5},{6,7},{8,9},{10,11},{12,13},{14,15},{16,17},{18,... | collective-permute-start | bytes 1572872 | tf_op jit(solution)/shard_map/ppermute | solution.py:192
  105.6 16.5 %collective-permute-start.11 = (f32[512,256]{1,0:T(8,128)S(1)}, f32[512,256]{1,0:T(8,128)S(1)}, u32[]{:S(2)}, u32[]{:S(2)}) collective-permute-start(f32[512,256]{1,0:T(8,128)S(1)} %get-tuple-element.42), channel_id=1, source_target_pairs={{1,2},{3,4},{5,6},{7,8},{9,10},{11,12},{13,14},{15,16},{17,18},{19... | collective-permute-start | bytes 1572872 | tf_op jit(solution)/shard_map/ppermute | solution.py:191
  123.0 19.4 %collective-permute-start.12 = (f32[256,256]{1,0:T(8,128)S(1)}, f32[256,256]{1,0:T(8,128)S(1)}, u32[]{:S(2)}, u32[]{:S(2)}) collective-permute-start(f32[256,256]{1,0:T(8,128)S(1)} %get-tuple-element.44), channel_id=1, source_target_pairs={{0,32},{32,64},{64,96},{96,128},{128,160},{160,192},{192,224},{224... | collective-permute-start | bytes 786440 | tf_op jit(solution)/shard_map/ppermute | solution.py:186
  132.8 29.3 %collective-permute-start.13 = (f32[256,256]{1,0:T(8,128)S(1)}, f32[256,256]{1,0:T(8,128)S(1)}, u32[]{:S(2)}, u32[]{:S(2)}) collective-permute-start(f32[256,256]{1,0:T(8,128)S(1)} %get-tuple-element.45), channel_id=1, source_target_pairs={{32,0},{64,32},{96,64},{128,96},{160,128},{192,160},{224,192},{256... | collective-permute-start | bytes 786440 | tf_op jit(solution)/shard_map/ppermute | solution.py:187

commit v2 on v1

--- a/solution.py
+++ b/solution.py
@@ -9,6 +9,7 @@
 bf16 = jnp.bfloat16
 VMEM = pl.BlockSpec(memory_space=pltpu.VMEM)
 SMEM = pl.BlockSpec(memory_space=pltpu.SMEM)
+CHUNK = 256
 
 
 def split(x):
@@ -43,7 +44,7 @@
 def prepare(fx, bx, fy, by, pos):
     blk = fx.shape[2]
 
-    def body(fx, bx, fy, by, pos, axh, axl, atxh, atxl, byh, byl, byth, bytl):
+    def body(fx, bx, fy, by, pos, axh, axl, atxh, atxl, byh, byl, byth, bytl, fb):
         row, rows, col, cols = pos[0], pos[1], pos[2], pos[3]
 
         def put(v, k, plain, trans):
@@ -64,12 +65,15 @@
             m = by[0, s].astype(f32)
             m = jnp.where((s == 0) & (col == 0), 0.0, m)
             m = jnp.where((s == 2) & (col == cols - 1), 0.0, m)
-            put(fy[0, s] * m, k, (byh, byl), (byth, bytl))
+            v = fy[0, s] * m
+            put(v, k, (byh, byl), (byth, bytl))
+        fb[...] = v
 
     outs = [((2, blk, 3 * blk), bf16)] * 2 + [((2, 3 * blk, blk), bf16)] * 2
     outs += [((blk, 3 * blk), bf16)] * 2 + [((3 * blk, blk), bf16)] * 2
+    outs += [((blk, blk), f32)]
     o = call(body, (fx, bx, fy, by, pos), outs, 1 << 24)
-    return o[0:2], o[2:4], o[4:6], o[6:8]
+    return o[0:2], o[2:4], o[4:6], o[6:8], o[8]
 
 
 def left(ax, xs, u):
@@ -92,36 +96,55 @@
     return call(body, (x, up, down, *ax), [(x.shape, f32)], 36 * blk * blk * n, scratch)[0]
 
 
-def right(ua, u, ub, observed, byt, by):
+def near_misfit(u, ua, observed, byt, *below):
     m, blk = u.shape
-    chunk = 256
-
-    def body(ua, u, ub, obs, byth, bytl, byh, byl, qa, q, qb):
-        for i in range(m // chunk):
-            r = slice(i * chunk, (i + 1) * chunk)
+
+    def body(u, ua, obs, byth, bytl, *rest):
+        w = rest[-1]
+        for v in rest[:-1]:
+            w[m:, :] = v[...]
+        for i in range(0, m, CHUNK):
+            r = slice(i, i + CHUNK)
             acc = -obs[r, :]
-            for k, v in enumerate((ua, u, ub)):
+            for k, v in enumerate((ua, u)):
                 s = slice(k * blk, (k + 1) * blk)
-                vh, vl = split(v[r, :])
-                acc = acc + dot3(vh, vl, byth[s, :], bytl[s, :])
+                acc = acc + dot3(*split(v[r, :]), byth[s, :], bytl[s, :])
+            w[r, :] = acc
+
+    out = (m + sum(v.shape[0] for v in below), blk)
+    return call(body, (u, ua, observed, *byt, *below), [(out, f32)], 24 * m * blk * blk)[0]
+
+
+def full_misfit(w, ub, byt, by):
+    m, blk = ub.shape
+
+    def body(w, ub, byth, bytl, byh, byl, qa, q):
+        b = slice(2 * blk, 3 * blk)
+        for i in range(0, m, CHUNK):
+            r = slice(i, i + CHUNK)
+            acc = w[r, :] + dot3(*split(ub[r, :]), byth[b, :], bytl[b, :])
             mh, ml = split(acc)
-            for k, o in enumerate((qa, q, qb)):
+            for k, o in enumerate((qa, q)):
                 s = slice(k * blk, (k + 1) * blk)
                 o[r, :] = dot3(mh, ml, byh[:, s], byl[:, s])
 
-    return call(body, (ua, u, ub, observed, *byt, *by), [(u.shape, f32)] * 3, 72 * m * blk * blk)
-
-
-def back_left(q, ra, rb, atx, merged):
+    return call(body, (w, ub, *byt, *by), [(ub.shape, f32)] * 2, 36 * m * blk * blk)
+
+
+def back(q, ra, wb, u, fb, atx, merged):
     m, n = q.shape
     blk = m // 2
 
-    def body(q, ra, rb, ah, al, *outs):
+    def body(q, ra, wb, u, fb, ah, al, *outs):
+        g = fb[fb.shape[0] - blk :, :]
+        gh, gl = split(g)
+        th, tl = split(g.T)
         p = []
         for r in range(2):
             s = slice(r * blk, (r + 1) * blk)
-            vh, vl = split(q[s, :] + ra[s, :] + rb[s, :])
-            p.append(dot3(ah[r], al[r], vh, vl))
+            other = wb[s, :] + dot3(*split(u[s, :]), th, tl)
+            v = q[s, :] + ra[s, :] + dot3(*split(other), gh, gl)
+            p.append(dot3(ah[r], al[r], *split(v)))
         p0 = p[0][:blk]
         p1 = p[0][blk : 2 * blk] + p[1][:blk]
         p2 = p[0][2 * blk :] + p[1][blk : 2 * blk]
@@ -136,7 +159,7 @@
             mid[:blk, :], mid[blk:, :] = p1, p2
 
     outs = [((m, n), f32)] * 2 if merged else [((blk, n), f32), ((m, n), f32), ((blk, n), f32)]
-    return call(body, (q, ra, rb, *atx), outs, 36 * blk * blk * n)
+    return call(body, (q, ra, wb, u, fb, *atx), outs, 60 * blk * blk * n)
 
 
 def update_left(top, bottom, rtop, rbottom, x, up, down, sc, ax):
@@ -187,26 +210,31 @@
         from_down = lax.ppermute(to_up, "row", upward)
         return from_up, from_down
 
-    def col_swap(a, b):
-        rb = lax.ppermute(b, "col", pairs[1])
-        ra = lax.ppermute(a, "col", pairs[0])
-        return ra, rb
+    def chip_swap(a):
+        return lax.ppermute(a, "col", pairs[0])
+
+    def col_swap(b):
+        return lax.ppermute(b, "col", pairs[1])
+
+    def columns(u, fb, merged):
+        ua = chip_swap(u)
+        ub = col_swap(u)
+        w = near_misfit(u, ua, observed, byt, fb if merged else jnp.zeros((8, fb.shape[1]), f32))
+        wb = col_swap(w)
+        qa, q = full_misfit(w, ub, byt, byf)
+        ra = chip_swap(qa)
+        fb = wb if merged else fb
+        return (*back(q, ra, wb, u, fb, atx, merged), fb)
 
     pos = jnp.stack([lax.axis_index("row"), rows, lax.axis_index("col"), cols]).astype(jnp.int32)
     sc = jnp.concatenate([step_size, threshold])
     up, down = row_swap(x[:blk], x[blk:])
-    ax, atx, byf, byt = prepare(fx, bx, fy, by, pos)
+    ax, atx, byf, byt, fb = prepare(fx, bx, fy, by, pos)
     u = apply_left(x, up, down, ax)
-    ua, ub = col_swap(u, u)
-    qa, q, qb = right(ua, u, ub, observed, byt, byf)
-    ra, rb = col_swap(qa, qb)
-    top, bottom = back_left(q, ra, rb, atx, True)
+    top, bottom, fb = columns(u, fb, True)
     rtop, rbottom = row_swap(top, bottom)
     x, u = update_left(top, bottom, rtop, rbottom, x, up, down, sc, ax)
-    ua, ub = col_swap(u, u)
-    qa, q, qb = right(ua, u, ub, observed, byt, byf)
-    ra, rb = col_swap(qa, qb)
-    top, mid, bottom = back_left(q, ra, rb, atx, False)
+    top, mid, bottom, _ = columns(u, fb, False)
     rup, rdown = row_swap(top, bottom)
     return update(mid, rup, rdown, x, sc)
 

time: 164 us -> 149 us (0.909)
  the two profiles are of different devices: /device:TPU:56 before, /device:TPU:58 now
where the time goes in v2:
time: 149 us; the launch traced here: 148 us
  waiting for transfers between devices  67.5 us (45%)
  starting transfers between devices  60.5 us (41%)
  Pallas kernels  13.3 us (9%)
  local copies, waits for them, and re-layouts  5.01 us (3%)
  between operations  1.52 us (1%)
    ppermute x3, waiting for transfers between devices, row_swap(): from_down = lax.ppermute(to_up, 'row', upward)  28 us
    ppermute x4, starting transfers between devices, col_swap(): return lax.ppermute(b, 'col', pairs[1])  25.7 us
    ppermute x4, waiting for transfers between devices, col_swap(): return lax.ppermute(b, 'col', pairs[1])  22.5 us
    ppermute x3, starting transfers between devices, row_swap(): from_down = lax.ppermute(to_up, 'row', upward)  14.8 us
    pallas_call x10, Pallas kernels, call(): pl.pallas_call(body, out_shape=[jax.ShapeDtypeStruct(s, d) for s, d in ou...  13.3 us
    ppermute x3, waiting for transfers between devices, row_swap(): from_up = lax.ppermute(to_down, 'row', downward)  13.2 us
    ppermute x3, starting transfers between devices, row_swap(): from_up = lax.ppermute(to_down, 'row', downward)  12.3 us
    ppermute x4, starting transfers between devices, chip_swap(): return lax.ppermute(a, 'col', pairs[0])  7.68 us
  transfers between devices with their start and end apart: 14, of which 11 were waited for; matrix products, arithmetic and copies ran while one was open for 0% of the time, Pallas kernels for 3%

profile of v2, /device:TPU:58, one launch (start us, length us, event | category | flops | bytes accessed | tf_op | source)
XLA Modules:
  0.0 148.0 jit_solution(13607087250011496355)
XLA Ops:
  1.1 5.8 %collective-permute-start = (f32[256,256]{1,0:T(8,128)S(1)}, f32[256,256]{1,0:T(8,128)S(1)}, u32[]{:S(2)}, u32[]{:S(2)}) collective-permute-start(f32[256,256]{1,0:T(8,128)S(1)} %get-tuple-element.46), channel_id=1, source_target_pairs={{0,32},{32,64},{64,96},{96,128},{128,160},{160,192},{192,224},{224... | collective-permute-start | bytes 786440 | tf_op jit(solution)/shard_map/ppermute | solution.py:209
  6.9 1.9 %collective-permute-start.1 = (f32[256,256]{1,0:T(8,128)S(1)}, f32[256,256]{1,0:T(8,128)S(1)}, u32[]{:S(2)}, u32[]{:S(2)}) collective-permute-start(f32[256,256]{1,0:T(8,128)S(1)} %get-tuple-element.45), channel_id=1, source_target_pairs={{32,0},{64,32},{96,64},{128,96},{160,128},{192,160},{224,192},{256... | collective-permute-start | bytes 786440 | tf_op jit(solution)/shard_map/ppermute | solution.py:210
  8.9 1.4 copy-done.1
  10.3 1.1 copy-done.2
  12.8 1.3 shard_map.82
  14.1 5.2 %collective-permute-done.1.down = f32[256,256]{1,0:T(8,128)S(1)} collective-permute-done((f32[256,256]{1,0:T(8,128)S(1)}, f32[256,256]{1,0:T(8,128)S(1)}, u32[]{:S(2)}, u32[]{:S(2)}) %collective-permute-start.1) | collective-permute-done | bytes 262176 | tf_op jit(solution)/shard_map/ppermute | solution.py:210
  20.1 1.9 %collective-permute-start.2 = (f32[512,256]{1,0:T(8,128)S(1)}, f32[512,256]{1,0:T(8,128)S(1)}, u32[]{:S(2)}, u32[]{:S(2)}) collective-permute-start(f32[512,256]{1,0:T(8,128)S(1)} %shard_map.83.u), channel_id=1, source_target_pairs={{0,1},{2,3},{4,5},{6,7},{8,9},{10,11},{12,13},{14,15},{16,17},{18,... | collective-permute-start | bytes 1572872 | tf_op jit(solution)/shard_map/ppermute | solution.py:214
  22.0 11.6 %collective-permute-start.3 = (f32[512,256]{1,0:T(8,128)S(1)}, f32[512,256]{1,0:T(8,128)S(1)}, u32[]{:S(2)}, u32[]{:S(2)}) collective-permute-start(f32[512,256]{1,0:T(8,128)S(1)} %shard_map.83.u), channel_id=1, source_target_pairs={{1,2},{3,4},{5,6},{7,8},{9,10},{11,12},{13,14},{15,16},{17,18},{19... | collective-permute-start | bytes 1572872 | tf_op jit(solution)/shard_map/ppermute | solution.py:217
  34.2 1.9 %collective-permute-start.5 = (f32[768,256]{1,0:T(8,128)S(1)}, f32[768,256]{1,0:T(8,128)S(1)}, u32[]{:S(2)}, u32[]{:S(2)}) collective-permute-start(f32[768,256]{1,0:T(8,128)S(1)} %shard_map.84.w), channel_id=1, source_target_pairs={{1,2},{3,4},{5,6},{7,8},{9,10},{11,12},{13,14},{15,16},{17,18},{19... | collective-permute-start | bytes 2359304 | tf_op jit(solution)/shard_map/ppermute | solution.py:217
  36.1 4.4 %collective-permute-done.3.ub = f32[512,256]{1,0:T(8,128)S(1)} collective-permute-done((f32[512,256]{1,0:T(8,128)S(1)}, f32[512,256]{1,0:T(8,128)S(1)}, u32[]{:S(2)}, u32[]{:S(2)}) %collective-permute-start.3) | collective-permute-done | bytes 524320 | tf_op jit(solution)/shard_map/ppermute | solution.py:217
  41.7 1.9 %collective-permute-start.4 = (f32[512,256]{1,0:T(8,128)S(1)}, f32[512,256]{1,0:T(8,128)S(1)}, u32[]{:S(2)}, u32[]{:S(2)}) collective-permute-start(f32[512,256]{1,0:T(8,128)S(1)} %get-tuple-element.33), channel_id=1, source_target_pairs={{0,1},{2,3},{4,5},{6,7},{8,9},{10,11},{12,13},{14,15},{16,17},{18,... | collective-permute-start | bytes 1572872 | tf_op jit(solution)/shard_map/ppermute | solution.py:214
  43.6 1.9 %collective-permute-done.4.ra = f32[512,256]{1,0:T(8,128)S(1)} collective-permute-done((f32[512,256]{1,0:T(8,128)S(1)}, f32[512,256]{1,0:T(8,128)S(1)}, u32[]{:S(2)}, u32[]{:S(2)}) %collective-permute-start.4) | collective-permute-done | bytes 524320 | tf_op jit(solution)/shard_map/ppermute | solution.py:214
  45.5 8.2 %collective-permute-done.5.wb.fb = f32[768,256]{1,0:T(8,128)S(1)} collective-permute-done((f32[768,256]{1,0:T(8,128)S(1)}, f32[768,256]{1,0:T(8,128)S(1)}, u32[]{:S(2)}, u32[]{:S(2)}) %collective-permute-start.5) | collective-permute-done | bytes 786464 | tf_op jit(solution)/shard_map/ppermute | solution.py:217
  53.6 2.4 %shard_map.86 = (f32[512,256]{1,0:T(8,128)S(1)}, f32[512,256]{1,0:T(8,128)S(1)}) custom-call(f32[512,256]{1,0:T(8,128)S(1)} %get-tuple-element.32.q, f32[512,256]{1,0:T(8,128)S(1)} %collective-permute-done.4.ra, f32[768,256]{1,0:T(8,128)S(1)} %collective-permute-done.5.wb.fb, f32[512,256]{1,0:T(8,128)S(1)} %shard_map.83.u, ...), custom_call_target="tpu_custom_call" | custom-call | flops 1006632960 | bytes 4718592 | tf_op jit(solution)/shard_map/pallas_call | solution.py:31
  56.1 4.6 %collective-permute-start.6 = (f32[512,256]{1,0:T(8,128)S(1)}, f32[512,256]{1,0:T(8,128)S(1)}, u32[]{:S(2)}, u32[]{:S(2)}) collective-permute-start(f32[512,256]{1,0:T(8,128)S(1)} %get-tuple-element.37.bottom), channel_id=1, source_target_pairs={{0,32},{32,64},{64,96},{96,128},{128,160},{160,192},{192,224},{224... | collective-permute-start | bytes 1572872 | tf_op jit(solution)/shard_map/ppermute | solution.py:209
  60.7 9.0 %collective-permute-start.7 = (f32[512,256]{1,0:T(8,128)S(1)}, f32[512,256]{1,0:T(8,128)S(1)}, u32[]{:S(2)}, u32[]{:S(2)}) collective-permute-start(f32[512,256]{1,0:T(8,128)S(1)} %get-tuple-element.36.top), channel_id=1, source_target_pairs={{32,0},{64,32},{96,64},{128,96},{160,128},{192,160},{224,192},{256... | collective-permute-start | bytes 1572872 | tf_op jit(solution)/shard_map/ppermute | solution.py:210
  71.1 5.1 %collective-permute-done.6.rtop = f32[512,256]{1,0:T(8,128)S(1)} collective-permute-done((f32[512,256]{1,0:T(8,128)S(1)}, f32[512,256]{1,0:T(8,128)S(1)}, u32[]{:S(2)}, u32[]{:S(2)}) %collective-permute-start.6) | collective-permute-done | bytes 524320 | tf_op jit(solution)/shard_map/ppermute | solution.py:209
  76.1 19.5 %collective-permute-done.7.rbottom = f32[512,256]{1,0:T(8,128)S(1)} collective-permute-done((f32[512,256]{1,0:T(8,128)S(1)}, f32[512,256]{1,0:T(8,128)S(1)}, u32[]{:S(2)}, u32[]{:S(2)}) %collective-permute-start.7) | collective-permute-done | bytes 524320 | tf_op jit(solution)/shard_map/ppermute | solution.py:210
  95.7 1.5 %shard_map.87 = (f32[512,256]{1,0:T(8,128)S(1)}, f32[512,256]{1,0:T(8,128)S(1)}) custom-call(f32[512,256]{1,0:T(8,128)S(1)} %get-tuple-element.36.top, f32[512,256]{1,0:T(8,128)S(1)} %get-tuple-element.37.bottom, f32[512,256]{1,0:T(8,128)S(1)} %collective-permute-done.6.rtop, f32[512,256]{1,0:T(8,128)S(1)} %collective-permute-done.7.rbottom, ...), custom_call_target="tpu_custom_call" | custom-call | flops 603979776 | bytes 4718600 | tf_op jit(solution)/shard_map/pallas_call | solution.py:31
  97.2 1.9 %collective-permute-start.8 = (f32[512,256]{1,0:T(8,128)S(1)}, f32[512,256]{1,0:T(8,128)S(1)}, u32[]{:S(2)}, u32[]{:S(2)}) collective-permute-start(f32[512,256]{1,0:T(8,128)S(1)} %get-tuple-element.38.u), channel_id=1, source_target_pairs={{0,1},{2,3},{4,5},{6,7},{8,9},{10,11},{12,13},{14,15},{16,17},{18,... | collective-permute-start | bytes 1572872 | tf_op jit(solution)/shard_map/ppermute | solution.py:214
  99.1 10.3 %collective-permute-start.9 = (f32[512,256]{1,0:T(8,128)S(1)}, f32[512,256]{1,0:T(8,128)S(1)}, u32[]{:S(2)}, u32[]{:S(2)}) collective-permute-start(f32[512,256]{1,0:T(8,128)S(1)} %get-tuple-element.38.u), channel_id=1, source_target_pairs={{1,2},{3,4},{5,6},{7,8},{9,10},{11,12},{13,14},{15,16},{17,18},{19... | collective-permute-start | bytes 1572872 | tf_op jit(solution)/shard_map/ppermute | solution.py:217
  110.0 1.9 %collective-permute-start.11 = (f32[520,256]{1,0:T(8,128)S(1)}, f32[520,256]{1,0:T(8,128)S(1)}, u32[]{:S(2)}, u32[]{:S(2)}) collective-permute-start(f32[520,256]{1,0:T(8,128)S(1)} %shard_map.88.w), channel_id=1, source_target_pairs={{1,2},{3,4},{5,6},{7,8},{9,10},{11,12},{13,14},{15,16},{17,18},{19... | collective-permute-start | bytes 1597448 | tf_op jit(solution)/shard_map/ppermute | solution.py:217
  111.9 4.4 %collective-permute-done.9.ub = f32[512,256]{1,0:T(8,128)S(1)} collective-permute-done((f32[512,256]{1,0:T(8,128)S(1)}, f32[512,256]{1,0:T(8,128)S(1)}, u32[]{:S(2)}, u32[]{:S(2)}) %collective-permute-start.9) | collective-permute-done | bytes 524320 | tf_op jit(solution)/shard_map/ppermute | solution.py:217
  117.5 1.9 %collective-permute-start.10 = (f32[512,256]{1,0:T(8,128)S(1)}, f32[512,256]{1,0:T(8,128)S(1)}, u32[]{:S(2)}, u32[]{:S(2)}) collective-permute-start(f32[512,256]{1,0:T(8,128)S(1)} %get-tuple-element.40), channel_id=1, source_target_pairs={{0,1},{2,3},{4,5},{6,7},{8,9},{10,11},{12,13},{14,15},{16,17},{18,... | collective-permute-start | bytes 1572872 | tf_op jit(solution)/shard_map/ppermute | solution.py:214
  119.4 1.9 %collective-permute-done.10.ra = f32[512,256]{1,0:T(8,128)S(1)} collective-permute-done((f32[512,256]{1,0:T(8,128)S(1)}, f32[512,256]{1,0:T(8,128)S(1)}, u32[]{:S(2)}, u32[]{:S(2)}) %collective-permute-start.10) | collective-permute-done | bytes 524320 | tf_op jit(solution)/shard_map/ppermute | solution.py:214
  121.3 5.5 %collective-permute-done.11.wb = f32[520,256]{1,0:T(8,128)S(1)} collective-permute-done((f32[520,256]{1,0:T(8,128)S(1)}, f32[520,256]{1,0:T(8,128)S(1)}, u32[]{:S(2)}, u32[]{:S(2)}) %collective-permute-start.11) | collective-permute-done | bytes 532512 | tf_op jit(solution)/shard_map/ppermute | solution.py:217
  126.7 2.5 %shard_map.90 = (f32[256,256]{1,0:T(8,128)S(1)}, f32[512,256]{1,0:T(8,128)S(1)}, f32[256,256]{1,0:T(8,128)S(1)}) custom-call(f32[512,256]{1,0:T(8,128)S(1)} %get-tuple-element.39.q, f32[512,256]{1,0:T(8,128)S(1)} %collective-permute-done.10.ra, f32[520,256]{1,0:T(8,128)S(1)} %collective-permute-done.11.wb, f32[512,256]{1,0:T(8,128)S(1)} %get-tuple-element.38.u, ...), custom_call_target="tpu_custom_call" | custom-call | flops 1006632960 | bytes 4464640 | tf_op jit(solution)/shard_map/pallas_call | solution.py:31
  129.2 1.9 %collective-permute-start.12 = (f32[256,256]{1,0:T(8,128)S(1)}, f32[256,256]{1,0:T(8,128)S(1)}, u32[]{:S(2)}, u32[]{:S(2)}) collective-permute-start(f32[256,256]{1,0:T(8,128)S(1)} %get-tuple-element.42), channel_id=1, source_target_pairs={{0,32},{32,64},{64,96},{96,128},{128,160},{160,192},{192,224},{224... | collective-permute-start | bytes 786440 | tf_op jit(solution)/shard_map/ppermute | solution.py:209
  131.1 3.9 %collective-permute-start.13 = (f32[256,256]{1,0:T(8,128)S(1)}, f32[256,256]{1,0:T(8,128)S(1)}, u32[]{:S(2)}, u32[]{:S(2)}) collective-permute-start(f32[256,256]{1,0:T(8,128)S(1)} %get-tuple-element.43), channel_id=1, source_target_pairs={{32,0},{64,32},{96,64},{128,96},{160,128},{192,160},{224,192},{256... | collective-permute-start | bytes 786440 | tf_op jit(solution)/shard_map/ppermute | solution.py:210
  135.1 8.2 %collective-permute-done.12.rup = f32[256,256]{1,0:T(8,128)S(1)} collective-permute-done((f32[256,256]{1,0:T(8,128)S(1)}, f32[256,256]{1,0:T(8,128)S(1)}, u32[]{:S(2)}, u32[]{:S(2)}) %collective-permute-start.12) | collective-permute-done | bytes 262176 | tf_op jit(solution)/shard_map/ppermute | solution.py:209
  143.2 3.3 %collective-permute-done.13.rdown = f32[256,256]{1,0:T(8,128)S(1)} collective-permute-done((f32[256,256]{1,0:T(8,128)S(1)}, f32[256,256]{1,0:T(8,128)S(1)}, u32[]{:S(2)}, u32[]{:S(2)}) %collective-permute-start.13) | collective-permute-done | bytes 262176 | tf_op jit(solution)/shard_map/ppermute | solution.py:210
  146.5 1.5 shard_map.91
  (22 shorter events, 6.8 us)
Async XLA Ops:
  0.0 19.2 %copy-start = (f32[512,256]{1,0:T(8,128)S(1)}, f32[512,256]{1,0:T(8,128)}, u32[]{:S(2)}) copy-start(f32[512,256]{1,0:T(8,128)} %x.3) | copy-start | bytes 1572868
  1.1 12.9 %collective-permute-start = (f32[256,256]{1,0:T(8,128)S(1)}, f32[256,256]{1,0:T(8,128)S(1)}, u32[]{:S(2)}, u32[]{:S(2)}) collective-permute-start(f32[256,256]{1,0:T(8,128)S(1)} %get-tuple-element.46), channel_id=1, source_target_pairs={{0,32},{32,64},{64,96},{96,128},{128,160},{160,192},{192,224},{224... | collective-permute-start | bytes 786440 | tf_op jit(solution)/shard_map/ppermute | solution.py:209
  6.9 12.4 %collective-permute-start.1 = (f32[256,256]{1,0:T(8,128)S(1)}, f32[256,256]{1,0:T(8,128)S(1)}, u32[]{:S(2)}, u32[]{:S(2)}) collective-permute-start(f32[256,256]{1,0:T(8,128)S(1)} %get-tuple-element.45), channel_id=1, source_target_pairs={{32,0},{64,32},{96,64},{128,96},{160,128},{192,160},{224,192},{256... | collective-permute-start | bytes 786440 | tf_op jit(solution)/shard_map/ppermute | solution.py:210
  8.9 1.4 copy-start.1
  10.3 1.1 copy-start.2
  11.4 0.7 copy-start.4
  12.1 0.7 copy-start.5
  19.2 14.4 %copy-start.3 = (f32[512,256]{1,0:T(8,128)S(1)}, f32[512,256]{1,0:T(8,128)}, u32[]{:S(2)}) copy-start(f32[512,256]{1,0:T(8,128)} %obs.3) | copy-start | bytes 1572868
  20.1 13.5 %collective-permute-start.2 = (f32[512,256]{1,0:T(8,128)S(1)}, f32[512,256]{1,0:T(8,128)S(1)}, u32[]{:S(2)}, u32[]{:S(2)}) collective-permute-start(f32[512,256]{1,0:T(8,128)S(1)} %shard_map.83.u), channel_id=1, source_target_pairs={{0,1},{2,3},{4,5},{6,7},{8,9},{10,11},{12,13},{14,15},{16,17},{18,... | collective-permute-start | bytes 1572872 | tf_op jit(solution)/shard_map/ppermute | solution.py:214
  22.0 18.6 %collective-permute-start.3 = (f32[512,256]{1,0:T(8,128)S(1)}, f32[512,256]{1,0:T(8,128)S(1)}, u32[]{:S(2)}, u32[]{:S(2)}) collective-permute-start(f32[512,256]{1,0:T(8,128)S(1)} %shard_map.83.u), channel_id=1, source_target_pairs={{1,2},{3,4},{5,6},{7,8},{9,10},{11,12},{13,14},{15,16},{17,18},{19... | collective-permute-start | bytes 1572872 | tf_op jit(solution)/shard_map/ppermute | solution.py:217
  34.2 19.4 %collective-permute-start.5 = (f32[768,256]{1,0:T(8,128)S(1)}, f32[768,256]{1,0:T(8,128)S(1)}, u32[]{:S(2)}, u32[]{:S(2)}) collective-permute-start(f32[768,256]{1,0:T(8,128)S(1)} %shard_map.84.w), channel_id=1, source_target_pairs={{1,2},{3,4},{5,6},{7,8},{9,10},{11,12},{13,14},{15,16},{17,18},{19... | collective-permute-start | bytes 2359304 | tf_op jit(solution)/shard_map/ppermute | solution.py:217
  41.7 3.8 %collective-permute-start.4 = (f32[512,256]{1,0:T(8,128)S(1)}, f32[512,256]{1,0:T(8,128)S(1)}, u32[]{:S(2)}, u32[]{:S(2)}) collective-permute-start(f32[512,256]{1,0:T(8,128)S(1)} %get-tuple-element.33), channel_id=1, source_target_pairs={{0,1},{2,3},{4,5},{6,7},{8,9},{10,11},{12,13},{14,15},{16,17},{18,... | collective-permute-start | bytes 1572872 | tf_op jit(solution)/shard_map/ppermute | solution.py:214
  56.1 20.1 %collective-permute-start.6 = (f32[512,256]{1,0:T(8,128)S(1)}, f32[512,256]{1,0:T(8,128)S(1)}, u32[]{:S(2)}, u32[]{:S(2)}) collective-permute-start(f32[512,256]{1,0:T(8,128)S(1)} %get-tuple-element.37.bottom), channel_id=1, source_target_pairs={{0,32},{32,64},{64,96},{96,128},{128,160},{160,192},{192,224},{224... | collective-permute-start | bytes 1572872 | tf_op jit(solution)/shard_map/ppermute | solution.py:209
  60.7 35.0 %collective-permute-start.7 = (f32[512,256]{1,0:T(8,128)S(1)}, f32[512,256]{1,0:T(8,128)S(1)}, u32[]{:S(2)}, u32[]{:S(2)}) collective-permute-start(f32[512,256]{1,0:T(8,128)S(1)} %get-tuple-element.36.top), channel_id=1, source_target_pairs={{32,0},{64,32},{96,64},{128,96},{160,128},{192,160},{224,192},{256... | collective-permute-start | bytes 1572872 | tf_op jit(solution)/shard_map/ppermute | solution.py:210
  97.2 12.2 %collective-permute-start.8 = (f32[512,256]{1,0:T(8,128)S(1)}, f32[512,256]{1,0:T(8,128)S(1)}, u32[]{:S(2)}, u32[]{:S(2)}) collective-permute-start(f32[512,256]{1,0:T(8,128)S(1)} %get-tuple-element.38.u), channel_id=1, source_target_pairs={{0,1},{2,3},{4,5},{6,7},{8,9},{10,11},{12,13},{14,15},{16,17},{18,... | collective-permute-start | bytes 1572872 | tf_op jit(solution)/shard_map/ppermute | solution.py:214
  99.1 17.2 %collective-permute-start.9 = (f32[512,256]{1,0:T(8,128)S(1)}, f32[512,256]{1,0:T(8,128)S(1)}, u32[]{:S(2)}, u32[]{:S(2)}) collective-permute-start(f32[512,256]{1,0:T(8,128)S(1)} %get-tuple-element.38.u), channel_id=1, source_target_pairs={{1,2},{3,4},{5,6},{7,8},{9,10},{11,12},{13,14},{15,16},{17,18},{19... | collective-permute-start | bytes 1572872 | tf_op jit(solution)/shard_map/ppermute | solution.py:217
  110.0 16.8 %collective-permute-start.11 = (f32[520,256]{1,0:T(8,128)S(1)}, f32[520,256]{1,0:T(8,128)S(1)}, u32[]{:S(2)}, u32[]{:S(2)}) collective-permute-start(f32[520,256]{1,0:T(8,128)S(1)} %shard_map.88.w), channel_id=1, source_target_pairs={{1,2},{3,4},{5,6},{7,8},{9,10},{11,12},{13,14},{15,16},{17,18},{19... | collective-permute-start | bytes 1597448 | tf_op jit(solution)/shard_map/ppermute | solution.py:217
  117.5 3.8 %collective-permute-start.10 = (f32[512,256]{1,0:T(8,128)S(1)}, f32[512,256]{1,0:T(8,128)S(1)}, u32[]{:S(2)}, u32[]{:S(2)}) collective-permute-start(f32[512,256]{1,0:T(8,128)S(1)} %get-tuple-element.40), channel_id=1, source_target_pairs={{0,1},{2,3},{4,5},{6,7},{8,9},{10,11},{12,13},{14,15},{16,17},{18,... | collective-permute-start | bytes 1572872 | tf_op jit(solution)/shard_map/ppermute | solution.py:214
  129.2 14.0 %collective-permute-start.12 = (f32[256,256]{1,0:T(8,128)S(1)}, f32[256,256]{1,0:T(8,128)S(1)}, u32[]{:S(2)}, u32[]{:S(2)}) collective-permute-start(f32[256,256]{1,0:T(8,128)S(1)} %get-tuple-element.42), channel_id=1, source_target_pairs={{0,32},{32,64},{64,96},{96,128},{128,160},{160,192},{192,224},{224... | collective-permute-start | bytes 786440 | tf_op jit(solution)/shard_map/ppermute | solution.py:209
  131.1 15.4 %collective-permute-start.13 = (f32[256,256]{1,0:T(8,128)S(1)}, f32[256,256]{1,0:T(8,128)S(1)}, u32[]{:S(2)}, u32[]{:S(2)}) collective-permute-start(f32[256,256]{1,0:T(8,128)S(1)} %get-tuple-element.43), channel_id=1, source_target_pairs={{32,0},{64,32},{96,64},{128,96},{160,128},{192,160},{224,192},{256... | collective-permute-start | bytes 786440 | tf_op jit(solution)/shard_map/ppermute | solution.py:210

commit v3 on v0

v3 whole, which is shorter than its diff:
```python
import jax
import jax.numpy as jnp
from jax import lax
from jax.experimental import pallas as pl
from jax.experimental.pallas import tpu as pltpu
from jax.sharding import PartitionSpec as P


f32 = jnp.float32
bf16 = jnp.bfloat16
VMEM = pl.BlockSpec(memory_space=pltpu.VMEM)
SMEM = pl.BlockSpec(memory_space=pltpu.SMEM)


def split(x):
    hi = x.astype(bf16)
    return hi, (x - hi.astype(f32)).astype(bf16)


def dot3(x, y):
    (xh, xl), (yh, yl) = x, y
    mm = lambda a, b: jnp.dot(a, b, preferred_element_type=f32)
    return mm(xh, yh) + (mm(xh, yl) + mm(xl, yh))


def soft(v, h):
    return v - jnp.minimum(jnp.maximum(v, -h), h)


def call(body, ins, outs, flops, scratch=(), limit=24 << 20):
    size = lambda a: a.size * a.dtype.itemsize
    return pl.pallas_call(
        body,
        out_shape=[jax.ShapeDtypeStruct(s, d) for s, d in outs],
        in_specs=[SMEM if a.size < 64 else VMEM for a in ins],
        out_specs=[VMEM for _ in outs],
        scratch_shapes=list(scratch),
        compiler_params=pltpu.CompilerParams(vmem_limit_bytes=limit),
        cost_estimate=pl.CostEstimate(
            flops=flops, bytes_accessed=sum(size(a) for a in ins), transcendentals=0
        ),
    )(*ins)


def own_is_e(pos):
    return (pos[2] // 2 + pos[2] % 2) % 2 == 1


def prepare(fx, bx, fy, by, pos):
    blk = fx.shape[2]

    def body(fx, bx, fy, by, pos, ah, al, th, tl, fo, outer):
        row, rows, col, cols = pos[0], pos[1], pos[2], pos[3]
        core = col % 2
        for k, s in enumerate((1, 2 - 2 * core, 2 * core)):
            r = slice(k * blk, (k + 1) * blk)
            mx = bx[core, s].astype(f32)
            my = by[0, s].astype(f32)
            if k == 2:
                last = jnp.where(core == 0, 0, rows - 1)
                mx = jnp.where(row == last, 0.0, mx)
                last = jnp.where(core == 0, 0, cols - 1)
                my = jnp.where(col == last, 0.0, my)
            v = fx[core, s] * mx
            ah[:, r], al[:, r] = split(v)
            th[r, :], tl[r, :] = split(v.T)
            w = fy[0, s] * my
            fo[r, :] = w
        outer[:blk, :] = w
        outer[blk:, :] = jnp.zeros((outer.shape[0] - blk, blk), f32)

    outs = [((blk, 3 * blk), bf16)] * 2 + [((3 * blk, blk), bf16)] * 2
    outs += [((3 * blk, blk), f32), ((2 * blk + 8, blk), f32)]
    o = call(body, (fx, bx, fy, by, pos), outs, 1 << 24)
    return o[0:2], o[2:4], o[4], o[5]


def prepare_columns(own, other, pos):
    blk = own.shape[1]

    def body(own, other, pos, wh, wl, nh, nl, eh, el, oh, ol):
        flag = own_is_e(pos)
        e = lambda k: jnp.where(flag, own[k * blk : (k + 1) * blk, :], other[k * blk : (k + 1) * blk, :])
        o = lambda k: jnp.where(flag, other[k * blk : (k + 1) * blk, :], own[k * blk : (k + 1) * blk, :])
        a, b = slice(0, blk), slice(blk, 2 * blk)
        for v, i, j in ((e(0), a, a), (e(1), a, b), (o(0), b, b), (o(1), b, a)):
            nh[i, j], nl[i, j] = split(v)
            wh[j, i], wl[j, i] = split(v.T)
        eh[...], el[...] = split(e(2).T)
        oh[...], ol[...] = split(o(2).T)

    outs = [((2 * blk, 2 * blk), bf16)] * 4 + [((blk, blk), bf16)] * 4
    o = call(body, (own, other, pos), outs, 1 << 24)
    return o[0:2], o[2:4], o[4:6], o[6:8]


def messages(xh, xl, ah, al, wh, wl, obs, e, o):
    blk = ah.shape[0]
    u = dot3((ah[...], al[...]), (xh[...], xl[...]))
    w = dot3(split(u), (wh[...], wl[...])) - obs
    for out, s in ((e, slice(0, blk)), (o, slice(blk, 2 * blk))):
        out[:blk, :] = u[:, s]
        out[blk:, :] = w[:, s]


def first_messages(x, xp, bown, bother, obs, obsp, ax, fw, pos):
    m, blk = x.shape

    def body(x, xp, bown, bother, obs, obsp, ah, al, wh, wl, pos, e, o, x0, ob, xh, xl):
        flag = own_is_e(pos)
        core = pos[2] % 2
        here = pl.ds(pl.multiple_of(core * blk, blk), blk)
        there = pl.ds(pl.multiple_of(blk - core * blk, blk), blk)
        rows = ((x[here, :], xp[here, :]), (x[there, :], xp[there, :]), (bown[...], bother[...]))
        a, b = slice(0, blk), slice(blk, 2 * blk)
        for k, (p, q) in enumerate(rows):
            r = slice(k * blk, (k + 1) * blk)
            ve, vo = jnp.where(flag, p, q), jnp.where(flag, q, p)
            if k == 0:
                x0[:, a], x0[:, b] = ve, vo
            xh[r, a], xl[r, a] = split(ve)
            xh[r, b], xl[r, b] = split(vo)
        p, q = obs[here, :], obsp[...]
        ob[:, a], ob[:, b] = jnp.where(flag, p, q), jnp.where(flag, q, p)
        messages(xh, xl, ah, al, wh, wl, ob[...], e, o)

    outs = [((2 * blk, blk), f32)] * 2 + [((blk, 2 * blk), f32)] * 2
    scratch = [pltpu.VMEM((3 * blk, 2 * blk), bf16)] * 2
    ins = (x, xp, bown, bother, obs, obsp, *ax, *fw, pos)
    return call(body, ins, outs, 60 * blk**3, scratch)


def later_messages(x, xa, xb, obs, ax, fw):
    blk = x.shape[0]

    def body(x, xa, xb, obs, ah, al, wh, wl, e, o, xh, xl):
        for k, v in enumerate((x, xa, xb)):
            r = slice(k * blk, (k + 1) * blk)
            xh[r, :], xl[r, :] = split(v[...])
        messages(xh, xl, ah, al, wh, wl, obs[...], e, o)

    scratch = [pltpu.VMEM((3 * blk, 2 * blk), bf16)] * 2
    return call(body, (x, xa, xb, obs, *ax, *fw), [((2 * blk, blk), f32)] * 2, 60 * blk**3, scratch)


def back(e, o, re, ro, gown, gother, fe, fo, fn, atx, pos):
    blk = e.shape[1]

    def body(e, o, re, ro, gown, gother, eh, el, oh, ol, nh, nl, th, tl, pos, ps, pa, pb, mh, ml):
        flag = own_is_e(pos)
        gp, gq = gown[:blk, :], gother[...]
        outer = []
        sides = (
            (e, re, (eh, el), jnp.where(flag, gp, gq), slice(0, blk)),
            (o, ro, (oh, ol), jnp.where(flag, gq, gp), slice(blk, 2 * blk)),
        )
        for own, got, (fh, fl), g, s in sides:
            m = own[blk:, :] + dot3(split(got[:blk, :]), (fh[...], fl[...]))
            mh[:, s], ml[:, s] = split(m)
            beyond = got[blk:, :] + dot3(split(own[:blk, :]), split(g.T))
            outer.append(dot3(split(beyond), split(g)))
        n = dot3((mh[...], ml[...]), (nh[...], nl[...])) + jnp.concatenate(outer, axis=1)
        nsplit = split(n)
        for k, out in enumerate((ps, pa, pb)):
            r = slice(k * blk, (k + 1) * blk)
            out[...] = dot3((th[r, :], tl[r, :]), nsplit)

    scratch = [pltpu.VMEM((blk, 2 * blk), bf16)] * 2
    ins = (e, o, re, ro, gown, gother, *fe, *fo, *fn, *atx, pos)
    return call(body, ins, [((blk, 2 * blk), f32)] * 3, 96 * blk**3, scratch)


def update(x, ps, ra, rb, sc):
    def body(x, ps, ra, rb, sc, o):
        o[...] = soft(x[...] - sc[0] * (ps[...] + (ra[...] + rb[...])), sc[1])

    return call(body, (x, ps, ra, rb, sc), [(x.shape, f32)], 1 << 20)[0]


def last_update(x, ps, ra, rb, sc, pos):
    blk = x.shape[0]

    def body(x, ps, ra, rb, sc, pos, keep, give):
        flag = own_is_e(pos)
        v = soft(x[...] - sc[0] * (ps[...] + (ra[...] + rb[...])), sc[1])
        keep[...] = jnp.where(flag, v[:, :blk], v[:, blk:])
        give[...] = jnp.where(flag, v[:, blk:], v[:, :blk])

    return call(body, (x, ps, ra, rb, sc, pos), [((blk, blk), f32)] * 2, 1 << 20)


def stack(keep, got, pos):
    blk = keep.shape[0]

    def body(keep, got, pos, o):
        core = pos[2] % 2
        o[pl.ds(pl.multiple_of(core * blk, blk), blk), :] = keep[...]
        o[pl.ds(pl.multiple_of(blk - core * blk, blk), blk), :] = got[...]

    return call(body, (keep, got, pos), [((2 * blk, blk), f32)], 1 << 20)[0]


def per_device(x, observed, fx, bx, fy, by, step_size, threshold):
    blk = fx.shape[2]
    rows, cols = lax.axis_size("row"), lax.axis_size("col")
    chips = cols // 2
    at = lambda r, c: r * cols + c
    both = lambda forth: forth + [(j, i) for i, j in forth]
    chip_pairs = both([(2 * k, 2 * k + 1) for k in range(chips)])
    outer_pairs = both([(2 * k + 1, 2 * k + 2) for k in range(chips - 1)])
    side_pairs = [
        both([(2 * k + i, 2 * k + 2 + i) for k in range(first, chips - 1, 2) for i in range(2)])
        for first in (0, 1)
    ]
    row_pairs = both(
        [(at(r, 2 * k), at(r - 1, 2 * k + 1)) for r in range(1, rows) for k in range(chips)]
    )
    same_core = [(at(r, 2 * k), at(r + 1, 2 * k)) for r in range(rows - 1) for k in range(chips)]
    same_core += [(at(r, 2 * k + 1), at(r - 1, 2 * k + 1)) for r in range(1, rows) for k in range(chips)]

    swap_chip = lambda v: lax.ppermute(v, "col", chip_pairs)
    swap_row = lambda v: lax.ppermute(v, ("row", "col"), row_pairs)

    def swap_sides(e, o):
        ro = lax.ppermute(o, "col", side_pairs[1])
        re = lax.ppermute(e, "col", side_pairs[0])
        return re, ro

    col = lax.axis_index("col")
    core = col % 2
    pos = jnp.stack([lax.axis_index("row"), rows, col, cols]).astype(jnp.int32)
    sc = jnp.concatenate([step_size, threshold])
    mine = lax.dynamic_slice_in_dim(x, core * blk, blk)
    other = lax.dynamic_slice_in_dim(x, blk - core * blk, blk)
    bother = swap_row(mine)
    bown = lax.ppermute(other, ("row", "col"), same_core)
    xp = swap_chip(x)
    obsp = swap_chip(lax.dynamic_slice_in_dim(observed, blk - core * blk, blk))
    ax, atx, own, outer = prepare(fx, bx, fy, by, pos)
    gown = lax.ppermute(outer, "col", outer_pairs)
    gother = swap_chip(gown[:blk])
    fw, fn, fe, fo = prepare_columns(own, swap_chip(own), pos)

    e, o, x, obs = first_messages(x, xp, bown, bother, observed, obsp, ax, fw, pos)
    re, ro = swap_sides(e, o)
    ps, pa, pb = back(e, o, re, ro, gown, gother, fe, fo, fn, atx, pos)
    x = update(x, ps, swap_chip(pa), swap_row(pb), sc)
    e, o = later_messages(x, swap_chip(x), swap_row(x), obs, ax, fw)
    re, ro = swap_sides(e, o)
    ps, pa, pb = back(e, o, re, ro, gown, gother, fe, fo, fn, atx, pos)
    keep, give = last_update(x, ps, swap_chip(pa), swap_row(pb), sc, pos)
    return stack(keep, swap_chip(give), pos)


def solution(mesh):
    in_specs = (
        P("row", "col"),
        P("row", "col"),
        P("row", None, None, None),
        P("row", None),
        P("col", None, None, None),
        P("col", None),
        P(),
        P(),
    )
    return jax.shard_map(
        per_device, mesh=mesh, in_specs=in_specs, out_specs=P("row", "col"), check_vma=False
    )
```

time: 254 us -> 168 us (0.66)
  the two profiles are of different devices: /device:TPU:48 before, /device:TPU:51 now
where the time goes in v3:
time: 168 us; the launch traced here: 167 us
  starting transfers between devices  77.9 us (46%)
  waiting for transfers between devices  66.8 us (40%)
  Pallas kernels  14.3 us (9%)
  local copies, waits for them, and re-layouts  6.33 us (4%)
    ppermute x2, waiting for transfers between devices, swap_sides(): ro = lax.ppermute(o, 'col', side_pairs[1])  39.5 us
    ppermute x8, starting transfers between devices, per_device(): swap_chip = lambda v: lax.ppermute(v, 'col', chip_pairs)  35.1 us
    ppermute x4, waiting for transfers between devices, per_device(): swap_row = lambda v: lax.ppermute(v, ('row', 'col'), row_pairs)  20.6 us
    ppermute x2, starting transfers between devices, swap_sides(): ro = lax.ppermute(o, 'col', side_pairs[1])  17.9 us
    pallas_call x9, Pallas kernels, call(): pl.pallas_call(body, out_shape=[jax.ShapeDtypeStruct(s, d) for s, d in ou...  14.3 us
    ppermute x4, starting transfers between devices, per_device(): swap_row = lambda v: lax.ppermute(v, ('row', 'col'), row_pairs)  11.2 us
    unnamed x24, local copies, waits for them, and re-layouts  6.24 us
    ppermute x2, starting transfers between devices, swap_sides(): re = lax.ppermute(e, 'col', side_pairs[0])  6.22 us
  transfers between devices with their start and end apart: 18, of which 9 were waited for; matrix products, arithmetic and copies ran while one was open for 0% of the time, Pallas kernels for 2%

profile of v3, /device:TPU:51, one launch (start us, length us, event | category | flops | bytes accessed | tf_op | source)
XLA Modules:
  0.0 167.2 jit_solution(18105459752166740228)
XLA Ops:
  0.1 1.5 copy-done.1
  1.5 1.1 copy-done.3
  7.2 2.6 %collective-permute-start.4 = (f32[768,256]{1,0:T(8,128)S(1)}, f32[768,256]{1,0:T(8,128)S(1)}, u32[]{:S(2)}, u32[]{:S(2)}) collective-permute-start(f32[768,256]{1,0:T(8,128)S(1)} %get-tuple-element.35.own), channel_id=1, source_target_pairs={{0,1},{2,3},{4,5},{6,7},{8,9},{10,11},{12,13},{14,15},{16,17},{18,... | collective-permute-start | bytes 2359304 | tf_op jit(solution)/shard_map/ppermute | solution.py:221
  9.8 1.9 %collective-permute-start = (f32[512,256]{1,0:T(8,128)S(1)}, f32[512,256]{1,0:T(8,128)}, u32[]{:S(2)}, u32[]{:S(2)}) collective-permute-start(f32[512,256]{1,0:T(8,128)S(1)} %copy-done), channel_id=1, source_target_pairs={{0,1},{2,3},{4,5},{6,7},{8,9},{10,11},{12,13},{14,15},{16,17},{18,... | collective-permute-start | bytes 1572872 | tf_op jit(solution)/shard_map/ppermute | solution.py:221
  11.8 3.1 %collective-permute-start.1 = (f32[256,256]{1,0:T(8,128)S(1)}, f32[256,256]{1,0:T(8,128)S(1)}, u32[]{:S(2)}, u32[]{:S(2)}) collective-permute-start(f32[256,256]{1,0:T(8,128)S(1)} %get-tuple-element.62), channel_id=1, source_target_pairs={{0,32},{2,34},{4,36},{6,38},{8,40},{10,42},{12,44},{14,46},{16,48}... | collective-permute-start | bytes 786440 | tf_op jit(solution)/shard_map/ppermute | solution.py:236
  14.9 5.5 %collective-permute-start.2 = (f32[256,256]{1,0:T(8,128)S(1)}, f32[256,256]{1,0:T(8,128)S(1)}, u32[]{:S(2)}, u32[]{:S(2)}) collective-permute-start(f32[256,256]{1,0:T(8,128)S(1)} %get-tuple-element.61), channel_id=1, source_target_pairs={{32,1},{34,3},{36,5},{38,7},{40,9},{42,11},{44,13},{46,15},{48,17}... | collective-permute-start | bytes 786440 | tf_op jit(solution)/shard_map/ppermute | solution.py:222
  20.4 1.9 %collective-permute-start.3 = (f32[256,256]{1,0:T(8,128)S(1)}, f32[256,256]{1,0:T(8,128)S(1)}, u32[]{:S(2)}, u32[]{:S(2)}) collective-permute-start(f32[256,256]{1,0:T(8,128)S(1)} %constant_dynamic-slice_fusion), channel_id=1, source_target_pairs={{0,1},{2,3},{4,5},{6,7},{8,9},{10,11},{12,13},{14,15},{16,17},{18,... | collective-permute-start | bytes 786440 | tf_op jit(solution)/shard_map/ppermute | solution.py:221
  22.4 4.4 %collective-permute-start.7 = (f32[520,256]{1,0:T(8,128)S(1)}, f32[520,256]{1,0:T(8,128)S(1)}, u32[]{:S(2)}, u32[]{:S(2)}) collective-permute-start(f32[520,256]{1,0:T(8,128)S(1)} %copy-done.7), channel_id=1, source_target_pairs={{1,2},{3,4},{5,6},{7,8},{9,10},{11,12},{13,14},{15,16},{17,18},{19... | collective-permute-start | bytes 1597448 | tf_op jit(solution)/shard_map/ppermute | solution.py:240
  28.2 2.5 %shard_map.84 = (f32[512,256]{1,0:T(8,128)S(1)}, f32[512,256]{1,0:T(8,128)S(1)}, f32[256,512]{1,0:T(8,128)S(1)}, f32[256,512]{1,0:T(8,128)S(1)}) custom-call(f32[512,256]{1,0:T(8,128)S(1)} %copy-done, f32[512,256]{1,0:T(8,128)} %collective-permute-done.xp, f32[256,256]{1,0:T(8,128)S(1)} %collective-permute-done.1.bown, ...), custom_call_target="tpu_custom_call" | custom-call | flops 1006632960 | bytes 4194320 | tf_op jit(solution)/shard_map/pallas_call | solution.py:32
  30.7 4.3 %collective-permute-start.5 = (f32[512,256]{1,0:T(8,128)S(1)}, f32[512,256]{1,0:T(8,128)S(1)}, u32[]{:S(2)}, u32[]{:S(2)}) collective-permute-start(f32[512,256]{1,0:T(8,128)S(1)} %get-tuple-element.39.e), channel_id=1, source_target_pairs={{0,2},{1,3},{4,6},{5,7},{8,10},{9,11},{12,14},{13,15},{16,18},{17,... | collective-permute-start | bytes 1572872 | tf_op jit(solution)/shard_map/ppermute | solution.py:226
  35.0 10.3 %collective-permute-start.6 = (f32[512,256]{1,0:T(8,128)S(1)}, f32[512,256]{1,0:T(8,128)S(1)}, u32[]{:S(2)}, u32[]{:S(2)}) collective-permute-start(f32[512,256]{1,0:T(8,128)S(1)} %get-tuple-element.40.o), channel_id=1, source_target_pairs={{2,4},{3,5},{6,8},{7,9},{10,12},{11,13},{14,16},{15,17},{18,20},{1... | collective-permute-start | bytes 1572872 | tf_op jit(solution)/shard_map/ppermute | solution.py:225
  45.3 7.5 %collective-permute-start.8 = (f32[256,256]{1,0:T(8,128)S(1)}, f32[256,256]{1,0:T(8,128)S(1)}, u32[]{:S(2)}, u32[]{:S(2)}) collective-permute-start(f32[256,256]{1,0:T(8,128)S(1)} %slice.4), channel_id=1, source_target_pairs={{0,1},{2,3},{4,5},{6,7},{8,9},{10,11},{12,13},{14,15},{16,17},{18,... | collective-permute-start | bytes 786440 | tf_op jit(solution)/shard_map/ppermute | solution.py:221
  52.8 1.1 collective-permute-done.8.gother
  54.0 18.5 %collective-permute-done.6.ro = f32[512,256]{1,0:T(8,128)S(1)} collective-permute-done((f32[512,256]{1,0:T(8,128)S(1)}, f32[512,256]{1,0:T(8,128)S(1)}, u32[]{:S(2)}, u32[]{:S(2)}) %collective-permute-start.6) | collective-permute-done | bytes 524320 | tf_op jit(solution)/shard_map/ppermute | solution.py:225
  72.5 2.9 %shard_map.85 = (f32[256,512]{1,0:T(8,128)S(1)}, f32[256,512]{1,0:T(8,128)S(1)}, f32[256,512]{1,0:T(8,128)S(1)}) custom-call(f32[512,256]{1,0:T(8,128)S(1)} %get-tuple-element.39.e, f32[512,256]{1,0:T(8,128)S(1)} %get-tuple-element.40.o, f32[512,256]{1,0:T(8,128)S(1)} %collective-permute-done.5.re, f32[512,256]{1,0:T(8,128)S(1)} %collective-permute-done.6.ro, ...), custom_call_target="tpu_custom_call" | custom-call | flops 1610612736 | bytes 5251088 | tf_op jit(solution)/shard_map/pallas_call | solution.py:32
  75.4 1.9 %collective-permute-start.10 = (f32[256,512]{1,0:T(8,128)S(1)}, f32[256,512]{1,0:T(8,128)S(1)}, u32[]{:S(2)}, u32[]{:S(2)}) collective-permute-start(f32[256,512]{1,0:T(8,128)S(1)} %get-tuple-element.52), channel_id=1, source_target_pairs={{32,1},{34,3},{36,5},{38,7},{40,9},{42,11},{44,13},{46,15},{48,17}... | collective-permute-start | bytes 1572872 | tf_op jit(solution)/shard_map/ppermute | solution.py:222
  77.4 7.9 %collective-permute-start.9 = (f32[256,512]{1,0:T(8,128)S(1)}, f32[256,512]{1,0:T(8,128)S(1)}, u32[]{:S(2)}, u32[]{:S(2)}) collective-permute-start(f32[256,512]{1,0:T(8,128)S(1)} %get-tuple-element.51), channel_id=1, source_target_pairs={{0,1},{2,3},{4,5},{6,7},{8,9},{10,11},{12,13},{14,15},{16,17},{18,... | collective-permute-start | bytes 1572872 | tf_op jit(solution)/shard_map/ppermute | solution.py:221
  87.4 5.3 %collective-permute-start.11 = (f32[256,512]{1,0:T(8,128)S(1)}, f32[256,512]{1,0:T(8,128)S(1)}, u32[]{:S(2)}, u32[]{:S(2)}) collective-permute-start(f32[256,512]{1,0:T(8,128)S(1)} %shard_map.86.x), channel_id=1, source_target_pairs={{0,1},{2,3},{4,5},{6,7},{8,9},{10,11},{12,13},{14,15},{16,17},{18,... | collective-permute-start | bytes 1572872 | tf_op jit(solution)/shard_map/ppermute | solution.py:221
  92.8 1.9 %collective-permute-start.12 = (f32[256,512]{1,0:T(8,128)S(1)}, f32[256,512]{1,0:T(8,128)S(1)}, u32[]{:S(2)}, u32[]{:S(2)}) collective-permute-start(f32[256,512]{1,0:T(8,128)S(1)} %shard_map.86.x), channel_id=1, source_target_pairs={{32,1},{34,3},{36,5},{38,7},{40,9},{42,11},{44,13},{46,15},{48,17}... | collective-permute-start | bytes 1572872 | tf_op jit(solution)/shard_map/ppermute | solution.py:222
  94.7 11.7 %collective-permute-done.12.xb = f32[256,512]{1,0:T(8,128)S(1)} collective-permute-done((f32[256,512]{1,0:T(8,128)S(1)}, f32[256,512]{1,0:T(8,128)S(1)}, u32[]{:S(2)}, u32[]{:S(2)}) %collective-permute-start.12) | collective-permute-done | bytes 524320 | tf_op jit(solution)/shard_map/ppermute | solution.py:222
  106.4 1.3 shard_map.87
  107.7 1.9 %collective-permute-start.13 = (f32[512,256]{1,0:T(8,128)S(1)}, f32[512,256]{1,0:T(8,128)S(1)}, u32[]{:S(2)}, u32[]{:S(2)}) collective-permute-start(f32[512,256]{1,0:T(8,128)S(1)} %get-tuple-element.54.e), channel_id=1, source_target_pairs={{0,2},{1,3},{4,6},{5,7},{8,10},{9,11},{12,14},{13,15},{16,18},{17,... | collective-permute-start | bytes 1572872 | tf_op jit(solution)/shard_map/ppermute | solution.py:226
  109.7 7.6 %collective-permute-start.14 = (f32[512,256]{1,0:T(8,128)S(1)}, f32[512,256]{1,0:T(8,128)S(1)}, u32[]{:S(2)}, u32[]{:S(2)}) collective-permute-start(f32[512,256]{1,0:T(8,128)S(1)} %get-tuple-element.55.o), channel_id=1, source_target_pairs={{2,4},{3,5},{6,8},{7,9},{10,12},{11,13},{14,16},{15,17},{18,20},{1... | collective-permute-start | bytes 1572872 | tf_op jit(solution)/shard_map/ppermute | solution.py:225
  117.3 3.9 %collective-permute-done.13.re = f32[512,256]{1,0:T(8,128)S(1)} collective-permute-done((f32[512,256]{1,0:T(8,128)S(1)}, f32[512,256]{1,0:T(8,128)S(1)}, u32[]{:S(2)}, u32[]{:S(2)}) %collective-permute-start.13) | collective-permute-done | bytes 524320 | tf_op jit(solution)/shard_map/ppermute | solution.py:226
  121.2 20.9 %collective-permute-done.14.ro = f32[512,256]{1,0:T(8,128)S(1)} collective-permute-done((f32[512,256]{1,0:T(8,128)S(1)}, f32[512,256]{1,0:T(8,128)S(1)}, u32[]{:S(2)}, u32[]{:S(2)}) %collective-permute-start.14) | collective-permute-done | bytes 524320 | tf_op jit(solution)/shard_map/ppermute | solution.py:225
  142.1 2.9 %shard_map.88 = (f32[256,512]{1,0:T(8,128)S(1)}, f32[256,512]{1,0:T(8,128)S(1)}, f32[256,512]{1,0:T(8,128)S(1)}) custom-call(f32[512,256]{1,0:T(8,128)S(1)} %get-tuple-element.54.e, f32[512,256]{1,0:T(8,128)S(1)} %get-tuple-element.55.o, f32[512,256]{1,0:T(8,128)S(1)} %collective-permute-done.13.re, f32[512,256]{1,0:T(8,128)S(1)} %collective-permute-done.14.ro, ...), custom_call_target="tpu_custom_call" | custom-call | flops 1610612736 | bytes 5251088 | tf_op jit(solution)/shard_map/pallas_call | solution.py:32
  145.1 6.0 %collective-permute-start.15 = (f32[256,512]{1,0:T(8,128)S(1)}, f32[256,512]{1,0:T(8,128)S(1)}, u32[]{:S(2)}, u32[]{:S(2)}) collective-permute-start(f32[256,512]{1,0:T(8,128)S(1)} %get-tuple-element.57), channel_id=1, source_target_pairs={{0,1},{2,3},{4,5},{6,7},{8,9},{10,11},{12,13},{14,15},{16,17},{18,... | collective-permute-start | bytes 1572872 | tf_op jit(solution)/shard_map/ppermute | solution.py:221
  151.1 1.9 %collective-permute-start.16 = (f32[256,512]{1,0:T(8,128)S(1)}, f32[256,512]{1,0:T(8,128)S(1)}, u32[]{:S(2)}, u32[]{:S(2)}) collective-permute-start(f32[256,512]{1,0:T(8,128)S(1)} %get-tuple-element.58), channel_id=1, source_target_pairs={{32,1},{34,3},{36,5},{38,7},{40,9},{42,11},{44,13},{46,15},{48,17}... | collective-permute-start | bytes 1572872 | tf_op jit(solution)/shard_map/ppermute | solution.py:222
  153.1 8.6 %collective-permute-done.16.rb = f32[256,512]{1,0:T(8,128)S(1)} collective-permute-done((f32[256,512]{1,0:T(8,128)S(1)}, f32[256,512]{1,0:T(8,128)S(1)}, u32[]{:S(2)}, u32[]{:S(2)}) %collective-permute-start.16) | collective-permute-done | bytes 524320 | tf_op jit(solution)/shard_map/ppermute | solution.py:222
  162.3 1.9 %collective-permute-start.17 = (f32[256,256]{1,0:T(8,128)S(1)}, f32[256,256]{1,0:T(8,128)S(1)}, u32[]{:S(2)}, u32[]{:S(2)}) collective-permute-start(f32[256,256]{1,0:T(8,128)S(1)} %get-tuple-element.60), channel_id=1, source_target_pairs={{0,1},{2,3},{4,5},{6,7},{8,9},{10,11},{12,13},{14,15},{16,17},{18,... | collective-permute-start | bytes 786440 | tf_op jit(solution)/shard_map/ppermute | solution.py:221
  164.3 1.5 collective-permute-done.17.got
  165.8 1.4 shard_map.90
  (42 shorter events, 7.7 us)
Async XLA Ops:
  0.0 9.8 %copy-start = (f32[512,256]{1,0:T(8,128)S(1)}, f32[512,256]{1,0:T(8,128)}, u32[]{:S(2)}) copy-start(f32[512,256]{1,0:T(8,128)} %x.1) | copy-start | bytes 1572868
  0.1 1.5 copy-start.1
  1.5 1.1 copy-start.3
  2.7 0.7 copy-start.4
  3.3 0.7 copy-start.5
  4.0 16.4 %copy-start.2 = (f32[512,256]{1,0:T(8,128)S(1)}, f32[512,256]{1,0:T(8,128)}, u32[]{:S(2)}) copy-start(f32[512,256]{1,0:T(8,128)} %obs.1) | copy-start | bytes 1572868
  4.9 0.8 copy-start.6
  5.7 0.7 copy-start.8
  6.4 0.8 copy-start.10
  7.2 15.2 %collective-permute-start.4 = (f32[768,256]{1,0:T(8,128)S(1)}, f32[768,256]{1,0:T(8,128)S(1)}, u32[]{:S(2)}, u32[]{:S(2)}) collective-permute-start(f32[768,256]{1,0:T(8,128)S(1)} %get-tuple-element.35.own), channel_id=1, source_target_pairs={{0,1},{2,3},{4,5},{6,7},{8,9},{10,11},{12,13},{14,15},{16,17},{18,... | collective-permute-start | bytes 2359304 | tf_op jit(solution)/shard_map/ppermute | solution.py:221
  9.8 18.4 %collective-permute-start = (f32[512,256]{1,0:T(8,128)S(1)}, f32[512,256]{1,0:T(8,128)}, u32[]{:S(2)}, u32[]{:S(2)}) collective-permute-start(f32[512,256]{1,0:T(8,128)S(1)} %copy-done), channel_id=1, source_target_pairs={{0,1},{2,3},{4,5},{6,7},{8,9},{10,11},{12,13},{14,15},{16,17},{18,... | collective-permute-start | bytes 1572872 | tf_op jit(solution)/shard_map/ppermute | solution.py:221
  11.7 10.6 %copy-start.7 = (f32[520,256]{1,0:T(8,128)S(1)}, f32[520,256]{1,0:T(8,128)}, u32[]{:S(2)}) copy-start(f32[520,256]{1,0:T(8,128)} %copy-done.6) | copy-start | bytes 1597444
  11.8 16.0 %collective-permute-start.1 = (f32[256,256]{1,0:T(8,128)S(1)}, f32[256,256]{1,0:T(8,128)S(1)}, u32[]{:S(2)}, u32[]{:S(2)}) collective-permute-start(f32[256,256]{1,0:T(8,128)S(1)} %get-tuple-element.62), channel_id=1, source_target_pairs={{0,32},{2,34},{4,36},{6,38},{8,40},{10,42},{12,44},{14,46},{16,48}... | collective-permute-start | bytes 786440 | tf_op jit(solution)/shard_map/ppermute | solution.py:236
  14.9 13.2 %collective-permute-start.2 = (f32[256,256]{1,0:T(8,128)S(1)}, f32[256,256]{1,0:T(8,128)S(1)}, u32[]{:S(2)}, u32[]{:S(2)}) collective-permute-start(f32[256,256]{1,0:T(8,128)S(1)} %get-tuple-element.61), channel_id=1, source_target_pairs={{32,1},{34,3},{36,5},{38,7},{40,9},{42,11},{44,13},{46,15},{48,17}... | collective-permute-start | bytes 786440 | tf_op jit(solution)/shard_map/ppermute | solution.py:222
  20.4 7.7 %collective-permute-start.3 = (f32[256,256]{1,0:T(8,128)S(1)}, f32[256,256]{1,0:T(8,128)S(1)}, u32[]{:S(2)}, u32[]{:S(2)}) collective-permute-start(f32[256,256]{1,0:T(8,128)S(1)} %constant_dynamic-slice_fusion), channel_id=1, source_target_pairs={{0,1},{2,3},{4,5},{6,7},{8,9},{10,11},{12,13},{14,15},{16,17},{18,... | collective-permute-start | bytes 786440 | tf_op jit(solution)/shard_map/ppermute | solution.py:221
  22.4 22.9 %collective-permute-start.7 = (f32[520,256]{1,0:T(8,128)S(1)}, f32[520,256]{1,0:T(8,128)S(1)}, u32[]{:S(2)}, u32[]{:S(2)}) collective-permute-start(f32[520,256]{1,0:T(8,128)S(1)} %copy-done.7), channel_id=1, source_target_pairs={{1,2},{3,4},{5,6},{7,8},{9,10},{11,12},{13,14},{15,16},{17,18},{19... | collective-permute-start | bytes 1597448 | tf_op jit(solution)/shard_map/ppermute | solution.py:240
  28.2 44.3 %copy-start.9 = (bf16[768,256]{1,0:T(8,128)(2,1)S(1)}, bf16[768,256]{1,0:T(8,128)(2,1)}, u32[]{:S(2)}) copy-start(bf16[768,256]{1,0:T(8,128)(2,1)} %copy-done.8) | copy-start | bytes 1179652
  28.2 44.3 %copy-start.11 = (bf16[768,256]{1,0:T(8,128)(2,1)S(1)}, bf16[768,256]{1,0:T(8,128)(2,1)}, u32[]{:S(2)}) copy-start(bf16[768,256]{1,0:T(8,128)(2,1)} %copy-done.10) | copy-start | bytes 1179652
  30.7 23.3 %collective-permute-start.5 = (f32[512,256]{1,0:T(8,128)S(1)}, f32[512,256]{1,0:T(8,128)S(1)}, u32[]{:S(2)}, u32[]{:S(2)}) collective-permute-start(f32[512,256]{1,0:T(8,128)S(1)} %get-tuple-element.39.e), channel_id=1, source_target_pairs={{0,2},{1,3},{4,6},{5,7},{8,10},{9,11},{12,14},{13,15},{16,18},{17,... | collective-permute-start | bytes 1572872 | tf_op jit(solution)/shard_map/ppermute | solution.py:226
  35.0 37.5 %collective-permute-start.6 = (f32[512,256]{1,0:T(8,128)S(1)}, f32[512,256]{1,0:T(8,128)S(1)}, u32[]{:S(2)}, u32[]{:S(2)}) collective-permute-start(f32[512,256]{1,0:T(8,128)S(1)} %get-tuple-element.40.o), channel_id=1, source_target_pairs={{2,4},{3,5},{6,8},{7,9},{10,12},{11,13},{14,16},{15,17},{18,20},{1... | collective-permute-start | bytes 1572872 | tf_op jit(solution)/shard_map/ppermute | solution.py:225
  45.3 8.7 %collective-permute-start.8 = (f32[256,256]{1,0:T(8,128)S(1)}, f32[256,256]{1,0:T(8,128)S(1)}, u32[]{:S(2)}, u32[]{:S(2)}) collective-permute-start(f32[256,256]{1,0:T(8,128)S(1)} %slice.4), channel_id=1, source_target_pairs={{0,1},{2,3},{4,5},{6,7},{8,9},{10,11},{12,13},{14,15},{16,17},{18,... | collective-permute-start | bytes 786440 | tf_op jit(solution)/shard_map/ppermute | solution.py:221
  75.4 11.2 %collective-permute-start.10 = (f32[256,512]{1,0:T(8,128)S(1)}, f32[256,512]{1,0:T(8,128)S(1)}, u32[]{:S(2)}, u32[]{:S(2)}) collective-permute-start(f32[256,512]{1,0:T(8,128)S(1)} %get-tuple-element.52), channel_id=1, source_target_pairs={{32,1},{34,3},{36,5},{38,7},{40,9},{42,11},{44,13},{46,15},{48,17}... | collective-permute-start | bytes 1572872 | tf_op jit(solution)/shard_map/ppermute | solution.py:222
  77.4 9.4 %collective-permute-start.9 = (f32[256,512]{1,0:T(8,128)S(1)}, f32[256,512]{1,0:T(8,128)S(1)}, u32[]{:S(2)}, u32[]{:S(2)}) collective-permute-start(f32[256,512]{1,0:T(8,128)S(1)} %get-tuple-element.51), channel_id=1, source_target_pairs={{0,1},{2,3},{4,5},{6,7},{8,9},{10,11},{12,13},{14,15},{16,17},{18,... | collective-permute-start | bytes 1572872 | tf_op jit(solution)/shard_map/ppermute | solution.py:221
  87.4 7.3 %collective-permute-start.11 = (f32[256,512]{1,0:T(8,128)S(1)}, f32[256,512]{1,0:T(8,128)S(1)}, u32[]{:S(2)}, u32[]{:S(2)}) collective-permute-start(f32[256,512]{1,0:T(8,128)S(1)} %shard_map.86.x), channel_id=1, source_target_pairs={{0,1},{2,3},{4,5},{6,7},{8,9},{10,11},{12,13},{14,15},{16,17},{18,... | collective-permute-start | bytes 1572872 | tf_op jit(solution)/shard_map/ppermute | solution.py:221
  92.8 13.7 %collective-permute-start.12 = (f32[256,512]{1,0:T(8,128)S(1)}, f32[256,512]{1,0:T(8,128)S(1)}, u32[]{:S(2)}, u32[]{:S(2)}) collective-permute-start(f32[256,512]{1,0:T(8,128)S(1)} %shard_map.86.x), channel_id=1, source_target_pairs={{32,1},{34,3},{36,5},{38,7},{40,9},{42,11},{44,13},{46,15},{48,17}... | collective-permute-start | bytes 1572872 | tf_op jit(solution)/shard_map/ppermute | solution.py:222
  107.7 13.5 %collective-permute-start.13 = (f32[512,256]{1,0:T(8,128)S(1)}, f32[512,256]{1,0:T(8,128)S(1)}, u32[]{:S(2)}, u32[]{:S(2)}) collective-permute-start(f32[512,256]{1,0:T(8,128)S(1)} %get-tuple-element.54.e), channel_id=1, source_target_pairs={{0,2},{1,3},{4,6},{5,7},{8,10},{9,11},{12,14},{13,15},{16,18},{17,... | collective-permute-start | bytes 1572872 | tf_op jit(solution)/shard_map/ppermute | solution.py:226
  109.7 32.5 %collective-permute-start.14 = (f32[512,256]{1,0:T(8,128)S(1)}, f32[512,256]{1,0:T(8,128)S(1)}, u32[]{:S(2)}, u32[]{:S(2)}) collective-permute-start(f32[512,256]{1,0:T(8,128)S(1)} %get-tuple-element.55.o), channel_id=1, source_target_pairs={{2,4},{3,5},{6,8},{7,9},{10,12},{11,13},{14,16},{15,17},{18,20},{1... | collective-permute-start | bytes 1572872 | tf_op jit(solution)/shard_map/ppermute | solution.py:225
  145.1 8.0 %collective-permute-start.15 = (f32[256,512]{1,0:T(8,128)S(1)}, f32[256,512]{1,0:T(8,128)S(1)}, u32[]{:S(2)}, u32[]{:S(2)}) collective-permute-start(f32[256,512]{1,0:T(8,128)S(1)} %get-tuple-element.57), channel_id=1, source_target_pairs={{0,1},{2,3},{4,5},{6,7},{8,9},{10,11},{12,13},{14,15},{16,17},{18,... | collective-permute-start | bytes 1572872 | tf_op jit(solution)/shard_map/ppermute | solution.py:221
  151.1 10.5 %collective-permute-start.16 = (f32[256,512]{1,0:T(8,128)S(1)}, f32[256,512]{1,0:T(8,128)S(1)}, u32[]{:S(2)}, u32[]{:S(2)}) collective-permute-start(f32[256,512]{1,0:T(8,128)S(1)} %get-tuple-element.58), channel_id=1, source_target_pairs={{32,1},{34,3},{36,5},{38,7},{40,9},{42,11},{44,13},{46,15},{48,17}... | collective-permute-start | bytes 1572872 | tf_op jit(solution)/shard_map/ppermute | solution.py:222
  162.3 3.4 %collective-permute-start.17 = (f32[256,256]{1,0:T(8,128)S(1)}, f32[256,256]{1,0:T(8,128)S(1)}, u32[]{:S(2)}, u32[]{:S(2)}) collective-permute-start(f32[256,256]{1,0:T(8,128)S(1)} %get-tuple-element.60), channel_id=1, source_target_pairs={{0,1},{2,3},{4,5},{6,7},{8,9},{10,11},{12,13},{14,15},{16,17},{18,... | collective-permute-start | bytes 786440 | tf_op jit(solution)/shard_map/ppermute | solution.py:221

commit v4 on v3

v4 whole, which is shorter than its diff:
```python
import jax
import jax.numpy as jnp
from jax import lax
from jax.experimental import pallas as pl
from jax.experimental.pallas import tpu as pltpu
from jax.sharding import PartitionSpec as P


f32 = jnp.float32
bf16 = jnp.bfloat16
VMEM = pl.BlockSpec(memory_space=pltpu.VMEM)
SMEM = pl.BlockSpec(memory_space=pltpu.SMEM)


def split(x):
    hi = x.astype(bf16)
    return hi, (x - hi.astype(f32)).astype(bf16)


def dot3(x, y):
    (xh, xl), (yh, yl) = x, y
    mm = lambda a, b: jnp.dot(a, b, preferred_element_type=f32)
    return mm(xh, yh) + (mm(xh, yl) + mm(xl, yh))


def soft(v, h):
    return v - jnp.minimum(jnp.maximum(v, -h), h)


def call(body, ins, outs, flops, scratch=(), limit=16 << 20):
    size = lambda a: a.size * a.dtype.itemsize
    return pl.pallas_call(
        body,
        out_shape=[jax.ShapeDtypeStruct(s, d) for s, d in outs],
        in_specs=[SMEM if a.size < 64 else VMEM for a in ins],
        out_specs=[VMEM for _ in outs],
        scratch_shapes=list(scratch),
        compiler_params=pltpu.CompilerParams(vmem_limit_bytes=limit),
        cost_estimate=pl.CostEstimate(
            flops=flops, bytes_accessed=sum(size(a) for a in ins), transcendentals=0
        ),
    )(*ins)


def own_is_e(pos):
    return (pos[2] // 2 + pos[2] % 2) % 2 == 1


def prepare(fx, bx, pos):
    blk = fx.shape[2]

    def body(fx, bx, pos, ah, al, th, tl):
        row, rows, core = pos[0], pos[1], pos[2] % 2
        for k, s in enumerate((1, 2 - 2 * core, 2 * core)):
            r = slice(k * blk, (k + 1) * blk)
            m = bx[core, s].astype(f32)
            if k == 2:
                m = jnp.where(row == jnp.where(core == 0, 0, rows - 1), 0.0, m)
            v = fx[core, s] * m
            ah[:, r], al[:, r] = split(v)
            th[r, :], tl[r, :] = split(v.T)

    outs = [((blk, 3 * blk), bf16)] * 2 + [((3 * blk, blk), bf16)] * 2
    o = call(body, (fx, bx, pos), outs, 0)
    return o[0:2], o[2:4]


def prepare_columns(own, other, pos):
    blk = own.shape[2]

    def body(own, other, pos, wh, wl, nh, nl, eh, el, oh, ol):
        flag = own_is_e(pos)
        core = pos[2] % 2

        def pick(i):
            p = own[(1, 2 - 2 * core, 2 * core)[i]]
            k = (1, 2 * core, 2 - 2 * core)[i]
            q = other[pl.ds(pl.multiple_of(k * blk, blk), blk), :]
            return jnp.where(flag, p, q), jnp.where(flag, q, p)

        (ee, oo), (eo, oe), (ex, ox) = pick(0), pick(1), pick(2)
        a, b = slice(0, blk), slice(blk, 2 * blk)
        for v, i, j in ((ee, a, a), (eo, a, b), (oo, b, b), (oe, b, a)):
            nh[i, j], nl[i, j] = split(v)
            wh[j, i], wl[j, i] = split(v.T)
        eh[...], el[...] = split(ex.T)
        oh[...], ol[...] = split(ox.T)

    outs = [((2 * blk, 2 * blk), bf16)] * 4 + [((blk, blk), bf16)] * 4
    o = call(body, (own, other, pos), outs, 0)
    return o[0:2], o[2:4], o[4:6], o[6:8]


def messages(xh, xl, ah, al, wh, wl, obs, e, o, o2):
    blk = ah.shape[0]
    u = dot3((ah[...], al[...]), (xh[...], xl[...]))
    w = dot3(split(u), (wh[...], wl[...])) - obs
    cut = o.shape[0] - blk
    a, b = slice(0, blk), slice(blk, 2 * blk)
    e[:blk, :], e[blk:, :] = u[:, a], w[:, a]
    o[:blk, :], o[blk:, :] = u[:, b], w[:cut, b]
    o2[...] = w[cut:, b]


def message_shapes(blk):
    cut = blk // 4
    return [((2 * blk, blk), f32), ((blk + cut, blk), f32), ((blk - cut, blk), f32)]


def first_messages(x, packed, bown, bother, obs, ax, fw, pos):
    m, blk = x.shape

    def body(x, pk, bown, bother, obs, ah, al, wh, wl, pos, e, o, o2, x0, ob, xh, xl):
        flag = own_is_e(pos)
        core = pos[2] % 2
        at = lambda first: pl.ds(pl.multiple_of(first, blk), blk)
        here, there = core * blk, blk - core * blk
        rows = ((x[at(here), :], pk[at(3 * blk + here), :]), (x[at(there), :], pk[at(3 * blk + there), :]))
        rows += ((bown[...], bother[...]),)
        a, b = slice(0, blk), slice(blk, 2 * blk)
        for k, (p, q) in enumerate(rows):
            r = slice(k * blk, (k + 1) * blk)
            ve, vo = jnp.where(flag, p, q), jnp.where(flag, q, p)
            if k == 0:
                x0[:, a], x0[:, b] = ve, vo
            xh[r, a], xl[r, a] = split(ve)
            xh[r, b], xl[r, b] = split(vo)
        p, q = obs[at(here), :], pk[5 * blk :, :]
        ob[:, a], ob[:, b] = jnp.where(flag, p, q), jnp.where(flag, q, p)
        messages(xh, xl, ah, al, wh, wl, ob[...], e, o, o2)

    outs = message_shapes(blk) + [((blk, 2 * blk), f32)] * 2
    scratch = [pltpu.VMEM((3 * blk, 2 * blk), bf16)] * 2
    ins = (x, packed, bown, bother, obs, *ax, *fw, pos)
    return call(body, ins, outs, 60 * blk**3, scratch)


def later_messages(x, xa, xb, obs, ax, fw):
    blk = x.shape[0]

    def body(x, xa, xb, obs, ah, al, wh, wl, e, o, o2, xh, xl):
        for k, v in enumerate((x, xa, xb)):
            r = slice(k * blk, (k + 1) * blk)
            xh[r, :], xl[r, :] = split(v[...])
        messages(xh, xl, ah, al, wh, wl, obs[...], e, o, o2)

    scratch = [pltpu.VMEM((3 * blk, 2 * blk), bf16)] * 2
    return call(body, (x, xa, xb, obs, *ax, *fw), message_shapes(blk), 60 * blk**3, scratch)


def back(sent, got, gown, gother, fe, fo, fn, atx, pos):
    blk = sent[0].shape[1]

    def body(e, o, o2, re, ro, ro2, relayed, gown, gother, eh, el, oh, ol, nh, nl, th, tl, pos, ps, pa, pb, mh, ml):
        flag = own_is_e(pos)
        half = pos[3] // 4
        chip = pos[2] // 2
        middle = (chip == half - 1) | (chip == half)
        gp, gq = gown[:blk, :], gother[...]
        join = lambda a, b: jnp.concatenate([a[blk:, :], b], axis=0)
        tail = jnp.where(middle, relayed[...], ro2[...])
        sides = (
            (e, e[blk:, :], re, re[blk:, :], (eh, el), jnp.where(flag, gp, gq), slice(0, blk)),
            (o, join(o, o2[...]), ro, join(ro, tail), (oh, ol), jnp.where(flag, gq, gp), slice(blk, 2 * blk)),
        )
        outer = []
        for u, w, ru, rw, (fh, fl), g, s in sides:
            m = w + dot3(split(ru[:blk, :]), (fh[...], fl[...]))
            mh[:, s], ml[:, s] = split(m)
            beyond = rw + dot3(split(u[:blk, :]), split(g.T))
            outer.append(dot3(split(beyond), split(g)))
        n = dot3((mh[...], ml[...]), (nh[...], nl[...])) + jnp.concatenate(outer, axis=1)
        nsplit = split(n)
        for k, out in enumerate((ps, pa, pb)):
            r = slice(k * blk, (k + 1) * blk)
            out[...] = dot3((th[r, :], tl[r, :]), nsplit)

    scratch = [pltpu.VMEM((blk, 2 * blk), bf16)] * 2
    ins = (*sent, *got, gown, gother, *fe, *fo, *fn, *atx, pos)
    return call(body, ins, [((blk, 2 * blk), f32)] * 3, 96 * blk**3, scratch)


def update(x, ps, ra, rb, sc):
    def body(x, ps, ra, rb, sc, o):
        o[...] = soft(x[...] - sc[0] * (ps[...] + (ra[...] + rb[...])), sc[1])

    return call(body, (x, ps, ra, rb, sc), [(x.shape, f32)], 1 << 20)[0]


def last_update(x, ps, ra, rb, sc, pos):
    blk = x.shape[0]

    def body(x, ps, ra, rb, sc, pos, keep, give):
        flag = own_is_e(pos)
        v = soft(x[...] - sc[0] * (ps[...] + (ra[...] + rb[...])), sc[1])
        keep[...] = jnp.where(flag, v[:, :blk], v[:, blk:])
        give[...] = jnp.where(flag, v[:, blk:], v[:, :blk])

    return call(body, (x, ps, ra, rb, sc, pos), [((blk, blk), f32)] * 2, 1 << 20)


def stack(keep, got, pos):
    blk = keep.shape[0]

    def body(keep, got, pos, o):
        core = pos[2] % 2
        o[pl.ds(pl.multiple_of(core * blk, blk), blk), :] = keep[...]
        o[pl.ds(pl.multiple_of(blk - core * blk, blk), blk), :] = got[...]

    return call(body, (keep, got, pos), [((2 * blk, blk), f32)], 1 << 20)[0]


def per_device(x, observed, fx, bx, fy, by, step_size, threshold):
    blk = fx.shape[2]
    rows, cols = lax.axis_size("row"), lax.axis_size("col")
    chips = cols // 2
    at = lambda r, c: r * cols + c
    both = lambda forth: forth + [(j, i) for i, j in forth]
    chip_pairs = both([(2 * k, 2 * k + 1) for k in range(chips)])
    outer_pairs = both([(2 * k + 1, 2 * k + 2) for k in range(chips - 1)])
    side_pairs = [
        both([(2 * k + i, 2 * k + 2 + i) for k in range(first, chips - 1, 2) for i in range(2)])
        for first in (0, 1)
    ]
    row_pairs = both(
        [(at(r, 2 * k), at(r - 1, 2 * k + 1)) for r in range(1, rows) for k in range(chips)]
    )
    same_core = [(at(r, 2 * k), at(r + 1, 2 * k)) for r in range(rows - 1) for k in range(chips)]
    same_core += [(at(r, 2 * k + 1), at(r - 1, 2 * k + 1)) for r in range(1, rows) for k in range(chips)]

    half = chips // 2
    cores = lambda hops: [(2 * i + c, 2 * j + c) for i, j in hops for c in range(2)]
    first_hop = [p for p in side_pairs[1] if {p[0] // 2, p[1] // 2} != {half - 1, half}]
    first_hop += cores([(half - 1, 0), (half, chips - 1)])
    second_hop = cores([(0, half), (chips - 1, half - 1)])

    swap_chip = lambda v: lax.ppermute(v, "col", chip_pairs)
    swap_row = lambda v: lax.ppermute(v, ("row", "col"), row_pairs)

    def swap_sides(e, o, o2):
        ro2 = lax.ppermute(o2, "col", first_hop)
        ro = lax.ppermute(o, "col", side_pairs[1])
        re = lax.ppermute(e, "col", side_pairs[0])
        return re, ro, ro2, lax.ppermute(ro2, "col", second_hop)

    col = lax.axis_index("col")
    core = col % 2
    pos = jnp.stack([lax.axis_index("row"), rows, col, cols]).astype(jnp.int32)
    sc = jnp.concatenate([step_size, threshold])
    mine = lax.dynamic_slice_in_dim(x, core * blk, blk)
    other = lax.dynamic_slice_in_dim(x, blk - core * blk, blk)
    bother = swap_row(mine)
    bown = lax.ppermute(other, ("row", "col"), same_core)
    slot = jnp.arange(3)
    inside = ((slot > 0) | (col > 0)) & ((slot < 2) | (col < cols - 1))
    fy = fy[0] * (by[0] * inside).astype(f32)[:, None, None]
    far = lax.dynamic_slice_in_dim(observed, blk - core * blk, blk)
    packed = swap_chip(jnp.concatenate([fy.reshape(3 * blk, blk), x, far]))
    outer = lax.dynamic_slice_in_dim(fy, 2 * core, 1)[0]
    gown = lax.ppermute(jnp.pad(outer, ((0, blk + 8), (0, 0))), "col", outer_pairs)
    gother = swap_chip(gown[:blk])
    ax, atx = prepare(fx, bx, pos)
    fw, fn, fe, fo = prepare_columns(fy, packed, pos)

    *sent, x, obs = first_messages(x, packed, bown, bother, observed, ax, fw, pos)
    got = swap_sides(*sent)
    ps, pa, pb = back(sent, got, gown, gother, fe, fo, fn, atx, pos)
    x = update(x, ps, swap_chip(pa), swap_row(pb), sc)
    sent = later_messages(x, swap_chip(x), swap_row(x), obs, ax, fw)
    got = swap_sides(*sent)
    ps, pa, pb = back(sent, got, gown, gother, fe, fo, fn, atx, pos)
    keep, give = last_update(x, ps, swap_chip(pa), swap_row(pb), sc, pos)
    return stack(keep, swap_chip(give), pos)


def solution(mesh):
    in_specs = (
        P("row", "col"),
        P("row", "col"),
        P("row", None, None, None),
        P("row", None),
        P("col", None, None, None),
        P("col", None),
        P(),
        P(),
    )
    return jax.shard_map(
        per_device, mesh=mesh, in_specs=in_specs, out_specs=P("row", "col"), check_vma=False
    )
```

time: 168 us -> 164 us (0.976)
  the two profiles are of different devices: /device:TPU:51 before, /device:TPU:59 now
where the time goes in v4:
time: 164 us; the launch traced here: 163 us
  starting transfers between devices  71 us (43%)
  waiting for transfers between devices  65.7 us (40%)
  Pallas kernels  14.9 us (9%)
  local copies, waits for them, and re-layouts  5.13 us (3%)
  other arithmetic  4.73 us (3%)
    ppermute x4, waiting for transfers between devices, per_device(): swap_row = lambda v: lax.ppermute(v, ('row', 'col'), row_pairs)  37.1 us
    ppermute x4, starting transfers between devices, per_device(): swap_row = lambda v: lax.ppermute(v, ('row', 'col'), row_pairs)  18.8 us
    ppermute x6, starting transfers between devices, per_device(): swap_chip = lambda v: lax.ppermute(v, 'col', chip_pairs)  18 us
    pallas_call x9, Pallas kernels, call(): pl.pallas_call(body, out_shape=[jax.ShapeDtypeStruct(s, d) for s, d in ou...  14.9 us
    ppermute x2, waiting for transfers between devices, swap_sides(): ro = lax.ppermute(o, 'col', side_pairs[1])  13.6 us
    ppermute x2, waiting for transfers between devices, swap_sides(): return (re, ro, ro2, lax.ppermute(ro2, 'col', second_hop))  13.4 us
    ppermute x2, starting transfers between devices, swap_sides(): ro2 = lax.ppermute(o2, 'col', first_hop)  10.2 us
    ppermute x2, starting transfers between devices, swap_sides(): ro = lax.ppermute(o, 'col', side_pairs[1])  8.82 us
  transfers between devices with their start and end apart: 20, of which 9 were waited for; matrix products, arithmetic and copies ran while one was open for 2% of the time, Pallas kernels for 2%

profile of v4, /device:TPU:59, one launch (start us, length us, event | category | flops | bytes accessed | tf_op | source)
XLA Modules:
  0.0 163.1 jit_solution(16304594828767636863)
XLA Ops:
  4.4 2.6 %collective-permute-start = (f32[1536,256]{1,0:T(8,128)}, f32[1536,256]{1,0:T(8,128)S(1)}, u32[]{:S(2)}, u32[]{:S(2)}) collective-permute-start(f32[1536,256]{1,0:T(8,128)} %pad_maximum_fusion), channel_id=1, source_target_pairs={{0,1},{2,3},{4,5},{6,7},{8,9},{10,11},{12,13},{14,15},{16,17},{18,... | collective-permute-start | bytes 4718600 | tf_op jit(solution)/shard_map/ppermute | solution.py:237
  7.8 3.1 %collective-permute-start.1 = (f32[256,256]{1,0:T(8,128)}, f32[256,256]{1,0:T(8,128)S(1)}, u32[]{:S(2)}, u32[]{:S(2)}) collective-permute-start(f32[256,256]{1,0:T(8,128)} %get-tuple-element.62), channel_id=1, source_target_pairs={{0,32},{2,34},{4,36},{6,38},{8,40},{10,42},{12,44},{14,46},{16,48}... | collective-permute-start | bytes 786440 | tf_op jit(solution)/shard_map/ppermute | solution.py:253
  10.9 5.0 %collective-permute-start.2 = (f32[256,256]{1,0:T(8,128)}, f32[256,256]{1,0:T(8,128)S(1)}, u32[]{:S(2)}, u32[]{:S(2)}) collective-permute-start(f32[256,256]{1,0:T(8,128)} %get-tuple-element.61), channel_id=1, source_target_pairs={{32,1},{34,3},{36,5},{38,7},{40,9},{42,11},{44,13},{46,15},{48,17}... | collective-permute-start | bytes 786440 | tf_op jit(solution)/shard_map/ppermute | solution.py:238
  18.1 3.6 %collective-permute-start.7 = (f32[520,256]{1,0:T(8,128)}, f32[520,256]{1,0:T(8,128)}, u32[]{:S(2)}, u32[]{:S(2)}) collective-permute-start(f32[520,256]{1,0:T(8,128)} %pad.4), channel_id=1, source_target_pairs={{1,2},{3,4},{5,6},{7,8},{9,10},{11,12},{13,14},{15,16},{17,18},{19... | collective-permute-start | bytes 1597448 | tf_op jit(solution)/shard_map/ppermute | solution.py:260
  21.8 1.4 copy-done.1
  26.4 1.9 %shard_map.84 = (f32[512,256]{1,0:T(8,128)S(1)}, f32[320,256]{1,0:T(8,128)S(1)}, f32[192,256]{1,0:T(8,128)S(1)}, f32[256,512]{1,0:T(8,128)S(1)}, f32[256,512]{1,0:T(8,128)S(1)}) custom-call(f32[512,256]{1,0:T(8,128)S(1)} %copy-done, f32[1536,256]{1,0:T(8,128)S(1)} %collective-permute-done.other.pk, f32[256,256]{1,0:T(8,128)S(1)} %collective-permute-done.1.bown, ...), custom_call_target="tpu_custom_call" | custom-call | flops 1006632960 | bytes 4980752 | tf_op jit(solution)/shard_map/pallas_call | solution.py:32
  28.3 4.0 %collective-permute-start.3 = (f32[512,256]{1,0:T(8,128)S(1)}, f32[512,256]{1,0:T(8,128)S(1)}, u32[]{:S(2)}, u32[]{:S(2)}) collective-permute-start(f32[512,256]{1,0:T(8,128)S(1)} %get-tuple-element.38.e), channel_id=1, source_target_pairs={{0,2},{1,3},{4,6},{5,7},{8,10},{9,11},{12,14},{13,15},{16,18},{17,... | collective-permute-start | bytes 1572872 | tf_op jit(solution)/shard_map/ppermute | solution.py:243
  32.3 8.9 %collective-permute-start.5 = (f32[192,256]{1,0:T(8,128)S(1)}, f32[192,256]{1,0:T(8,128)S(1)}, u32[]{:S(2)}, u32[]{:S(2)}) collective-permute-start(f32[192,256]{1,0:T(8,128)S(1)} %get-tuple-element.40.o2), channel_id=1, source_target_pairs={{2,4},{3,5},{6,8},{7,9},{10,12},{11,13},{18,20},{19,21},{22,24},{2... | collective-permute-start | bytes 589832 | tf_op jit(solution)/shard_map/ppermute | solution.py:241
  41.2 1.9 %collective-permute-start.4 = (f32[320,256]{1,0:T(8,128)S(1)}, f32[320,256]{1,0:T(8,128)S(1)}, u32[]{:S(2)}, u32[]{:S(2)}) collective-permute-start(f32[320,256]{1,0:T(8,128)S(1)} %get-tuple-element.39.o), channel_id=1, source_target_pairs={{2,4},{3,5},{6,8},{7,9},{10,12},{11,13},{14,16},{15,17},{18,20},{1... | collective-permute-start | bytes 983048 | tf_op jit(solution)/shard_map/ppermute | solution.py:242
  44.1 7.7 %collective-permute-start.8 = (f32[256,256]{1,0:T(8,128)S(1)}, f32[256,256]{1,0:T(8,128)S(1)}, u32[]{:S(2)}, u32[]{:S(2)}) collective-permute-start(f32[256,256]{1,0:T(8,128)S(1)} %slice.4), channel_id=1, source_target_pairs={{0,1},{2,3},{4,5},{6,7},{8,9},{10,11},{12,13},{14,15},{16,17},{18,... | collective-permute-start | bytes 786440 | tf_op jit(solution)/shard_map/ppermute | solution.py:237
  53.1 4.3 %collective-permute-done.4.ro = f32[320,256]{1,0:T(8,128)S(1)} collective-permute-done((f32[320,256]{1,0:T(8,128)S(1)}, f32[320,256]{1,0:T(8,128)S(1)}, u32[]{:S(2)}, u32[]{:S(2)}) %collective-permute-start.4) | collective-permute-done | bytes 327712 | tf_op jit(solution)/shard_map/ppermute | solution.py:242
  57.4 8.7 %collective-permute-done.6.relayed = f32[192,256]{1,0:T(8,128)S(1)} collective-permute-done((f32[192,256]{1,0:T(8,128)S(1)}, f32[192,256]{1,0:T(8,128)S(1)}, u32[]{:S(2)}, u32[]{:S(2)}) %collective-permute-start.6) | collective-permute-done | bytes 196640 | tf_op jit(solution)/shard_map/ppermute | solution.py:244
  66.1 3.5 %shard_map.85 = (f32[256,512]{1,0:T(8,128)S(1)}, f32[256,512]{1,0:T(8,128)S(1)}, f32[256,512]{1,0:T(8,128)S(1)}) custom-call(f32[512,256]{1,0:T(8,128)S(1)} %get-tuple-element.38.e, f32[320,256]{1,0:T(8,128)S(1)} %get-tuple-element.39.o, f32[192,256]{1,0:T(8,128)S(1)} %get-tuple-element.40.o2, f32[512,256]{1,0:T(8,128)S(1)} %collective-permute-done.3.re, ...), custom_call_target="tpu_custom_call" | custom-call | flops 1610612736 | bytes 5447696 | tf_op jit(solution)/shard_map/pallas_call | solution.py:32
  69.6 4.8 %collective-permute-start.10 = (f32[256,512]{1,0:T(8,128)S(1)}, f32[256,512]{1,0:T(8,128)S(1)}, u32[]{:S(2)}, u32[]{:S(2)}) collective-permute-start(f32[256,512]{1,0:T(8,128)S(1)} %get-tuple-element.51), channel_id=1, source_target_pairs={{32,1},{34,3},{36,5},{38,7},{40,9},{42,11},{44,13},{46,15},{48,17}... | collective-permute-start | bytes 1572872 | tf_op jit(solution)/shard_map/ppermute | solution.py:238
  74.3 1.9 %collective-permute-start.9 = (f32[256,512]{1,0:T(8,128)S(1)}, f32[256,512]{1,0:T(8,128)S(1)}, u32[]{:S(2)}, u32[]{:S(2)}) collective-permute-start(f32[256,512]{1,0:T(8,128)S(1)} %get-tuple-element.50), channel_id=1, source_target_pairs={{0,1},{2,3},{4,5},{6,7},{8,9},{10,11},{12,13},{14,15},{16,17},{18,... | collective-permute-start | bytes 1572872 | tf_op jit(solution)/shard_map/ppermute | solution.py:237
  77.6 9.2 %collective-permute-done.10.rb = f32[256,512]{1,0:T(8,128)S(1)} collective-permute-done((f32[256,512]{1,0:T(8,128)S(1)}, f32[256,512]{1,0:T(8,128)S(1)}, u32[]{:S(2)}, u32[]{:S(2)}) %collective-permute-start.10) | collective-permute-done | bytes 524320 | tf_op jit(solution)/shard_map/ppermute | solution.py:238
  87.5 1.9 %collective-permute-start.11 = (f32[256,512]{1,0:T(8,128)S(1)}, f32[256,512]{1,0:T(8,128)S(1)}, u32[]{:S(2)}, u32[]{:S(2)}) collective-permute-start(f32[256,512]{1,0:T(8,128)S(1)} %shard_map.86.x), channel_id=1, source_target_pairs={{0,1},{2,3},{4,5},{6,7},{8,9},{10,11},{12,13},{14,15},{16,17},{18,... | collective-permute-start | bytes 1572872 | tf_op jit(solution)/shard_map/ppermute | solution.py:237
  89.4 5.2 %collective-permute-start.12 = (f32[256,512]{1,0:T(8,128)S(1)}, f32[256,512]{1,0:T(8,128)S(1)}, u32[]{:S(2)}, u32[]{:S(2)}) collective-permute-start(f32[256,512]{1,0:T(8,128)S(1)} %shard_map.86.x), channel_id=1, source_target_pairs={{32,1},{34,3},{36,5},{38,7},{40,9},{42,11},{44,13},{46,15},{48,17}... | collective-permute-start | bytes 1572872 | tf_op jit(solution)/shard_map/ppermute | solution.py:238
  94.7 12.8 %collective-permute-done.12.xb = f32[256,512]{1,0:T(8,128)S(1)} collective-permute-done((f32[256,512]{1,0:T(8,128)S(1)}, f32[256,512]{1,0:T(8,128)S(1)}, u32[]{:S(2)}, u32[]{:S(2)}) %collective-permute-start.12) | collective-permute-done | bytes 524320 | tf_op jit(solution)/shard_map/ppermute | solution.py:238
  107.5 1.3 shard_map.87
  108.8 1.9 %collective-permute-start.13 = (f32[512,256]{1,0:T(8,128)S(1)}, f32[512,256]{1,0:T(8,128)S(1)}, u32[]{:S(2)}, u32[]{:S(2)}) collective-permute-start(f32[512,256]{1,0:T(8,128)S(1)} %get-tuple-element.53.e), channel_id=1, source_target_pairs={{0,2},{1,3},{4,6},{5,7},{8,10},{9,11},{12,14},{13,15},{16,18},{17,... | collective-permute-start | bytes 1572872 | tf_op jit(solution)/shard_map/ppermute | solution.py:243
  110.7 1.3 collective-permute-start.15
  112.0 6.9 %collective-permute-start.14 = (f32[320,256]{1,0:T(8,128)S(1)}, f32[320,256]{1,0:T(8,128)S(1)}, u32[]{:S(2)}, u32[]{:S(2)}) collective-permute-start(f32[320,256]{1,0:T(8,128)S(1)} %get-tuple-element.54.o), channel_id=1, source_target_pairs={{2,4},{3,5},{6,8},{7,9},{10,12},{11,13},{14,16},{15,17},{18,20},{1... | collective-permute-start | bytes 983048 | tf_op jit(solution)/shard_map/ppermute | solution.py:242
  120.3 9.4 %collective-permute-done.14.ro = f32[320,256]{1,0:T(8,128)S(1)} collective-permute-done((f32[320,256]{1,0:T(8,128)S(1)}, f32[320,256]{1,0:T(8,128)S(1)}, u32[]{:S(2)}, u32[]{:S(2)}) %collective-permute-start.14) | collective-permute-done | bytes 327712 | tf_op jit(solution)/shard_map/ppermute | solution.py:242
  129.6 4.7 %collective-permute-done.16.relayed = f32[192,256]{1,0:T(8,128)S(1)} collective-permute-done((f32[192,256]{1,0:T(8,128)S(1)}, f32[192,256]{1,0:T(8,128)S(1)}, u32[]{:S(2)}, u32[]{:S(2)}) %collective-permute-start.16) | collective-permute-done | bytes 196640 | tf_op jit(solution)/shard_map/ppermute | solution.py:244
  134.3 3.5 %shard_map.88 = (f32[256,512]{1,0:T(8,128)S(1)}, f32[256,512]{1,0:T(8,128)S(1)}, f32[256,512]{1,0:T(8,128)S(1)}) custom-call(f32[512,256]{1,0:T(8,128)S(1)} %get-tuple-element.53.e, f32[320,256]{1,0:T(8,128)S(1)} %get-tuple-element.54.o, f32[192,256]{1,0:T(8,128)S(1)} %get-tuple-element.55.o2, f32[512,256]{1,0:T(8,128)S(1)} %collective-permute-done.13.re, ...), custom_call_target="tpu_custom_call" | custom-call | flops 1610612736 | bytes 5447696 | tf_op jit(solution)/shard_map/pallas_call | solution.py:32
  137.8 1.9 %collective-permute-start.17 = (f32[256,512]{1,0:T(8,128)S(1)}, f32[256,512]{1,0:T(8,128)S(1)}, u32[]{:S(2)}, u32[]{:S(2)}) collective-permute-start(f32[256,512]{1,0:T(8,128)S(1)} %get-tuple-element.57), channel_id=1, source_target_pairs={{0,1},{2,3},{4,5},{6,7},{8,9},{10,11},{12,13},{14,15},{16,17},{18,... | collective-permute-start | bytes 1572872 | tf_op jit(solution)/shard_map/ppermute | solution.py:237
  139.7 3.8 %collective-permute-start.18 = (f32[256,512]{1,0:T(8,128)S(1)}, f32[256,512]{1,0:T(8,128)S(1)}, u32[]{:S(2)}, u32[]{:S(2)}) collective-permute-start(f32[256,512]{1,0:T(8,128)S(1)} %get-tuple-element.58), channel_id=1, source_target_pairs={{32,1},{34,3},{36,5},{38,7},{40,9},{42,11},{44,13},{46,15},{48,17}... | collective-permute-start | bytes 1572872 | tf_op jit(solution)/shard_map/ppermute | solution.py:238
  143.6 13.9 %collective-permute-done.18.rb = f32[256,512]{1,0:T(8,128)S(1)} collective-permute-done((f32[256,512]{1,0:T(8,128)S(1)}, f32[256,512]{1,0:T(8,128)S(1)}, u32[]{:S(2)}, u32[]{:S(2)}) %collective-permute-start.18) | collective-permute-done | bytes 524320 | tf_op jit(solution)/shard_map/ppermute | solution.py:238
  158.3 1.9 %collective-permute-start.19 = (f32[256,256]{1,0:T(8,128)S(1)}, f32[256,256]{1,0:T(8,128)S(1)}, u32[]{:S(2)}, u32[]{:S(2)}) collective-permute-start(f32[256,256]{1,0:T(8,128)S(1)} %get-tuple-element.60), channel_id=1, source_target_pairs={{0,1},{2,3},{4,5},{6,7},{8,9},{10,11},{12,13},{14,15},{16,17},{18,... | collective-permute-start | bytes 786440 | tf_op jit(solution)/shard_map/ppermute | solution.py:237
  160.2 1.5 collective-permute-done.19.got
  161.7 1.4 shard_map.90
  (38 shorter events, 15.7 us)
Async XLA Ops:
  0.0 3.1 %copy-start = (f32[512,256]{1,0:T(8,128)S(1)}, f32[512,256]{1,0:T(8,128)}, u32[]{:S(2)}) copy-start(f32[512,256]{1,0:T(8,128)} %x.3) | copy-start | bytes 1572868
  4.4 19.6 %collective-permute-start = (f32[1536,256]{1,0:T(8,128)}, f32[1536,256]{1,0:T(8,128)S(1)}, u32[]{:S(2)}, u32[]{:S(2)}) collective-permute-start(f32[1536,256]{1,0:T(8,128)} %pad_maximum_fusion), channel_id=1, source_target_pairs={{0,1},{2,3},{4,5},{6,7},{8,9},{10,11},{12,13},{14,15},{16,17},{18,... | collective-permute-start | bytes 4718600 | tf_op jit(solution)/shard_map/ppermute | solution.py:237
  7.8 13.9 %copy-start.3 = (s32[2,3]{1,0:T(2,128)S(1)}, s32[2,3]{1,0:T(2,128)}, u32[]{:S(2)}) copy-start(s32[2,3]{1,0:T(2,128)} %bx.1) | copy-start | bytes 76
  7.8 17.3 %collective-permute-start.1 = (f32[256,256]{1,0:T(8,128)}, f32[256,256]{1,0:T(8,128)S(1)}, u32[]{:S(2)}, u32[]{:S(2)}) collective-permute-start(f32[256,256]{1,0:T(8,128)} %get-tuple-element.62), channel_id=1, source_target_pairs={{0,32},{2,34},{4,36},{6,38},{8,40},{10,42},{12,44},{14,46},{16,48}... | collective-permute-start | bytes 786440 | tf_op jit(solution)/shard_map/ppermute | solution.py:253
  10.9 15.5 %collective-permute-start.2 = (f32[256,256]{1,0:T(8,128)}, f32[256,256]{1,0:T(8,128)S(1)}, u32[]{:S(2)}, u32[]{:S(2)}) collective-permute-start(f32[256,256]{1,0:T(8,128)} %get-tuple-element.61), channel_id=1, source_target_pairs={{32,1},{34,3},{36,5},{38,7},{40,9},{42,11},{44,13},{46,15},{48,17}... | collective-permute-start | bytes 786440 | tf_op jit(solution)/shard_map/ppermute | solution.py:238
  18.1 25.0 %collective-permute-start.7 = (f32[520,256]{1,0:T(8,128)}, f32[520,256]{1,0:T(8,128)}, u32[]{:S(2)}, u32[]{:S(2)}) collective-permute-start(f32[520,256]{1,0:T(8,128)} %pad.4), channel_id=1, source_target_pairs={{1,2},{3,4},{5,6},{7,8},{9,10},{11,12},{13,14},{15,16},{17,18},{19... | collective-permute-start | bytes 1597448 | tf_op jit(solution)/shard_map/ppermute | solution.py:260
  21.8 1.4 copy-start.1
  24.0 2.4 %copy-start.2 = (f32[512,256]{1,0:T(8,128)S(1)}, f32[512,256]{1,0:T(8,128)}, u32[]{:S(2)}) copy-start(f32[512,256]{1,0:T(8,128)} %obs.1) | copy-start | bytes 1572868
  28.3 37.8 %collective-permute-start.3 = (f32[512,256]{1,0:T(8,128)S(1)}, f32[512,256]{1,0:T(8,128)S(1)}, u32[]{:S(2)}, u32[]{:S(2)}) collective-permute-start(f32[512,256]{1,0:T(8,128)S(1)} %get-tuple-element.38.e), channel_id=1, source_target_pairs={{0,2},{1,3},{4,6},{5,7},{8,10},{9,11},{12,14},{13,15},{16,18},{17,... | collective-permute-start | bytes 1572872 | tf_op jit(solution)/shard_map/ppermute | solution.py:243
  32.3 19.5 %collective-permute-start.5 = (f32[192,256]{1,0:T(8,128)S(1)}, f32[192,256]{1,0:T(8,128)S(1)}, u32[]{:S(2)}, u32[]{:S(2)}) collective-permute-start(f32[192,256]{1,0:T(8,128)S(1)} %get-tuple-element.40.o2), channel_id=1, source_target_pairs={{2,4},{3,5},{6,8},{7,9},{10,12},{11,13},{18,20},{19,21},{22,24},{2... | collective-permute-start | bytes 589832 | tf_op jit(solution)/shard_map/ppermute | solution.py:241
  41.2 16.2 %collective-permute-start.4 = (f32[320,256]{1,0:T(8,128)S(1)}, f32[320,256]{1,0:T(8,128)S(1)}, u32[]{:S(2)}, u32[]{:S(2)}) collective-permute-start(f32[320,256]{1,0:T(8,128)S(1)} %get-tuple-element.39.o), channel_id=1, source_target_pairs={{2,4},{3,5},{6,8},{7,9},{10,12},{11,13},{14,16},{15,17},{18,20},{1... | collective-permute-start | bytes 983048 | tf_op jit(solution)/shard_map/ppermute | solution.py:242
  44.1 9.0 %collective-permute-start.8 = (f32[256,256]{1,0:T(8,128)S(1)}, f32[256,256]{1,0:T(8,128)S(1)}, u32[]{:S(2)}, u32[]{:S(2)}) collective-permute-start(f32[256,256]{1,0:T(8,128)S(1)} %slice.4), channel_id=1, source_target_pairs={{0,1},{2,3},{4,5},{6,7},{8,9},{10,11},{12,13},{14,15},{16,17},{18,... | collective-permute-start | bytes 786440 | tf_op jit(solution)/shard_map/ppermute | solution.py:237
  51.8 14.3 %collective-permute-start.6 = (f32[192,256]{1,0:T(8,128)S(1)}, f32[192,256]{1,0:T(8,128)S(1)}, u32[]{:S(2)}, u32[]{:S(2)}) collective-permute-start(f32[192,256]{1,0:T(8,128)S(1)} %collective-permute-done.5.ro2), channel_id=1, source_target_pairs={{0,16},{1,17},{30,14},{31,15},{32,48},{33,49},{62,46},{63,47},{64,... | collective-permute-start | bytes 589832 | tf_op jit(solution)/shard_map/ppermute | solution.py:244
  69.6 17.2 %collective-permute-start.10 = (f32[256,512]{1,0:T(8,128)S(1)}, f32[256,512]{1,0:T(8,128)S(1)}, u32[]{:S(2)}, u32[]{:S(2)}) collective-permute-start(f32[256,512]{1,0:T(8,128)S(1)} %get-tuple-element.51), channel_id=1, source_target_pairs={{32,1},{34,3},{36,5},{38,7},{40,9},{42,11},{44,13},{46,15},{48,17}... | collective-permute-start | bytes 1572872 | tf_op jit(solution)/shard_map/ppermute | solution.py:238
  74.3 12.5 %collective-permute-start.9 = (f32[256,512]{1,0:T(8,128)S(1)}, f32[256,512]{1,0:T(8,128)S(1)}, u32[]{:S(2)}, u32[]{:S(2)}) collective-permute-start(f32[256,512]{1,0:T(8,128)S(1)} %get-tuple-element.50), channel_id=1, source_target_pairs={{0,1},{2,3},{4,5},{6,7},{8,9},{10,11},{12,13},{14,15},{16,17},{18,... | collective-permute-start | bytes 1572872 | tf_op jit(solution)/shard_map/ppermute | solution.py:237
  87.5 7.2 %collective-permute-start.11 = (f32[256,512]{1,0:T(8,128)S(1)}, f32[256,512]{1,0:T(8,128)S(1)}, u32[]{:S(2)}, u32[]{:S(2)}) collective-permute-start(f32[256,512]{1,0:T(8,128)S(1)} %shard_map.86.x), channel_id=1, source_target_pairs={{0,1},{2,3},{4,5},{6,7},{8,9},{10,11},{12,13},{14,15},{16,17},{18,... | collective-permute-start | bytes 1572872 | tf_op jit(solution)/shard_map/ppermute | solution.py:237
  89.4 18.1 %collective-permute-start.12 = (f32[256,512]{1,0:T(8,128)S(1)}, f32[256,512]{1,0:T(8,128)S(1)}, u32[]{:S(2)}, u32[]{:S(2)}) collective-permute-start(f32[256,512]{1,0:T(8,128)S(1)} %shard_map.86.x), channel_id=1, source_target_pairs={{32,1},{34,3},{36,5},{38,7},{40,9},{42,11},{44,13},{46,15},{48,17}... | collective-permute-start | bytes 1572872 | tf_op jit(solution)/shard_map/ppermute | solution.py:238
  108.8 25.5 %collective-permute-start.13 = (f32[512,256]{1,0:T(8,128)S(1)}, f32[512,256]{1,0:T(8,128)S(1)}, u32[]{:S(2)}, u32[]{:S(2)}) collective-permute-start(f32[512,256]{1,0:T(8,128)S(1)} %get-tuple-element.53.e), channel_id=1, source_target_pairs={{0,2},{1,3},{4,6},{5,7},{8,10},{9,11},{12,14},{13,15},{16,18},{17,... | collective-permute-start | bytes 1572872 | tf_op jit(solution)/shard_map/ppermute | solution.py:243
  110.7 8.2 %collective-permute-start.15 = (f32[192,256]{1,0:T(8,128)S(1)}, f32[192,256]{1,0:T(8,128)S(1)}, u32[]{:S(2)}, u32[]{:S(2)}) collective-permute-start(f32[192,256]{1,0:T(8,128)S(1)} %get-tuple-element.55.o2), channel_id=1, source_target_pairs={{2,4},{3,5},{6,8},{7,9},{10,12},{11,13},{18,20},{19,21},{22,24},{2... | collective-permute-start | bytes 589832 | tf_op jit(solution)/shard_map/ppermute | solution.py:241
  112.0 17.6 %collective-permute-start.14 = (f32[320,256]{1,0:T(8,128)S(1)}, f32[320,256]{1,0:T(8,128)S(1)}, u32[]{:S(2)}, u32[]{:S(2)}) collective-permute-start(f32[320,256]{1,0:T(8,128)S(1)} %get-tuple-element.54.o), channel_id=1, source_target_pairs={{2,4},{3,5},{6,8},{7,9},{10,12},{11,13},{14,16},{15,17},{18,20},{1... | collective-permute-start | bytes 983048 | tf_op jit(solution)/shard_map/ppermute | solution.py:242
  119.0 15.4 %collective-permute-start.16 = (f32[192,256]{1,0:T(8,128)S(1)}, f32[192,256]{1,0:T(8,128)S(1)}, u32[]{:S(2)}, u32[]{:S(2)}) collective-permute-start(f32[192,256]{1,0:T(8,128)S(1)} %collective-permute-done.15.ro2), channel_id=1, source_target_pairs={{0,16},{1,17},{30,14},{31,15},{32,48},{33,49},{62,46},{63,47},{64,... | collective-permute-start | bytes 589832 | tf_op jit(solution)/shard_map/ppermute | solution.py:244
  137.8 5.8 %collective-permute-start.17 = (f32[256,512]{1,0:T(8,128)S(1)}, f32[256,512]{1,0:T(8,128)S(1)}, u32[]{:S(2)}, u32[]{:S(2)}) collective-permute-start(f32[256,512]{1,0:T(8,128)S(1)} %get-tuple-element.57), channel_id=1, source_target_pairs={{0,1},{2,3},{4,5},{6,7},{8,9},{10,11},{12,13},{14,15},{16,17},{18,... | collective-permute-start | bytes 1572872 | tf_op jit(solution)/shard_map/ppermute | solution.py:237
  139.7 17.8 %collective-permute-start.18 = (f32[256,512]{1,0:T(8,128)S(1)}, f32[256,512]{1,0:T(8,128)S(1)}, u32[]{:S(2)}, u32[]{:S(2)}) collective-permute-start(f32[256,512]{1,0:T(8,128)S(1)} %get-tuple-element.58), channel_id=1, source_target_pairs={{32,1},{34,3},{36,5},{38,7},{40,9},{42,11},{44,13},{46,15},{48,17}... | collective-permute-start | bytes 1572872 | tf_op jit(solution)/shard_map/ppermute | solution.py:238
  158.3 3.4 %collective-permute-start.19 = (f32[256,256]{1,0:T(8,128)S(1)}, f32[256,256]{1,0:T(8,128)S(1)}, u32[]{:S(2)}, u32[]{:S(2)}) collective-permute-start(f32[256,256]{1,0:T(8,128)S(1)} %get-tuple-element.60), channel_id=1, source_target_pairs={{0,1},{2,3},{4,5},{6,7},{8,9},{10,11},{12,13},{14,15},{16,17},{18,... | collective-permute-start | bytes 786440 | tf_op jit(solution)/shard_map/ppermute | solution.py:237

commit v5 on v2

--- a/solution.py
+++ b/solution.py
@@ -96,54 +96,81 @@
     return call(body, (x, up, down, *ax), [(x.shape, f32)], 36 * blk * blk * n, scratch)[0]
 
 
-def near_misfit(u, ua, observed, byt, *below):
+def rows_of(first, second, r):
+    cut, (a, b) = first.shape[0], r
+    parts = []
+    if a < cut:
+        parts.append(first[a : min(b, cut), :])
+    if b > cut:
+        parts.append(second[max(a - cut, 0) : b - cut, :])
+    return parts[0] if len(parts) == 1 else jnp.concatenate(parts, axis=0)
+
+
+def near_misfit(u, ua, observed, byt, below, cut):
     m, blk = u.shape
-
-    def body(u, ua, obs, byth, bytl, *rest):
-        w = rest[-1]
-        for v in rest[:-1]:
-            w[m:, :] = v[...]
+    extra = below.shape[0]
+
+    def body(u, ua, obs, byth, bytl, below, w, v):
+        v[m - cut :, :] = below[...]
         for i in range(0, m, CHUNK):
             r = slice(i, i + CHUNK)
             acc = -obs[r, :]
-            for k, v in enumerate((ua, u)):
+            for k, x in enumerate((ua, u)):
                 s = slice(k * blk, (k + 1) * blk)
-                acc = acc + dot3(*split(v[r, :]), byth[s, :], bytl[s, :])
-            w[r, :] = acc
-
-    out = (m + sum(v.shape[0] for v in below), blk)
-    return call(body, (u, ua, observed, *byt, *below), [(out, f32)], 24 * m * blk * blk)[0]
-
-
-def full_misfit(w, ub, byt, by):
+                acc = acc + dot3(*split(x[r, :]), byth[s, :], bytl[s, :])
+            here = min(max(cut - i, 0), CHUNK)
+            if here:
+                w[i : i + here, :] = acc[:here]
+            if here < CHUNK:
+                v[i + here - cut : i + CHUNK - cut, :] = acc[here:]
+
+    outs = [((cut, blk), f32), ((m - cut + extra, blk), f32)]
+    return call(body, (u, ua, observed, *byt, below), outs, 24 * m * blk * blk)
+
+
+def full_misfit(w, v, ub, byt, by):
     m, blk = ub.shape
 
-    def body(w, ub, byth, bytl, byh, byl, qa, q):
+    def body(w, v, ub, byth, bytl, byh, byl, qa, qa2, q):
         b = slice(2 * blk, 3 * blk)
-        for i in range(0, m, CHUNK):
-            r = slice(i, i + CHUNK)
-            acc = w[r, :] + dot3(*split(ub[r, :]), byth[b, :], bytl[b, :])
+        for i, qa in ((0, qa), (m // 2, qa2)):
+            r = slice(i, i + m // 2)
+            acc = rows_of(w, v, (i, i + m // 2)) + dot3(*split(ub[r, :]), byth[b, :], bytl[b, :])
             mh, ml = split(acc)
-            for k, o in enumerate((qa, q)):
-                s = slice(k * blk, (k + 1) * blk)
-                o[r, :] = dot3(mh, ml, byh[:, s], byl[:, s])
-
-    return call(body, (w, ub, *byt, *by), [(ub.shape, f32)] * 2, 36 * m * blk * blk)
-
-
-def back(q, ra, wb, u, fb, atx, merged):
+            qa[...] = dot3(mh, ml, byh[:, :blk], byl[:, :blk])
+            q[r, :] = dot3(mh, ml, byh[:, blk : 2 * blk], byl[:, blk : 2 * blk])
+
+    outs = [((m // 2, blk), f32)] * 2 + [((m, blk), f32)]
+    return call(body, (w, v, ub, *byt, *by), outs, 36 * m * blk * blk)
+
+
+def back(q, ra, ra2, wb, vb, relayed, u, fb, atx, pos, merged):
     m, n = q.shape
     blk = m // 2
-
-    def body(q, ra, wb, u, fb, ah, al, *outs):
-        g = fb[fb.shape[0] - blk :, :]
+    cut = wb.shape[0]
+    ins = (q, ra, ra2, wb, vb, relayed, u, *([] if merged else [fb]), *atx, pos)
+
+    def body(q, ra, ra2, wb, vb, relayed, u, *rest):
+        fb = None
+        if not merged:
+            fb, *rest = rest
+        ah, al, pos, *outs = rest
+        half = pos[3] // 2
+        special = (pos[2] == half - 1) | (pos[2] == half) | (pos[2] == 0) | (pos[2] == pos[3] - 1)
+        tail = jnp.where(special, relayed[...], vb[...])
+        if merged:
+            *outs, keep = outs
+            g = tail[m - cut : m - cut + blk]
+            keep[...] = g
+        else:
+            g = fb[...]
         gh, gl = split(g)
         th, tl = split(g.T)
         p = []
-        for r in range(2):
+        for r, a in ((0, ra), (1, ra2)):
             s = slice(r * blk, (r + 1) * blk)
-            other = wb[s, :] + dot3(*split(u[s, :]), th, tl)
-            v = q[s, :] + ra[s, :] + dot3(*split(other), gh, gl)
+            other = rows_of(wb, tail, (r * blk, (r + 1) * blk)) + dot3(*split(u[s, :]), th, tl)
+            v = q[s, :] + a[...] + dot3(*split(other), gh, gl)
             p.append(dot3(ah[r], al[r], *split(v)))
         p0 = p[0][:blk]
         p1 = p[0][blk : 2 * blk] + p[1][:blk]
@@ -158,8 +185,8 @@
             top[...], bottom[...] = p0, p3
             mid[:blk, :], mid[blk:, :] = p1, p2
 
-    outs = [((m, n), f32)] * 2 if merged else [((blk, n), f32), ((m, n), f32), ((blk, n), f32)]
-    return call(body, (q, ra, wb, u, fb, *atx), outs, 60 * blk * blk * n)
+    outs = [((m, n), f32)] * 2 if merged else [((blk, n), f32), ((m, n), f32)]
+    return call(body, ins, outs + [((blk, n), f32)], 60 * blk * blk * n)
 
 
 def update_left(top, bottom, rtop, rbottom, x, up, down, sc, ax):
@@ -216,15 +243,24 @@
     def col_swap(b):
         return lax.ppermute(b, "col", pairs[1])
 
+    half = cols // 2
+    first_hop = [p for p in pairs[1] if set(p) != {half - 1, half}] + [(half - 1, 0), (half, cols - 1)]
+    second_hop = [(0, half), (cols - 1, half - 1)]
+
     def columns(u, fb, merged):
         ua = chip_swap(u)
         ub = col_swap(u)
-        w = near_misfit(u, ua, observed, byt, fb if merged else jnp.zeros((8, fb.shape[1]), f32))
+        if merged:
+            w, v = near_misfit(u, ua, observed, byt, fb, 7 * blk // 4)
+        else:
+            pad = jnp.zeros((16, fb.shape[1]), f32)
+            w, v = near_misfit(u, ua, observed, byt, pad, blk + 8)
+        vb = lax.ppermute(v, "col", first_hop)
         wb = col_swap(w)
-        qa, q = full_misfit(w, ub, byt, byf)
-        ra = chip_swap(qa)
-        fb = wb if merged else fb
-        return (*back(q, ra, wb, u, fb, atx, merged), fb)
+        relayed = lax.ppermute(vb, "col", second_hop)
+        qa, qa2, q = full_misfit(w, v, ub, byt, byf)
+        ra, ra2 = chip_swap(qa), chip_swap(qa2)
+        return back(q, ra, ra2, wb, vb, relayed, u, fb, atx, pos, merged)
 
     pos = jnp.stack([lax.axis_index("row"), rows, lax.axis_index("col"), cols]).astype(jnp.int32)
     sc = jnp.concatenate([step_size, threshold])
@@ -234,7 +270,7 @@
     top, bottom, fb = columns(u, fb, True)
     rtop, rbottom = row_swap(top, bottom)
     x, u = update_left(top, bottom, rtop, rbottom, x, up, down, sc, ax)
-    top, mid, bottom, _ = columns(u, fb, False)
+    top, mid, bottom = columns(u, fb, False)
     rup, rdown = row_swap(top, bottom)
     return update(mid, rup, rdown, x, sc)
 

time: 149 us -> 144 us (0.966)
  the two profiles are of different devices: /device:TPU:58 before, /device:TPU:4 now
where the time goes in v5:
time: 144 us; the launch traced here: 143 us
  waiting for transfers between devices  65.8 us (46%)
  starting transfers between devices  56.3 us (39%)
  Pallas kernels  14.5 us (10%)
  local copies, waits for them, and re-layouts  5.01 us (3%)
  between operations  1.56 us (1%)
    ppermute x2, waiting for transfers between devices, columns(): vb = lax.ppermute(v, 'col', first_hop)  26.8 us
    ppermute x3, waiting for transfers between devices, row_swap(): from_down = lax.ppermute(to_up, 'row', upward)  16.6 us
    ppermute x3, starting transfers between devices, row_swap(): from_down = lax.ppermute(to_up, 'row', upward)  16.4 us
    ppermute x2, starting transfers between devices, columns(): relayed = lax.ppermute(vb, 'col', second_hop)  14.7 us
    pallas_call x10, Pallas kernels, call(): pl.pallas_call(body, out_shape=[jax.ShapeDtypeStruct(s, d) for s, d in ou...  14.5 us
    ppermute x6, starting transfers between devices, chip_swap(): return lax.ppermute(a, 'col', pairs[0])  12.5 us
    ppermute x3, waiting for transfers between devices, row_swap(): from_up = lax.ppermute(to_down, 'row', downward)  11.1 us
    ppermute x3, starting transfers between devices, row_swap(): from_up = lax.ppermute(to_down, 'row', downward)  7.33 us
  transfers between devices with their start and end apart: 20, of which 12 were waited for; matrix products, arithmetic and copies ran while one was open for 0% of the time, Pallas kernels for 3%

profile of v5, /device:TPU:4, one launch (start us, length us, event | category | flops | bytes accessed | tf_op | source)
XLA Modules:
  0.0 143.3 jit_solution(2476886708419571389)
XLA Ops:
  1.1 3.5 %collective-permute-start = (f32[256,256]{1,0:T(8,128)S(1)}, f32[256,256]{1,0:T(8,128)S(1)}, u32[]{:S(2)}, u32[]{:S(2)}) collective-permute-start(f32[256,256]{1,0:T(8,128)S(1)} %get-tuple-element.60), channel_id=1, source_target_pairs={{0,32},{32,64},{64,96},{96,128},{128,160},{160,192},{192,224},{224... | collective-permute-start | bytes 786440 | tf_op jit(solution)/shard_map/ppermute | solution.py:236
  4.6 5.1 %collective-permute-start.1 = (f32[256,256]{1,0:T(8,128)S(1)}, f32[256,256]{1,0:T(8,128)S(1)}, u32[]{:S(2)}, u32[]{:S(2)}) collective-permute-start(f32[256,256]{1,0:T(8,128)S(1)} %get-tuple-element.59), channel_id=1, source_target_pairs={{32,0},{64,32},{96,64},{128,96},{160,128},{192,160},{224,192},{256... | collective-permute-start | bytes 786440 | tf_op jit(solution)/shard_map/ppermute | solution.py:237
  9.8 1.4 copy-done.1
  13.6 1.3 shard_map.82
  15.0 4.2 %collective-permute-done.1.down = f32[256,256]{1,0:T(8,128)S(1)} collective-permute-done((f32[256,256]{1,0:T(8,128)S(1)}, f32[256,256]{1,0:T(8,128)S(1)}, u32[]{:S(2)}, u32[]{:S(2)}) %collective-permute-start.1) | collective-permute-done | bytes 262176 | tf_op jit(solution)/shard_map/ppermute | solution.py:237
  19.9 1.9 %collective-permute-start.2 = (f32[512,256]{1,0:T(8,128)S(1)}, f32[512,256]{1,0:T(8,128)S(1)}, u32[]{:S(2)}, u32[]{:S(2)}) collective-permute-start(f32[512,256]{1,0:T(8,128)S(1)} %shard_map.83.u), channel_id=1, source_target_pairs={{0,1},{2,3},{4,5},{6,7},{8,9},{10,11},{12,13},{14,15},{16,17},{18,... | collective-permute-start | bytes 1572872 | tf_op jit(solution)/shard_map/ppermute | solution.py:241
  22.6 1.2 collective-permute-done.2.ua
  24.3 1.3 collective-permute-start.7
  26.3 13.2 %collective-permute-done.7.vb = f32[320,256]{1,0:T(8,128)S(1)} collective-permute-done((f32[320,256]{1,0:T(8,128)S(1)}, f32[320,256]{1,0:T(8,128)S(1)}, u32[]{:S(2)}, u32[]{:S(2)}) %collective-permute-start.7) | collective-permute-done | bytes 327712 | tf_op jit(solution)/shard_map/ppermute | solution.py:258
  39.6 7.6 %collective-permute-start.8 = (f32[320,256]{1,0:T(8,128)S(1)}, f32[320,256]{1,0:T(8,128)S(1)}, u32[]{:S(2)}, u32[]{:S(2)}) collective-permute-start(f32[320,256]{1,0:T(8,128)S(1)} %collective-permute-done.7.vb), channel_id=1, source_target_pairs={{0,16},{31,15},{32,48},{63,47},{64,80},{95,79},{96,112},{127,111},... | collective-permute-start | bytes 983048 | tf_op jit(solution)/shard_map/ppermute | solution.py:260
  48.4 1.9 %collective-permute-start.4 = (f32[256,256]{1,0:T(8,128)S(1)}, f32[256,256]{1,0:T(8,128)S(1)}, u32[]{:S(2)}, u32[]{:S(2)}) collective-permute-start(f32[256,256]{1,0:T(8,128)S(1)} %get-tuple-element.42), channel_id=1, source_target_pairs={{0,1},{2,3},{4,5},{6,7},{8,9},{10,11},{12,13},{14,15},{16,17},{18,... | collective-permute-start | bytes 786440 | tf_op jit(solution)/shard_map/ppermute | solution.py:241
  50.3 2.4 %collective-permute-start.5 = (f32[256,256]{1,0:T(8,128)S(1)}, f32[256,256]{1,0:T(8,128)S(1)}, u32[]{:S(2)}, u32[]{:S(2)}) collective-permute-start(f32[256,256]{1,0:T(8,128)S(1)} %get-tuple-element.43), channel_id=1, source_target_pairs={{0,1},{2,3},{4,5},{6,7},{8,9},{10,11},{12,13},{14,15},{16,17},{18,... | collective-permute-start | bytes 786440 | tf_op jit(solution)/shard_map/ppermute | solution.py:241
  53.9 6.6 %collective-permute-done.8.relayed = f32[320,256]{1,0:T(8,128)S(1)} collective-permute-done((f32[320,256]{1,0:T(8,128)S(1)}, f32[320,256]{1,0:T(8,128)S(1)}, u32[]{:S(2)}, u32[]{:S(2)}) %collective-permute-start.8) | collective-permute-done | bytes 327712 | tf_op jit(solution)/shard_map/ppermute | solution.py:260
  60.4 3.0 %shard_map.86 = (f32[512,256]{1,0:T(8,128)S(1)}, f32[512,256]{1,0:T(8,128)S(1)}, f32[256,256]{1,0:T(8,128)S(1)}) custom-call(f32[512,256]{1,0:T(8,128)S(1)} %get-tuple-element.41.q, f32[256,256]{1,0:T(8,128)S(1)} %collective-permute-done.4.ra, f32[256,256]{1,0:T(8,128)S(1)} %collective-permute-done.5.ra2, f32[448,256]{1,0:T(8,128)S(1)} %collective-permute-done.6.wb, ...), custom_call_target="tpu_custom_call" | custom-call | flops 1006632960 | bytes 4259856 | tf_op jit(solution)/shard_map/pallas_call | solution.py:31
  63.5 4.7 %collective-permute-start.10 = (f32[512,256]{1,0:T(8,128)S(1)}, f32[512,256]{1,0:T(8,128)S(1)}, u32[]{:S(2)}, u32[]{:S(2)}) collective-permute-start(f32[512,256]{1,0:T(8,128)S(1)} %get-tuple-element.46.top), channel_id=1, source_target_pairs={{32,0},{64,32},{96,64},{128,96},{160,128},{192,160},{224,192},{256... | collective-permute-start | bytes 1572872 | tf_op jit(solution)/shard_map/ppermute | solution.py:237
  68.2 1.9 %collective-permute-start.9 = (f32[512,256]{1,0:T(8,128)S(1)}, f32[512,256]{1,0:T(8,128)S(1)}, u32[]{:S(2)}, u32[]{:S(2)}) collective-permute-start(f32[512,256]{1,0:T(8,128)S(1)} %get-tuple-element.47.bottom), channel_id=1, source_target_pairs={{0,32},{32,64},{64,96},{96,128},{128,160},{160,192},{192,224},{224... | collective-permute-start | bytes 1572872 | tf_op jit(solution)/shard_map/ppermute | solution.py:236
  71.5 8.2 %collective-permute-done.10.rbottom = f32[512,256]{1,0:T(8,128)S(1)} collective-permute-done((f32[512,256]{1,0:T(8,128)S(1)}, f32[512,256]{1,0:T(8,128)S(1)}, u32[]{:S(2)}, u32[]{:S(2)}) %collective-permute-start.10) | collective-permute-done | bytes 524320 | tf_op jit(solution)/shard_map/ppermute | solution.py:237
  79.7 5.9 %collective-permute-done.9.rtop = f32[512,256]{1,0:T(8,128)S(1)} collective-permute-done((f32[512,256]{1,0:T(8,128)S(1)}, f32[512,256]{1,0:T(8,128)S(1)}, u32[]{:S(2)}, u32[]{:S(2)}) %collective-permute-start.9) | collective-permute-done | bytes 524320 | tf_op jit(solution)/shard_map/ppermute | solution.py:236
  85.5 1.5 %shard_map.87 = (f32[512,256]{1,0:T(8,128)S(1)}, f32[512,256]{1,0:T(8,128)S(1)}) custom-call(f32[512,256]{1,0:T(8,128)S(1)} %get-tuple-element.46.top, f32[512,256]{1,0:T(8,128)S(1)} %get-tuple-element.47.bottom, f32[512,256]{1,0:T(8,128)S(1)} %collective-permute-done.9.rtop, f32[512,256]{1,0:T(8,128)S(1)} %collective-permute-done.10.rbottom, ...), custom_call_target="tpu_custom_call" | custom-call | flops 603979776 | bytes 4718600 | tf_op jit(solution)/shard_map/pallas_call | solution.py:31
  87.1 1.9 %collective-permute-start.11 = (f32[512,256]{1,0:T(8,128)S(1)}, f32[512,256]{1,0:T(8,128)S(1)}, u32[]{:S(2)}, u32[]{:S(2)}) collective-permute-start(f32[512,256]{1,0:T(8,128)S(1)} %get-tuple-element.48.u), channel_id=1, source_target_pairs={{0,1},{2,3},{4,5},{6,7},{8,9},{10,11},{12,13},{14,15},{16,17},{18,... | collective-permute-start | bytes 1572872 | tf_op jit(solution)/shard_map/ppermute | solution.py:241
  89.7 1.2 collective-permute-done.11.ua
  91.5 1.3 collective-permute-start.16
  93.4 13.6 %collective-permute-done.16.vb = f32[264,256]{1,0:T(8,128)S(1)} collective-permute-done((f32[264,256]{1,0:T(8,128)S(1)}, f32[264,256]{1,0:T(8,128)S(1)}, u32[]{:S(2)}, u32[]{:S(2)}) %collective-permute-start.16) | collective-permute-done | bytes 270368 | tf_op jit(solution)/shard_map/ppermute | solution.py:258
  107.0 7.1 %collective-permute-start.17 = (f32[264,256]{1,0:T(8,128)S(1)}, f32[264,256]{1,0:T(8,128)S(1)}, u32[]{:S(2)}, u32[]{:S(2)}) collective-permute-start(f32[264,256]{1,0:T(8,128)S(1)} %collective-permute-done.16.vb), channel_id=1, source_target_pairs={{0,16},{31,15},{32,48},{63,47},{64,80},{95,79},{96,112},{127,111},... | collective-permute-start | bytes 811016 | tf_op jit(solution)/shard_map/ppermute | solution.py:260
  115.3 1.9 %collective-permute-start.13 = (f32[256,256]{1,0:T(8,128)S(1)}, f32[256,256]{1,0:T(8,128)S(1)}, u32[]{:S(2)}, u32[]{:S(2)}) collective-permute-start(f32[256,256]{1,0:T(8,128)S(1)} %get-tuple-element.52), channel_id=1, source_target_pairs={{0,1},{2,3},{4,5},{6,7},{8,9},{10,11},{12,13},{14,15},{16,17},{18,... | collective-permute-start | bytes 786440 | tf_op jit(solution)/shard_map/ppermute | solution.py:241
  117.2 2.4 %collective-permute-start.14 = (f32[256,256]{1,0:T(8,128)S(1)}, f32[256,256]{1,0:T(8,128)S(1)}, u32[]{:S(2)}, u32[]{:S(2)}) collective-permute-start(f32[256,256]{1,0:T(8,128)S(1)} %get-tuple-element.53), channel_id=1, source_target_pairs={{0,1},{2,3},{4,5},{6,7},{8,9},{10,11},{12,13},{14,15},{16,17},{18,... | collective-permute-start | bytes 786440 | tf_op jit(solution)/shard_map/ppermute | solution.py:241
  120.8 3.0 %shard_map.90 = (f32[256,256]{1,0:T(8,128)S(1)}, f32[512,256]{1,0:T(8,128)S(1)}, f32[256,256]{1,0:T(8,128)S(1)}) custom-call(f32[512,256]{1,0:T(8,128)S(1)} %get-tuple-element.51.q, f32[256,256]{1,0:T(8,128)S(1)} %collective-permute-done.13.ra, f32[256,256]{1,0:T(8,128)S(1)} %collective-permute-done.14.ra2, f32[264,256]{1,0:T(8,128)S(1)} %collective-permute-done.15.wb, ...), custom_call_target="tpu_custom_call" | custom-call | flops 1006632960 | bytes 4218896 | tf_op jit(solution)/shard_map/pallas_call | solution.py:31
  123.8 1.9 %collective-permute-start.18 = (f32[256,256]{1,0:T(8,128)S(1)}, f32[256,256]{1,0:T(8,128)S(1)}, u32[]{:S(2)}, u32[]{:S(2)}) collective-permute-start(f32[256,256]{1,0:T(8,128)S(1)} %get-tuple-element.56), channel_id=1, source_target_pairs={{0,32},{32,64},{64,96},{96,128},{128,160},{160,192},{192,224},{224... | collective-permute-start | bytes 786440 | tf_op jit(solution)/shard_map/ppermute | solution.py:236
  125.7 6.6 %collective-permute-start.19 = (f32[256,256]{1,0:T(8,128)S(1)}, f32[256,256]{1,0:T(8,128)S(1)}, u32[]{:S(2)}, u32[]{:S(2)}) collective-permute-start(f32[256,256]{1,0:T(8,128)S(1)} %get-tuple-element.57), channel_id=1, source_target_pairs={{32,0},{64,32},{96,64},{128,96},{160,128},{192,160},{224,192},{256... | collective-permute-start | bytes 786440 | tf_op jit(solution)/shard_map/ppermute | solution.py:237
  132.3 5.2 %collective-permute-done.18.rup = f32[256,256]{1,0:T(8,128)S(1)} collective-permute-done((f32[256,256]{1,0:T(8,128)S(1)}, f32[256,256]{1,0:T(8,128)S(1)}, u32[]{:S(2)}, u32[]{:S(2)}) %collective-permute-start.18) | collective-permute-done | bytes 262176 | tf_op jit(solution)/shard_map/ppermute | solution.py:236
  137.5 4.2 %collective-permute-done.19.rdown = f32[256,256]{1,0:T(8,128)S(1)} collective-permute-done((f32[256,256]{1,0:T(8,128)S(1)}, f32[256,256]{1,0:T(8,128)S(1)}, u32[]{:S(2)}, u32[]{:S(2)}) %collective-permute-start.19) | collective-permute-done | bytes 262176 | tf_op jit(solution)/shard_map/ppermute | solution.py:237
  141.8 1.5 %shard_map.91 = f32[512,256]{1,0:T(8,128)} custom-call(f32[512,256]{1,0:T(8,128)S(1)} %get-tuple-element.55.mid, f32[256,256]{1,0:T(8,128)S(1)} %collective-permute-done.18.rup, f32[256,256]{1,0:T(8,128)S(1)} %collective-permute-done.19.rdown, f32[512,256]{1,0:T(8,128)S(1)} %get-tuple-element.58.x, f32[2]{0:T(128)S(1)} %pad_maximum_fusion.sc), custom_call_target="tpu_custom_call" | custom-call | flops 1048576 | bytes 1572872 | tf_op jit(solution)/shard_map/pallas_call | solution.py:31
  (34 shorter events, 13.0 us)
Async XLA Ops:
  0.0 19.1 %copy-start = (f32[512,256]{1,0:T(8,128)S(1)}, f32[512,256]{1,0:T(8,128)}, u32[]{:S(2)}) copy-start(f32[512,256]{1,0:T(8,128)} %x.3) | copy-start | bytes 1572868
  1.1 13.8 %collective-permute-start = (f32[256,256]{1,0:T(8,128)S(1)}, f32[256,256]{1,0:T(8,128)S(1)}, u32[]{:S(2)}, u32[]{:S(2)}) collective-permute-start(f32[256,256]{1,0:T(8,128)S(1)} %get-tuple-element.60), channel_id=1, source_target_pairs={{0,32},{32,64},{64,96},{96,128},{128,160},{160,192},{192,224},{224... | collective-permute-start | bytes 786440 | tf_op jit(solution)/shard_map/ppermute | solution.py:236
  4.6 14.5 %collective-permute-start.1 = (f32[256,256]{1,0:T(8,128)S(1)}, f32[256,256]{1,0:T(8,128)S(1)}, u32[]{:S(2)}, u32[]{:S(2)}) collective-permute-start(f32[256,256]{1,0:T(8,128)S(1)} %get-tuple-element.59), channel_id=1, source_target_pairs={{32,0},{64,32},{96,64},{128,96},{160,128},{192,160},{224,192},{256... | collective-permute-start | bytes 786440 | tf_op jit(solution)/shard_map/ppermute | solution.py:237
  9.8 1.4 copy-start.1
  11.2 1.1 copy-start.2
  12.3 0.7 copy-start.3
  13.0 0.7 copy-start.4
  19.1 4.6 %copy-start.5 = (f32[512,256]{1,0:T(8,128)S(1)}, f32[512,256]{1,0:T(8,128)}, u32[]{:S(2)}) copy-start(f32[512,256]{1,0:T(8,128)} %obs.3) | copy-start | bytes 1572868
  19.9 3.8 %collective-permute-start.2 = (f32[512,256]{1,0:T(8,128)S(1)}, f32[512,256]{1,0:T(8,128)S(1)}, u32[]{:S(2)}, u32[]{:S(2)}) collective-permute-start(f32[512,256]{1,0:T(8,128)S(1)} %shard_map.83.u), channel_id=1, source_target_pairs={{0,1},{2,3},{4,5},{6,7},{8,9},{10,11},{12,13},{14,15},{16,17},{18,... | collective-permute-start | bytes 1572872 | tf_op jit(solution)/shard_map/ppermute | solution.py:241
  21.9 25.3 %collective-permute-start.3 = (f32[512,256]{1,0:T(8,128)S(1)}, f32[512,256]{1,0:T(8,128)S(1)}, u32[]{:S(2)}, u32[]{:S(2)}) collective-permute-start(f32[512,256]{1,0:T(8,128)S(1)} %shard_map.83.u), channel_id=1, source_target_pairs={{1,2},{3,4},{5,6},{7,8},{9,10},{11,12},{13,14},{15,16},{17,18},{19... | collective-permute-start | bytes 1572872 | tf_op jit(solution)/shard_map/ppermute | solution.py:244
  24.3 15.2 %collective-permute-start.7 = (f32[320,256]{1,0:T(8,128)S(1)}, f32[320,256]{1,0:T(8,128)S(1)}, u32[]{:S(2)}, u32[]{:S(2)}) collective-permute-start(f32[320,256]{1,0:T(8,128)S(1)} %get-tuple-element.38.v), channel_id=1, source_target_pairs={{1,2},{3,4},{5,6},{7,8},{9,10},{11,12},{13,14},{17,18},{19,20},{21... | collective-permute-start | bytes 983048 | tf_op jit(solution)/shard_map/ppermute | solution.py:258
  25.6 28.2 %collective-permute-start.6 = (f32[448,256]{1,0:T(8,128)S(1)}, f32[448,256]{1,0:T(8,128)S(1)}, u32[]{:S(2)}, u32[]{:S(2)}) collective-permute-start(f32[448,256]{1,0:T(8,128)S(1)} %get-tuple-element.37.w), channel_id=1, source_target_pairs={{1,2},{3,4},{5,6},{7,8},{9,10},{11,12},{13,14},{15,16},{17,18},{19... | collective-permute-start | bytes 1376264 | tf_op jit(solution)/shard_map/ppermute | solution.py:244
  39.6 20.9 %collective-permute-start.8 = (f32[320,256]{1,0:T(8,128)S(1)}, f32[320,256]{1,0:T(8,128)S(1)}, u32[]{:S(2)}, u32[]{:S(2)}) collective-permute-start(f32[320,256]{1,0:T(8,128)S(1)} %collective-permute-done.7.vb), channel_id=1, source_target_pairs={{0,16},{31,15},{32,48},{63,47},{64,80},{95,79},{96,112},{127,111},... | collective-permute-start | bytes 983048 | tf_op jit(solution)/shard_map/ppermute | solution.py:260
  48.4 4.3 %collective-permute-start.4 = (f32[256,256]{1,0:T(8,128)S(1)}, f32[256,256]{1,0:T(8,128)S(1)}, u32[]{:S(2)}, u32[]{:S(2)}) collective-permute-start(f32[256,256]{1,0:T(8,128)S(1)} %get-tuple-element.42), channel_id=1, source_target_pairs={{0,1},{2,3},{4,5},{6,7},{8,9},{10,11},{12,13},{14,15},{16,17},{18,... | collective-permute-start | bytes 786440 | tf_op jit(solution)/shard_map/ppermute | solution.py:241
  50.3 3.6 %collective-permute-start.5 = (f32[256,256]{1,0:T(8,128)S(1)}, f32[256,256]{1,0:T(8,128)S(1)}, u32[]{:S(2)}, u32[]{:S(2)}) collective-permute-start(f32[256,256]{1,0:T(8,128)S(1)} %get-tuple-element.43), channel_id=1, source_target_pairs={{0,1},{2,3},{4,5},{6,7},{8,9},{10,11},{12,13},{14,15},{16,17},{18,... | collective-permute-start | bytes 786440 | tf_op jit(solution)/shard_map/ppermute | solution.py:241
  63.5 16.2 %collective-permute-start.10 = (f32[512,256]{1,0:T(8,128)S(1)}, f32[512,256]{1,0:T(8,128)S(1)}, u32[]{:S(2)}, u32[]{:S(2)}) collective-permute-start(f32[512,256]{1,0:T(8,128)S(1)} %get-tuple-element.46.top), channel_id=1, source_target_pairs={{32,0},{64,32},{96,64},{128,96},{160,128},{192,160},{224,192},{256... | collective-permute-start | bytes 1572872 | tf_op jit(solution)/shard_map/ppermute | solution.py:237
  68.2 17.4 %collective-permute-start.9 = (f32[512,256]{1,0:T(8,128)S(1)}, f32[512,256]{1,0:T(8,128)S(1)}, u32[]{:S(2)}, u32[]{:S(2)}) collective-permute-start(f32[512,256]{1,0:T(8,128)S(1)} %get-tuple-element.47.bottom), channel_id=1, source_target_pairs={{0,32},{32,64},{64,96},{96,128},{128,160},{160,192},{192,224},{224... | collective-permute-start | bytes 1572872 | tf_op jit(solution)/shard_map/ppermute | solution.py:236
  87.1 3.8 %collective-permute-start.11 = (f32[512,256]{1,0:T(8,128)S(1)}, f32[512,256]{1,0:T(8,128)S(1)}, u32[]{:S(2)}, u32[]{:S(2)}) collective-permute-start(f32[512,256]{1,0:T(8,128)S(1)} %get-tuple-element.48.u), channel_id=1, source_target_pairs={{0,1},{2,3},{4,5},{6,7},{8,9},{10,11},{12,13},{14,15},{16,17},{18,... | collective-permute-start | bytes 1572872 | tf_op jit(solution)/shard_map/ppermute | solution.py:241
  89.0 25.1 %collective-permute-start.12 = (f32[512,256]{1,0:T(8,128)S(1)}, f32[512,256]{1,0:T(8,128)S(1)}, u32[]{:S(2)}, u32[]{:S(2)}) collective-permute-start(f32[512,256]{1,0:T(8,128)S(1)} %get-tuple-element.48.u), channel_id=1, source_target_pairs={{1,2},{3,4},{5,6},{7,8},{9,10},{11,12},{13,14},{15,16},{17,18},{19... | collective-permute-start | bytes 1572872 | tf_op jit(solution)/shard_map/ppermute | solution.py:244
  91.5 15.6 %collective-permute-start.16 = (f32[264,256]{1,0:T(8,128)S(1)}, f32[264,256]{1,0:T(8,128)S(1)}, u32[]{:S(2)}, u32[]{:S(2)}) collective-permute-start(f32[264,256]{1,0:T(8,128)S(1)} %get-tuple-element.50.v), channel_id=1, source_target_pairs={{1,2},{3,4},{5,6},{7,8},{9,10},{11,12},{13,14},{17,18},{19,20},{21... | collective-permute-start | bytes 811016 | tf_op jit(solution)/shard_map/ppermute | solution.py:258
  92.8 28.0 %collective-permute-start.15 = (f32[264,256]{1,0:T(8,128)S(1)}, f32[264,256]{1,0:T(8,128)S(1)}, u32[]{:S(2)}, u32[]{:S(2)}) collective-permute-start(f32[264,256]{1,0:T(8,128)S(1)} %get-tuple-element.49.w), channel_id=1, source_target_pairs={{1,2},{3,4},{5,6},{7,8},{9,10},{11,12},{13,14},{15,16},{17,18},{19... | collective-permute-start | bytes 811016 | tf_op jit(solution)/shard_map/ppermute | solution.py:244
  107.0 13.8 %collective-permute-start.17 = (f32[264,256]{1,0:T(8,128)S(1)}, f32[264,256]{1,0:T(8,128)S(1)}, u32[]{:S(2)}, u32[]{:S(2)}) collective-permute-start(f32[264,256]{1,0:T(8,128)S(1)} %collective-permute-done.16.vb), channel_id=1, source_target_pairs={{0,16},{31,15},{32,48},{63,47},{64,80},{95,79},{96,112},{127,111},... | collective-permute-start | bytes 811016 | tf_op jit(solution)/shard_map/ppermute | solution.py:260
  115.3 4.3 %collective-permute-start.13 = (f32[256,256]{1,0:T(8,128)S(1)}, f32[256,256]{1,0:T(8,128)S(1)}, u32[]{:S(2)}, u32[]{:S(2)}) collective-permute-start(f32[256,256]{1,0:T(8,128)S(1)} %get-tuple-element.52), channel_id=1, source_target_pairs={{0,1},{2,3},{4,5},{6,7},{8,9},{10,11},{12,13},{14,15},{16,17},{18,... | collective-permute-start | bytes 786440 | tf_op jit(solution)/shard_map/ppermute | solution.py:241
  117.2 3.6 %collective-permute-start.14 = (f32[256,256]{1,0:T(8,128)S(1)}, f32[256,256]{1,0:T(8,128)S(1)}, u32[]{:S(2)}, u32[]{:S(2)}) collective-permute-start(f32[256,256]{1,0:T(8,128)S(1)} %get-tuple-element.53), channel_id=1, source_target_pairs={{0,1},{2,3},{4,5},{6,7},{8,9},{10,11},{12,13},{14,15},{16,17},{18,... | collective-permute-start | bytes 786440 | tf_op jit(solution)/shard_map/ppermute | solution.py:241
  123.8 13.8 %collective-permute-start.18 = (f32[256,256]{1,0:T(8,128)S(1)}, f32[256,256]{1,0:T(8,128)S(1)}, u32[]{:S(2)}, u32[]{:S(2)}) collective-permute-start(f32[256,256]{1,0:T(8,128)S(1)} %get-tuple-element.56), channel_id=1, source_target_pairs={{0,32},{32,64},{64,96},{96,128},{128,160},{160,192},{192,224},{224... | collective-permute-start | bytes 786440 | tf_op jit(solution)/shard_map/ppermute | solution.py:236
  125.7 16.1 %collective-permute-start.19 = (f32[256,256]{1,0:T(8,128)S(1)}, f32[256,256]{1,0:T(8,128)S(1)}, u32[]{:S(2)}, u32[]{:S(2)}) collective-permute-start(f32[256,256]{1,0:T(8,128)S(1)} %get-tuple-element.57), channel_id=1, source_target_pairs={{32,0},{64,32},{96,64},{128,96},{160,128},{192,160},{224,192},{256... | collective-permute-start | bytes 786440 | tf_op jit(solution)/shard_map/ppermute | solution.py:237

commit v6 on v5

--- a/solution.py
+++ b/solution.py
@@ -148,29 +148,27 @@
     m, n = q.shape
     blk = m // 2
     cut = wb.shape[0]
-    ins = (q, ra, ra2, wb, vb, relayed, u, *([] if merged else [fb]), *atx, pos)
+    ins = (q, ra, ra2, wb, vb, relayed, u, *(() if merged else fb), *atx, pos)
 
     def body(q, ra, ra2, wb, vb, relayed, u, *rest):
-        fb = None
-        if not merged:
-            fb, *rest = rest
-        ah, al, pos, *outs = rest
+        if merged:
+            ah, al, pos, *outs = rest
+        else:
+            gh, gl, th, tl, ah, al, pos, *outs = rest
         half = pos[3] // 2
         special = (pos[2] == half - 1) | (pos[2] == half) | (pos[2] == 0) | (pos[2] == pos[3] - 1)
         tail = jnp.where(special, relayed[...], vb[...])
         if merged:
-            *outs, keep = outs
+            *outs, gh, gl, th, tl = outs
             g = tail[m - cut : m - cut + blk]
-            keep[...] = g
-        else:
-            g = fb[...]
-        gh, gl = split(g)
-        th, tl = split(g.T)
+            gh[...], gl[...] = split(g)
+            th[...], tl[...] = split(g.T)
+        block, flipped = (gh[...], gl[...]), (th[...], tl[...])
         p = []
         for r, a in ((0, ra), (1, ra2)):
             s = slice(r * blk, (r + 1) * blk)
-            other = rows_of(wb, tail, (r * blk, (r + 1) * blk)) + dot3(*split(u[s, :]), th, tl)
-            v = q[s, :] + a[...] + dot3(*split(other), gh, gl)
+            other = rows_of(wb, tail, (r * blk, (r + 1) * blk)) + dot3(*split(u[s, :]), *flipped)
+            v = q[s, :] + a[...] + dot3(*split(other), *block)
             p.append(dot3(ah[r], al[r], *split(v)))
         p0 = p[0][:blk]
         p1 = p[0][blk : 2 * blk] + p[1][:blk]
@@ -185,8 +183,11 @@
             top[...], bottom[...] = p0, p3
             mid[:blk, :], mid[blk:, :] = p1, p2
 
-    outs = [((m, n), f32)] * 2 if merged else [((blk, n), f32), ((m, n), f32)]
-    return call(body, ins, outs + [((blk, n), f32)], 60 * blk * blk * n)
+    if merged:
+        outs = [((m, n), f32)] * 2 + [((n, n), bf16)] * 4
+    else:
+        outs = [((blk, n), f32), ((m, n), f32), ((blk, n), f32)]
+    return call(body, ins, outs, 60 * blk * blk * n)
 
 
 def update_left(top, bottom, rtop, rbottom, x, up, down, sc, ax):
@@ -251,9 +252,9 @@
         ua = chip_swap(u)
         ub = col_swap(u)
         if merged:
-            w, v = near_misfit(u, ua, observed, byt, fb, 7 * blk // 4)
+            w, v = near_misfit(u, ua, observed, byt, fb, 31 * blk // 16)
         else:
-            pad = jnp.zeros((16, fb.shape[1]), f32)
+            pad = jnp.zeros((16, blk), f32)
             w, v = near_misfit(u, ua, observed, byt, pad, blk + 8)
         vb = lax.ppermute(v, "col", first_hop)
         wb = col_swap(w)
@@ -267,7 +268,7 @@
     up, down = row_swap(x[:blk], x[blk:])
     ax, atx, byf, byt, fb = prepare(fx, bx, fy, by, pos)
     u = apply_left(x, up, down, ax)
-    top, bottom, fb = columns(u, fb, True)
+    top, bottom, *fb = columns(u, fb, True)
     rtop, rbottom = row_swap(top, bottom)
     x, u = update_left(top, bottom, rtop, rbottom, x, up, down, sc, ax)
     top, mid, bottom = columns(u, fb, False)

time: 144 us -> 145 us (level)
    ppermute x3, waiting for transfers between devices: 16.6 us -> 23.5 us  [row_swap(): from_down = lax.ppermute(to_up, 'row', upward)]
    ppermute x3, waiting for transfers between devices: 11.1 us -> 5.24 us  [row_swap(): from_up = lax.ppermute(to_down, 'row', downward)]
    ppermute x3, starting transfers between devices: 16.4 us -> 13.6 us  [row_swap(): from_down = lax.ppermute(to_up, 'row', upward)]
    ppermute x3, starting transfers between devices: 7.33 us -> 9.33 us  [row_swap(): from_up = lax.ppermute(to_down, 'row', downward)]
  transfers between devices with their start and end apart: 20 -> 20, of which waited for: 12 -> 11; matrix products, arithmetic and copies ran while one was open for 0% -> 0% of each run, Pallas kernels for 3% -> 3%
where the time goes in v6:
time: 145 us; the launch traced here: 144 us
  waiting for transfers between devices  67.2 us (46%)
  starting transfers between devices  55.5 us (38%)
  Pallas kernels  14.4 us (10%)
  local copies, waits for them, and re-layouts  5.01 us (3%)
  between operations  1.56 us (1%)
    ppermute x2, waiting for transfers between devices, columns(): vb = lax.ppermute(v, 'col', first_hop)  27.3 us
    ppermute x3, waiting for transfers between devices, row_swap(): from_down = lax.ppermute(to_up, 'row', upward)  23.5 us
    ppermute x2, starting transfers between devices, columns(): relayed = lax.ppermute(vb, 'col', second_hop)  14.7 us
    pallas_call x10, Pallas kernels, call(): pl.pallas_call(body, out_shape=[jax.ShapeDtypeStruct(s, d) for s, d in ou...  14.4 us
    ppermute x3, starting transfers between devices, row_swap(): from_down = lax.ppermute(to_up, 'row', upward)  13.6 us
    ppermute x6, starting transfers between devices, chip_swap(): return lax.ppermute(a, 'col', pairs[0])  12.5 us
    ppermute x3, starting transfers between devices, row_swap(): from_up = lax.ppermute(to_down, 'row', downward)  9.33 us
    ppermute x2, waiting for transfers between devices, columns(): relayed = lax.ppermute(vb, 'col', second_hop)  6.58 us
  transfers between devices with their start and end apart: 20, of which 11 were waited for; matrix products, arithmetic and copies ran while one was open for 0% of the time, Pallas kernels for 3%

profile of v6, /device:TPU:4, one launch (start us, length us, event | category | flops | bytes accessed | tf_op | source)
XLA Modules:
  0.0 143.9 jit_solution(17650768900556821820)
XLA Ops:
  1.1 3.5 %collective-permute-start = (f32[256,256]{1,0:T(8,128)S(1)}, f32[256,256]{1,0:T(8,128)S(1)}, u32[]{:S(2)}, u32[]{:S(2)}) collective-permute-start(f32[256,256]{1,0:T(8,128)S(1)} %get-tuple-element.66), channel_id=1, source_target_pairs={{0,32},{32,64},{64,96},{96,128},{128,160},{160,192},{192,224},{224... | collective-permute-start | bytes 786440 | tf_op jit(solution)/shard_map/ppermute | solution.py:237
  4.6 5.1 %collective-permute-start.1 = (f32[256,256]{1,0:T(8,128)S(1)}, f32[256,256]{1,0:T(8,128)S(1)}, u32[]{:S(2)}, u32[]{:S(2)}) collective-permute-start(f32[256,256]{1,0:T(8,128)S(1)} %get-tuple-element.65), channel_id=1, source_target_pairs={{32,0},{64,32},{96,64},{128,96},{160,128},{192,160},{224,192},{256... | collective-permute-start | bytes 786440 | tf_op jit(solution)/shard_map/ppermute | solution.py:238
  9.8 1.4 copy-done.1
  11.2 1.1 copy-done.2
  13.6 1.3 shard_map.82
  15.0 4.2 %collective-permute-done.1.down = f32[256,256]{1,0:T(8,128)S(1)} collective-permute-done((f32[256,256]{1,0:T(8,128)S(1)}, f32[256,256]{1,0:T(8,128)S(1)}, u32[]{:S(2)}, u32[]{:S(2)}) %collective-permute-start.1) | collective-permute-done | bytes 262176 | tf_op jit(solution)/shard_map/ppermute | solution.py:238
  19.9 1.9 %collective-permute-start.2 = (f32[512,256]{1,0:T(8,128)S(1)}, f32[512,256]{1,0:T(8,128)S(1)}, u32[]{:S(2)}, u32[]{:S(2)}) collective-permute-start(f32[512,256]{1,0:T(8,128)S(1)} %shard_map.83.u), channel_id=1, source_target_pairs={{0,1},{2,3},{4,5},{6,7},{8,9},{10,11},{12,13},{14,15},{16,17},{18,... | collective-permute-start | bytes 1572872 | tf_op jit(solution)/shard_map/ppermute | solution.py:242
  22.6 1.2 collective-permute-done.2.ua
  24.3 1.3 collective-permute-start.7
  26.3 12.7 %collective-permute-done.7.vb = f32[272,256]{1,0:T(8,128)S(1)} collective-permute-done((f32[272,256]{1,0:T(8,128)S(1)}, f32[272,256]{1,0:T(8,128)S(1)}, u32[]{:S(2)}, u32[]{:S(2)}) %collective-permute-start.7) | collective-permute-done | bytes 278560 | tf_op jit(solution)/shard_map/ppermute | solution.py:259
  39.0 7.6 %collective-permute-start.8 = (f32[272,256]{1,0:T(8,128)S(1)}, f32[272,256]{1,0:T(8,128)S(1)}, u32[]{:S(2)}, u32[]{:S(2)}) collective-permute-start(f32[272,256]{1,0:T(8,128)S(1)} %collective-permute-done.7.vb), channel_id=1, source_target_pairs={{0,16},{31,15},{32,48},{63,47},{64,80},{95,79},{96,112},{127,111},... | collective-permute-start | bytes 835592 | tf_op jit(solution)/shard_map/ppermute | solution.py:261
  47.8 1.9 %collective-permute-start.4 = (f32[256,256]{1,0:T(8,128)S(1)}, f32[256,256]{1,0:T(8,128)S(1)}, u32[]{:S(2)}, u32[]{:S(2)}) collective-permute-start(f32[256,256]{1,0:T(8,128)S(1)} %get-tuple-element.45), channel_id=1, source_target_pairs={{0,1},{2,3},{4,5},{6,7},{8,9},{10,11},{12,13},{14,15},{16,17},{18,... | collective-permute-start | bytes 786440 | tf_op jit(solution)/shard_map/ppermute | solution.py:242
  49.8 2.4 %collective-permute-start.5 = (f32[256,256]{1,0:T(8,128)S(1)}, f32[256,256]{1,0:T(8,128)S(1)}, u32[]{:S(2)}, u32[]{:S(2)}) collective-permute-start(f32[256,256]{1,0:T(8,128)S(1)} %get-tuple-element.46), channel_id=1, source_target_pairs={{0,1},{2,3},{4,5},{6,7},{8,9},{10,11},{12,13},{14,15},{16,17},{18,... | collective-permute-start | bytes 786440 | tf_op jit(solution)/shard_map/ppermute | solution.py:242
  53.3 6.6 %collective-permute-done.8.relayed = f32[272,256]{1,0:T(8,128)S(1)} collective-permute-done((f32[272,256]{1,0:T(8,128)S(1)}, f32[272,256]{1,0:T(8,128)S(1)}, u32[]{:S(2)}, u32[]{:S(2)}) %collective-permute-start.8) | collective-permute-done | bytes 278560 | tf_op jit(solution)/shard_map/ppermute | solution.py:261
  59.9 3.0 %shard_map.86 = (f32[512,256]{1,0:T(8,128)S(1)}, f32[512,256]{1,0:T(8,128)S(1)}, bf16[256,256]{1,0:T(8,128)(2,1)S(1)}, bf16[256,256]{1,0:T(8,128)(2,1)S(1)}, bf1...) custom-call(f32[512,256]{1,0:T(8,128)S(1)} %get-tuple-element.44.q, f32[256,256]{1,0:T(8,128)S(1)} %collective-permute-done.4.ra, ...), custom_call_target="tpu_custom_call" | custom-call | flops 1006632960 | bytes 4210704 | tf_op jit(solution)/shard_map/pallas_call | solution.py:31
  62.9 1.9 %collective-permute-start.10 = (f32[512,256]{1,0:T(8,128)S(1)}, f32[512,256]{1,0:T(8,128)S(1)}, u32[]{:S(2)}, u32[]{:S(2)}) collective-permute-start(f32[512,256]{1,0:T(8,128)S(1)} %get-tuple-element.49.top), channel_id=1, source_target_pairs={{32,0},{64,32},{96,64},{128,96},{160,128},{192,160},{224,192},{256... | collective-permute-start | bytes 1572872 | tf_op jit(solution)/shard_map/ppermute | solution.py:238
  64.8 3.9 %collective-permute-start.9 = (f32[512,256]{1,0:T(8,128)S(1)}, f32[512,256]{1,0:T(8,128)S(1)}, u32[]{:S(2)}, u32[]{:S(2)}) collective-permute-start(f32[512,256]{1,0:T(8,128)S(1)} %get-tuple-element.50.bottom), channel_id=1, source_target_pairs={{0,32},{32,64},{64,96},{96,128},{128,160},{160,192},{192,224},{224... | collective-permute-start | bytes 1572872 | tf_op jit(solution)/shard_map/ppermute | solution.py:237
  70.1 15.1 %collective-permute-done.10.rbottom = f32[512,256]{1,0:T(8,128)S(1)} collective-permute-done((f32[512,256]{1,0:T(8,128)S(1)}, f32[512,256]{1,0:T(8,128)S(1)}, u32[]{:S(2)}, u32[]{:S(2)}) %collective-permute-start.10) | collective-permute-done | bytes 524320 | tf_op jit(solution)/shard_map/ppermute | solution.py:238
  85.2 1.5 %shard_map.87 = (f32[512,256]{1,0:T(8,128)S(1)}, f32[512,256]{1,0:T(8,128)S(1)}) custom-call(f32[512,256]{1,0:T(8,128)S(1)} %get-tuple-element.49.top, f32[512,256]{1,0:T(8,128)S(1)} %get-tuple-element.50.bottom, f32[512,256]{1,0:T(8,128)S(1)} %collective-permute-done.9.rtop, f32[512,256]{1,0:T(8,128)S(1)} %collective-permute-done.10.rbottom, ...), custom_call_target="tpu_custom_call" | custom-call | flops 603979776 | bytes 4718600 | tf_op jit(solution)/shard_map/pallas_call | solution.py:31
  86.8 1.9 %collective-permute-start.11 = (f32[512,256]{1,0:T(8,128)S(1)}, f32[512,256]{1,0:T(8,128)S(1)}, u32[]{:S(2)}, u32[]{:S(2)}) collective-permute-start(f32[512,256]{1,0:T(8,128)S(1)} %get-tuple-element.51.u), channel_id=1, source_target_pairs={{0,1},{2,3},{4,5},{6,7},{8,9},{10,11},{12,13},{14,15},{16,17},{18,... | collective-permute-start | bytes 1572872 | tf_op jit(solution)/shard_map/ppermute | solution.py:242
  89.4 1.2 collective-permute-done.11.ua
  91.1 1.3 collective-permute-start.16
  93.1 14.6 %collective-permute-done.16.vb = f32[264,256]{1,0:T(8,128)S(1)} collective-permute-done((f32[264,256]{1,0:T(8,128)S(1)}, f32[264,256]{1,0:T(8,128)S(1)}, u32[]{:S(2)}, u32[]{:S(2)}) %collective-permute-start.16) | collective-permute-done | bytes 270368 | tf_op jit(solution)/shard_map/ppermute | solution.py:259
  107.7 7.1 %collective-permute-start.17 = (f32[264,256]{1,0:T(8,128)S(1)}, f32[264,256]{1,0:T(8,128)S(1)}, u32[]{:S(2)}, u32[]{:S(2)}) collective-permute-start(f32[264,256]{1,0:T(8,128)S(1)} %collective-permute-done.16.vb), channel_id=1, source_target_pairs={{0,16},{31,15},{32,48},{63,47},{64,80},{95,79},{96,112},{127,111},... | collective-permute-start | bytes 811016 | tf_op jit(solution)/shard_map/ppermute | solution.py:261
  116.0 1.9 %collective-permute-start.13 = (f32[256,256]{1,0:T(8,128)S(1)}, f32[256,256]{1,0:T(8,128)S(1)}, u32[]{:S(2)}, u32[]{:S(2)}) collective-permute-start(f32[256,256]{1,0:T(8,128)S(1)} %get-tuple-element.55), channel_id=1, source_target_pairs={{0,1},{2,3},{4,5},{6,7},{8,9},{10,11},{12,13},{14,15},{16,17},{18,... | collective-permute-start | bytes 786440 | tf_op jit(solution)/shard_map/ppermute | solution.py:242
  117.9 2.4 %collective-permute-start.14 = (f32[256,256]{1,0:T(8,128)S(1)}, f32[256,256]{1,0:T(8,128)S(1)}, u32[]{:S(2)}, u32[]{:S(2)}) collective-permute-start(f32[256,256]{1,0:T(8,128)S(1)} %get-tuple-element.56), channel_id=1, source_target_pairs={{0,1},{2,3},{4,5},{6,7},{8,9},{10,11},{12,13},{14,15},{16,17},{18,... | collective-permute-start | bytes 786440 | tf_op jit(solution)/shard_map/ppermute | solution.py:242
  121.5 2.9 %shard_map.90 = (f32[256,256]{1,0:T(8,128)S(1)}, f32[512,256]{1,0:T(8,128)S(1)}, f32[256,256]{1,0:T(8,128)S(1)}) custom-call(f32[512,256]{1,0:T(8,128)S(1)} %get-tuple-element.54.q, f32[256,256]{1,0:T(8,128)S(1)} %collective-permute-done.13.ra, f32[256,256]{1,0:T(8,128)S(1)} %collective-permute-done.14.ra2, f32[264,256]{1,0:T(8,128)S(1)} %collective-permute-done.15.wb, ...), custom_call_target="tpu_custom_call" | custom-call | flops 1006632960 | bytes 4481040 | tf_op jit(solution)/shard_map/pallas_call | solution.py:31
  124.4 1.9 %collective-permute-start.18 = (f32[256,256]{1,0:T(8,128)S(1)}, f32[256,256]{1,0:T(8,128)S(1)}, u32[]{:S(2)}, u32[]{:S(2)}) collective-permute-start(f32[256,256]{1,0:T(8,128)S(1)} %get-tuple-element.62), channel_id=1, source_target_pairs={{0,32},{32,64},{64,96},{96,128},{128,160},{160,192},{192,224},{224... | collective-permute-start | bytes 786440 | tf_op jit(solution)/shard_map/ppermute | solution.py:237
  126.3 6.6 %collective-permute-start.19 = (f32[256,256]{1,0:T(8,128)S(1)}, f32[256,256]{1,0:T(8,128)S(1)}, u32[]{:S(2)}, u32[]{:S(2)}) collective-permute-start(f32[256,256]{1,0:T(8,128)S(1)} %get-tuple-element.63), channel_id=1, source_target_pairs={{32,0},{64,32},{96,64},{128,96},{160,128},{192,160},{224,192},{256... | collective-permute-start | bytes 786440 | tf_op jit(solution)/shard_map/ppermute | solution.py:238
  132.9 5.2 %collective-permute-done.18.rup = f32[256,256]{1,0:T(8,128)S(1)} collective-permute-done((f32[256,256]{1,0:T(8,128)S(1)}, f32[256,256]{1,0:T(8,128)S(1)}, u32[]{:S(2)}, u32[]{:S(2)}) %collective-permute-start.18) | collective-permute-done | bytes 262176 | tf_op jit(solution)/shard_map/ppermute | solution.py:237
  138.1 4.2 %collective-permute-done.19.rdown = f32[256,256]{1,0:T(8,128)S(1)} collective-permute-done((f32[256,256]{1,0:T(8,128)S(1)}, f32[256,256]{1,0:T(8,128)S(1)}, u32[]{:S(2)}, u32[]{:S(2)}) %collective-permute-start.19) | collective-permute-done | bytes 262176 | tf_op jit(solution)/shard_map/ppermute | solution.py:238
  142.4 1.5 %shard_map.91 = f32[512,256]{1,0:T(8,128)} custom-call(f32[512,256]{1,0:T(8,128)S(1)} %get-tuple-element.61.mid, f32[256,256]{1,0:T(8,128)S(1)} %collective-permute-done.18.rup, f32[256,256]{1,0:T(8,128)S(1)} %collective-permute-done.19.rdown, f32[512,256]{1,0:T(8,128)S(1)} %get-tuple-element.64.x, f32[2]{0:T(128)S(1)} %pad_maximum_fusion.sc), custom_call_target="tpu_custom_call" | custom-call | flops 1048576 | bytes 1572872 | tf_op jit(solution)/shard_map/pallas_call | solution.py:31
  (34 shorter events, 11.9 us)
Async XLA Ops:
  0.0 19.1 %copy-start = (f32[512,256]{1,0:T(8,128)S(1)}, f32[512,256]{1,0:T(8,128)}, u32[]{:S(2)}) copy-start(f32[512,256]{1,0:T(8,128)} %x.3) | copy-start | bytes 1572868
  1.1 13.8 %collective-permute-start = (f32[256,256]{1,0:T(8,128)S(1)}, f32[256,256]{1,0:T(8,128)S(1)}, u32[]{:S(2)}, u32[]{:S(2)}) collective-permute-start(f32[256,256]{1,0:T(8,128)S(1)} %get-tuple-element.66), channel_id=1, source_target_pairs={{0,32},{32,64},{64,96},{96,128},{128,160},{160,192},{192,224},{224... | collective-permute-start | bytes 786440 | tf_op jit(solution)/shard_map/ppermute | solution.py:237
  4.6 14.5 %collective-permute-start.1 = (f32[256,256]{1,0:T(8,128)S(1)}, f32[256,256]{1,0:T(8,128)S(1)}, u32[]{:S(2)}, u32[]{:S(2)}) collective-permute-start(f32[256,256]{1,0:T(8,128)S(1)} %get-tuple-element.65), channel_id=1, source_target_pairs={{32,0},{64,32},{96,64},{128,96},{160,128},{192,160},{224,192},{256... | collective-permute-start | bytes 786440 | tf_op jit(solution)/shard_map/ppermute | solution.py:238
  9.8 1.4 copy-start.1
  11.2 1.1 copy-start.2
  12.3 0.7 copy-start.3
  13.0 0.7 copy-start.4
  19.1 4.6 %copy-start.5 = (f32[512,256]{1,0:T(8,128)S(1)}, f32[512,256]{1,0:T(8,128)}, u32[]{:S(2)}) copy-start(f32[512,256]{1,0:T(8,128)} %obs.3) | copy-start | bytes 1572868
  19.9 3.8 %collective-permute-start.2 = (f32[512,256]{1,0:T(8,128)S(1)}, f32[512,256]{1,0:T(8,128)S(1)}, u32[]{:S(2)}, u32[]{:S(2)}) collective-permute-start(f32[512,256]{1,0:T(8,128)S(1)} %shard_map.83.u), channel_id=1, source_target_pairs={{0,1},{2,3},{4,5},{6,7},{8,9},{10,11},{12,13},{14,15},{16,17},{18,... | collective-permute-start | bytes 1572872 | tf_op jit(solution)/shard_map/ppermute | solution.py:242
  21.9 24.8 %collective-permute-start.3 = (f32[512,256]{1,0:T(8,128)S(1)}, f32[512,256]{1,0:T(8,128)S(1)}, u32[]{:S(2)}, u32[]{:S(2)}) collective-permute-start(f32[512,256]{1,0:T(8,128)S(1)} %shard_map.83.u), channel_id=1, source_target_pairs={{1,2},{3,4},{5,6},{7,8},{9,10},{11,12},{13,14},{15,16},{17,18},{19... | collective-permute-start | bytes 1572872 | tf_op jit(solution)/shard_map/ppermute | solution.py:245
  24.3 14.7 %collective-permute-start.7 = (f32[272,256]{1,0:T(8,128)S(1)}, f32[272,256]{1,0:T(8,128)S(1)}, u32[]{:S(2)}, u32[]{:S(2)}) collective-permute-start(f32[272,256]{1,0:T(8,128)S(1)} %get-tuple-element.41.v), channel_id=1, source_target_pairs={{1,2},{3,4},{5,6},{7,8},{9,10},{11,12},{13,14},{17,18},{19,20},{21... | collective-permute-start | bytes 835592 | tf_op jit(solution)/shard_map/ppermute | solution.py:259
  25.6 27.7 %collective-permute-start.6 = (f32[496,256]{1,0:T(8,128)S(1)}, f32[496,256]{1,0:T(8,128)S(1)}, u32[]{:S(2)}, u32[]{:S(2)}) collective-permute-start(f32[496,256]{1,0:T(8,128)S(1)} %get-tuple-element.40.w), channel_id=1, source_target_pairs={{1,2},{3,4},{5,6},{7,8},{9,10},{11,12},{13,14},{15,16},{17,18},{19... | collective-permute-start | bytes 1523720 | tf_op jit(solution)/shard_map/ppermute | solution.py:245
  39.0 20.8 %collective-permute-start.8 = (f32[272,256]{1,0:T(8,128)S(1)}, f32[272,256]{1,0:T(8,128)S(1)}, u32[]{:S(2)}, u32[]{:S(2)}) collective-permute-start(f32[272,256]{1,0:T(8,128)S(1)} %collective-permute-done.7.vb), channel_id=1, source_target_pairs={{0,16},{31,15},{32,48},{63,47},{64,80},{95,79},{96,112},{127,111},... | collective-permute-start | bytes 835592 | tf_op jit(solution)/shard_map/ppermute | solution.py:261
  47.8 4.3 %collective-permute-start.4 = (f32[256,256]{1,0:T(8,128)S(1)}, f32[256,256]{1,0:T(8,128)S(1)}, u32[]{:S(2)}, u32[]{:S(2)}) collective-permute-start(f32[256,256]{1,0:T(8,128)S(1)} %get-tuple-element.45), channel_id=1, source_target_pairs={{0,1},{2,3},{4,5},{6,7},{8,9},{10,11},{12,13},{14,15},{16,17},{18,... | collective-permute-start | bytes 786440 | tf_op jit(solution)/shard_map/ppermute | solution.py:242
  49.8 3.6 %collective-permute-start.5 = (f32[256,256]{1,0:T(8,128)S(1)}, f32[256,256]{1,0:T(8,128)S(1)}, u32[]{:S(2)}, u32[]{:S(2)}) collective-permute-start(f32[256,256]{1,0:T(8,128)S(1)} %get-tuple-element.46), channel_id=1, source_target_pairs={{0,1},{2,3},{4,5},{6,7},{8,9},{10,11},{12,13},{14,15},{16,17},{18,... | collective-permute-start | bytes 786440 | tf_op jit(solution)/shard_map/ppermute | solution.py:242
  62.9 22.3 %collective-permute-start.10 = (f32[512,256]{1,0:T(8,128)S(1)}, f32[512,256]{1,0:T(8,128)S(1)}, u32[]{:S(2)}, u32[]{:S(2)}) collective-permute-start(f32[512,256]{1,0:T(8,128)S(1)} %get-tuple-element.49.top), channel_id=1, source_target_pairs={{32,0},{64,32},{96,64},{128,96},{160,128},{192,160},{224,192},{256... | collective-permute-start | bytes 1572872 | tf_op jit(solution)/shard_map/ppermute | solution.py:238
  64.8 20.4 %collective-permute-start.9 = (f32[512,256]{1,0:T(8,128)S(1)}, f32[512,256]{1,0:T(8,128)S(1)}, u32[]{:S(2)}, u32[]{:S(2)}) collective-permute-start(f32[512,256]{1,0:T(8,128)S(1)} %get-tuple-element.50.bottom), channel_id=1, source_target_pairs={{0,32},{32,64},{64,96},{96,128},{128,160},{160,192},{192,224},{224... | collective-permute-start | bytes 1572872 | tf_op jit(solution)/shard_map/ppermute | solution.py:237
  86.8 3.8 %collective-permute-start.11 = (f32[512,256]{1,0:T(8,128)S(1)}, f32[512,256]{1,0:T(8,128)S(1)}, u32[]{:S(2)}, u32[]{:S(2)}) collective-permute-start(f32[512,256]{1,0:T(8,128)S(1)} %get-tuple-element.51.u), channel_id=1, source_target_pairs={{0,1},{2,3},{4,5},{6,7},{8,9},{10,11},{12,13},{14,15},{16,17},{18,... | collective-permute-start | bytes 1572872 | tf_op jit(solution)/shard_map/ppermute | solution.py:242
  88.7 26.1 %collective-permute-start.12 = (f32[512,256]{1,0:T(8,128)S(1)}, f32[512,256]{1,0:T(8,128)S(1)}, u32[]{:S(2)}, u32[]{:S(2)}) collective-permute-start(f32[512,256]{1,0:T(8,128)S(1)} %get-tuple-element.51.u), channel_id=1, source_target_pairs={{1,2},{3,4},{5,6},{7,8},{9,10},{11,12},{13,14},{15,16},{17,18},{19... | collective-permute-start | bytes 1572872 | tf_op jit(solution)/shard_map/ppermute | solution.py:245
  91.1 16.6 %collective-permute-start.16 = (f32[264,256]{1,0:T(8,128)S(1)}, f32[264,256]{1,0:T(8,128)S(1)}, u32[]{:S(2)}, u32[]{:S(2)}) collective-permute-start(f32[264,256]{1,0:T(8,128)S(1)} %get-tuple-element.53.v), channel_id=1, source_target_pairs={{1,2},{3,4},{5,6},{7,8},{9,10},{11,12},{13,14},{17,18},{19,20},{21... | collective-permute-start | bytes 811016 | tf_op jit(solution)/shard_map/ppermute | solution.py:259
  92.4 29.0 %collective-permute-start.15 = (f32[264,256]{1,0:T(8,128)S(1)}, f32[264,256]{1,0:T(8,128)S(1)}, u32[]{:S(2)}, u32[]{:S(2)}) collective-permute-start(f32[264,256]{1,0:T(8,128)S(1)} %get-tuple-element.52.w), channel_id=1, source_target_pairs={{1,2},{3,4},{5,6},{7,8},{9,10},{11,12},{13,14},{15,16},{17,18},{19... | collective-permute-start | bytes 811016 | tf_op jit(solution)/shard_map/ppermute | solution.py:245
  107.7 13.8 %collective-permute-start.17 = (f32[264,256]{1,0:T(8,128)S(1)}, f32[264,256]{1,0:T(8,128)S(1)}, u32[]{:S(2)}, u32[]{:S(2)}) collective-permute-start(f32[264,256]{1,0:T(8,128)S(1)} %collective-permute-done.16.vb), channel_id=1, source_target_pairs={{0,16},{31,15},{32,48},{63,47},{64,80},{95,79},{96,112},{127,111},... | collective-permute-start | bytes 811016 | tf_op jit(solution)/shard_map/ppermute | solution.py:261
  116.0 4.3 %collective-permute-start.13 = (f32[256,256]{1,0:T(8,128)S(1)}, f32[256,256]{1,0:T(8,128)S(1)}, u32[]{:S(2)}, u32[]{:S(2)}) collective-permute-start(f32[256,256]{1,0:T(8,128)S(1)} %get-tuple-element.55), channel_id=1, source_target_pairs={{0,1},{2,3},{4,5},{6,7},{8,9},{10,11},{12,13},{14,15},{16,17},{18,... | collective-permute-start | bytes 786440 | tf_op jit(solution)/shard_map/ppermute | solution.py:242
  117.9 3.6 %collective-permute-start.14 = (f32[256,256]{1,0:T(8,128)S(1)}, f32[256,256]{1,0:T(8,128)S(1)}, u32[]{:S(2)}, u32[]{:S(2)}) collective-permute-start(f32[256,256]{1,0:T(8,128)S(1)} %get-tuple-element.56), channel_id=1, source_target_pairs={{0,1},{2,3},{4,5},{6,7},{8,9},{10,11},{12,13},{14,15},{16,17},{18,... | collective-permute-start | bytes 786440 | tf_op jit(solution)/shard_map/ppermute | solution.py:242
  124.4 13.8 %collective-permute-start.18 = (f32[256,256]{1,0:T(8,128)S(1)}, f32[256,256]{1,0:T(8,128)S(1)}, u32[]{:S(2)}, u32[]{:S(2)}) collective-permute-start(f32[256,256]{1,0:T(8,128)S(1)} %get-tuple-element.62), channel_id=1, source_target_pairs={{0,32},{32,64},{64,96},{96,128},{128,160},{160,192},{192,224},{224... | collective-permute-start | bytes 786440 | tf_op jit(solution)/shard_map/ppermute | solution.py:237
  126.3 16.1 %collective-permute-start.19 = (f32[256,256]{1,0:T(8,128)S(1)}, f32[256,256]{1,0:T(8,128)S(1)}, u32[]{:S(2)}, u32[]{:S(2)}) collective-permute-start(f32[256,256]{1,0:T(8,128)S(1)} %get-tuple-element.63), channel_id=1, source_target_pairs={{32,0},{64,32},{96,64},{128,96},{160,128},{192,160},{224,192},{256... | collective-permute-start | bytes 786440 | tf_op jit(solution)/shard_map/ppermute | solution.py:238

commit v7 on v6

--- a/solution.py
+++ b/solution.py
@@ -10,6 +10,7 @@
 VMEM = pl.BlockSpec(memory_space=pltpu.VMEM)
 SMEM = pl.BlockSpec(memory_space=pltpu.SMEM)
 CHUNK = 256
+PAD = 8
 
 
 def split(x):
@@ -26,12 +27,13 @@
     return v - jnp.minimum(jnp.maximum(v, -h), h)
 
 
-def call(body, ins, outs, flops, scratch=(), limit=24 << 20):
+def call(body, ins, outs, flops, scratch=(), limit=24 << 20, whole=()):
     size = lambda a: a.size * a.dtype.itemsize
+    spec = lambda a: pl.BlockSpec(memory_space=pltpu.HBM) if any(a is w for w in whole) else VMEM
     return pl.pallas_call(
         body,
         out_shape=[jax.ShapeDtypeStruct(s, d) for s, d in outs],
-        in_specs=[SMEM if a.size < 64 else VMEM for a in ins],
+        in_specs=[SMEM if a.size < 64 else spec(a) for a in ins],
         out_specs=[VMEM for _ in outs],
         scratch_shapes=list(scratch),
         compiler_params=pltpu.CompilerParams(vmem_limit_bytes=limit),
@@ -41,10 +43,16 @@
     )(*ins)
 
 
-def prepare(fx, bx, fy, by, pos):
+def prepare(fx, fy, pos):
     blk = fx.shape[2]
 
-    def body(fx, bx, fy, by, pos, axh, axl, atxh, atxl, byh, byl, byth, bytl, fb):
+    def body(fx_hbm, fy_hbm, pos, axh, axl, atxh, atxl, byh, byl, byth, bytl, fb, fx, fy, sem):
+        copies = [
+            pltpu.make_async_copy(fy_hbm, fy, sem.at[0]),
+            pltpu.make_async_copy(fx_hbm, fx, sem.at[1]),
+        ]
+        for c in copies:
+            c.start()
         row, rows, col, cols = pos[0], pos[1], pos[2], pos[3]
 
         def put(v, k, plain, trans):
@@ -52,27 +60,31 @@
             plain[0][:, s], plain[1][:, s] = split(v)
             trans[0][s, :], trans[1][s, :] = split(v.T)
 
+        copies[0].wait()
+        first = jnp.where(col % 2 == 0, 2, 0)
+        for k, s in enumerate((first, 1, 2 - first)):
+            m = pos[10 + s].astype(f32)
+            m = jnp.where((s == 0) & (col == 0), 0.0, m)
+            m = jnp.where((s == 2) & (col == cols - 1), 0.0, m)
+            v = fy[0, s] * m
+            put(v, k, (byh, byl), (byth, bytl))
+        fb[:blk, :] = v
+        fb[blk:, :] = jnp.zeros((fb.shape[0] - blk, blk), f32)
+        copies[1].wait()
         for r in range(2):
             for s in range(3):
-                m = bx[r, s].astype(f32)
+                m = pos[4 + 3 * r + s].astype(f32)
                 if (r, s) == (0, 0):
                     m = jnp.where(row == 0, 0.0, m)
                 if (r, s) == (1, 2):
                     m = jnp.where(row == rows - 1, 0.0, m)
                 put(fx[r, s] * m, s, (axh.at[r], axl.at[r]), (atxh.at[r], atxl.at[r]))
-        first = jnp.where(col % 2 == 0, 2, 0)
-        for k, s in enumerate((first, 1, 2 - first)):
-            m = by[0, s].astype(f32)
-            m = jnp.where((s == 0) & (col == 0), 0.0, m)
-            m = jnp.where((s == 2) & (col == cols - 1), 0.0, m)
-            v = fy[0, s] * m
-            put(v, k, (byh, byl), (byth, bytl))
-        fb[...] = v
 
     outs = [((2, blk, 3 * blk), bf16)] * 2 + [((2, 3 * blk, blk), bf16)] * 2
     outs += [((blk, 3 * blk), bf16)] * 2 + [((3 * blk, blk), bf16)] * 2
-    outs += [((blk, blk), f32)]
-    o = call(body, (fx, bx, fy, by, pos), outs, 1 << 24)
+    outs += [((2 * blk + 8, blk), f32)]
+    scratch = [pltpu.VMEM(fx.shape, f32), pltpu.VMEM(fy.shape, f32), pltpu.SemaphoreType.DMA((2,))]
+    o = call(body, (fx, fy, pos), outs, 1 << 24, scratch, whole=(fx, fy))
     return o[0:2], o[2:4], o[4:6], o[6:8], o[8]
 
 
@@ -106,12 +118,18 @@
     return parts[0] if len(parts) == 1 else jnp.concatenate(parts, axis=0)
 
 
-def near_misfit(u, ua, observed, byt, below, cut):
+def near_misfit(u, ua, observed, byt, cut, fb=None):
     m, blk = u.shape
-    extra = below.shape[0]
-
-    def body(u, ua, obs, byth, bytl, below, w, v):
-        v[m - cut :, :] = below[...]
+    ins = (u, ua, observed, *byt) + (() if fb is None else (fb,))
+
+    def body(u, ua, obs, byth, bytl, *rest):
+        if fb is not None:
+            g, *rest = rest
+            g = g[:blk, :]
+            rest[2][...], rest[3][...] = split(g)
+            rest[4][...], rest[5][...] = split(g.T)
+        w, v = rest[:2]
+        v[m - cut :, :] = jnp.zeros((PAD + cut - m // 2, blk), f32)
         for i in range(0, m, CHUNK):
             r = slice(i, i + CHUNK)
             acc = -obs[r, :]
@@ -124,8 +142,9 @@
             if here < CHUNK:
                 v[i + here - cut : i + CHUNK - cut, :] = acc[here:]
 
-    outs = [((cut, blk), f32), ((m - cut + extra, blk), f32)]
-    return call(body, (u, ua, observed, *byt, below), outs, 24 * m * blk * blk)
+    outs = [((cut, blk), f32), ((m // 2 + PAD, blk), f32)]
+    outs += [] if fb is None else [((blk, blk), bf16)] * 4
+    return call(body, ins, outs, 24 * m * blk * blk)
 
 
 def full_misfit(w, v, ub, byt, by):
@@ -147,22 +166,13 @@
 def back(q, ra, ra2, wb, vb, relayed, u, fb, atx, pos, merged):
     m, n = q.shape
     blk = m // 2
-    cut = wb.shape[0]
-    ins = (q, ra, ra2, wb, vb, relayed, u, *(() if merged else fb), *atx, pos)
+    ins = (q, ra, ra2, wb, vb, relayed, u, *fb, *atx, pos)
 
     def body(q, ra, ra2, wb, vb, relayed, u, *rest):
-        if merged:
-            ah, al, pos, *outs = rest
-        else:
-            gh, gl, th, tl, ah, al, pos, *outs = rest
+        gh, gl, th, tl, ah, al, pos, *outs = rest
         half = pos[3] // 2
         special = (pos[2] == half - 1) | (pos[2] == half) | (pos[2] == 0) | (pos[2] == pos[3] - 1)
         tail = jnp.where(special, relayed[...], vb[...])
-        if merged:
-            *outs, gh, gl, th, tl = outs
-            g = tail[m - cut : m - cut + blk]
-            gh[...], gl[...] = split(g)
-            th[...], tl[...] = split(g.T)
         block, flipped = (gh[...], gl[...]), (th[...], tl[...])
         p = []
         for r, a in ((0, ra), (1, ra2)):
@@ -184,7 +194,7 @@
             mid[:blk, :], mid[blk:, :] = p1, p2
 
     if merged:
-        outs = [((m, n), f32)] * 2 + [((n, n), bf16)] * 4
+        outs = [((m, n), f32)] * 2
     else:
         outs = [((blk, n), f32), ((m, n), f32), ((blk, n), f32)]
     return call(body, ins, outs, 60 * blk * blk * n)
@@ -251,27 +261,28 @@
     def columns(u, fb, merged):
         ua = chip_swap(u)
         ub = col_swap(u)
+        cut = blk + PAD
         if merged:
-            w, v = near_misfit(u, ua, observed, byt, fb, 31 * blk // 16)
+            w, v, *fb = near_misfit(u, ua, observed, byt, cut, fb)
         else:
-            pad = jnp.zeros((16, blk), f32)
-            w, v = near_misfit(u, ua, observed, byt, pad, blk + 8)
+            w, v = near_misfit(u, ua, observed, byt, cut)
         vb = lax.ppermute(v, "col", first_hop)
         wb = col_swap(w)
         relayed = lax.ppermute(vb, "col", second_hop)
         qa, qa2, q = full_misfit(w, v, ub, byt, byf)
         ra, ra2 = chip_swap(qa), chip_swap(qa2)
-        return back(q, ra, ra2, wb, vb, relayed, u, fb, atx, pos, merged)
+        return (*back(q, ra, ra2, wb, vb, relayed, u, fb, atx, pos, merged), fb)
 
     pos = jnp.stack([lax.axis_index("row"), rows, lax.axis_index("col"), cols]).astype(jnp.int32)
+    pos = jnp.concatenate([pos, bx.reshape(-1), by.reshape(-1)])
     sc = jnp.concatenate([step_size, threshold])
     up, down = row_swap(x[:blk], x[blk:])
-    ax, atx, byf, byt, fb = prepare(fx, bx, fy, by, pos)
+    ax, atx, byf, byt, fb = prepare(fx, fy, pos)
     u = apply_left(x, up, down, ax)
-    top, bottom, *fb = columns(u, fb, True)
+    top, bottom, fb = columns(u, col_swap(fb), True)
     rtop, rbottom = row_swap(top, bottom)
     x, u = update_left(top, bottom, rtop, rbottom, x, up, down, sc, ax)
-    top, mid, bottom = columns(u, fb, False)
+    top, mid, bottom, _ = columns(u, fb, False)
     rup, rdown = row_swap(top, bottom)
     return update(mid, rup, rdown, x, sc)
 

time: 145 us -> 147 us (1.014)
  the two profiles are of different devices: /device:TPU:4 before, /device:TPU:56 now
where the time goes in v7:
time: 147 us; the launch traced here: 146 us
  starting transfers between devices  81.2 us (55%)
  waiting for transfers between devices  43.3 us (29%)
  Pallas kernels  14.5 us (10%)
  local copies, waits for them, and re-layouts  5.17 us (4%)
  between operations  1.64 us (1%)
    ppermute x5, starting transfers between devices, col_swap(): return lax.ppermute(b, 'col', pairs[1])  36.8 us
    ppermute x3, waiting for transfers between devices, row_swap(): from_down = lax.ppermute(to_up, 'row', upward)  20.3 us
    ppermute x3, starting transfers between devices, row_swap(): from_up = lax.ppermute(to_down, 'row', downward)  20.3 us
    pallas_call x10, Pallas kernels, call(): pl.pallas_call(body, out_shape=[jax.ShapeDtypeStruct(s, d) for s, d in ou...  14.5 us
    ppermute x6, starting transfers between devices, chip_swap(): return lax.ppermute(a, 'col', pairs[0])  12.5 us
    ppermute x2, waiting for transfers between devices, columns(): relayed = lax.ppermute(vb, 'col', second_hop)  10.3 us
    ppermute x3, waiting for transfers between devices, row_swap(): from_up = lax.ppermute(to_down, 'row', downward)  10.1 us
    ppermute x3, starting transfers between devices, row_swap(): from_down = lax.ppermute(to_up, 'row', upward)  5.76 us
  transfers between devices with their start and end apart: 21, of which 9 were waited for; matrix products, arithmetic and copies ran while one was open for 1% of the time, Pallas kernels for 4%

profile of v7, /device:TPU:56, one launch (start us, length us, event | category | flops | bytes accessed | tf_op | source)
XLA Modules:
  0.0 145.9 jit_solution(13019251545066402512)
XLA Ops:
  1.1 5.8 %collective-permute-start = (f32[256,256]{1,0:T(8,128)S(1)}, f32[256,256]{1,0:T(8,128)S(1)}, u32[]{:S(2)}, u32[]{:S(2)}) collective-permute-start(f32[256,256]{1,0:T(8,128)S(1)} %get-tuple-element.66), channel_id=1, source_target_pairs={{0,32},{32,64},{64,96},{96,128},{128,160},{160,192},{192,224},{224... | collective-permute-start | bytes 786440 | tf_op jit(solution)/shard_map/ppermute | solution.py:247
  6.9 1.9 %collective-permute-start.1 = (f32[256,256]{1,0:T(8,128)S(1)}, f32[256,256]{1,0:T(8,128)S(1)}, u32[]{:S(2)}, u32[]{:S(2)}) collective-permute-start(f32[256,256]{1,0:T(8,128)S(1)} %get-tuple-element.65), channel_id=1, source_target_pairs={{32,0},{64,32},{96,64},{128,96},{160,128},{192,160},{224,192},{256... | collective-permute-start | bytes 786440 | tf_op jit(solution)/shard_map/ppermute | solution.py:248
  10.3 1.4 copy-done.1
  12.9 1.5 %shard_map.82 = (bf16[2,256,768]{2,1,0:T(8,128)(2,1)S(1)}, bf16[2,256,768]{2,1,0:T(8,128)(2,1)S(1)}, bf16[2,768,256]{2,1,0:T(8,128)(2,1)S(1)}, bf16[2,768,256]{2...) custom-call(f32[2,3,256,256]{3,2,1,0:T(8,128)S(1)} %copy-done.1, ...), custom_call_target="tpu_custom_call" | custom-call | flops 16777216 | bytes 2359348 | tf_op jit(solution)/shard_map/pallas_call | solution.py:33
  14.4 10.2 %collective-permute-start.3 = (f32[520,256]{1,0:T(8,128)S(1)}, f32[520,256]{1,0:T(8,128)S(1)}, u32[]{:S(2)}, u32[]{:S(2)}) collective-permute-start(f32[520,256]{1,0:T(8,128)S(1)} %get-tuple-element.39), channel_id=1, source_target_pairs={{1,2},{3,4},{5,6},{7,8},{9,10},{11,12},{13,14},{15,16},{17,18},{19... | collective-permute-start | bytes 1597448 | tf_op jit(solution)/shard_map/ppermute | solution.py:255
  25.5 1.9 %collective-permute-start.2 = (f32[512,256]{1,0:T(8,128)S(1)}, f32[512,256]{1,0:T(8,128)S(1)}, u32[]{:S(2)}, u32[]{:S(2)}) collective-permute-start(f32[512,256]{1,0:T(8,128)S(1)} %shard_map.83.u), channel_id=1, source_target_pairs={{0,1},{2,3},{4,5},{6,7},{8,9},{10,11},{12,13},{14,15},{16,17},{18,... | collective-permute-start | bytes 1572872 | tf_op jit(solution)/shard_map/ppermute | solution.py:252
  27.4 6.2 %collective-permute-start.4 = (f32[512,256]{1,0:T(8,128)S(1)}, f32[512,256]{1,0:T(8,128)S(1)}, u32[]{:S(2)}, u32[]{:S(2)}) collective-permute-start(f32[512,256]{1,0:T(8,128)S(1)} %shard_map.83.u), channel_id=1, source_target_pairs={{1,2},{3,4},{5,6},{7,8},{9,10},{11,12},{13,14},{15,16},{17,18},{19... | collective-permute-start | bytes 1572872 | tf_op jit(solution)/shard_map/ppermute | solution.py:255
  34.2 1.3 collective-permute-start.8
  35.5 7.7 %collective-permute-start.7 = (f32[264,256]{1,0:T(8,128)S(1)}, f32[264,256]{1,0:T(8,128)S(1)}, u32[]{:S(2)}, u32[]{:S(2)}) collective-permute-start(f32[264,256]{1,0:T(8,128)S(1)} %get-tuple-element.40.w), channel_id=1, source_target_pairs={{1,2},{3,4},{5,6},{7,8},{9,10},{11,12},{13,14},{15,16},{17,18},{19... | collective-permute-start | bytes 811016 | tf_op jit(solution)/shard_map/ppermute | solution.py:255
  43.3 1.3 collective-permute-start.9
  45.7 1.9 %collective-permute-start.5 = (f32[256,256]{1,0:T(8,128)S(1)}, f32[256,256]{1,0:T(8,128)S(1)}, u32[]{:S(2)}, u32[]{:S(2)}) collective-permute-start(f32[256,256]{1,0:T(8,128)S(1)} %get-tuple-element.45), channel_id=1, source_target_pairs={{0,1},{2,3},{4,5},{6,7},{8,9},{10,11},{12,13},{14,15},{16,17},{18,... | collective-permute-start | bytes 786440 | tf_op jit(solution)/shard_map/ppermute | solution.py:252
  47.6 2.4 %collective-permute-start.6 = (f32[256,256]{1,0:T(8,128)S(1)}, f32[256,256]{1,0:T(8,128)S(1)}, u32[]{:S(2)}, u32[]{:S(2)}) collective-permute-start(f32[256,256]{1,0:T(8,128)S(1)} %get-tuple-element.46), channel_id=1, source_target_pairs={{0,1},{2,3},{4,5},{6,7},{8,9},{10,11},{12,13},{14,15},{16,17},{18,... | collective-permute-start | bytes 786440 | tf_op jit(solution)/shard_map/ppermute | solution.py:252
  51.2 6.2 %collective-permute-done.9.relayed = f32[264,256]{1,0:T(8,128)S(1)} collective-permute-done((f32[264,256]{1,0:T(8,128)S(1)}, f32[264,256]{1,0:T(8,128)S(1)}, u32[]{:S(2)}, u32[]{:S(2)}) %collective-permute-start.9) | collective-permute-done | bytes 270368 | tf_op jit(solution)/shard_map/ppermute | solution.py:271
  57.4 2.9 %shard_map.86 = (f32[512,256]{1,0:T(8,128)S(1)}, f32[512,256]{1,0:T(8,128)S(1)}) custom-call(f32[512,256]{1,0:T(8,128)S(1)} %get-tuple-element.44.q, f32[256,256]{1,0:T(8,128)S(1)} %collective-permute-done.5.ra, f32[256,256]{1,0:T(8,128)S(1)} %collective-permute-done.6.ra2, f32[264,256]{1,0:T(8,128)S(1)} %collective-permute-done.7.wb, ...), custom_call_target="tpu_custom_call" | custom-call | flops 1006632960 | bytes 4481076 | tf_op jit(solution)/shard_map/pallas_call | solution.py:33
  60.3 8.3 %collective-permute-start.10 = (f32[512,256]{1,0:T(8,128)S(1)}, f32[512,256]{1,0:T(8,128)S(1)}, u32[]{:S(2)}, u32[]{:S(2)}) collective-permute-start(f32[512,256]{1,0:T(8,128)S(1)} %get-tuple-element.54.bottom), channel_id=1, source_target_pairs={{0,32},{32,64},{64,96},{96,128},{128,160},{160,192},{192,224},{224... | collective-permute-start | bytes 1572872 | tf_op jit(solution)/shard_map/ppermute | solution.py:247
  68.6 1.9 %collective-permute-start.11 = (f32[512,256]{1,0:T(8,128)S(1)}, f32[512,256]{1,0:T(8,128)S(1)}, u32[]{:S(2)}, u32[]{:S(2)}) collective-permute-start(f32[512,256]{1,0:T(8,128)S(1)} %get-tuple-element.53.top), channel_id=1, source_target_pairs={{32,0},{64,32},{96,64},{128,96},{160,128},{192,160},{224,192},{256... | collective-permute-start | bytes 1572872 | tf_op jit(solution)/shard_map/ppermute | solution.py:248
  71.9 8.1 %collective-permute-done.10.rtop = f32[512,256]{1,0:T(8,128)S(1)} collective-permute-done((f32[512,256]{1,0:T(8,128)S(1)}, f32[512,256]{1,0:T(8,128)S(1)}, u32[]{:S(2)}, u32[]{:S(2)}) %collective-permute-start.10) | collective-permute-done | bytes 524320 | tf_op jit(solution)/shard_map/ppermute | solution.py:247
  80.1 13.3 %collective-permute-done.11.rbottom = f32[512,256]{1,0:T(8,128)S(1)} collective-permute-done((f32[512,256]{1,0:T(8,128)S(1)}, f32[512,256]{1,0:T(8,128)S(1)}, u32[]{:S(2)}, u32[]{:S(2)}) %collective-permute-start.11) | collective-permute-done | bytes 524320 | tf_op jit(solution)/shard_map/ppermute | solution.py:248
  93.3 1.5 %shard_map.87 = (f32[512,256]{1,0:T(8,128)S(1)}, f32[512,256]{1,0:T(8,128)S(1)}) custom-call(f32[512,256]{1,0:T(8,128)S(1)} %get-tuple-element.53.top, f32[512,256]{1,0:T(8,128)S(1)} %get-tuple-element.54.bottom, f32[512,256]{1,0:T(8,128)S(1)} %collective-permute-done.10.rtop, f32[512,256]{1,0:T(8,128)S(1)} %collective-permute-done.11.rbottom, ...), custom_call_target="tpu_custom_call" | custom-call | flops 603979776 | bytes 4718600 | tf_op jit(solution)/shard_map/pallas_call | solution.py:33
  94.9 1.9 %collective-permute-start.12 = (f32[512,256]{1,0:T(8,128)S(1)}, f32[512,256]{1,0:T(8,128)S(1)}, u32[]{:S(2)}, u32[]{:S(2)}) collective-permute-start(f32[512,256]{1,0:T(8,128)S(1)} %get-tuple-element.55.u), channel_id=1, source_target_pairs={{0,1},{2,3},{4,5},{6,7},{8,9},{10,11},{12,13},{14,15},{16,17},{18,... | collective-permute-start | bytes 1572872 | tf_op jit(solution)/shard_map/ppermute | solution.py:252
  96.8 5.8 %collective-permute-start.13 = (f32[512,256]{1,0:T(8,128)S(1)}, f32[512,256]{1,0:T(8,128)S(1)}, u32[]{:S(2)}, u32[]{:S(2)}) collective-permute-start(f32[512,256]{1,0:T(8,128)S(1)} %get-tuple-element.55.u), channel_id=1, source_target_pairs={{1,2},{3,4},{5,6},{7,8},{9,10},{11,12},{13,14},{15,16},{17,18},{19... | collective-permute-start | bytes 1572872 | tf_op jit(solution)/shard_map/ppermute | solution.py:255
  103.2 2.0 %collective-permute-start.17 = (f32[264,256]{1,0:T(8,128)S(1)}, f32[264,256]{1,0:T(8,128)S(1)}, u32[]{:S(2)}, u32[]{:S(2)}) collective-permute-start(f32[264,256]{1,0:T(8,128)S(1)} %get-tuple-element.57.v), channel_id=1, source_target_pairs={{1,2},{3,4},{5,6},{7,8},{9,10},{11,12},{13,14},{17,18},{19,20},{21... | collective-permute-start | bytes 811016 | tf_op jit(solution)/shard_map/ppermute | solution.py:269
  105.1 6.9 %collective-permute-start.16 = (f32[264,256]{1,0:T(8,128)S(1)}, f32[264,256]{1,0:T(8,128)S(1)}, u32[]{:S(2)}, u32[]{:S(2)}) collective-permute-start(f32[264,256]{1,0:T(8,128)S(1)} %get-tuple-element.56.w), channel_id=1, source_target_pairs={{1,2},{3,4},{5,6},{7,8},{9,10},{11,12},{13,14},{15,16},{17,18},{19... | collective-permute-start | bytes 811016 | tf_op jit(solution)/shard_map/ppermute | solution.py:255
  114.5 1.9 %collective-permute-start.14 = (f32[256,256]{1,0:T(8,128)S(1)}, f32[256,256]{1,0:T(8,128)S(1)}, u32[]{:S(2)}, u32[]{:S(2)}) collective-permute-start(f32[256,256]{1,0:T(8,128)S(1)} %get-tuple-element.59), channel_id=1, source_target_pairs={{0,1},{2,3},{4,5},{6,7},{8,9},{10,11},{12,13},{14,15},{16,17},{18,... | collective-permute-start | bytes 786440 | tf_op jit(solution)/shard_map/ppermute | solution.py:252
  116.5 2.4 %collective-permute-start.15 = (f32[256,256]{1,0:T(8,128)S(1)}, f32[256,256]{1,0:T(8,128)S(1)}, u32[]{:S(2)}, u32[]{:S(2)}) collective-permute-start(f32[256,256]{1,0:T(8,128)S(1)} %get-tuple-element.60), channel_id=1, source_target_pairs={{0,1},{2,3},{4,5},{6,7},{8,9},{10,11},{12,13},{14,15},{16,17},{18,... | collective-permute-start | bytes 786440 | tf_op jit(solution)/shard_map/ppermute | solution.py:252
  120.3 4.0 %collective-permute-done.18.relayed = f32[264,256]{1,0:T(8,128)S(1)} collective-permute-done((f32[264,256]{1,0:T(8,128)S(1)}, f32[264,256]{1,0:T(8,128)S(1)}, u32[]{:S(2)}, u32[]{:S(2)}) %collective-permute-start.18) | collective-permute-done | bytes 270368 | tf_op jit(solution)/shard_map/ppermute | solution.py:271
  124.3 2.9 %shard_map.90 = (f32[256,256]{1,0:T(8,128)S(1)}, f32[512,256]{1,0:T(8,128)S(1)}, f32[256,256]{1,0:T(8,128)S(1)}) custom-call(f32[512,256]{1,0:T(8,128)S(1)} %get-tuple-element.58.q, f32[256,256]{1,0:T(8,128)S(1)} %collective-permute-done.14.ra, f32[256,256]{1,0:T(8,128)S(1)} %collective-permute-done.15.ra2, f32[264,256]{1,0:T(8,128)S(1)} %collective-permute-done.16.wb, ...), custom_call_target="tpu_custom_call" | custom-call | flops 1006632960 | bytes 4481076 | tf_op jit(solution)/shard_map/pallas_call | solution.py:33
  127.2 6.2 %collective-permute-start.19 = (f32[256,256]{1,0:T(8,128)S(1)}, f32[256,256]{1,0:T(8,128)S(1)}, u32[]{:S(2)}, u32[]{:S(2)}) collective-permute-start(f32[256,256]{1,0:T(8,128)S(1)} %get-tuple-element.62), channel_id=1, source_target_pairs={{0,32},{32,64},{64,96},{96,128},{128,160},{160,192},{192,224},{224... | collective-permute-start | bytes 786440 | tf_op jit(solution)/shard_map/ppermute | solution.py:247
  133.5 1.9 %collective-permute-start.20 = (f32[256,256]{1,0:T(8,128)S(1)}, f32[256,256]{1,0:T(8,128)S(1)}, u32[]{:S(2)}, u32[]{:S(2)}) collective-permute-start(f32[256,256]{1,0:T(8,128)S(1)} %get-tuple-element.63), channel_id=1, source_target_pairs={{32,0},{64,32},{96,64},{128,96},{160,128},{192,160},{224,192},{256... | collective-permute-start | bytes 786440 | tf_op jit(solution)/shard_map/ppermute | solution.py:248
  135.4 2.0 %collective-permute-done.19.rup = f32[256,256]{1,0:T(8,128)S(1)} collective-permute-done((f32[256,256]{1,0:T(8,128)S(1)}, f32[256,256]{1,0:T(8,128)S(1)}, u32[]{:S(2)}, u32[]{:S(2)}) %collective-permute-start.19) | collective-permute-done | bytes 262176 | tf_op jit(solution)/shard_map/ppermute | solution.py:247
  137.4 7.0 %collective-permute-done.20.rdown = f32[256,256]{1,0:T(8,128)S(1)} collective-permute-done((f32[256,256]{1,0:T(8,128)S(1)}, f32[256,256]{1,0:T(8,128)S(1)}, u32[]{:S(2)}, u32[]{:S(2)}) %collective-permute-start.20) | collective-permute-done | bytes 262176 | tf_op jit(solution)/shard_map/ppermute | solution.py:248
  144.4 1.5 %shard_map.91 = f32[512,256]{1,0:T(8,128)} custom-call(f32[512,256]{1,0:T(8,128)S(1)} %get-tuple-element.61.mid, f32[256,256]{1,0:T(8,128)S(1)} %collective-permute-done.19.rup, f32[256,256]{1,0:T(8,128)S(1)} %collective-permute-done.20.rdown, f32[512,256]{1,0:T(8,128)S(1)} %get-tuple-element.64.x, f32[2]{0:T(128)S(1)} %pad_maximum_fusion.sc), custom_call_target="tpu_custom_call" | custom-call | flops 1048576 | bytes 1572872 | tf_op jit(solution)/shard_map/pallas_call | solution.py:33
  (32 shorter events, 12.0 us)
Async XLA Ops:
  0.0 24.7 %copy-start = (f32[512,256]{1,0:T(8,128)S(1)}, f32[512,256]{1,0:T(8,128)}, u32[]{:S(2)}) copy-start(f32[512,256]{1,0:T(8,128)} %x.3) | copy-start | bytes 1572868
  1.1 23.5 %collective-permute-start = (f32[256,256]{1,0:T(8,128)S(1)}, f32[256,256]{1,0:T(8,128)S(1)}, u32[]{:S(2)}, u32[]{:S(2)}) collective-permute-start(f32[256,256]{1,0:T(8,128)S(1)} %get-tuple-element.66), channel_id=1, source_target_pairs={{0,32},{32,64},{64,96},{96,128},{128,160},{160,192},{192,224},{224... | collective-permute-start | bytes 786440 | tf_op jit(solution)/shard_map/ppermute | solution.py:247
  6.9 17.8 %collective-permute-start.1 = (f32[256,256]{1,0:T(8,128)S(1)}, f32[256,256]{1,0:T(8,128)S(1)}, u32[]{:S(2)}, u32[]{:S(2)}) collective-permute-start(f32[256,256]{1,0:T(8,128)S(1)} %get-tuple-element.65), channel_id=1, source_target_pairs={{32,0},{64,32},{96,64},{128,96},{160,128},{192,160},{224,192},{256... | collective-permute-start | bytes 786440 | tf_op jit(solution)/shard_map/ppermute | solution.py:248
  10.3 1.4 copy-start.1
  11.7 1.1 copy-start.2
  14.4 19.2 %collective-permute-start.3 = (f32[520,256]{1,0:T(8,128)S(1)}, f32[520,256]{1,0:T(8,128)S(1)}, u32[]{:S(2)}, u32[]{:S(2)}) collective-permute-start(f32[520,256]{1,0:T(8,128)S(1)} %get-tuple-element.39), channel_id=1, source_target_pairs={{1,2},{3,4},{5,6},{7,8},{9,10},{11,12},{13,14},{15,16},{17,18},{19... | collective-permute-start | bytes 1597448 | tf_op jit(solution)/shard_map/ppermute | solution.py:255
  24.7 9.0 %copy-start.3 = (f32[512,256]{1,0:T(8,128)S(1)}, f32[512,256]{1,0:T(8,128)}, u32[]{:S(2)}) copy-start(f32[512,256]{1,0:T(8,128)} %obs.3) | copy-start | bytes 1572868
  25.5 8.1 %collective-permute-start.2 = (f32[512,256]{1,0:T(8,128)S(1)}, f32[512,256]{1,0:T(8,128)S(1)}, u32[]{:S(2)}, u32[]{:S(2)}) collective-permute-start(f32[512,256]{1,0:T(8,128)S(1)} %shard_map.83.u), channel_id=1, source_target_pairs={{0,1},{2,3},{4,5},{6,7},{8,9},{10,11},{12,13},{14,15},{16,17},{18,... | collective-permute-start | bytes 1572872 | tf_op jit(solution)/shard_map/ppermute | solution.py:252
  27.4 17.1 %collective-permute-start.4 = (f32[512,256]{1,0:T(8,128)S(1)}, f32[512,256]{1,0:T(8,128)S(1)}, u32[]{:S(2)}, u32[]{:S(2)}) collective-permute-start(f32[512,256]{1,0:T(8,128)S(1)} %shard_map.83.u), channel_id=1, source_target_pairs={{1,2},{3,4},{5,6},{7,8},{9,10},{11,12},{13,14},{15,16},{17,18},{19... | collective-permute-start | bytes 1572872 | tf_op jit(solution)/shard_map/ppermute | solution.py:255
  34.2 9.0 %collective-permute-start.8 = (f32[264,256]{1,0:T(8,128)S(1)}, f32[264,256]{1,0:T(8,128)S(1)}, u32[]{:S(2)}, u32[]{:S(2)}) collective-permute-start(f32[264,256]{1,0:T(8,128)S(1)} %get-tuple-element.41.v), channel_id=1, source_target_pairs={{1,2},{3,4},{5,6},{7,8},{9,10},{11,12},{13,14},{17,18},{19,20},{21... | collective-permute-start | bytes 811016 | tf_op jit(solution)/shard_map/ppermute | solution.py:269
  35.5 15.7 %collective-permute-start.7 = (f32[264,256]{1,0:T(8,128)S(1)}, f32[264,256]{1,0:T(8,128)S(1)}, u32[]{:S(2)}, u32[]{:S(2)}) collective-permute-start(f32[264,256]{1,0:T(8,128)S(1)} %get-tuple-element.40.w), channel_id=1, source_target_pairs={{1,2},{3,4},{5,6},{7,8},{9,10},{11,12},{13,14},{15,16},{17,18},{19... | collective-permute-start | bytes 811016 | tf_op jit(solution)/shard_map/ppermute | solution.py:255
  43.3 14.2 %collective-permute-start.9 = (f32[264,256]{1,0:T(8,128)S(1)}, f32[264,256]{1,0:T(8,128)S(1)}, u32[]{:S(2)}, u32[]{:S(2)}) collective-permute-start(f32[264,256]{1,0:T(8,128)S(1)} %collective-permute-done.8.vb), channel_id=1, source_target_pairs={{0,16},{31,15},{32,48},{63,47},{64,80},{95,79},{96,112},{127,111},... | collective-permute-start | bytes 811016 | tf_op jit(solution)/shard_map/ppermute | solution.py:271
  45.7 4.3 %collective-permute-start.5 = (f32[256,256]{1,0:T(8,128)S(1)}, f32[256,256]{1,0:T(8,128)S(1)}, u32[]{:S(2)}, u32[]{:S(2)}) collective-permute-start(f32[256,256]{1,0:T(8,128)S(1)} %get-tuple-element.45), channel_id=1, source_target_pairs={{0,1},{2,3},{4,5},{6,7},{8,9},{10,11},{12,13},{14,15},{16,17},{18,... | collective-permute-start | bytes 786440 | tf_op jit(solution)/shard_map/ppermute | solution.py:252
  47.6 3.6 %collective-permute-start.6 = (f32[256,256]{1,0:T(8,128)S(1)}, f32[256,256]{1,0:T(8,128)S(1)}, u32[]{:S(2)}, u32[]{:S(2)}) collective-permute-start(f32[256,256]{1,0:T(8,128)S(1)} %get-tuple-element.46), channel_id=1, source_target_pairs={{0,1},{2,3},{4,5},{6,7},{8,9},{10,11},{12,13},{14,15},{16,17},{18,... | collective-permute-start | bytes 786440 | tf_op jit(solution)/shard_map/ppermute | solution.py:252
  60.3 19.7 %collective-permute-start.10 = (f32[512,256]{1,0:T(8,128)S(1)}, f32[512,256]{1,0:T(8,128)S(1)}, u32[]{:S(2)}, u32[]{:S(2)}) collective-permute-start(f32[512,256]{1,0:T(8,128)S(1)} %get-tuple-element.54.bottom), channel_id=1, source_target_pairs={{0,32},{32,64},{64,96},{96,128},{128,160},{160,192},{192,224},{224... | collective-permute-start | bytes 1572872 | tf_op jit(solution)/shard_map/ppermute | solution.py:247
  68.6 24.7 %collective-permute-start.11 = (f32[512,256]{1,0:T(8,128)S(1)}, f32[512,256]{1,0:T(8,128)S(1)}, u32[]{:S(2)}, u32[]{:S(2)}) collective-permute-start(f32[512,256]{1,0:T(8,128)S(1)} %get-tuple-element.53.top), channel_id=1, source_target_pairs={{32,0},{64,32},{96,64},{128,96},{160,128},{192,160},{224,192},{256... | collective-permute-start | bytes 1572872 | tf_op jit(solution)/shard_map/ppermute | solution.py:248
  94.9 7.7 %collective-permute-start.12 = (f32[512,256]{1,0:T(8,128)S(1)}, f32[512,256]{1,0:T(8,128)S(1)}, u32[]{:S(2)}, u32[]{:S(2)}) collective-permute-start(f32[512,256]{1,0:T(8,128)S(1)} %get-tuple-element.55.u), channel_id=1, source_target_pairs={{0,1},{2,3},{4,5},{6,7},{8,9},{10,11},{12,13},{14,15},{16,17},{18,... | collective-permute-start | bytes 1572872 | tf_op jit(solution)/shard_map/ppermute | solution.py:252
  96.8 16.6 %collective-permute-start.13 = (f32[512,256]{1,0:T(8,128)S(1)}, f32[512,256]{1,0:T(8,128)S(1)}, u32[]{:S(2)}, u32[]{:S(2)}) collective-permute-start(f32[512,256]{1,0:T(8,128)S(1)} %get-tuple-element.55.u), channel_id=1, source_target_pairs={{1,2},{3,4},{5,6},{7,8},{9,10},{11,12},{13,14},{15,16},{17,18},{19... | collective-permute-start | bytes 1572872 | tf_op jit(solution)/shard_map/ppermute | solution.py:255
  103.2 8.9 %collective-permute-start.17 = (f32[264,256]{1,0:T(8,128)S(1)}, f32[264,256]{1,0:T(8,128)S(1)}, u32[]{:S(2)}, u32[]{:S(2)}) collective-permute-start(f32[264,256]{1,0:T(8,128)S(1)} %get-tuple-element.57.v), channel_id=1, source_target_pairs={{1,2},{3,4},{5,6},{7,8},{9,10},{11,12},{13,14},{17,18},{19,20},{21... | collective-permute-start | bytes 811016 | tf_op jit(solution)/shard_map/ppermute | solution.py:269
  105.1 15.2 %collective-permute-start.16 = (f32[264,256]{1,0:T(8,128)S(1)}, f32[264,256]{1,0:T(8,128)S(1)}, u32[]{:S(2)}, u32[]{:S(2)}) collective-permute-start(f32[264,256]{1,0:T(8,128)S(1)} %get-tuple-element.56.w), channel_id=1, source_target_pairs={{1,2},{3,4},{5,6},{7,8},{9,10},{11,12},{13,14},{15,16},{17,18},{19... | collective-permute-start | bytes 811016 | tf_op jit(solution)/shard_map/ppermute | solution.py:255
  112.1 12.3 %collective-permute-start.18 = (f32[264,256]{1,0:T(8,128)S(1)}, f32[264,256]{1,0:T(8,128)S(1)}, u32[]{:S(2)}, u32[]{:S(2)}) collective-permute-start(f32[264,256]{1,0:T(8,128)S(1)} %collective-permute-done.17.vb), channel_id=1, source_target_pairs={{0,16},{31,15},{32,48},{63,47},{64,80},{95,79},{96,112},{127,111},... | collective-permute-start | bytes 811016 | tf_op jit(solution)/shard_map/ppermute | solution.py:271
  114.5 4.3 %collective-permute-start.14 = (f32[256,256]{1,0:T(8,128)S(1)}, f32[256,256]{1,0:T(8,128)S(1)}, u32[]{:S(2)}, u32[]{:S(2)}) collective-permute-start(f32[256,256]{1,0:T(8,128)S(1)} %get-tuple-element.59), channel_id=1, source_target_pairs={{0,1},{2,3},{4,5},{6,7},{8,9},{10,11},{12,13},{14,15},{16,17},{18,... | collective-permute-start | bytes 786440 | tf_op jit(solution)/shard_map/ppermute | solution.py:252
  116.5 3.6 %collective-permute-start.15 = (f32[256,256]{1,0:T(8,128)S(1)}, f32[256,256]{1,0:T(8,128)S(1)}, u32[]{:S(2)}, u32[]{:S(2)}) collective-permute-start(f32[256,256]{1,0:T(8,128)S(1)} %get-tuple-element.60), channel_id=1, source_target_pairs={{0,1},{2,3},{4,5},{6,7},{8,9},{10,11},{12,13},{14,15},{16,17},{18,... | collective-permute-start | bytes 786440 | tf_op jit(solution)/shard_map/ppermute | solution.py:252
  127.2 10.1 %collective-permute-start.19 = (f32[256,256]{1,0:T(8,128)S(1)}, f32[256,256]{1,0:T(8,128)S(1)}, u32[]{:S(2)}, u32[]{:S(2)}) collective-permute-start(f32[256,256]{1,0:T(8,128)S(1)} %get-tuple-element.62), channel_id=1, source_target_pairs={{0,32},{32,64},{64,96},{96,128},{128,160},{160,192},{192,224},{224... | collective-permute-start | bytes 786440 | tf_op jit(solution)/shard_map/ppermute | solution.py:247
  133.5 11.0 %collective-permute-start.20 = (f32[256,256]{1,0:T(8,128)S(1)}, f32[256,256]{1,0:T(8,128)S(1)}, u32[]{:S(2)}, u32[]{:S(2)}) collective-permute-start(f32[256,256]{1,0:T(8,128)S(1)} %get-tuple-element.63), channel_id=1, source_target_pairs={{32,0},{64,32},{96,64},{128,96},{160,128},{192,160},{224,192},{256... | collective-permute-start | bytes 786440 | tf_op jit(solution)/shard_map/ppermute | solution.py:248

commit v8 on v7

--- a/solution.py
+++ b/solution.py
@@ -186,7 +186,8 @@
         p3 = p[1][2 * blk :]
         if merged:
             top, bottom = outs
-            top[:blk, :], top[blk:, :] = p0, p1
+            top[:blk, :], top[blk:m, :] = p0, p1
+            top[m:, :] = jnp.zeros((PAD, n), f32)
             bottom[:blk, :], bottom[blk:, :] = p2, p3
         else:
             top, mid, bottom = outs
@@ -194,7 +195,7 @@
             mid[:blk, :], mid[blk:, :] = p1, p2
 
     if merged:
-        outs = [((m, n), f32)] * 2
+        outs = [((m + PAD, n), f32), ((m, n), f32)]
     else:
         outs = [((blk, n), f32), ((m, n), f32), ((blk, n), f32)]
     return call(body, ins, outs, 60 * blk * blk * n)

time: 147 us -> 148 us (level)
  waiting for transfers between devices: 43.3 us -> 48.2 us
  starting transfers between devices: 81.2 us -> 77.1 us
    ppermute x3, waiting for transfers between devices: 20.3 us -> 7.13 us  [row_swap(): from_down = lax.ppermute(to_up, 'row', upward)]
    ppermute x3, starting transfers between devices: 20.3 us -> 11.1 us  [row_swap(): from_up = lax.ppermute(to_down, 'row', downward)]
    ppermute x3, waiting for transfers between devices: 10.1 us -> 18.5 us  [row_swap(): from_up = lax.ppermute(to_down, 'row', downward)]
    ppermute x3, starting transfers between devices: 5.76 us -> 12.6 us  [row_swap(): from_down = lax.ppermute(to_up, 'row', upward)]
    ppermute x2, waiting for transfers between devices: 10.3 us -> 16.9 us  [columns(): relayed = lax.ppermute(vb, 'col', second_hop)]
    ppermute x5, waiting for transfers between devices: 0.32 us -> 2.06 us  [col_swap(): return lax.ppermute(b, 'col', pairs[1])]
  transfers between devices with their start and end apart: 21 -> 21, of which waited for: 9 -> 10; matrix products, arithmetic and copies ran while one was open for 1% -> 1% of each run, Pallas kernels for 4% -> 4%
where the time goes in v8:
time: 148 us; the launch traced here: 147 us
  starting transfers between devices  77.1 us (52%)
  waiting for transfers between devices  48.2 us (33%)
  Pallas kernels  14.5 us (10%)
  local copies, waits for them, and re-layouts  5.17 us (3%)
  between operations  1.63 us (1%)
    ppermute x5, starting transfers between devices, col_swap(): return lax.ppermute(b, 'col', pairs[1])  35.7 us
    ppermute x3, waiting for transfers between devices, row_swap(): from_up = lax.ppermute(to_down, 'row', downward)  18.5 us
    ppermute x2, waiting for transfers between devices, columns(): relayed = lax.ppermute(vb, 'col', second_hop)  16.9 us
    pallas_call x10, Pallas kernels, call(): pl.pallas_call(body, out_shape=[jax.ShapeDtypeStruct(s, d) for s, d in ou...  14.5 us
    ppermute x3, starting transfers between devices, row_swap(): from_down = lax.ppermute(to_up, 'row', upward)  12.6 us
    ppermute x6, starting transfers between devices, chip_swap(): return lax.ppermute(a, 'col', pairs[0])  12.5 us
    ppermute x3, starting transfers between devices, row_swap(): from_up = lax.ppermute(to_down, 'row', downward)  11.1 us
    ppermute x3, waiting for transfers between devices, row_swap(): from_down = lax.ppermute(to_up, 'row', upward)  7.13 us
  transfers between devices with their start and end apart: 21, of which 10 were waited for; matrix products, arithmetic and copies ran while one was open for 1% of the time, Pallas kernels for 4%

profile of v8, /device:TPU:56, one launch (start us, length us, event | category | flops | bytes accessed | tf_op | source)
XLA Modules:
  0.0 146.7 jit_solution(11908319536590103534)
XLA Ops:
  1.1 5.8 %collective-permute-start = (f32[256,256]{1,0:T(8,128)S(1)}, f32[256,256]{1,0:T(8,128)S(1)}, u32[]{:S(2)}, u32[]{:S(2)}) collective-permute-start(f32[256,256]{1,0:T(8,128)S(1)} %get-tuple-element.66), channel_id=1, source_target_pairs={{0,32},{32,64},{64,96},{96,128},{128,160},{160,192},{192,224},{224... | collective-permute-start | bytes 786440 | tf_op jit(solution)/shard_map/ppermute | solution.py:248
  6.9 1.9 %collective-permute-start.1 = (f32[256,256]{1,0:T(8,128)S(1)}, f32[256,256]{1,0:T(8,128)S(1)}, u32[]{:S(2)}, u32[]{:S(2)}) collective-permute-start(f32[256,256]{1,0:T(8,128)S(1)} %get-tuple-element.65), channel_id=1, source_target_pairs={{32,0},{64,32},{96,64},{128,96},{160,128},{192,160},{224,192},{256... | collective-permute-start | bytes 786440 | tf_op jit(solution)/shard_map/ppermute | solution.py:249
  10.3 1.4 copy-done.1
  12.9 1.5 %shard_map.82 = (bf16[2,256,768]{2,1,0:T(8,128)(2,1)S(1)}, bf16[2,256,768]{2,1,0:T(8,128)(2,1)S(1)}, bf16[2,768,256]{2,1,0:T(8,128)(2,1)S(1)}, bf16[2,768,256]{2...) custom-call(f32[2,3,256,256]{3,2,1,0:T(8,128)S(1)} %copy-done.1, ...), custom_call_target="tpu_custom_call" | custom-call | flops 16777216 | bytes 2359348 | tf_op jit(solution)/shard_map/pallas_call | solution.py:33
  14.4 10.2 %collective-permute-start.3 = (f32[520,256]{1,0:T(8,128)S(1)}, f32[520,256]{1,0:T(8,128)S(1)}, u32[]{:S(2)}, u32[]{:S(2)}) collective-permute-start(f32[520,256]{1,0:T(8,128)S(1)} %get-tuple-element.39), channel_id=1, source_target_pairs={{1,2},{3,4},{5,6},{7,8},{9,10},{11,12},{13,14},{15,16},{17,18},{19... | collective-permute-start | bytes 1597448 | tf_op jit(solution)/shard_map/ppermute | solution.py:256
  25.5 1.9 %collective-permute-start.2 = (f32[512,256]{1,0:T(8,128)S(1)}, f32[512,256]{1,0:T(8,128)S(1)}, u32[]{:S(2)}, u32[]{:S(2)}) collective-permute-start(f32[512,256]{1,0:T(8,128)S(1)} %shard_map.83.u), channel_id=1, source_target_pairs={{0,1},{2,3},{4,5},{6,7},{8,9},{10,11},{12,13},{14,15},{16,17},{18,... | collective-permute-start | bytes 1572872 | tf_op jit(solution)/shard_map/ppermute | solution.py:253
  27.4 6.2 %collective-permute-start.4 = (f32[512,256]{1,0:T(8,128)S(1)}, f32[512,256]{1,0:T(8,128)S(1)}, u32[]{:S(2)}, u32[]{:S(2)}) collective-permute-start(f32[512,256]{1,0:T(8,128)S(1)} %shard_map.83.u), channel_id=1, source_target_pairs={{1,2},{3,4},{5,6},{7,8},{9,10},{11,12},{13,14},{15,16},{17,18},{19... | collective-permute-start | bytes 1572872 | tf_op jit(solution)/shard_map/ppermute | solution.py:256
  34.2 1.3 collective-permute-start.8
  35.5 7.7 %collective-permute-start.7 = (f32[264,256]{1,0:T(8,128)S(1)}, f32[264,256]{1,0:T(8,128)S(1)}, u32[]{:S(2)}, u32[]{:S(2)}) collective-permute-start(f32[264,256]{1,0:T(8,128)S(1)} %get-tuple-element.40.w), channel_id=1, source_target_pairs={{1,2},{3,4},{5,6},{7,8},{9,10},{11,12},{13,14},{15,16},{17,18},{19... | collective-permute-start | bytes 811016 | tf_op jit(solution)/shard_map/ppermute | solution.py:256
  43.3 1.3 collective-permute-start.9
  45.7 1.9 %collective-permute-start.5 = (f32[256,256]{1,0:T(8,128)S(1)}, f32[256,256]{1,0:T(8,128)S(1)}, u32[]{:S(2)}, u32[]{:S(2)}) collective-permute-start(f32[256,256]{1,0:T(8,128)S(1)} %get-tuple-element.45), channel_id=1, source_target_pairs={{0,1},{2,3},{4,5},{6,7},{8,9},{10,11},{12,13},{14,15},{16,17},{18,... | collective-permute-start | bytes 786440 | tf_op jit(solution)/shard_map/ppermute | solution.py:253
  47.6 2.4 %collective-permute-start.6 = (f32[256,256]{1,0:T(8,128)S(1)}, f32[256,256]{1,0:T(8,128)S(1)}, u32[]{:S(2)}, u32[]{:S(2)}) collective-permute-start(f32[256,256]{1,0:T(8,128)S(1)} %get-tuple-element.46), channel_id=1, source_target_pairs={{0,1},{2,3},{4,5},{6,7},{8,9},{10,11},{12,13},{14,15},{16,17},{18,... | collective-permute-start | bytes 786440 | tf_op jit(solution)/shard_map/ppermute | solution.py:253
  51.2 6.2 %collective-permute-done.9.relayed = f32[264,256]{1,0:T(8,128)S(1)} collective-permute-done((f32[264,256]{1,0:T(8,128)S(1)}, f32[264,256]{1,0:T(8,128)S(1)}, u32[]{:S(2)}, u32[]{:S(2)}) %collective-permute-start.9) | collective-permute-done | bytes 270368 | tf_op jit(solution)/shard_map/ppermute | solution.py:272
  57.4 2.9 %shard_map.86 = (f32[520,256]{1,0:T(8,128)S(1)}, f32[512,256]{1,0:T(8,128)S(1)}) custom-call(f32[512,256]{1,0:T(8,128)S(1)} %get-tuple-element.44.q, f32[256,256]{1,0:T(8,128)S(1)} %collective-permute-done.5.ra, f32[256,256]{1,0:T(8,128)S(1)} %collective-permute-done.6.ra2, f32[264,256]{1,0:T(8,128)S(1)} %collective-permute-done.7.wb, ...), custom_call_target="tpu_custom_call" | custom-call | flops 1006632960 | bytes 4481076 | tf_op jit(solution)/shard_map/pallas_call | solution.py:33
  60.3 7.5 %collective-permute-start.11 = (f32[520,256]{1,0:T(8,128)S(1)}, f32[520,256]{1,0:T(8,128)S(1)}, u32[]{:S(2)}, u32[]{:S(2)}) collective-permute-start(f32[520,256]{1,0:T(8,128)S(1)} %get-tuple-element.53.top), channel_id=1, source_target_pairs={{32,0},{64,32},{96,64},{128,96},{160,128},{192,160},{224,192},{256... | collective-permute-start | bytes 1597448 | tf_op jit(solution)/shard_map/ppermute | solution.py:249
  67.9 2.7 %collective-permute-start.10 = (f32[512,256]{1,0:T(8,128)S(1)}, f32[512,256]{1,0:T(8,128)S(1)}, u32[]{:S(2)}, u32[]{:S(2)}) collective-permute-start(f32[512,256]{1,0:T(8,128)S(1)} %get-tuple-element.54.bottom), channel_id=1, source_target_pairs={{0,32},{32,64},{64,96},{96,128},{128,160},{160,192},{192,224},{224... | collective-permute-start | bytes 1572872 | tf_op jit(solution)/shard_map/ppermute | solution.py:248
  71.9 14.5 %collective-permute-done.10.rtop = f32[512,256]{1,0:T(8,128)S(1)} collective-permute-done((f32[512,256]{1,0:T(8,128)S(1)}, f32[512,256]{1,0:T(8,128)S(1)}, u32[]{:S(2)}, u32[]{:S(2)}) %collective-permute-start.10) | collective-permute-done | bytes 524320 | tf_op jit(solution)/shard_map/ppermute | solution.py:248
  86.4 1.5 %shard_map.87 = (f32[512,256]{1,0:T(8,128)S(1)}, f32[512,256]{1,0:T(8,128)S(1)}) custom-call(f32[520,256]{1,0:T(8,128)S(1)} %get-tuple-element.53.top, f32[512,256]{1,0:T(8,128)S(1)} %get-tuple-element.54.bottom, f32[512,256]{1,0:T(8,128)S(1)} %collective-permute-done.10.rtop, f32[520,256]{1,0:T(8,128)S(1)} %collective-permute-done.11.rbottom, ...), custom_call_target="tpu_custom_call" | custom-call | flops 603979776 | bytes 4734984 | tf_op jit(solution)/shard_map/pallas_call | solution.py:33
  87.9 1.9 %collective-permute-start.12 = (f32[512,256]{1,0:T(8,128)S(1)}, f32[512,256]{1,0:T(8,128)S(1)}, u32[]{:S(2)}, u32[]{:S(2)}) collective-permute-start(f32[512,256]{1,0:T(8,128)S(1)} %get-tuple-element.55.u), channel_id=1, source_target_pairs={{0,1},{2,3},{4,5},{6,7},{8,9},{10,11},{12,13},{14,15},{16,17},{18,... | collective-permute-start | bytes 1572872 | tf_op jit(solution)/shard_map/ppermute | solution.py:253
  89.9 8.9 %collective-permute-start.13 = (f32[512,256]{1,0:T(8,128)S(1)}, f32[512,256]{1,0:T(8,128)S(1)}, u32[]{:S(2)}, u32[]{:S(2)}) collective-permute-start(f32[512,256]{1,0:T(8,128)S(1)} %get-tuple-element.55.u), channel_id=1, source_target_pairs={{1,2},{3,4},{5,6},{7,8},{9,10},{11,12},{13,14},{15,16},{17,18},{19... | collective-permute-start | bytes 1572872 | tf_op jit(solution)/shard_map/ppermute | solution.py:256
  99.4 1.3 collective-permute-start.17
  100.7 2.7 %collective-permute-start.16 = (f32[264,256]{1,0:T(8,128)S(1)}, f32[264,256]{1,0:T(8,128)S(1)}, u32[]{:S(2)}, u32[]{:S(2)}) collective-permute-start(f32[264,256]{1,0:T(8,128)S(1)} %get-tuple-element.56.w), channel_id=1, source_target_pairs={{1,2},{3,4},{5,6},{7,8},{9,10},{11,12},{13,14},{15,16},{17,18},{19... | collective-permute-start | bytes 811016 | tf_op jit(solution)/shard_map/ppermute | solution.py:256
  107.6 1.9 %collective-permute-start.14 = (f32[256,256]{1,0:T(8,128)S(1)}, f32[256,256]{1,0:T(8,128)S(1)}, u32[]{:S(2)}, u32[]{:S(2)}) collective-permute-start(f32[256,256]{1,0:T(8,128)S(1)} %get-tuple-element.59), channel_id=1, source_target_pairs={{0,1},{2,3},{4,5},{6,7},{8,9},{10,11},{12,13},{14,15},{16,17},{18,... | collective-permute-start | bytes 786440 | tf_op jit(solution)/shard_map/ppermute | solution.py:253
  109.5 2.4 %collective-permute-start.15 = (f32[256,256]{1,0:T(8,128)S(1)}, f32[256,256]{1,0:T(8,128)S(1)}, u32[]{:S(2)}, u32[]{:S(2)}) collective-permute-start(f32[256,256]{1,0:T(8,128)S(1)} %get-tuple-element.60), channel_id=1, source_target_pairs={{0,1},{2,3},{4,5},{6,7},{8,9},{10,11},{12,13},{14,15},{16,17},{18,... | collective-permute-start | bytes 786440 | tf_op jit(solution)/shard_map/ppermute | solution.py:253
  113.1 1.5 %collective-permute-done.16.wb = f32[264,256]{1,0:T(8,128)S(1)} collective-permute-done((f32[264,256]{1,0:T(8,128)S(1)}, f32[264,256]{1,0:T(8,128)S(1)}, u32[]{:S(2)}, u32[]{:S(2)}) %collective-permute-start.16) | collective-permute-done | bytes 270368 | tf_op jit(solution)/shard_map/ppermute | solution.py:256
  114.6 10.7 %collective-permute-done.18.relayed = f32[264,256]{1,0:T(8,128)S(1)} collective-permute-done((f32[264,256]{1,0:T(8,128)S(1)}, f32[264,256]{1,0:T(8,128)S(1)}, u32[]{:S(2)}, u32[]{:S(2)}) %collective-permute-start.18) | collective-permute-done | bytes 270368 | tf_op jit(solution)/shard_map/ppermute | solution.py:272
  125.3 2.9 %shard_map.90 = (f32[256,256]{1,0:T(8,128)S(1)}, f32[512,256]{1,0:T(8,128)S(1)}, f32[256,256]{1,0:T(8,128)S(1)}) custom-call(f32[512,256]{1,0:T(8,128)S(1)} %get-tuple-element.58.q, f32[256,256]{1,0:T(8,128)S(1)} %collective-permute-done.14.ra, f32[256,256]{1,0:T(8,128)S(1)} %collective-permute-done.15.ra2, f32[264,256]{1,0:T(8,128)S(1)} %collective-permute-done.16.wb, ...), custom_call_target="tpu_custom_call" | custom-call | flops 1006632960 | bytes 4481076 | tf_op jit(solution)/shard_map/pallas_call | solution.py:33
  128.2 2.7 %collective-permute-start.19 = (f32[256,256]{1,0:T(8,128)S(1)}, f32[256,256]{1,0:T(8,128)S(1)}, u32[]{:S(2)}, u32[]{:S(2)}) collective-permute-start(f32[256,256]{1,0:T(8,128)S(1)} %get-tuple-element.62), channel_id=1, source_target_pairs={{0,32},{32,64},{64,96},{96,128},{128,160},{160,192},{192,224},{224... | collective-permute-start | bytes 786440 | tf_op jit(solution)/shard_map/ppermute | solution.py:248
  130.9 3.2 %collective-permute-start.20 = (f32[256,256]{1,0:T(8,128)S(1)}, f32[256,256]{1,0:T(8,128)S(1)}, u32[]{:S(2)}, u32[]{:S(2)}) collective-permute-start(f32[256,256]{1,0:T(8,128)S(1)} %get-tuple-element.63), channel_id=1, source_target_pairs={{32,0},{64,32},{96,64},{128,96},{160,128},{192,160},{224,192},{256... | collective-permute-start | bytes 786440 | tf_op jit(solution)/shard_map/ppermute | solution.py:249
  134.1 4.0 %collective-permute-done.19.rup = f32[256,256]{1,0:T(8,128)S(1)} collective-permute-done((f32[256,256]{1,0:T(8,128)S(1)}, f32[256,256]{1,0:T(8,128)S(1)}, u32[]{:S(2)}, u32[]{:S(2)}) %collective-permute-start.19) | collective-permute-done | bytes 262176 | tf_op jit(solution)/shard_map/ppermute | solution.py:248
  138.1 7.1 %collective-permute-done.20.rdown = f32[256,256]{1,0:T(8,128)S(1)} collective-permute-done((f32[256,256]{1,0:T(8,128)S(1)}, f32[256,256]{1,0:T(8,128)S(1)}, u32[]{:S(2)}, u32[]{:S(2)}) %collective-permute-start.20) | collective-permute-done | bytes 262176 | tf_op jit(solution)/shard_map/ppermute | solution.py:249
  145.2 1.5 %shard_map.91 = f32[512,256]{1,0:T(8,128)} custom-call(f32[512,256]{1,0:T(8,128)S(1)} %get-tuple-element.61.mid, f32[256,256]{1,0:T(8,128)S(1)} %collective-permute-done.19.rup, f32[256,256]{1,0:T(8,128)S(1)} %collective-permute-done.20.rdown, f32[512,256]{1,0:T(8,128)S(1)} %get-tuple-element.64.x, f32[2]{0:T(128)S(1)} %pad_maximum_fusion.sc), custom_call_target="tpu_custom_call" | custom-call | flops 1048576 | bytes 1572872 | tf_op jit(solution)/shard_map/pallas_call | solution.py:33
  (32 shorter events, 13.5 us)
Async XLA Ops:
  0.0 24.7 %copy-start = (f32[512,256]{1,0:T(8,128)S(1)}, f32[512,256]{1,0:T(8,128)}, u32[]{:S(2)}) copy-start(f32[512,256]{1,0:T(8,128)} %x.3) | copy-start | bytes 1572868
  1.1 23.5 %collective-permute-start = (f32[256,256]{1,0:T(8,128)S(1)}, f32[256,256]{1,0:T(8,128)S(1)}, u32[]{:S(2)}, u32[]{:S(2)}) collective-permute-start(f32[256,256]{1,0:T(8,128)S(1)} %get-tuple-element.66), channel_id=1, source_target_pairs={{0,32},{32,64},{64,96},{96,128},{128,160},{160,192},{192,224},{224... | collective-permute-start | bytes 786440 | tf_op jit(solution)/shard_map/ppermute | solution.py:248
  6.9 17.8 %collective-permute-start.1 = (f32[256,256]{1,0:T(8,128)S(1)}, f32[256,256]{1,0:T(8,128)S(1)}, u32[]{:S(2)}, u32[]{:S(2)}) collective-permute-start(f32[256,256]{1,0:T(8,128)S(1)} %get-tuple-element.65), channel_id=1, source_target_pairs={{32,0},{64,32},{96,64},{128,96},{160,128},{192,160},{224,192},{256... | collective-permute-start | bytes 786440 | tf_op jit(solution)/shard_map/ppermute | solution.py:249
  10.3 1.4 copy-start.1
  11.7 1.1 copy-start.2
  14.4 19.2 %collective-permute-start.3 = (f32[520,256]{1,0:T(8,128)S(1)}, f32[520,256]{1,0:T(8,128)S(1)}, u32[]{:S(2)}, u32[]{:S(2)}) collective-permute-start(f32[520,256]{1,0:T(8,128)S(1)} %get-tuple-element.39), channel_id=1, source_target_pairs={{1,2},{3,4},{5,6},{7,8},{9,10},{11,12},{13,14},{15,16},{17,18},{19... | collective-permute-start | bytes 1597448 | tf_op jit(solution)/shard_map/ppermute | solution.py:256
  24.7 9.0 %copy-start.3 = (f32[512,256]{1,0:T(8,128)S(1)}, f32[512,256]{1,0:T(8,128)}, u32[]{:S(2)}) copy-start(f32[512,256]{1,0:T(8,128)} %obs.3) | copy-start | bytes 1572868
  25.5 8.1 %collective-permute-start.2 = (f32[512,256]{1,0:T(8,128)S(1)}, f32[512,256]{1,0:T(8,128)S(1)}, u32[]{:S(2)}, u32[]{:S(2)}) collective-permute-start(f32[512,256]{1,0:T(8,128)S(1)} %shard_map.83.u), channel_id=1, source_target_pairs={{0,1},{2,3},{4,5},{6,7},{8,9},{10,11},{12,13},{14,15},{16,17},{18,... | collective-permute-start | bytes 1572872 | tf_op jit(solution)/shard_map/ppermute | solution.py:253
  27.4 17.2 %collective-permute-start.4 = (f32[512,256]{1,0:T(8,128)S(1)}, f32[512,256]{1,0:T(8,128)S(1)}, u32[]{:S(2)}, u32[]{:S(2)}) collective-permute-start(f32[512,256]{1,0:T(8,128)S(1)} %shard_map.83.u), channel_id=1, source_target_pairs={{1,2},{3,4},{5,6},{7,8},{9,10},{11,12},{13,14},{15,16},{17,18},{19... | collective-permute-start | bytes 1572872 | tf_op jit(solution)/shard_map/ppermute | solution.py:256
  34.2 9.0 %collective-permute-start.8 = (f32[264,256]{1,0:T(8,128)S(1)}, f32[264,256]{1,0:T(8,128)S(1)}, u32[]{:S(2)}, u32[]{:S(2)}) collective-permute-start(f32[264,256]{1,0:T(8,128)S(1)} %get-tuple-element.41.v), channel_id=1, source_target_pairs={{1,2},{3,4},{5,6},{7,8},{9,10},{11,12},{13,14},{17,18},{19,20},{21... | collective-permute-start | bytes 811016 | tf_op jit(solution)/shard_map/ppermute | solution.py:270
  35.5 15.7 %collective-permute-start.7 = (f32[264,256]{1,0:T(8,128)S(1)}, f32[264,256]{1,0:T(8,128)S(1)}, u32[]{:S(2)}, u32[]{:S(2)}) collective-permute-start(f32[264,256]{1,0:T(8,128)S(1)} %get-tuple-element.40.w), channel_id=1, source_target_pairs={{1,2},{3,4},{5,6},{7,8},{9,10},{11,12},{13,14},{15,16},{17,18},{19... | collective-permute-start | bytes 811016 | tf_op jit(solution)/shard_map/ppermute | solution.py:256
  43.3 14.2 %collective-permute-start.9 = (f32[264,256]{1,0:T(8,128)S(1)}, f32[264,256]{1,0:T(8,128)S(1)}, u32[]{:S(2)}, u32[]{:S(2)}) collective-permute-start(f32[264,256]{1,0:T(8,128)S(1)} %collective-permute-done.8.vb), channel_id=1, source_target_pairs={{0,16},{31,15},{32,48},{63,47},{64,80},{95,79},{96,112},{127,111},... | collective-permute-start | bytes 811016 | tf_op jit(solution)/shard_map/ppermute | solution.py:272
  45.7 4.3 %collective-permute-start.5 = (f32[256,256]{1,0:T(8,128)S(1)}, f32[256,256]{1,0:T(8,128)S(1)}, u32[]{:S(2)}, u32[]{:S(2)}) collective-permute-start(f32[256,256]{1,0:T(8,128)S(1)} %get-tuple-element.45), channel_id=1, source_target_pairs={{0,1},{2,3},{4,5},{6,7},{8,9},{10,11},{12,13},{14,15},{16,17},{18,... | collective-permute-start | bytes 786440 | tf_op jit(solution)/shard_map/ppermute | solution.py:253
  47.6 3.6 %collective-permute-start.6 = (f32[256,256]{1,0:T(8,128)S(1)}, f32[256,256]{1,0:T(8,128)S(1)}, u32[]{:S(2)}, u32[]{:S(2)}) collective-permute-start(f32[256,256]{1,0:T(8,128)S(1)} %get-tuple-element.46), channel_id=1, source_target_pairs={{0,1},{2,3},{4,5},{6,7},{8,9},{10,11},{12,13},{14,15},{16,17},{18,... | collective-permute-start | bytes 786440 | tf_op jit(solution)/shard_map/ppermute | solution.py:253
  60.3 26.1 %collective-permute-start.11 = (f32[520,256]{1,0:T(8,128)S(1)}, f32[520,256]{1,0:T(8,128)S(1)}, u32[]{:S(2)}, u32[]{:S(2)}) collective-permute-start(f32[520,256]{1,0:T(8,128)S(1)} %get-tuple-element.53.top), channel_id=1, source_target_pairs={{32,0},{64,32},{96,64},{128,96},{160,128},{192,160},{224,192},{256... | collective-permute-start | bytes 1597448 | tf_op jit(solution)/shard_map/ppermute | solution.py:249
  67.9 18.5 %collective-permute-start.10 = (f32[512,256]{1,0:T(8,128)S(1)}, f32[512,256]{1,0:T(8,128)S(1)}, u32[]{:S(2)}, u32[]{:S(2)}) collective-permute-start(f32[512,256]{1,0:T(8,128)S(1)} %get-tuple-element.54.bottom), channel_id=1, source_target_pairs={{0,32},{32,64},{64,96},{96,128},{128,160},{160,192},{192,224},{224... | collective-permute-start | bytes 1572872 | tf_op jit(solution)/shard_map/ppermute | solution.py:248
  87.9 10.9 %collective-permute-start.12 = (f32[512,256]{1,0:T(8,128)S(1)}, f32[512,256]{1,0:T(8,128)S(1)}, u32[]{:S(2)}, u32[]{:S(2)}) collective-permute-start(f32[512,256]{1,0:T(8,128)S(1)} %get-tuple-element.55.u), channel_id=1, source_target_pairs={{0,1},{2,3},{4,5},{6,7},{8,9},{10,11},{12,13},{14,15},{16,17},{18,... | collective-permute-start | bytes 1572872 | tf_op jit(solution)/shard_map/ppermute | solution.py:253
  89.9 16.6 %collective-permute-start.13 = (f32[512,256]{1,0:T(8,128)S(1)}, f32[512,256]{1,0:T(8,128)S(1)}, u32[]{:S(2)}, u32[]{:S(2)}) collective-permute-start(f32[512,256]{1,0:T(8,128)S(1)} %get-tuple-element.55.u), channel_id=1, source_target_pairs={{1,2},{3,4},{5,6},{7,8},{9,10},{11,12},{13,14},{15,16},{17,18},{19... | collective-permute-start | bytes 1572872 | tf_op jit(solution)/shard_map/ppermute | solution.py:256
  99.4 5.3 %collective-permute-start.17 = (f32[264,256]{1,0:T(8,128)S(1)}, f32[264,256]{1,0:T(8,128)S(1)}, u32[]{:S(2)}, u32[]{:S(2)}) collective-permute-start(f32[264,256]{1,0:T(8,128)S(1)} %get-tuple-element.57.v), channel_id=1, source_target_pairs={{1,2},{3,4},{5,6},{7,8},{9,10},{11,12},{13,14},{17,18},{19,20},{21... | collective-permute-start | bytes 811016 | tf_op jit(solution)/shard_map/ppermute | solution.py:270
  100.7 13.9 %collective-permute-start.16 = (f32[264,256]{1,0:T(8,128)S(1)}, f32[264,256]{1,0:T(8,128)S(1)}, u32[]{:S(2)}, u32[]{:S(2)}) collective-permute-start(f32[264,256]{1,0:T(8,128)S(1)} %get-tuple-element.56.w), channel_id=1, source_target_pairs={{1,2},{3,4},{5,6},{7,8},{9,10},{11,12},{13,14},{15,16},{17,18},{19... | collective-permute-start | bytes 811016 | tf_op jit(solution)/shard_map/ppermute | solution.py:256
  104.6 20.7 %collective-permute-start.18 = (f32[264,256]{1,0:T(8,128)S(1)}, f32[264,256]{1,0:T(8,128)S(1)}, u32[]{:S(2)}, u32[]{:S(2)}) collective-permute-start(f32[264,256]{1,0:T(8,128)S(1)} %collective-permute-done.17.vb), channel_id=1, source_target_pairs={{0,16},{31,15},{32,48},{63,47},{64,80},{95,79},{96,112},{127,111},... | collective-permute-start | bytes 811016 | tf_op jit(solution)/shard_map/ppermute | solution.py:272
  107.6 4.3 %collective-permute-start.14 = (f32[256,256]{1,0:T(8,128)S(1)}, f32[256,256]{1,0:T(8,128)S(1)}, u32[]{:S(2)}, u32[]{:S(2)}) collective-permute-start(f32[256,256]{1,0:T(8,128)S(1)} %get-tuple-element.59), channel_id=1, source_target_pairs={{0,1},{2,3},{4,5},{6,7},{8,9},{10,11},{12,13},{14,15},{16,17},{18,... | collective-permute-start | bytes 786440 | tf_op jit(solution)/shard_map/ppermute | solution.py:253
  109.5 3.6 %collective-permute-start.15 = (f32[256,256]{1,0:T(8,128)S(1)}, f32[256,256]{1,0:T(8,128)S(1)}, u32[]{:S(2)}, u32[]{:S(2)}) collective-permute-start(f32[256,256]{1,0:T(8,128)S(1)} %get-tuple-element.60), channel_id=1, source_target_pairs={{0,1},{2,3},{4,5},{6,7},{8,9},{10,11},{12,13},{14,15},{16,17},{18,... | collective-permute-start | bytes 786440 | tf_op jit(solution)/shard_map/ppermute | solution.py:253
  128.2 9.9 %collective-permute-start.19 = (f32[256,256]{1,0:T(8,128)S(1)}, f32[256,256]{1,0:T(8,128)S(1)}, u32[]{:S(2)}, u32[]{:S(2)}) collective-permute-start(f32[256,256]{1,0:T(8,128)S(1)} %get-tuple-element.62), channel_id=1, source_target_pairs={{0,32},{32,64},{64,96},{96,128},{128,160},{160,192},{192,224},{224... | collective-permute-start | bytes 786440 | tf_op jit(solution)/shard_map/ppermute | solution.py:248
  130.9 14.4 %collective-permute-start.20 = (f32[256,256]{1,0:T(8,128)S(1)}, f32[256,256]{1,0:T(8,128)S(1)}, u32[]{:S(2)}, u32[]{:S(2)}) collective-permute-start(f32[256,256]{1,0:T(8,128)S(1)} %get-tuple-element.63), channel_id=1, source_target_pairs={{32,0},{64,32},{96,64},{128,96},{160,128},{192,160},{224,192},{256... | collective-permute-start | bytes 786440 | tf_op jit(solution)/shard_map/ppermute | solution.py:249

commit v9 on v8

--- a/solution.py
+++ b/solution.py
@@ -82,7 +82,7 @@
 
     outs = [((2, blk, 3 * blk), bf16)] * 2 + [((2, 3 * blk, blk), bf16)] * 2
     outs += [((blk, 3 * blk), bf16)] * 2 + [((3 * blk, blk), bf16)] * 2
-    outs += [((2 * blk + 8, blk), f32)]
+    outs += [((blk + PAD, blk), f32)]
     scratch = [pltpu.VMEM(fx.shape, f32), pltpu.VMEM(fy.shape, f32), pltpu.SemaphoreType.DMA((2,))]
     o = call(body, (fx, fy, pos), outs, 1 << 24, scratch, whole=(fx, fy))
     return o[0:2], o[2:4], o[4:6], o[6:8], o[8]
@@ -98,14 +98,16 @@
 def apply_left(x, up, down, ax):
     blk, n = up.shape
 
-    def body(x, up, down, axh, axl, u, xh, xl):
+    def body(x, up, down, axh, axl, u, first, second, xh, xl):
         for t, v in enumerate((up[...], x[:blk, :], x[blk:, :], down[...])):
             s = slice(t * blk, (t + 1) * blk)
             xh[s, :], xl[s, :] = split(v)
         left((axh, axl), (xh, xl), u)
+        first[...], second[...] = u[:blk, :], u[blk:, :]
 
     scratch = [pltpu.VMEM((4 * blk, n), bf16)] * 2
-    return call(body, (x, up, down, *ax), [(x.shape, f32)], 36 * blk * blk * n, scratch)[0]
+    outs = [(x.shape, f32)] + [(up.shape, f32)] * 2
+    return call(body, (x, up, down, *ax), outs, 36 * blk * blk * n, scratch)
 
 
 def rows_of(first, second, r):
@@ -118,11 +120,13 @@
     return parts[0] if len(parts) == 1 else jnp.concatenate(parts, axis=0)
 
 
-def near_misfit(u, ua, observed, byt, cut, fb=None):
+def near_misfit(u, parts, observed, byt, cut, fb=None):
     m, blk = u.shape
-    ins = (u, ua, observed, *byt) + (() if fb is None else (fb,))
-
-    def body(u, ua, obs, byth, bytl, *rest):
+    ins = (u, observed, *byt, *parts) + (() if fb is None else (fb,))
+
+    def body(u, obs, byth, bytl, *rest):
+        uas, rest = rest[: len(parts)], rest[len(parts) :]
+        rows = m // len(parts)
         if fb is not None:
             g, *rest = rest
             g = g[:blk, :]
@@ -133,9 +137,10 @@
         for i in range(0, m, CHUNK):
             r = slice(i, i + CHUNK)
             acc = -obs[r, :]
-            for k, x in enumerate((ua, u)):
+            ua = uas[i // rows][i % rows : i % rows + CHUNK, :]
+            for k, x in enumerate((ua, u[r, :])):
                 s = slice(k * blk, (k + 1) * blk)
-                acc = acc + dot3(*split(x[r, :]), byth[s, :], bytl[s, :])
+                acc = acc + dot3(*split(x), byth[s, :], bytl[s, :])
             here = min(max(cut - i, 0), CHUNK)
             if here:
                 w[i : i + here, :] = acc[:here]
@@ -259,14 +264,14 @@
     first_hop = [p for p in pairs[1] if set(p) != {half - 1, half}] + [(half - 1, 0), (half, cols - 1)]
     second_hop = [(0, half), (cols - 1, half - 1)]
 
-    def columns(u, fb, merged):
-        ua = chip_swap(u)
+    def columns(u, halves, fb, merged):
         ub = col_swap(u)
         cut = blk + PAD
         if merged:
-            w, v, *fb = near_misfit(u, ua, observed, byt, cut, fb)
+            parts = [chip_swap(v) for v in halves]
+            w, v, *fb = near_misfit(u, parts, observed, byt, cut, fb)
         else:
-            w, v = near_misfit(u, ua, observed, byt, cut)
+            w, v = near_misfit(u, [chip_swap(u)], observed, byt, cut)
         vb = lax.ppermute(v, "col", first_hop)
         wb = col_swap(w)
         relayed = lax.ppermute(vb, "col", second_hop)
@@ -279,11 +284,11 @@
     sc = jnp.concatenate([step_size, threshold])
     up, down = row_swap(x[:blk], x[blk:])
     ax, atx, byf, byt, fb = prepare(fx, fy, pos)
-    u = apply_left(x, up, down, ax)
-    top, bottom, fb = columns(u, col_swap(fb), True)
+    u, *halves = apply_left(x, up, down, ax)
+    top, bottom, fb = columns(u, halves, col_swap(fb), True)
     rtop, rbottom = row_swap(top, bottom)
     x, u = update_left(top, bottom, rtop, rbottom, x, up, down, sc, ax)
-    top, mid, bottom, _ = columns(u, fb, False)
+    top, mid, bottom, _ = columns(u, None, fb, False)
     rup, rdown = row_swap(top, bottom)
     return update(mid, rup, rdown, x, sc)
 

time: 148 us -> 146 us (0.986)
  waiting for transfers between devices: 48.2 us -> 43.8 us
    ppermute x3, starting transfers between devices: 11.1 us -> 18.5 us  [row_swap(): from_up = lax.ppermute(to_down, 'row', downward)]
    ppermute x3, starting transfers between devices: 12.6 us -> 5.76 us  [row_swap(): from_down = lax.ppermute(to_up, 'row', upward)]
    ppermute x3, waiting for transfers between devices: 7.13 us -> 4.57 us  [row_swap(): from_down = lax.ppermute(to_up, 'row', upward)]
    ppermute x2, waiting for transfers between devices: 16.9 us -> 14.5 us  [columns(): relayed = lax.ppermute(vb, 'col', second_hop)]
    ppermute x6 -> x7, starting transfers between devices: 12.5 us -> 14.9 us  [chip_swap(): return lax.ppermute(a, 'col', pairs[0])]
    ppermute x3, waiting for transfers between devices: 18.5 us -> 16.7 us  [row_swap(): from_up = lax.ppermute(to_down, 'row', downward)]
    ppermute x5, starting transfers between devices: 35.7 us -> 33.9 us  [col_swap(): return lax.ppermute(b, 'col', pairs[1])]
    ppermute x5, waiting for transfers between devices: 2.06 us -> 3.8 us  [col_swap(): return lax.ppermute(b, 'col', pairs[1])]
  transfers between devices with their start and end apart: 21 -> 22, of which waited for: 10 -> 10; matrix products, arithmetic and copies ran while one was open for 1% -> 1% of each run, Pallas kernels for 4% -> 4%
where the time goes in v9:
time: 146 us; the launch traced here: 143 us
  starting transfers between devices  78.2 us (54%)
  waiting for transfers between devices  43.8 us (30%)
  Pallas kernels  14.5 us (10%)
  local copies, waits for them, and re-layouts  5.17 us (4%)
  between operations  1.66 us (1%)
    ppermute x5, starting transfers between devices, col_swap(): return lax.ppermute(b, 'col', pairs[1])  33.9 us
    ppermute x3, starting transfers between devices, row_swap(): from_up = lax.ppermute(to_down, 'row', downward)  18.5 us
    ppermute x3, waiting for transfers between devices, row_swap(): from_up = lax.ppermute(to_down, 'row', downward)  16.7 us
    ppermute x7, starting transfers between devices, chip_swap(): return lax.ppermute(a, 'col', pairs[0])  14.9 us
    pallas_call x10, Pallas kernels, call(): pl.pallas_call(body, out_shape=[jax.ShapeDtypeStruct(s, d) for s, d in ou...  14.5 us
    ppermute x2, waiting for transfers between devices, columns(): relayed = lax.ppermute(vb, 'col', second_hop)  14.5 us
    ppermute x3, starting transfers between devices, row_swap(): from_down = lax.ppermute(to_up, 'row', upward)  5.76 us
    ppermute x3, waiting for transfers between devices, row_swap(): from_down = lax.ppermute(to_up, 'row', upward)  4.57 us
  transfers between devices with their start and end apart: 22, of which 10 were waited for; matrix products, arithmetic and copies ran while one was open for 1% of the time, Pallas kernels for 4%

profile of v9, /device:TPU:56, one launch (start us, length us, event | category | flops | bytes accessed | tf_op | source)
XLA Modules:
  0.0 143.5 jit_solution(18090261980815436757)
XLA Ops:
  1.1 5.8 %collective-permute-start = (f32[256,256]{1,0:T(8,128)S(1)}, f32[256,256]{1,0:T(8,128)S(1)}, u32[]{:S(2)}, u32[]{:S(2)}) collective-permute-start(f32[256,256]{1,0:T(8,128)S(1)} %get-tuple-element.72), channel_id=1, source_target_pairs={{0,32},{32,64},{64,96},{96,128},{128,160},{160,192},{192,224},{224... | collective-permute-start | bytes 786440 | tf_op jit(solution)/shard_map/ppermute | solution.py:253
  6.9 1.9 %collective-permute-start.1 = (f32[256,256]{1,0:T(8,128)S(1)}, f32[256,256]{1,0:T(8,128)S(1)}, u32[]{:S(2)}, u32[]{:S(2)}) collective-permute-start(f32[256,256]{1,0:T(8,128)S(1)} %get-tuple-element.71), channel_id=1, source_target_pairs={{32,0},{64,32},{96,64},{128,96},{160,128},{192,160},{224,192},{256... | collective-permute-start | bytes 786440 | tf_op jit(solution)/shard_map/ppermute | solution.py:254
  10.3 1.4 copy-done.1
  12.9 1.5 %shard_map.82 = (bf16[2,256,768]{2,1,0:T(8,128)(2,1)S(1)}, bf16[2,256,768]{2,1,0:T(8,128)(2,1)S(1)}, bf16[2,768,256]{2,1,0:T(8,128)(2,1)S(1)}, bf16[2,768,256]{2...) custom-call(f32[2,3,256,256]{3,2,1,0:T(8,128)S(1)} %copy-done.1, ...), custom_call_target="tpu_custom_call" | custom-call | flops 16777216 | bytes 2359348 | tf_op jit(solution)/shard_map/pallas_call | solution.py:33
  14.4 10.4 %collective-permute-start.4 = (f32[264,256]{1,0:T(8,128)S(1)}, f32[264,256]{1,0:T(8,128)S(1)}, u32[]{:S(2)}, u32[]{:S(2)}) collective-permute-start(f32[264,256]{1,0:T(8,128)S(1)} %get-tuple-element.45), channel_id=1, source_target_pairs={{1,2},{3,4},{5,6},{7,8},{9,10},{11,12},{13,14},{15,16},{17,18},{19... | collective-permute-start | bytes 811016 | tf_op jit(solution)/shard_map/ppermute | solution.py:261
  25.6 1.9 %collective-permute-start.2 = (f32[256,256]{1,0:T(8,128)S(1)}, f32[256,256]{1,0:T(8,128)S(1)}, u32[]{:S(2)}, u32[]{:S(2)}) collective-permute-start(f32[256,256]{1,0:T(8,128)S(1)} %get-tuple-element.43), channel_id=1, source_target_pairs={{0,1},{2,3},{4,5},{6,7},{8,9},{10,11},{12,13},{14,15},{16,17},{18,... | collective-permute-start | bytes 786440 | tf_op jit(solution)/shard_map/ppermute | solution.py:258
  27.6 2.4 %collective-permute-start.3 = (f32[256,256]{1,0:T(8,128)S(1)}, f32[256,256]{1,0:T(8,128)S(1)}, u32[]{:S(2)}, u32[]{:S(2)}) collective-permute-start(f32[256,256]{1,0:T(8,128)S(1)} %get-tuple-element.44), channel_id=1, source_target_pairs={{0,1},{2,3},{4,5},{6,7},{8,9},{10,11},{12,13},{14,15},{16,17},{18,... | collective-permute-start | bytes 786440 | tf_op jit(solution)/shard_map/ppermute | solution.py:258
  30.0 5.5 %collective-permute-start.5 = (f32[512,256]{1,0:T(8,128)S(1)}, f32[512,256]{1,0:T(8,128)S(1)}, u32[]{:S(2)}, u32[]{:S(2)}) collective-permute-start(f32[512,256]{1,0:T(8,128)S(1)} %get-tuple-element.40.u), channel_id=1, source_target_pairs={{1,2},{3,4},{5,6},{7,8},{9,10},{11,12},{13,14},{15,16},{17,18},{19... | collective-permute-start | bytes 1572872 | tf_op jit(solution)/shard_map/ppermute | solution.py:261
  37.5 6.0 %collective-permute-start.8 = (f32[264,256]{1,0:T(8,128)S(1)}, f32[264,256]{1,0:T(8,128)S(1)}, u32[]{:S(2)}, u32[]{:S(2)}) collective-permute-start(f32[264,256]{1,0:T(8,128)S(1)} %get-tuple-element.46.w), channel_id=1, source_target_pairs={{1,2},{3,4},{5,6},{7,8},{9,10},{11,12},{13,14},{15,16},{17,18},{19... | collective-permute-start | bytes 811016 | tf_op jit(solution)/shard_map/ppermute | solution.py:261
  44.8 1.8 %collective-permute-done.5.ub = f32[512,256]{1,0:T(8,128)S(1)} collective-permute-done((f32[512,256]{1,0:T(8,128)S(1)}, f32[512,256]{1,0:T(8,128)S(1)}, u32[]{:S(2)}, u32[]{:S(2)}) %collective-permute-start.5) | collective-permute-done | bytes 524320 | tf_op jit(solution)/shard_map/ppermute | solution.py:261
  47.7 1.9 %collective-permute-start.6 = (f32[256,256]{1,0:T(8,128)S(1)}, f32[256,256]{1,0:T(8,128)S(1)}, u32[]{:S(2)}, u32[]{:S(2)}) collective-permute-start(f32[256,256]{1,0:T(8,128)S(1)} %get-tuple-element.51), channel_id=1, source_target_pairs={{0,1},{2,3},{4,5},{6,7},{8,9},{10,11},{12,13},{14,15},{16,17},{18,... | collective-permute-start | bytes 786440 | tf_op jit(solution)/shard_map/ppermute | solution.py:258
  49.7 2.4 %collective-permute-start.7 = (f32[256,256]{1,0:T(8,128)S(1)}, f32[256,256]{1,0:T(8,128)S(1)}, u32[]{:S(2)}, u32[]{:S(2)}) collective-permute-start(f32[256,256]{1,0:T(8,128)S(1)} %get-tuple-element.52), channel_id=1, source_target_pairs={{0,1},{2,3},{4,5},{6,7},{8,9},{10,11},{12,13},{14,15},{16,17},{18,... | collective-permute-start | bytes 786440 | tf_op jit(solution)/shard_map/ppermute | solution.py:258
  53.2 8.5 %collective-permute-done.10.relayed = f32[264,256]{1,0:T(8,128)S(1)} collective-permute-done((f32[264,256]{1,0:T(8,128)S(1)}, f32[264,256]{1,0:T(8,128)S(1)}, u32[]{:S(2)}, u32[]{:S(2)}) %collective-permute-start.10) | collective-permute-done | bytes 270368 | tf_op jit(solution)/shard_map/ppermute | solution.py:277
  61.7 2.9 %shard_map.86 = (f32[520,256]{1,0:T(8,128)S(1)}, f32[512,256]{1,0:T(8,128)S(1)}) custom-call(f32[512,256]{1,0:T(8,128)S(1)} %get-tuple-element.50.q, f32[256,256]{1,0:T(8,128)S(1)} %collective-permute-done.6.ra, f32[256,256]{1,0:T(8,128)S(1)} %collective-permute-done.7.ra2, f32[264,256]{1,0:T(8,128)S(1)} %collective-permute-done.8.wb, ...), custom_call_target="tpu_custom_call" | custom-call | flops 1006632960 | bytes 4481076 | tf_op jit(solution)/shard_map/pallas_call | solution.py:33
  64.6 1.9 %collective-permute-start.12 = (f32[520,256]{1,0:T(8,128)S(1)}, f32[520,256]{1,0:T(8,128)S(1)}, u32[]{:S(2)}, u32[]{:S(2)}) collective-permute-start(f32[520,256]{1,0:T(8,128)S(1)} %get-tuple-element.59.top), channel_id=1, source_target_pairs={{32,0},{64,32},{96,64},{128,96},{160,128},{192,160},{224,192},{256... | collective-permute-start | bytes 1597448 | tf_op jit(solution)/shard_map/ppermute | solution.py:254
  66.5 6.6 %collective-permute-start.11 = (f32[512,256]{1,0:T(8,128)S(1)}, f32[512,256]{1,0:T(8,128)S(1)}, u32[]{:S(2)}, u32[]{:S(2)}) collective-permute-start(f32[512,256]{1,0:T(8,128)S(1)} %get-tuple-element.60.bottom), channel_id=1, source_target_pairs={{0,32},{32,64},{64,96},{96,128},{128,160},{160,192},{192,224},{224... | collective-permute-start | bytes 1572872 | tf_op jit(solution)/shard_map/ppermute | solution.py:253
  74.5 12.2 %collective-permute-done.11.rtop = f32[512,256]{1,0:T(8,128)S(1)} collective-permute-done((f32[512,256]{1,0:T(8,128)S(1)}, f32[512,256]{1,0:T(8,128)S(1)}, u32[]{:S(2)}, u32[]{:S(2)}) %collective-permute-start.11) | collective-permute-done | bytes 524320 | tf_op jit(solution)/shard_map/ppermute | solution.py:253
  86.7 1.5 %shard_map.87 = (f32[512,256]{1,0:T(8,128)S(1)}, f32[512,256]{1,0:T(8,128)S(1)}) custom-call(f32[520,256]{1,0:T(8,128)S(1)} %get-tuple-element.59.top, f32[512,256]{1,0:T(8,128)S(1)} %get-tuple-element.60.bottom, f32[512,256]{1,0:T(8,128)S(1)} %collective-permute-done.11.rtop, f32[520,256]{1,0:T(8,128)S(1)} %collective-permute-done.12.rbottom, ...), custom_call_target="tpu_custom_call" | custom-call | flops 603979776 | bytes 4734984 | tf_op jit(solution)/shard_map/pallas_call | solution.py:33
  88.2 1.9 %collective-permute-start.13 = (f32[512,256]{1,0:T(8,128)S(1)}, f32[512,256]{1,0:T(8,128)S(1)}, u32[]{:S(2)}, u32[]{:S(2)}) collective-permute-start(f32[512,256]{1,0:T(8,128)S(1)} %get-tuple-element.61.u), channel_id=1, source_target_pairs={{0,1},{2,3},{4,5},{6,7},{8,9},{10,11},{12,13},{14,15},{16,17},{18,... | collective-permute-start | bytes 1572872 | tf_op jit(solution)/shard_map/ppermute | solution.py:258
  90.1 10.0 %collective-permute-start.14 = (f32[512,256]{1,0:T(8,128)S(1)}, f32[512,256]{1,0:T(8,128)S(1)}, u32[]{:S(2)}, u32[]{:S(2)}) collective-permute-start(f32[512,256]{1,0:T(8,128)S(1)} %get-tuple-element.61.u), channel_id=1, source_target_pairs={{1,2},{3,4},{5,6},{7,8},{9,10},{11,12},{13,14},{15,16},{17,18},{19... | collective-permute-start | bytes 1572872 | tf_op jit(solution)/shard_map/ppermute | solution.py:261
  102.1 1.9 %collective-permute-start.17 = (f32[264,256]{1,0:T(8,128)S(1)}, f32[264,256]{1,0:T(8,128)S(1)}, u32[]{:S(2)}, u32[]{:S(2)}) collective-permute-start(f32[264,256]{1,0:T(8,128)S(1)} %get-tuple-element.62.w), channel_id=1, source_target_pairs={{1,2},{3,4},{5,6},{7,8},{9,10},{11,12},{13,14},{15,16},{17,18},{19... | collective-permute-start | bytes 811016 | tf_op jit(solution)/shard_map/ppermute | solution.py:261
  104.0 2.0 %collective-permute-done.18.vb = f32[264,256]{1,0:T(8,128)S(1)} collective-permute-done((f32[264,256]{1,0:T(8,128)S(1)}, f32[264,256]{1,0:T(8,128)S(1)}, u32[]{:S(2)}, u32[]{:S(2)}) %collective-permute-start.18) | collective-permute-done | bytes 270368 | tf_op jit(solution)/shard_map/ppermute | solution.py:275
  108.5 1.9 %collective-permute-start.15 = (f32[256,256]{1,0:T(8,128)S(1)}, f32[256,256]{1,0:T(8,128)S(1)}, u32[]{:S(2)}, u32[]{:S(2)}) collective-permute-start(f32[256,256]{1,0:T(8,128)S(1)} %get-tuple-element.65), channel_id=1, source_target_pairs={{0,1},{2,3},{4,5},{6,7},{8,9},{10,11},{12,13},{14,15},{16,17},{18,... | collective-permute-start | bytes 786440 | tf_op jit(solution)/shard_map/ppermute | solution.py:258
  110.4 2.4 %collective-permute-start.16 = (f32[256,256]{1,0:T(8,128)S(1)}, f32[256,256]{1,0:T(8,128)S(1)}, u32[]{:S(2)}, u32[]{:S(2)}) collective-permute-start(f32[256,256]{1,0:T(8,128)S(1)} %get-tuple-element.66), channel_id=1, source_target_pairs={{0,1},{2,3},{4,5},{6,7},{8,9},{10,11},{12,13},{14,15},{16,17},{18,... | collective-permute-start | bytes 786440 | tf_op jit(solution)/shard_map/ppermute | solution.py:258
  113.9 2.0 %collective-permute-done.17.wb = f32[264,256]{1,0:T(8,128)S(1)} collective-permute-done((f32[264,256]{1,0:T(8,128)S(1)}, f32[264,256]{1,0:T(8,128)S(1)}, u32[]{:S(2)}, u32[]{:S(2)}) %collective-permute-start.17) | collective-permute-done | bytes 270368 | tf_op jit(solution)/shard_map/ppermute | solution.py:261
  116.0 6.0 %collective-permute-done.19.relayed = f32[264,256]{1,0:T(8,128)S(1)} collective-permute-done((f32[264,256]{1,0:T(8,128)S(1)}, f32[264,256]{1,0:T(8,128)S(1)}, u32[]{:S(2)}, u32[]{:S(2)}) %collective-permute-start.19) | collective-permute-done | bytes 270368 | tf_op jit(solution)/shard_map/ppermute | solution.py:277
  122.0 2.9 %shard_map.90 = (f32[256,256]{1,0:T(8,128)S(1)}, f32[512,256]{1,0:T(8,128)S(1)}, f32[256,256]{1,0:T(8,128)S(1)}) custom-call(f32[512,256]{1,0:T(8,128)S(1)} %get-tuple-element.64.q, f32[256,256]{1,0:T(8,128)S(1)} %collective-permute-done.15.ra, f32[256,256]{1,0:T(8,128)S(1)} %collective-permute-done.16.ra2, f32[264,256]{1,0:T(8,128)S(1)} %collective-permute-done.17.wb, ...), custom_call_target="tpu_custom_call" | custom-call | flops 1006632960 | bytes 4481076 | tf_op jit(solution)/shard_map/pallas_call | solution.py:33
  124.9 6.1 %collective-permute-start.20 = (f32[256,256]{1,0:T(8,128)S(1)}, f32[256,256]{1,0:T(8,128)S(1)}, u32[]{:S(2)}, u32[]{:S(2)}) collective-permute-start(f32[256,256]{1,0:T(8,128)S(1)} %get-tuple-element.68), channel_id=1, source_target_pairs={{0,32},{32,64},{64,96},{96,128},{128,160},{160,192},{192,224},{224... | collective-permute-start | bytes 786440 | tf_op jit(solution)/shard_map/ppermute | solution.py:253
  131.1 1.9 %collective-permute-start.21 = (f32[256,256]{1,0:T(8,128)S(1)}, f32[256,256]{1,0:T(8,128)S(1)}, u32[]{:S(2)}, u32[]{:S(2)}) collective-permute-start(f32[256,256]{1,0:T(8,128)S(1)} %get-tuple-element.69), channel_id=1, source_target_pairs={{32,0},{64,32},{96,64},{128,96},{160,128},{192,160},{224,192},{256... | collective-permute-start | bytes 786440 | tf_op jit(solution)/shard_map/ppermute | solution.py:254
  133.0 4.5 %collective-permute-done.20.rup = f32[256,256]{1,0:T(8,128)S(1)} collective-permute-done((f32[256,256]{1,0:T(8,128)S(1)}, f32[256,256]{1,0:T(8,128)S(1)}, u32[]{:S(2)}, u32[]{:S(2)}) %collective-permute-start.20) | collective-permute-done | bytes 262176 | tf_op jit(solution)/shard_map/ppermute | solution.py:253
  137.5 4.6 %collective-permute-done.21.rdown = f32[256,256]{1,0:T(8,128)S(1)} collective-permute-done((f32[256,256]{1,0:T(8,128)S(1)}, f32[256,256]{1,0:T(8,128)S(1)}, u32[]{:S(2)}, u32[]{:S(2)}) %collective-permute-start.21) | collective-permute-done | bytes 262176 | tf_op jit(solution)/shard_map/ppermute | solution.py:254
  142.0 1.5 %shard_map.91 = f32[512,256]{1,0:T(8,128)} custom-call(f32[512,256]{1,0:T(8,128)S(1)} %get-tuple-element.67.mid, f32[256,256]{1,0:T(8,128)S(1)} %collective-permute-done.20.rup, f32[256,256]{1,0:T(8,128)S(1)} %collective-permute-done.21.rdown, f32[512,256]{1,0:T(8,128)S(1)} %get-tuple-element.70.x, f32[2]{0:T(128)S(1)} %pad_maximum_fusion.sc), custom_call_target="tpu_custom_call" | custom-call | flops 1048576 | bytes 1572872 | tf_op jit(solution)/shard_map/pallas_call | solution.py:33
  (34 shorter events, 15.5 us)
Async XLA Ops:
  0.0 24.8 %copy-start = (f32[512,256]{1,0:T(8,128)S(1)}, f32[512,256]{1,0:T(8,128)}, u32[]{:S(2)}) copy-start(f32[512,256]{1,0:T(8,128)} %x.3) | copy-start | bytes 1572868
  1.1 23.7 %collective-permute-start = (f32[256,256]{1,0:T(8,128)S(1)}, f32[256,256]{1,0:T(8,128)S(1)}, u32[]{:S(2)}, u32[]{:S(2)}) collective-permute-start(f32[256,256]{1,0:T(8,128)S(1)} %get-tuple-element.72), channel_id=1, source_target_pairs={{0,32},{32,64},{64,96},{96,128},{128,160},{160,192},{192,224},{224... | collective-permute-start | bytes 786440 | tf_op jit(solution)/shard_map/ppermute | solution.py:253
  6.9 17.9 %collective-permute-start.1 = (f32[256,256]{1,0:T(8,128)S(1)}, f32[256,256]{1,0:T(8,128)S(1)}, u32[]{:S(2)}, u32[]{:S(2)}) collective-permute-start(f32[256,256]{1,0:T(8,128)S(1)} %get-tuple-element.71), channel_id=1, source_target_pairs={{32,0},{64,32},{96,64},{128,96},{160,128},{192,160},{224,192},{256... | collective-permute-start | bytes 786440 | tf_op jit(solution)/shard_map/ppermute | solution.py:254
  10.3 1.4 copy-start.1
  11.7 1.1 copy-start.2
  14.4 21.2 %copy-start.3 = (f32[512,256]{1,0:T(8,128)S(1)}, f32[512,256]{1,0:T(8,128)}, u32[]{:S(2)}) copy-start(f32[512,256]{1,0:T(8,128)} %obs.3) | copy-start | bytes 1572868
  14.4 21.1 %collective-permute-start.4 = (f32[264,256]{1,0:T(8,128)S(1)}, f32[264,256]{1,0:T(8,128)S(1)}, u32[]{:S(2)}, u32[]{:S(2)}) collective-permute-start(f32[264,256]{1,0:T(8,128)S(1)} %get-tuple-element.45), channel_id=1, source_target_pairs={{1,2},{3,4},{5,6},{7,8},{9,10},{11,12},{13,14},{15,16},{17,18},{19... | collective-permute-start | bytes 811016 | tf_op jit(solution)/shard_map/ppermute | solution.py:261
  25.6 9.9 %collective-permute-start.2 = (f32[256,256]{1,0:T(8,128)S(1)}, f32[256,256]{1,0:T(8,128)S(1)}, u32[]{:S(2)}, u32[]{:S(2)}) collective-permute-start(f32[256,256]{1,0:T(8,128)S(1)} %get-tuple-element.43), channel_id=1, source_target_pairs={{0,1},{2,3},{4,5},{6,7},{8,9},{10,11},{12,13},{14,15},{16,17},{18,... | collective-permute-start | bytes 786440 | tf_op jit(solution)/shard_map/ppermute | solution.py:258
  27.6 8.0 %collective-permute-start.3 = (f32[256,256]{1,0:T(8,128)S(1)}, f32[256,256]{1,0:T(8,128)S(1)}, u32[]{:S(2)}, u32[]{:S(2)}) collective-permute-start(f32[256,256]{1,0:T(8,128)S(1)} %get-tuple-element.44), channel_id=1, source_target_pairs={{0,1},{2,3},{4,5},{6,7},{8,9},{10,11},{12,13},{14,15},{16,17},{18,... | collective-permute-start | bytes 786440 | tf_op jit(solution)/shard_map/ppermute | solution.py:258
  30.0 16.6 %collective-permute-start.5 = (f32[512,256]{1,0:T(8,128)S(1)}, f32[512,256]{1,0:T(8,128)S(1)}, u32[]{:S(2)}, u32[]{:S(2)}) collective-permute-start(f32[512,256]{1,0:T(8,128)S(1)} %get-tuple-element.40.u), channel_id=1, source_target_pairs={{1,2},{3,4},{5,6},{7,8},{9,10},{11,12},{13,14},{15,16},{17,18},{19... | collective-permute-start | bytes 1572872 | tf_op jit(solution)/shard_map/ppermute | solution.py:261
  36.2 7.4 %collective-permute-start.9 = (f32[264,256]{1,0:T(8,128)S(1)}, f32[264,256]{1,0:T(8,128)S(1)}, u32[]{:S(2)}, u32[]{:S(2)}) collective-permute-start(f32[264,256]{1,0:T(8,128)S(1)} %get-tuple-element.47.v), channel_id=1, source_target_pairs={{1,2},{3,4},{5,6},{7,8},{9,10},{11,12},{13,14},{17,18},{19,20},{21... | collective-permute-start | bytes 811016 | tf_op jit(solution)/shard_map/ppermute | solution.py:275
  37.5 14.6 %collective-permute-start.8 = (f32[264,256]{1,0:T(8,128)S(1)}, f32[264,256]{1,0:T(8,128)S(1)}, u32[]{:S(2)}, u32[]{:S(2)}) collective-permute-start(f32[264,256]{1,0:T(8,128)S(1)} %get-tuple-element.46.w), channel_id=1, source_target_pairs={{1,2},{3,4},{5,6},{7,8},{9,10},{11,12},{13,14},{15,16},{17,18},{19... | collective-permute-start | bytes 811016 | tf_op jit(solution)/shard_map/ppermute | solution.py:261
  43.5 18.1 %collective-permute-start.10 = (f32[264,256]{1,0:T(8,128)S(1)}, f32[264,256]{1,0:T(8,128)S(1)}, u32[]{:S(2)}, u32[]{:S(2)}) collective-permute-start(f32[264,256]{1,0:T(8,128)S(1)} %collective-permute-done.9.vb), channel_id=1, source_target_pairs={{0,16},{31,15},{32,48},{63,47},{64,80},{95,79},{96,112},{127,111},... | collective-permute-start | bytes 811016 | tf_op jit(solution)/shard_map/ppermute | solution.py:277
  47.7 4.4 %collective-permute-start.6 = (f32[256,256]{1,0:T(8,128)S(1)}, f32[256,256]{1,0:T(8,128)S(1)}, u32[]{:S(2)}, u32[]{:S(2)}) collective-permute-start(f32[256,256]{1,0:T(8,128)S(1)} %get-tuple-element.51), channel_id=1, source_target_pairs={{0,1},{2,3},{4,5},{6,7},{8,9},{10,11},{12,13},{14,15},{16,17},{18,... | collective-permute-start | bytes 786440 | tf_op jit(solution)/shard_map/ppermute | solution.py:258
  49.7 3.6 %collective-permute-start.7 = (f32[256,256]{1,0:T(8,128)S(1)}, f32[256,256]{1,0:T(8,128)S(1)}, u32[]{:S(2)}, u32[]{:S(2)}) collective-permute-start(f32[256,256]{1,0:T(8,128)S(1)} %get-tuple-element.52), channel_id=1, source_target_pairs={{0,1},{2,3},{4,5},{6,7},{8,9},{10,11},{12,13},{14,15},{16,17},{18,... | collective-permute-start | bytes 786440 | tf_op jit(solution)/shard_map/ppermute | solution.py:258
  64.6 22.1 %collective-permute-start.12 = (f32[520,256]{1,0:T(8,128)S(1)}, f32[520,256]{1,0:T(8,128)S(1)}, u32[]{:S(2)}, u32[]{:S(2)}) collective-permute-start(f32[520,256]{1,0:T(8,128)S(1)} %get-tuple-element.59.top), channel_id=1, source_target_pairs={{32,0},{64,32},{96,64},{128,96},{160,128},{192,160},{224,192},{256... | collective-permute-start | bytes 1597448 | tf_op jit(solution)/shard_map/ppermute | solution.py:254
  66.5 20.2 %collective-permute-start.11 = (f32[512,256]{1,0:T(8,128)S(1)}, f32[512,256]{1,0:T(8,128)S(1)}, u32[]{:S(2)}, u32[]{:S(2)}) collective-permute-start(f32[512,256]{1,0:T(8,128)S(1)} %get-tuple-element.60.bottom), channel_id=1, source_target_pairs={{0,32},{32,64},{64,96},{96,128},{128,160},{160,192},{192,224},{224... | collective-permute-start | bytes 1572872 | tf_op jit(solution)/shard_map/ppermute | solution.py:253
  88.2 12.0 %collective-permute-start.13 = (f32[512,256]{1,0:T(8,128)S(1)}, f32[512,256]{1,0:T(8,128)S(1)}, u32[]{:S(2)}, u32[]{:S(2)}) collective-permute-start(f32[512,256]{1,0:T(8,128)S(1)} %get-tuple-element.61.u), channel_id=1, source_target_pairs={{0,1},{2,3},{4,5},{6,7},{8,9},{10,11},{12,13},{14,15},{16,17},{18,... | collective-permute-start | bytes 1572872 | tf_op jit(solution)/shard_map/ppermute | solution.py:258
  90.1 17.2 %collective-permute-start.14 = (f32[512,256]{1,0:T(8,128)S(1)}, f32[512,256]{1,0:T(8,128)S(1)}, u32[]{:S(2)}, u32[]{:S(2)}) collective-permute-start(f32[512,256]{1,0:T(8,128)S(1)} %get-tuple-element.61.u), channel_id=1, source_target_pairs={{1,2},{3,4},{5,6},{7,8},{9,10},{11,12},{13,14},{15,16},{17,18},{19... | collective-permute-start | bytes 1572872 | tf_op jit(solution)/shard_map/ppermute | solution.py:261
  100.8 5.3 %collective-permute-start.18 = (f32[264,256]{1,0:T(8,128)S(1)}, f32[264,256]{1,0:T(8,128)S(1)}, u32[]{:S(2)}, u32[]{:S(2)}) collective-permute-start(f32[264,256]{1,0:T(8,128)S(1)} %get-tuple-element.63.v), channel_id=1, source_target_pairs={{1,2},{3,4},{5,6},{7,8},{9,10},{11,12},{13,14},{17,18},{19,20},{21... | collective-permute-start | bytes 811016 | tf_op jit(solution)/shard_map/ppermute | solution.py:275
  102.1 13.9 %collective-permute-start.17 = (f32[264,256]{1,0:T(8,128)S(1)}, f32[264,256]{1,0:T(8,128)S(1)}, u32[]{:S(2)}, u32[]{:S(2)}) collective-permute-start(f32[264,256]{1,0:T(8,128)S(1)} %get-tuple-element.62.w), channel_id=1, source_target_pairs={{1,2},{3,4},{5,6},{7,8},{9,10},{11,12},{13,14},{15,16},{17,18},{19... | collective-permute-start | bytes 811016 | tf_op jit(solution)/shard_map/ppermute | solution.py:261
  106.0 16.0 %collective-permute-start.19 = (f32[264,256]{1,0:T(8,128)S(1)}, f32[264,256]{1,0:T(8,128)S(1)}, u32[]{:S(2)}, u32[]{:S(2)}) collective-permute-start(f32[264,256]{1,0:T(8,128)S(1)} %collective-permute-done.18.vb), channel_id=1, source_target_pairs={{0,16},{31,15},{32,48},{63,47},{64,80},{95,79},{96,112},{127,111},... | collective-permute-start | bytes 811016 | tf_op jit(solution)/shard_map/ppermute | solution.py:277
  108.5 4.3 %collective-permute-start.15 = (f32[256,256]{1,0:T(8,128)S(1)}, f32[256,256]{1,0:T(8,128)S(1)}, u32[]{:S(2)}, u32[]{:S(2)}) collective-permute-start(f32[256,256]{1,0:T(8,128)S(1)} %get-tuple-element.65), channel_id=1, source_target_pairs={{0,1},{2,3},{4,5},{6,7},{8,9},{10,11},{12,13},{14,15},{16,17},{18,... | collective-permute-start | bytes 786440 | tf_op jit(solution)/shard_map/ppermute | solution.py:258
  110.4 3.6 %collective-permute-start.16 = (f32[256,256]{1,0:T(8,128)S(1)}, f32[256,256]{1,0:T(8,128)S(1)}, u32[]{:S(2)}, u32[]{:S(2)}) collective-permute-start(f32[256,256]{1,0:T(8,128)S(1)} %get-tuple-element.66), channel_id=1, source_target_pairs={{0,1},{2,3},{4,5},{6,7},{8,9},{10,11},{12,13},{14,15},{16,17},{18,... | collective-permute-start | bytes 786440 | tf_op jit(solution)/shard_map/ppermute | solution.py:258
  124.9 12.5 %collective-permute-start.20 = (f32[256,256]{1,0:T(8,128)S(1)}, f32[256,256]{1,0:T(8,128)S(1)}, u32[]{:S(2)}, u32[]{:S(2)}) collective-permute-start(f32[256,256]{1,0:T(8,128)S(1)} %get-tuple-element.68), channel_id=1, source_target_pairs={{0,32},{32,64},{64,96},{96,128},{128,160},{160,192},{192,224},{224... | collective-permute-start | bytes 786440 | tf_op jit(solution)/shard_map/ppermute | solution.py:253
  131.1 11.0 %collective-permute-start.21 = (f32[256,256]{1,0:T(8,128)S(1)}, f32[256,256]{1,0:T(8,128)S(1)}, u32[]{:S(2)}, u32[]{:S(2)}) collective-permute-start(f32[256,256]{1,0:T(8,128)S(1)} %get-tuple-element.69), channel_id=1, source_target_pairs={{32,0},{64,32},{96,64},{128,96},{160,128},{192,160},{224,192},{256... | collective-permute-start | bytes 786440 | tf_op jit(solution)/shard_map/ppermute | solution.py:254

commit v10 on v6

--- a/solution.py
+++ b/solution.py
@@ -252,7 +252,7 @@
         ua = chip_swap(u)
         ub = col_swap(u)
         if merged:
-            w, v = near_misfit(u, ua, observed, byt, fb, 31 * blk // 16)
+            w, v = near_misfit(u, ua, observed, byt, fb, blk + 120)
         else:
             pad = jnp.zeros((16, blk), f32)
             w, v = near_misfit(u, ua, observed, byt, pad, blk + 8)

time: 145 us -> 143 us (0.986)
  the two profiles are of different devices: /device:TPU:4 before, /device:TPU:56 now
where the time goes in v10:
time: 143 us; the launch traced here: 142 us
  starting transfers between devices  75.6 us (53%)
  waiting for transfers between devices  45.4 us (32%)
  Pallas kernels  14.4 us (10%)
  local copies, waits for them, and re-layouts  5.01 us (4%)
  between operations  1.6 us (1%)
    ppermute x3, starting transfers between devices, row_swap(): from_up = lax.ppermute(to_down, 'row', downward)  26.2 us
    ppermute x4, starting transfers between devices, col_swap(): return lax.ppermute(b, 'col', pairs[1])  25.7 us
    ppermute x3, waiting for transfers between devices, row_swap(): from_down = lax.ppermute(to_up, 'row', upward)  17.1 us
    pallas_call x10, Pallas kernels, call(): pl.pallas_call(body, out_shape=[jax.ShapeDtypeStruct(s, d) for s, d in ou...  14.4 us
    ppermute x4, waiting for transfers between devices, col_swap(): return lax.ppermute(b, 'col', pairs[1])  13.1 us
    ppermute x6, starting transfers between devices, chip_swap(): return lax.ppermute(a, 'col', pairs[0])  12.5 us
    ppermute x2, waiting for transfers between devices, columns(): vb = lax.ppermute(v, 'col', first_hop)  7.35 us
    ppermute x3, starting transfers between devices, row_swap(): from_down = lax.ppermute(to_up, 'row', upward)  6.06 us
  transfers between devices with their start and end apart: 20, of which 12 were waited for; matrix products, arithmetic and copies ran while one was open for 0% of the time, Pallas kernels for 3%

profile of v10, /device:TPU:56, one launch (start us, length us, event | category | flops | bytes accessed | tf_op | source)
XLA Modules:
  0.0 142.1 jit_solution(12928975850436116610)
XLA Ops:
  1.1 5.8 %collective-permute-start = (f32[256,256]{1,0:T(8,128)S(1)}, f32[256,256]{1,0:T(8,128)S(1)}, u32[]{:S(2)}, u32[]{:S(2)}) collective-permute-start(f32[256,256]{1,0:T(8,128)S(1)} %get-tuple-element.66), channel_id=1, source_target_pairs={{0,32},{32,64},{64,96},{96,128},{128,160},{160,192},{192,224},{224... | collective-permute-start | bytes 786440 | tf_op jit(solution)/shard_map/ppermute | solution.py:237
  6.9 1.9 %collective-permute-start.1 = (f32[256,256]{1,0:T(8,128)S(1)}, f32[256,256]{1,0:T(8,128)S(1)}, u32[]{:S(2)}, u32[]{:S(2)}) collective-permute-start(f32[256,256]{1,0:T(8,128)S(1)} %get-tuple-element.65), channel_id=1, source_target_pairs={{32,0},{64,32},{96,64},{128,96},{160,128},{192,160},{224,192},{256... | collective-permute-start | bytes 786440 | tf_op jit(solution)/shard_map/ppermute | solution.py:238
  8.9 1.4 copy-done.1
  14.1 5.2 %collective-permute-done.1.down = f32[256,256]{1,0:T(8,128)S(1)} collective-permute-done((f32[256,256]{1,0:T(8,128)S(1)}, f32[256,256]{1,0:T(8,128)S(1)}, u32[]{:S(2)}, u32[]{:S(2)}) %collective-permute-start.1) | collective-permute-done | bytes 262176 | tf_op jit(solution)/shard_map/ppermute | solution.py:238
  20.1 1.9 %collective-permute-start.2 = (f32[512,256]{1,0:T(8,128)S(1)}, f32[512,256]{1,0:T(8,128)S(1)}, u32[]{:S(2)}, u32[]{:S(2)}) collective-permute-start(f32[512,256]{1,0:T(8,128)S(1)} %shard_map.83.u), channel_id=1, source_target_pairs={{0,1},{2,3},{4,5},{6,7},{8,9},{10,11},{12,13},{14,15},{16,17},{18,... | collective-permute-start | bytes 1572872 | tf_op jit(solution)/shard_map/ppermute | solution.py:242
  22.0 11.6 %collective-permute-start.3 = (f32[512,256]{1,0:T(8,128)S(1)}, f32[512,256]{1,0:T(8,128)S(1)}, u32[]{:S(2)}, u32[]{:S(2)}) collective-permute-start(f32[512,256]{1,0:T(8,128)S(1)} %shard_map.83.u), channel_id=1, source_target_pairs={{1,2},{3,4},{5,6},{7,8},{9,10},{11,12},{13,14},{15,16},{17,18},{19... | collective-permute-start | bytes 1572872 | tf_op jit(solution)/shard_map/ppermute | solution.py:245
  34.2 1.3 collective-permute-start.7
  35.5 5.3 %collective-permute-done.7.vb = f32[392,256]{1,0:T(8,128)S(1)} collective-permute-done((f32[392,256]{1,0:T(8,128)S(1)}, f32[392,256]{1,0:T(8,128)S(1)}, u32[]{:S(2)}, u32[]{:S(2)}) %collective-permute-start.7) | collective-permute-done | bytes 401440 | tf_op jit(solution)/shard_map/ppermute | solution.py:259
  42.2 1.9 %collective-permute-start.6 = (f32[376,256]{1,0:T(8,128)S(1)}, f32[376,256]{1,0:T(8,128)S(1)}, u32[]{:S(2)}, u32[]{:S(2)}) collective-permute-start(f32[376,256]{1,0:T(8,128)S(1)} %get-tuple-element.40.w), channel_id=1, source_target_pairs={{1,2},{3,4},{5,6},{7,8},{9,10},{11,12},{13,14},{15,16},{17,18},{19... | collective-permute-start | bytes 1155080 | tf_op jit(solution)/shard_map/ppermute | solution.py:245
  45.2 1.9 %collective-permute-start.4 = (f32[256,256]{1,0:T(8,128)S(1)}, f32[256,256]{1,0:T(8,128)S(1)}, u32[]{:S(2)}, u32[]{:S(2)}) collective-permute-start(f32[256,256]{1,0:T(8,128)S(1)} %get-tuple-element.45), channel_id=1, source_target_pairs={{0,1},{2,3},{4,5},{6,7},{8,9},{10,11},{12,13},{14,15},{16,17},{18,... | collective-permute-start | bytes 786440 | tf_op jit(solution)/shard_map/ppermute | solution.py:242
  47.2 2.4 %collective-permute-start.5 = (f32[256,256]{1,0:T(8,128)S(1)}, f32[256,256]{1,0:T(8,128)S(1)}, u32[]{:S(2)}, u32[]{:S(2)}) collective-permute-start(f32[256,256]{1,0:T(8,128)S(1)} %get-tuple-element.46), channel_id=1, source_target_pairs={{0,1},{2,3},{4,5},{6,7},{8,9},{10,11},{12,13},{14,15},{16,17},{18,... | collective-permute-start | bytes 786440 | tf_op jit(solution)/shard_map/ppermute | solution.py:242
  50.7 9.9 %collective-permute-done.6.wb = f32[376,256]{1,0:T(8,128)S(1)} collective-permute-done((f32[376,256]{1,0:T(8,128)S(1)}, f32[376,256]{1,0:T(8,128)S(1)}, u32[]{:S(2)}, u32[]{:S(2)}) %collective-permute-start.6) | collective-permute-done | bytes 385056 | tf_op jit(solution)/shard_map/ppermute | solution.py:245
  60.6 3.0 %shard_map.86 = (f32[512,256]{1,0:T(8,128)S(1)}, f32[512,256]{1,0:T(8,128)S(1)}, bf16[256,256]{1,0:T(8,128)(2,1)S(1)}, bf16[256,256]{1,0:T(8,128)(2,1)S(1)}, bf1...) custom-call(f32[512,256]{1,0:T(8,128)S(1)} %get-tuple-element.44.q, f32[256,256]{1,0:T(8,128)S(1)} %collective-permute-done.4.ra, ...), custom_call_target="tpu_custom_call" | custom-call | flops 1006632960 | bytes 4333584 | tf_op jit(solution)/shard_map/pallas_call | solution.py:31
  63.6 2.2 %collective-permute-start.10 = (f32[512,256]{1,0:T(8,128)S(1)}, f32[512,256]{1,0:T(8,128)S(1)}, u32[]{:S(2)}, u32[]{:S(2)}) collective-permute-start(f32[512,256]{1,0:T(8,128)S(1)} %get-tuple-element.49.top), channel_id=1, source_target_pairs={{32,0},{64,32},{96,64},{128,96},{160,128},{192,160},{224,192},{256... | collective-permute-start | bytes 1572872 | tf_op jit(solution)/shard_map/ppermute | solution.py:238
  65.8 6.3 %collective-permute-start.9 = (f32[512,256]{1,0:T(8,128)S(1)}, f32[512,256]{1,0:T(8,128)S(1)}, u32[]{:S(2)}, u32[]{:S(2)}) collective-permute-start(f32[512,256]{1,0:T(8,128)S(1)} %get-tuple-element.50.bottom), channel_id=1, source_target_pairs={{0,32},{32,64},{64,96},{96,128},{128,160},{160,192},{192,224},{224... | collective-permute-start | bytes 1572872 | tf_op jit(solution)/shard_map/ppermute | solution.py:237
  73.5 4.8 %collective-permute-done.10.rbottom = f32[512,256]{1,0:T(8,128)S(1)} collective-permute-done((f32[512,256]{1,0:T(8,128)S(1)}, f32[512,256]{1,0:T(8,128)S(1)}, u32[]{:S(2)}, u32[]{:S(2)}) %collective-permute-start.10) | collective-permute-done | bytes 524320 | tf_op jit(solution)/shard_map/ppermute | solution.py:238
  78.3 2.5 %collective-permute-done.9.rtop = f32[512,256]{1,0:T(8,128)S(1)} collective-permute-done((f32[512,256]{1,0:T(8,128)S(1)}, f32[512,256]{1,0:T(8,128)S(1)}, u32[]{:S(2)}, u32[]{:S(2)}) %collective-permute-start.9) | collective-permute-done | bytes 524320 | tf_op jit(solution)/shard_map/ppermute | solution.py:237
  80.9 1.5 %shard_map.87 = (f32[512,256]{1,0:T(8,128)S(1)}, f32[512,256]{1,0:T(8,128)S(1)}) custom-call(f32[512,256]{1,0:T(8,128)S(1)} %get-tuple-element.49.top, f32[512,256]{1,0:T(8,128)S(1)} %get-tuple-element.50.bottom, f32[512,256]{1,0:T(8,128)S(1)} %collective-permute-done.9.rtop, f32[512,256]{1,0:T(8,128)S(1)} %collective-permute-done.10.rbottom, ...), custom_call_target="tpu_custom_call" | custom-call | flops 603979776 | bytes 4718600 | tf_op jit(solution)/shard_map/pallas_call | solution.py:31
  82.4 1.9 %collective-permute-start.11 = (f32[512,256]{1,0:T(8,128)S(1)}, f32[512,256]{1,0:T(8,128)S(1)}, u32[]{:S(2)}, u32[]{:S(2)}) collective-permute-start(f32[512,256]{1,0:T(8,128)S(1)} %get-tuple-element.51.u), channel_id=1, source_target_pairs={{0,1},{2,3},{4,5},{6,7},{8,9},{10,11},{12,13},{14,15},{16,17},{18,... | collective-permute-start | bytes 1572872 | tf_op jit(solution)/shard_map/ppermute | solution.py:242
  84.3 10.2 %collective-permute-start.12 = (f32[512,256]{1,0:T(8,128)S(1)}, f32[512,256]{1,0:T(8,128)S(1)}, u32[]{:S(2)}, u32[]{:S(2)}) collective-permute-start(f32[512,256]{1,0:T(8,128)S(1)} %get-tuple-element.51.u), channel_id=1, source_target_pairs={{1,2},{3,4},{5,6},{7,8},{9,10},{11,12},{13,14},{15,16},{17,18},{19... | collective-permute-start | bytes 1572872 | tf_op jit(solution)/shard_map/ppermute | solution.py:245
  95.2 1.3 collective-permute-start.16
  96.5 1.9 %collective-permute-start.15 = (f32[264,256]{1,0:T(8,128)S(1)}, f32[264,256]{1,0:T(8,128)S(1)}, u32[]{:S(2)}, u32[]{:S(2)}) collective-permute-start(f32[264,256]{1,0:T(8,128)S(1)} %get-tuple-element.52.w), channel_id=1, source_target_pairs={{1,2},{3,4},{5,6},{7,8},{9,10},{11,12},{13,14},{15,16},{17,18},{19... | collective-permute-start | bytes 811016 | tf_op jit(solution)/shard_map/ppermute | solution.py:245
  98.4 2.0 %collective-permute-done.16.vb = f32[264,256]{1,0:T(8,128)S(1)} collective-permute-done((f32[264,256]{1,0:T(8,128)S(1)}, f32[264,256]{1,0:T(8,128)S(1)}, u32[]{:S(2)}, u32[]{:S(2)}) %collective-permute-start.16) | collective-permute-done | bytes 270368 | tf_op jit(solution)/shard_map/ppermute | solution.py:259
  102.9 1.9 %collective-permute-start.13 = (f32[256,256]{1,0:T(8,128)S(1)}, f32[256,256]{1,0:T(8,128)S(1)}, u32[]{:S(2)}, u32[]{:S(2)}) collective-permute-start(f32[256,256]{1,0:T(8,128)S(1)} %get-tuple-element.55), channel_id=1, source_target_pairs={{0,1},{2,3},{4,5},{6,7},{8,9},{10,11},{12,13},{14,15},{16,17},{18,... | collective-permute-start | bytes 786440 | tf_op jit(solution)/shard_map/ppermute | solution.py:242
  104.8 2.4 %collective-permute-start.14 = (f32[256,256]{1,0:T(8,128)S(1)}, f32[256,256]{1,0:T(8,128)S(1)}, u32[]{:S(2)}, u32[]{:S(2)}) collective-permute-start(f32[256,256]{1,0:T(8,128)S(1)} %get-tuple-element.56), channel_id=1, source_target_pairs={{0,1},{2,3},{4,5},{6,7},{8,9},{10,11},{12,13},{14,15},{16,17},{18,... | collective-permute-start | bytes 786440 | tf_op jit(solution)/shard_map/ppermute | solution.py:242
  108.4 3.2 %collective-permute-done.15.wb = f32[264,256]{1,0:T(8,128)S(1)} collective-permute-done((f32[264,256]{1,0:T(8,128)S(1)}, f32[264,256]{1,0:T(8,128)S(1)}, u32[]{:S(2)}, u32[]{:S(2)}) %collective-permute-start.15) | collective-permute-done | bytes 270368 | tf_op jit(solution)/shard_map/ppermute | solution.py:245
  112.7 2.9 %shard_map.90 = (f32[256,256]{1,0:T(8,128)S(1)}, f32[512,256]{1,0:T(8,128)S(1)}, f32[256,256]{1,0:T(8,128)S(1)}) custom-call(f32[512,256]{1,0:T(8,128)S(1)} %get-tuple-element.54.q, f32[256,256]{1,0:T(8,128)S(1)} %collective-permute-done.13.ra, f32[256,256]{1,0:T(8,128)S(1)} %collective-permute-done.14.ra2, f32[264,256]{1,0:T(8,128)S(1)} %collective-permute-done.15.wb, ...), custom_call_target="tpu_custom_call" | custom-call | flops 1006632960 | bytes 4481040 | tf_op jit(solution)/shard_map/pallas_call | solution.py:31
  115.6 14.1 %collective-permute-start.18 = (f32[256,256]{1,0:T(8,128)S(1)}, f32[256,256]{1,0:T(8,128)S(1)}, u32[]{:S(2)}, u32[]{:S(2)}) collective-permute-start(f32[256,256]{1,0:T(8,128)S(1)} %get-tuple-element.62), channel_id=1, source_target_pairs={{0,32},{32,64},{64,96},{96,128},{128,160},{160,192},{192,224},{224... | collective-permute-start | bytes 786440 | tf_op jit(solution)/shard_map/ppermute | solution.py:237
  129.7 1.9 %collective-permute-start.19 = (f32[256,256]{1,0:T(8,128)S(1)}, f32[256,256]{1,0:T(8,128)S(1)}, u32[]{:S(2)}, u32[]{:S(2)}) collective-permute-start(f32[256,256]{1,0:T(8,128)S(1)} %get-tuple-element.63), channel_id=1, source_target_pairs={{32,0},{64,32},{96,64},{128,96},{160,128},{192,160},{224,192},{256... | collective-permute-start | bytes 786440 | tf_op jit(solution)/shard_map/ppermute | solution.py:238
  131.6 1.9 %collective-permute-done.18.rup = f32[256,256]{1,0:T(8,128)S(1)} collective-permute-done((f32[256,256]{1,0:T(8,128)S(1)}, f32[256,256]{1,0:T(8,128)S(1)}, u32[]{:S(2)}, u32[]{:S(2)}) %collective-permute-start.18) | collective-permute-done | bytes 262176 | tf_op jit(solution)/shard_map/ppermute | solution.py:237
  133.5 7.1 %collective-permute-done.19.rdown = f32[256,256]{1,0:T(8,128)S(1)} collective-permute-done((f32[256,256]{1,0:T(8,128)S(1)}, f32[256,256]{1,0:T(8,128)S(1)}, u32[]{:S(2)}, u32[]{:S(2)}) %collective-permute-start.19) | collective-permute-done | bytes 262176 | tf_op jit(solution)/shard_map/ppermute | solution.py:238
  140.6 1.5 %shard_map.91 = f32[512,256]{1,0:T(8,128)} custom-call(f32[512,256]{1,0:T(8,128)S(1)} %get-tuple-element.61.mid, f32[256,256]{1,0:T(8,128)S(1)} %collective-permute-done.18.rup, f32[256,256]{1,0:T(8,128)S(1)} %collective-permute-done.19.rdown, f32[512,256]{1,0:T(8,128)S(1)} %get-tuple-element.64.x, f32[2]{0:T(128)S(1)} %pad_maximum_fusion.sc), custom_call_target="tpu_custom_call" | custom-call | flops 1048576 | bytes 1572872 | tf_op jit(solution)/shard_map/pallas_call | solution.py:31
  (34 shorter events, 15.2 us)
Async XLA Ops:
  0.0 19.2 %copy-start = (f32[512,256]{1,0:T(8,128)S(1)}, f32[512,256]{1,0:T(8,128)}, u32[]{:S(2)}) copy-start(f32[512,256]{1,0:T(8,128)} %x.3) | copy-start | bytes 1572868
  1.1 12.9 %collective-permute-start = (f32[256,256]{1,0:T(8,128)S(1)}, f32[256,256]{1,0:T(8,128)S(1)}, u32[]{:S(2)}, u32[]{:S(2)}) collective-permute-start(f32[256,256]{1,0:T(8,128)S(1)} %get-tuple-element.66), channel_id=1, source_target_pairs={{0,32},{32,64},{64,96},{96,128},{128,160},{160,192},{192,224},{224... | collective-permute-start | bytes 786440 | tf_op jit(solution)/shard_map/ppermute | solution.py:237
  6.9 12.4 %collective-permute-start.1 = (f32[256,256]{1,0:T(8,128)S(1)}, f32[256,256]{1,0:T(8,128)S(1)}, u32[]{:S(2)}, u32[]{:S(2)}) collective-permute-start(f32[256,256]{1,0:T(8,128)S(1)} %get-tuple-element.65), channel_id=1, source_target_pairs={{32,0},{64,32},{96,64},{128,96},{160,128},{192,160},{224,192},{256... | collective-permute-start | bytes 786440 | tf_op jit(solution)/shard_map/ppermute | solution.py:238
  8.9 1.4 copy-start.1
  10.3 1.1 copy-start.2
  11.4 0.7 copy-start.3
  12.1 0.7 copy-start.4
  19.2 14.4 %copy-start.5 = (f32[512,256]{1,0:T(8,128)S(1)}, f32[512,256]{1,0:T(8,128)}, u32[]{:S(2)}) copy-start(f32[512,256]{1,0:T(8,128)} %obs.3) | copy-start | bytes 1572868
  20.1 13.5 %collective-permute-start.2 = (f32[512,256]{1,0:T(8,128)S(1)}, f32[512,256]{1,0:T(8,128)S(1)}, u32[]{:S(2)}, u32[]{:S(2)}) collective-permute-start(f32[512,256]{1,0:T(8,128)S(1)} %shard_map.83.u), channel_id=1, source_target_pairs={{0,1},{2,3},{4,5},{6,7},{8,9},{10,11},{12,13},{14,15},{16,17},{18,... | collective-permute-start | bytes 1572872 | tf_op jit(solution)/shard_map/ppermute | solution.py:242
  22.0 22.1 %collective-permute-start.3 = (f32[512,256]{1,0:T(8,128)S(1)}, f32[512,256]{1,0:T(8,128)S(1)}, u32[]{:S(2)}, u32[]{:S(2)}) collective-permute-start(f32[512,256]{1,0:T(8,128)S(1)} %shard_map.83.u), channel_id=1, source_target_pairs={{1,2},{3,4},{5,6},{7,8},{9,10},{11,12},{13,14},{15,16},{17,18},{19... | collective-permute-start | bytes 1572872 | tf_op jit(solution)/shard_map/ppermute | solution.py:245
  34.2 6.7 %collective-permute-start.7 = (f32[392,256]{1,0:T(8,128)S(1)}, f32[392,256]{1,0:T(8,128)S(1)}, u32[]{:S(2)}, u32[]{:S(2)}) collective-permute-start(f32[392,256]{1,0:T(8,128)S(1)} %get-tuple-element.41.v), channel_id=1, source_target_pairs={{1,2},{3,4},{5,6},{7,8},{9,10},{11,12},{13,14},{17,18},{19,20},{21... | collective-permute-start | bytes 1204232 | tf_op jit(solution)/shard_map/ppermute | solution.py:259
  40.9 19.7 %collective-permute-start.8 = (f32[392,256]{1,0:T(8,128)S(1)}, f32[392,256]{1,0:T(8,128)S(1)}, u32[]{:S(2)}, u32[]{:S(2)}) collective-permute-start(f32[392,256]{1,0:T(8,128)S(1)} %collective-permute-done.7.vb), channel_id=1, source_target_pairs={{0,16},{31,15},{32,48},{63,47},{64,80},{95,79},{96,112},{127,111},... | collective-permute-start | bytes 1204232 | tf_op jit(solution)/shard_map/ppermute | solution.py:261
  42.2 18.4 %collective-permute-start.6 = (f32[376,256]{1,0:T(8,128)S(1)}, f32[376,256]{1,0:T(8,128)S(1)}, u32[]{:S(2)}, u32[]{:S(2)}) collective-permute-start(f32[376,256]{1,0:T(8,128)S(1)} %get-tuple-element.40.w), channel_id=1, source_target_pairs={{1,2},{3,4},{5,6},{7,8},{9,10},{11,12},{13,14},{15,16},{17,18},{19... | collective-permute-start | bytes 1155080 | tf_op jit(solution)/shard_map/ppermute | solution.py:245
  45.2 4.3 %collective-permute-start.4 = (f32[256,256]{1,0:T(8,128)S(1)}, f32[256,256]{1,0:T(8,128)S(1)}, u32[]{:S(2)}, u32[]{:S(2)}) collective-permute-start(f32[256,256]{1,0:T(8,128)S(1)} %get-tuple-element.45), channel_id=1, source_target_pairs={{0,1},{2,3},{4,5},{6,7},{8,9},{10,11},{12,13},{14,15},{16,17},{18,... | collective-permute-start | bytes 786440 | tf_op jit(solution)/shard_map/ppermute | solution.py:242
  47.2 3.6 %collective-permute-start.5 = (f32[256,256]{1,0:T(8,128)S(1)}, f32[256,256]{1,0:T(8,128)S(1)}, u32[]{:S(2)}, u32[]{:S(2)}) collective-permute-start(f32[256,256]{1,0:T(8,128)S(1)} %get-tuple-element.46), channel_id=1, source_target_pairs={{0,1},{2,3},{4,5},{6,7},{8,9},{10,11},{12,13},{14,15},{16,17},{18,... | collective-permute-start | bytes 786440 | tf_op jit(solution)/shard_map/ppermute | solution.py:242
  63.6 14.7 %collective-permute-start.10 = (f32[512,256]{1,0:T(8,128)S(1)}, f32[512,256]{1,0:T(8,128)S(1)}, u32[]{:S(2)}, u32[]{:S(2)}) collective-permute-start(f32[512,256]{1,0:T(8,128)S(1)} %get-tuple-element.49.top), channel_id=1, source_target_pairs={{32,0},{64,32},{96,64},{128,96},{160,128},{192,160},{224,192},{256... | collective-permute-start | bytes 1572872 | tf_op jit(solution)/shard_map/ppermute | solution.py:238
  65.8 15.0 %collective-permute-start.9 = (f32[512,256]{1,0:T(8,128)S(1)}, f32[512,256]{1,0:T(8,128)S(1)}, u32[]{:S(2)}, u32[]{:S(2)}) collective-permute-start(f32[512,256]{1,0:T(8,128)S(1)} %get-tuple-element.50.bottom), channel_id=1, source_target_pairs={{0,32},{32,64},{64,96},{96,128},{128,160},{160,192},{192,224},{224... | collective-permute-start | bytes 1572872 | tf_op jit(solution)/shard_map/ppermute | solution.py:237
  82.4 12.2 %collective-permute-start.11 = (f32[512,256]{1,0:T(8,128)S(1)}, f32[512,256]{1,0:T(8,128)S(1)}, u32[]{:S(2)}, u32[]{:S(2)}) collective-permute-start(f32[512,256]{1,0:T(8,128)S(1)} %get-tuple-element.51.u), channel_id=1, source_target_pairs={{0,1},{2,3},{4,5},{6,7},{8,9},{10,11},{12,13},{14,15},{16,17},{18,... | collective-permute-start | bytes 1572872 | tf_op jit(solution)/shard_map/ppermute | solution.py:242
  84.3 17.4 %collective-permute-start.12 = (f32[512,256]{1,0:T(8,128)S(1)}, f32[512,256]{1,0:T(8,128)S(1)}, u32[]{:S(2)}, u32[]{:S(2)}) collective-permute-start(f32[512,256]{1,0:T(8,128)S(1)} %get-tuple-element.51.u), channel_id=1, source_target_pairs={{1,2},{3,4},{5,6},{7,8},{9,10},{11,12},{13,14},{15,16},{17,18},{19... | collective-permute-start | bytes 1572872 | tf_op jit(solution)/shard_map/ppermute | solution.py:245
  95.2 5.3 %collective-permute-start.16 = (f32[264,256]{1,0:T(8,128)S(1)}, f32[264,256]{1,0:T(8,128)S(1)}, u32[]{:S(2)}, u32[]{:S(2)}) collective-permute-start(f32[264,256]{1,0:T(8,128)S(1)} %get-tuple-element.53.v), channel_id=1, source_target_pairs={{1,2},{3,4},{5,6},{7,8},{9,10},{11,12},{13,14},{17,18},{19,20},{21... | collective-permute-start | bytes 811016 | tf_op jit(solution)/shard_map/ppermute | solution.py:259
  96.5 15.1 %collective-permute-start.15 = (f32[264,256]{1,0:T(8,128)S(1)}, f32[264,256]{1,0:T(8,128)S(1)}, u32[]{:S(2)}, u32[]{:S(2)}) collective-permute-start(f32[264,256]{1,0:T(8,128)S(1)} %get-tuple-element.52.w), channel_id=1, source_target_pairs={{1,2},{3,4},{5,6},{7,8},{9,10},{11,12},{13,14},{15,16},{17,18},{19... | collective-permute-start | bytes 811016 | tf_op jit(solution)/shard_map/ppermute | solution.py:245
  100.4 12.2 %collective-permute-start.17 = (f32[264,256]{1,0:T(8,128)S(1)}, f32[264,256]{1,0:T(8,128)S(1)}, u32[]{:S(2)}, u32[]{:S(2)}) collective-permute-start(f32[264,256]{1,0:T(8,128)S(1)} %collective-permute-done.16.vb), channel_id=1, source_target_pairs={{0,16},{31,15},{32,48},{63,47},{64,80},{95,79},{96,112},{127,111},... | collective-permute-start | bytes 811016 | tf_op jit(solution)/shard_map/ppermute | solution.py:261
  102.9 4.3 %collective-permute-start.13 = (f32[256,256]{1,0:T(8,128)S(1)}, f32[256,256]{1,0:T(8,128)S(1)}, u32[]{:S(2)}, u32[]{:S(2)}) collective-permute-start(f32[256,256]{1,0:T(8,128)S(1)} %get-tuple-element.55), channel_id=1, source_target_pairs={{0,1},{2,3},{4,5},{6,7},{8,9},{10,11},{12,13},{14,15},{16,17},{18,... | collective-permute-start | bytes 786440 | tf_op jit(solution)/shard_map/ppermute | solution.py:242
  104.8 3.6 %collective-permute-start.14 = (f32[256,256]{1,0:T(8,128)S(1)}, f32[256,256]{1,0:T(8,128)S(1)}, u32[]{:S(2)}, u32[]{:S(2)}) collective-permute-start(f32[256,256]{1,0:T(8,128)S(1)} %get-tuple-element.56), channel_id=1, source_target_pairs={{0,1},{2,3},{4,5},{6,7},{8,9},{10,11},{12,13},{14,15},{16,17},{18,... | collective-permute-start | bytes 786440 | tf_op jit(solution)/shard_map/ppermute | solution.py:242
  115.6 18.0 %collective-permute-start.18 = (f32[256,256]{1,0:T(8,128)S(1)}, f32[256,256]{1,0:T(8,128)S(1)}, u32[]{:S(2)}, u32[]{:S(2)}) collective-permute-start(f32[256,256]{1,0:T(8,128)S(1)} %get-tuple-element.62), channel_id=1, source_target_pairs={{0,32},{32,64},{64,96},{96,128},{128,160},{160,192},{192,224},{224... | collective-permute-start | bytes 786440 | tf_op jit(solution)/shard_map/ppermute | solution.py:237
  129.7 11.0 %collective-permute-start.19 = (f32[256,256]{1,0:T(8,128)S(1)}, f32[256,256]{1,0:T(8,128)S(1)}, u32[]{:S(2)}, u32[]{:S(2)}) collective-permute-start(f32[256,256]{1,0:T(8,128)S(1)} %get-tuple-element.63), channel_id=1, source_target_pairs={{32,0},{64,32},{96,64},{128,96},{160,128},{192,160},{224,192},{256... | collective-permute-start | bytes 786440 | tf_op jit(solution)/shard_map/ppermute | solution.py:238

commit v11 on v10

--- a/solution.py
+++ b/solution.py
@@ -180,13 +180,14 @@
             bottom[:blk, :], bottom[blk:, :] = p2, p3
         else:
             top, mid, bottom = outs
-            top[...], bottom[...] = p0, p3
+            top[:blk, :], bottom[...] = p0, p3
+            top[blk:, :] = jnp.zeros((8, n), f32)
             mid[:blk, :], mid[blk:, :] = p1, p2
 
     if merged:
         outs = [((m, n), f32)] * 2 + [((n, n), bf16)] * 4
     else:
-        outs = [((blk, n), f32), ((m, n), f32), ((blk, n), f32)]
+        outs = [((blk + 8, n), f32), ((m, n), f32), ((blk, n), f32)]
     return call(body, ins, outs, 60 * blk * blk * n)
 
 
@@ -218,7 +219,7 @@
         step, h = sc[0], sc[1]
         lo, hi = slice(0, blk), slice(blk, 2 * blk)
         for s, r in ((lo, rup), (hi, rdown)):
-            o[s, :] = soft(x[s, :] - step * (mid[s, :] + r[...]), h)
+            o[s, :] = soft(x[s, :] - step * (mid[s, :] + r[:blk, :]), h)
 
     return call(body, (mid, rup, rdown, x, sc), [(x.shape, f32)], 1 << 20)[0]
 

time: 143 us -> 141 us (0.986)
  the two profiles are of different devices: /device:TPU:56 before, /device:TPU:38 now
where the time goes in v11:
time: 141 us; the launch traced here: 140 us
  starting transfers between devices  66.1 us (47%)
  waiting for transfers between devices  52.7 us (37%)
  Pallas kernels  14.4 us (10%)
  local copies, waits for them, and re-layouts  5.01 us (4%)
  between operations  1.62 us (1%)
    ppermute x4, starting transfers between devices, col_swap(): return lax.ppermute(b, 'col', pairs[1])  25.5 us
    ppermute x3, waiting for transfers between devices, row_swap(): from_up = lax.ppermute(to_down, 'row', downward)  17 us
    ppermute x3, starting transfers between devices, row_swap(): from_down = lax.ppermute(to_up, 'row', upward)  16.2 us
    pallas_call x10, Pallas kernels, call(): pl.pallas_call(body, out_shape=[jax.ShapeDtypeStruct(s, d) for s, d in ou...  14.4 us
    ppermute x4, waiting for transfers between devices, col_swap(): return lax.ppermute(b, 'col', pairs[1])  12.8 us
    ppermute x6, starting transfers between devices, chip_swap(): return lax.ppermute(a, 'col', pairs[0])  12.5 us
    ppermute x2, waiting for transfers between devices, columns(): relayed = lax.ppermute(vb, 'col', second_hop)  9.41 us
    ppermute x2, waiting for transfers between devices, columns(): vb = lax.ppermute(v, 'col', first_hop)  7.36 us
  transfers between devices with their start and end apart: 20, of which 10 were waited for; matrix products, arithmetic and copies ran while one was open for 0% of the time, Pallas kernels for 3%

profile of v11, /device:TPU:38, one launch (start us, length us, event | category | flops | bytes accessed | tf_op | source)
XLA Modules:
  0.0 139.9 jit_solution(9244043401885890670)
XLA Ops:
  1.1 2.6 %collective-permute-start = (f32[256,256]{1,0:T(8,128)S(1)}, f32[256,256]{1,0:T(8,128)S(1)}, u32[]{:S(2)}, u32[]{:S(2)}) collective-permute-start(f32[256,256]{1,0:T(8,128)S(1)} %get-tuple-element.66), channel_id=1, source_target_pairs={{0,32},{32,64},{64,96},{96,128},{128,160},{160,192},{192,224},{224... | collective-permute-start | bytes 786440 | tf_op jit(solution)/shard_map/ppermute | solution.py:238
  3.7 6.0 %collective-permute-start.1 = (f32[256,256]{1,0:T(8,128)S(1)}, f32[256,256]{1,0:T(8,128)S(1)}, u32[]{:S(2)}, u32[]{:S(2)}) collective-permute-start(f32[256,256]{1,0:T(8,128)S(1)} %get-tuple-element.65), channel_id=1, source_target_pairs={{32,0},{64,32},{96,64},{128,96},{160,128},{192,160},{224,192},{256... | collective-permute-start | bytes 786440 | tf_op jit(solution)/shard_map/ppermute | solution.py:239
  9.8 1.4 %copy-done.1 = f32[2,3,256,256]{3,2,1,0:T(8,128)S(1)} copy-done((f32[2,3,256,256]{3,2,1,0:T(8,128)S(1)}, f32[2,3,256,256]{3,2,1,0:T(8,128)}, u32[]{:S(2)}) %copy-start.1) | copy-done | bytes 1572888
  13.6 1.3 shard_map.82
  15.8 1.9 %collective-permute-start.2 = (f32[512,256]{1,0:T(8,128)S(1)}, f32[512,256]{1,0:T(8,128)S(1)}, u32[]{:S(2)}, u32[]{:S(2)}) collective-permute-start(f32[512,256]{1,0:T(8,128)S(1)} %shard_map.83.u), channel_id=1, source_target_pairs={{0,1},{2,3},{4,5},{6,7},{8,9},{10,11},{12,13},{14,15},{16,17},{18,... | collective-permute-start | bytes 1572872 | tf_op jit(solution)/shard_map/ppermute | solution.py:243
  17.7 11.4 %collective-permute-start.3 = (f32[512,256]{1,0:T(8,128)S(1)}, f32[512,256]{1,0:T(8,128)S(1)}, u32[]{:S(2)}, u32[]{:S(2)}) collective-permute-start(f32[512,256]{1,0:T(8,128)S(1)} %shard_map.83.u), channel_id=1, source_target_pairs={{1,2},{3,4},{5,6},{7,8},{9,10},{11,12},{13,14},{15,16},{17,18},{19... | collective-permute-start | bytes 1572872 | tf_op jit(solution)/shard_map/ppermute | solution.py:246
  29.8 1.3 collective-permute-start.7
  31.1 5.3 %collective-permute-done.7.vb = f32[392,256]{1,0:T(8,128)S(1)} collective-permute-done((f32[392,256]{1,0:T(8,128)S(1)}, f32[392,256]{1,0:T(8,128)S(1)}, u32[]{:S(2)}, u32[]{:S(2)}) %collective-permute-start.7) | collective-permute-done | bytes 401440 | tf_op jit(solution)/shard_map/ppermute | solution.py:260
  37.7 1.9 %collective-permute-start.6 = (f32[376,256]{1,0:T(8,128)S(1)}, f32[376,256]{1,0:T(8,128)S(1)}, u32[]{:S(2)}, u32[]{:S(2)}) collective-permute-start(f32[376,256]{1,0:T(8,128)S(1)} %get-tuple-element.40.w), channel_id=1, source_target_pairs={{1,2},{3,4},{5,6},{7,8},{9,10},{11,12},{13,14},{15,16},{17,18},{19... | collective-permute-start | bytes 1155080 | tf_op jit(solution)/shard_map/ppermute | solution.py:246
  40.8 1.9 %collective-permute-start.4 = (f32[256,256]{1,0:T(8,128)S(1)}, f32[256,256]{1,0:T(8,128)S(1)}, u32[]{:S(2)}, u32[]{:S(2)}) collective-permute-start(f32[256,256]{1,0:T(8,128)S(1)} %get-tuple-element.45), channel_id=1, source_target_pairs={{0,1},{2,3},{4,5},{6,7},{8,9},{10,11},{12,13},{14,15},{16,17},{18,... | collective-permute-start | bytes 786440 | tf_op jit(solution)/shard_map/ppermute | solution.py:243
  42.7 2.4 %collective-permute-start.5 = (f32[256,256]{1,0:T(8,128)S(1)}, f32[256,256]{1,0:T(8,128)S(1)}, u32[]{:S(2)}, u32[]{:S(2)}) collective-permute-start(f32[256,256]{1,0:T(8,128)S(1)} %get-tuple-element.46), channel_id=1, source_target_pairs={{0,1},{2,3},{4,5},{6,7},{8,9},{10,11},{12,13},{14,15},{16,17},{18,... | collective-permute-start | bytes 786440 | tf_op jit(solution)/shard_map/ppermute | solution.py:243
  46.3 10.7 %collective-permute-done.6.wb = f32[376,256]{1,0:T(8,128)S(1)} collective-permute-done((f32[376,256]{1,0:T(8,128)S(1)}, f32[376,256]{1,0:T(8,128)S(1)}, u32[]{:S(2)}, u32[]{:S(2)}) %collective-permute-start.6) | collective-permute-done | bytes 385056 | tf_op jit(solution)/shard_map/ppermute | solution.py:246
  57.0 3.0 %shard_map.86 = (f32[512,256]{1,0:T(8,128)S(1)}, f32[512,256]{1,0:T(8,128)S(1)}, bf16[256,256]{1,0:T(8,128)(2,1)S(1)}, bf16[256,256]{1,0:T(8,128)(2,1)S(1)}, bf1...) custom-call(f32[512,256]{1,0:T(8,128)S(1)} %get-tuple-element.44.q, f32[256,256]{1,0:T(8,128)S(1)} %collective-permute-done.4.ra, ...), custom_call_target="tpu_custom_call" | custom-call | flops 1006632960 | bytes 4333584 | tf_op jit(solution)/shard_map/pallas_call | solution.py:31
  60.0 6.7 %collective-permute-start.10 = (f32[512,256]{1,0:T(8,128)S(1)}, f32[512,256]{1,0:T(8,128)S(1)}, u32[]{:S(2)}, u32[]{:S(2)}) collective-permute-start(f32[512,256]{1,0:T(8,128)S(1)} %get-tuple-element.49.top), channel_id=1, source_target_pairs={{32,0},{64,32},{96,64},{128,96},{160,128},{192,160},{224,192},{256... | collective-permute-start | bytes 1572872 | tf_op jit(solution)/shard_map/ppermute | solution.py:239
  66.7 1.9 %collective-permute-start.9 = (f32[512,256]{1,0:T(8,128)S(1)}, f32[512,256]{1,0:T(8,128)S(1)}, u32[]{:S(2)}, u32[]{:S(2)}) collective-permute-start(f32[512,256]{1,0:T(8,128)S(1)} %get-tuple-element.50.bottom), channel_id=1, source_target_pairs={{0,32},{32,64},{64,96},{96,128},{128,160},{160,192},{192,224},{224... | collective-permute-start | bytes 1572872 | tf_op jit(solution)/shard_map/ppermute | solution.py:238
  70.0 3.9 %collective-permute-done.10.rbottom = f32[512,256]{1,0:T(8,128)S(1)} collective-permute-done((f32[512,256]{1,0:T(8,128)S(1)}, f32[512,256]{1,0:T(8,128)S(1)}, u32[]{:S(2)}, u32[]{:S(2)}) %collective-permute-start.10) | collective-permute-done | bytes 524320 | tf_op jit(solution)/shard_map/ppermute | solution.py:239
  73.9 8.3 %collective-permute-done.9.rtop = f32[512,256]{1,0:T(8,128)S(1)} collective-permute-done((f32[512,256]{1,0:T(8,128)S(1)}, f32[512,256]{1,0:T(8,128)S(1)}, u32[]{:S(2)}, u32[]{:S(2)}) %collective-permute-start.9) | collective-permute-done | bytes 524320 | tf_op jit(solution)/shard_map/ppermute | solution.py:238
  82.2 1.5 %shard_map.87 = (f32[512,256]{1,0:T(8,128)S(1)}, f32[512,256]{1,0:T(8,128)S(1)}) custom-call(f32[512,256]{1,0:T(8,128)S(1)} %get-tuple-element.49.top, f32[512,256]{1,0:T(8,128)S(1)} %get-tuple-element.50.bottom, f32[512,256]{1,0:T(8,128)S(1)} %collective-permute-done.9.rtop, f32[512,256]{1,0:T(8,128)S(1)} %collective-permute-done.10.rbottom, ...), custom_call_target="tpu_custom_call" | custom-call | flops 603979776 | bytes 4718600 | tf_op jit(solution)/shard_map/pallas_call | solution.py:31
  83.7 1.9 %collective-permute-start.11 = (f32[512,256]{1,0:T(8,128)S(1)}, f32[512,256]{1,0:T(8,128)S(1)}, u32[]{:S(2)}, u32[]{:S(2)}) collective-permute-start(f32[512,256]{1,0:T(8,128)S(1)} %get-tuple-element.51.u), channel_id=1, source_target_pairs={{0,1},{2,3},{4,5},{6,7},{8,9},{10,11},{12,13},{14,15},{16,17},{18,... | collective-permute-start | bytes 1572872 | tf_op jit(solution)/shard_map/ppermute | solution.py:243
  85.7 10.2 %collective-permute-start.12 = (f32[512,256]{1,0:T(8,128)S(1)}, f32[512,256]{1,0:T(8,128)S(1)}, u32[]{:S(2)}, u32[]{:S(2)}) collective-permute-start(f32[512,256]{1,0:T(8,128)S(1)} %get-tuple-element.51.u), channel_id=1, source_target_pairs={{1,2},{3,4},{5,6},{7,8},{9,10},{11,12},{13,14},{15,16},{17,18},{19... | collective-permute-start | bytes 1572872 | tf_op jit(solution)/shard_map/ppermute | solution.py:246
  96.5 1.3 collective-permute-start.16
  97.8 1.9 %collective-permute-start.15 = (f32[264,256]{1,0:T(8,128)S(1)}, f32[264,256]{1,0:T(8,128)S(1)}, u32[]{:S(2)}, u32[]{:S(2)}) collective-permute-start(f32[264,256]{1,0:T(8,128)S(1)} %get-tuple-element.52.w), channel_id=1, source_target_pairs={{1,2},{3,4},{5,6},{7,8},{9,10},{11,12},{13,14},{15,16},{17,18},{19... | collective-permute-start | bytes 811016 | tf_op jit(solution)/shard_map/ppermute | solution.py:246
  99.7 2.0 %collective-permute-done.16.vb = f32[264,256]{1,0:T(8,128)S(1)} collective-permute-done((f32[264,256]{1,0:T(8,128)S(1)}, f32[264,256]{1,0:T(8,128)S(1)}, u32[]{:S(2)}, u32[]{:S(2)}) %collective-permute-start.16) | collective-permute-done | bytes 270368 | tf_op jit(solution)/shard_map/ppermute | solution.py:260
  104.2 1.9 %collective-permute-start.13 = (f32[256,256]{1,0:T(8,128)S(1)}, f32[256,256]{1,0:T(8,128)S(1)}, u32[]{:S(2)}, u32[]{:S(2)}) collective-permute-start(f32[256,256]{1,0:T(8,128)S(1)} %get-tuple-element.55), channel_id=1, source_target_pairs={{0,1},{2,3},{4,5},{6,7},{8,9},{10,11},{12,13},{14,15},{16,17},{18,... | collective-permute-start | bytes 786440 | tf_op jit(solution)/shard_map/ppermute | solution.py:243
  106.1 2.4 %collective-permute-start.14 = (f32[256,256]{1,0:T(8,128)S(1)}, f32[256,256]{1,0:T(8,128)S(1)}, u32[]{:S(2)}, u32[]{:S(2)}) collective-permute-start(f32[256,256]{1,0:T(8,128)S(1)} %get-tuple-element.56), channel_id=1, source_target_pairs={{0,1},{2,3},{4,5},{6,7},{8,9},{10,11},{12,13},{14,15},{16,17},{18,... | collective-permute-start | bytes 786440 | tf_op jit(solution)/shard_map/ppermute | solution.py:243
  109.6 2.0 %collective-permute-done.15.wb = f32[264,256]{1,0:T(8,128)S(1)} collective-permute-done((f32[264,256]{1,0:T(8,128)S(1)}, f32[264,256]{1,0:T(8,128)S(1)}, u32[]{:S(2)}, u32[]{:S(2)}) %collective-permute-start.15) | collective-permute-done | bytes 270368 | tf_op jit(solution)/shard_map/ppermute | solution.py:246
  111.7 9.4 %collective-permute-done.17.relayed = f32[264,256]{1,0:T(8,128)S(1)} collective-permute-done((f32[264,256]{1,0:T(8,128)S(1)}, f32[264,256]{1,0:T(8,128)S(1)}, u32[]{:S(2)}, u32[]{:S(2)}) %collective-permute-start.17) | collective-permute-done | bytes 270368 | tf_op jit(solution)/shard_map/ppermute | solution.py:262
  121.1 2.9 %shard_map.90 = (f32[264,256]{1,0:T(8,128)S(1)}, f32[512,256]{1,0:T(8,128)S(1)}, f32[256,256]{1,0:T(8,128)S(1)}) custom-call(f32[512,256]{1,0:T(8,128)S(1)} %get-tuple-element.54.q, f32[256,256]{1,0:T(8,128)S(1)} %collective-permute-done.13.ra, f32[256,256]{1,0:T(8,128)S(1)} %collective-permute-done.14.ra2, f32[264,256]{1,0:T(8,128)S(1)} %collective-permute-done.15.wb, ...), custom_call_target="tpu_custom_call" | custom-call | flops 1006632960 | bytes 4481040 | tf_op jit(solution)/shard_map/pallas_call | solution.py:31
  124.0 3.5 %collective-permute-start.19 = (f32[264,256]{1,0:T(8,128)S(1)}, f32[264,256]{1,0:T(8,128)S(1)}, u32[]{:S(2)}, u32[]{:S(2)}) collective-permute-start(f32[264,256]{1,0:T(8,128)S(1)} %get-tuple-element.63), channel_id=1, source_target_pairs={{32,0},{64,32},{96,64},{128,96},{160,128},{192,160},{224,192},{256... | collective-permute-start | bytes 811016 | tf_op jit(solution)/shard_map/ppermute | solution.py:239
  127.5 2.3 %collective-permute-start.18 = (f32[256,256]{1,0:T(8,128)S(1)}, f32[256,256]{1,0:T(8,128)S(1)}, u32[]{:S(2)}, u32[]{:S(2)}) collective-permute-start(f32[256,256]{1,0:T(8,128)S(1)} %get-tuple-element.62), channel_id=1, source_target_pairs={{0,32},{32,64},{64,96},{96,128},{128,160},{160,192},{192,224},{224... | collective-permute-start | bytes 786440 | tf_op jit(solution)/shard_map/ppermute | solution.py:238
  129.8 8.6 %collective-permute-done.18.rup = f32[256,256]{1,0:T(8,128)S(1)} collective-permute-done((f32[256,256]{1,0:T(8,128)S(1)}, f32[256,256]{1,0:T(8,128)S(1)}, u32[]{:S(2)}, u32[]{:S(2)}) %collective-permute-start.18) | collective-permute-done | bytes 262176 | tf_op jit(solution)/shard_map/ppermute | solution.py:238
  138.5 1.4 %shard_map.91 = f32[512,256]{1,0:T(8,128)} custom-call(f32[512,256]{1,0:T(8,128)S(1)} %get-tuple-element.61.mid, f32[256,256]{1,0:T(8,128)S(1)} %collective-permute-done.18.rup, f32[264,256]{1,0:T(8,128)S(1)} %collective-permute-done.19.rdown, f32[512,256]{1,0:T(8,128)S(1)} %get-tuple-element.64.x, f32[2]{0:T(128)S(1)} %pad_maximum_fusion.sc), custom_call_target="tpu_custom_call" | custom-call | flops 1048576 | bytes 1581064 | tf_op jit(solution)/shard_map/pallas_call | solution.py:31
  (34 shorter events, 12.8 us)
Async XLA Ops:
  0.0 15.0 %copy-start = (f32[512,256]{1,0:T(8,128)S(1)}, f32[512,256]{1,0:T(8,128)}, u32[]{:S(2)}) copy-start(f32[512,256]{1,0:T(8,128)} %x.3) | copy-start | bytes 1572868
  1.1 13.8 %collective-permute-start = (f32[256,256]{1,0:T(8,128)S(1)}, f32[256,256]{1,0:T(8,128)S(1)}, u32[]{:S(2)}, u32[]{:S(2)}) collective-permute-start(f32[256,256]{1,0:T(8,128)S(1)} %get-tuple-element.66), channel_id=1, source_target_pairs={{0,32},{32,64},{64,96},{96,128},{128,160},{160,192},{192,224},{224... | collective-permute-start | bytes 786440 | tf_op jit(solution)/shard_map/ppermute | solution.py:238
  3.7 11.2 %collective-permute-start.1 = (f32[256,256]{1,0:T(8,128)S(1)}, f32[256,256]{1,0:T(8,128)S(1)}, u32[]{:S(2)}, u32[]{:S(2)}) collective-permute-start(f32[256,256]{1,0:T(8,128)S(1)} %get-tuple-element.65), channel_id=1, source_target_pairs={{32,0},{64,32},{96,64},{128,96},{160,128},{192,160},{224,192},{256... | collective-permute-start | bytes 786440 | tf_op jit(solution)/shard_map/ppermute | solution.py:239
  9.8 1.4 %copy-start.1 = (f32[2,3,256,256]{3,2,1,0:T(8,128)S(1)}, f32[2,3,256,256]{3,2,1,0:T(8,128)}, u32[]{:S(2)}) copy-start(f32[2,3,256,256]{3,2,1,0:T(8,128)} %fx.1) | copy-start | bytes 4718596
  11.2 1.1 copy-start.2
  12.3 0.7 copy-start.3
  13.0 0.7 copy-start.4
  15.0 14.2 %copy-start.5 = (f32[512,256]{1,0:T(8,128)S(1)}, f32[512,256]{1,0:T(8,128)}, u32[]{:S(2)}) copy-start(f32[512,256]{1,0:T(8,128)} %obs.3) | copy-start | bytes 1572868
  15.8 13.4 %collective-permute-start.2 = (f32[512,256]{1,0:T(8,128)S(1)}, f32[512,256]{1,0:T(8,128)S(1)}, u32[]{:S(2)}, u32[]{:S(2)}) collective-permute-start(f32[512,256]{1,0:T(8,128)S(1)} %shard_map.83.u), channel_id=1, source_target_pairs={{0,1},{2,3},{4,5},{6,7},{8,9},{10,11},{12,13},{14,15},{16,17},{18,... | collective-permute-start | bytes 1572872 | tf_op jit(solution)/shard_map/ppermute | solution.py:243
  17.7 21.9 %collective-permute-start.3 = (f32[512,256]{1,0:T(8,128)S(1)}, f32[512,256]{1,0:T(8,128)S(1)}, u32[]{:S(2)}, u32[]{:S(2)}) collective-permute-start(f32[512,256]{1,0:T(8,128)S(1)} %shard_map.83.u), channel_id=1, source_target_pairs={{1,2},{3,4},{5,6},{7,8},{9,10},{11,12},{13,14},{15,16},{17,18},{19... | collective-permute-start | bytes 1572872 | tf_op jit(solution)/shard_map/ppermute | solution.py:246
  29.8 6.7 %collective-permute-start.7 = (f32[392,256]{1,0:T(8,128)S(1)}, f32[392,256]{1,0:T(8,128)S(1)}, u32[]{:S(2)}, u32[]{:S(2)}) collective-permute-start(f32[392,256]{1,0:T(8,128)S(1)} %get-tuple-element.41.v), channel_id=1, source_target_pairs={{1,2},{3,4},{5,6},{7,8},{9,10},{11,12},{13,14},{17,18},{19,20},{21... | collective-permute-start | bytes 1204232 | tf_op jit(solution)/shard_map/ppermute | solution.py:260
  36.4 20.6 %collective-permute-start.8 = (f32[392,256]{1,0:T(8,128)S(1)}, f32[392,256]{1,0:T(8,128)S(1)}, u32[]{:S(2)}, u32[]{:S(2)}) collective-permute-start(f32[392,256]{1,0:T(8,128)S(1)} %collective-permute-done.7.vb), channel_id=1, source_target_pairs={{0,16},{31,15},{32,48},{63,47},{64,80},{95,79},{96,112},{127,111},... | collective-permute-start | bytes 1204232 | tf_op jit(solution)/shard_map/ppermute | solution.py:262
  37.7 19.3 %collective-permute-start.6 = (f32[376,256]{1,0:T(8,128)S(1)}, f32[376,256]{1,0:T(8,128)S(1)}, u32[]{:S(2)}, u32[]{:S(2)}) collective-permute-start(f32[376,256]{1,0:T(8,128)S(1)} %get-tuple-element.40.w), channel_id=1, source_target_pairs={{1,2},{3,4},{5,6},{7,8},{9,10},{11,12},{13,14},{15,16},{17,18},{19... | collective-permute-start | bytes 1155080 | tf_op jit(solution)/shard_map/ppermute | solution.py:246
  40.8 4.3 %collective-permute-start.4 = (f32[256,256]{1,0:T(8,128)S(1)}, f32[256,256]{1,0:T(8,128)S(1)}, u32[]{:S(2)}, u32[]{:S(2)}) collective-permute-start(f32[256,256]{1,0:T(8,128)S(1)} %get-tuple-element.45), channel_id=1, source_target_pairs={{0,1},{2,3},{4,5},{6,7},{8,9},{10,11},{12,13},{14,15},{16,17},{18,... | collective-permute-start | bytes 786440 | tf_op jit(solution)/shard_map/ppermute | solution.py:243
  42.7 3.6 %collective-permute-start.5 = (f32[256,256]{1,0:T(8,128)S(1)}, f32[256,256]{1,0:T(8,128)S(1)}, u32[]{:S(2)}, u32[]{:S(2)}) collective-permute-start(f32[256,256]{1,0:T(8,128)S(1)} %get-tuple-element.46), channel_id=1, source_target_pairs={{0,1},{2,3},{4,5},{6,7},{8,9},{10,11},{12,13},{14,15},{16,17},{18,... | collective-permute-start | bytes 786440 | tf_op jit(solution)/shard_map/ppermute | solution.py:243
  60.0 13.9 %collective-permute-start.10 = (f32[512,256]{1,0:T(8,128)S(1)}, f32[512,256]{1,0:T(8,128)S(1)}, u32[]{:S(2)}, u32[]{:S(2)}) collective-permute-start(f32[512,256]{1,0:T(8,128)S(1)} %get-tuple-element.49.top), channel_id=1, source_target_pairs={{32,0},{64,32},{96,64},{128,96},{160,128},{192,160},{224,192},{256... | collective-permute-start | bytes 1572872 | tf_op jit(solution)/shard_map/ppermute | solution.py:239
  66.7 15.5 %collective-permute-start.9 = (f32[512,256]{1,0:T(8,128)S(1)}, f32[512,256]{1,0:T(8,128)S(1)}, u32[]{:S(2)}, u32[]{:S(2)}) collective-permute-start(f32[512,256]{1,0:T(8,128)S(1)} %get-tuple-element.50.bottom), channel_id=1, source_target_pairs={{0,32},{32,64},{64,96},{96,128},{128,160},{160,192},{192,224},{224... | collective-permute-start | bytes 1572872 | tf_op jit(solution)/shard_map/ppermute | solution.py:238
  83.7 12.1 %collective-permute-start.11 = (f32[512,256]{1,0:T(8,128)S(1)}, f32[512,256]{1,0:T(8,128)S(1)}, u32[]{:S(2)}, u32[]{:S(2)}) collective-permute-start(f32[512,256]{1,0:T(8,128)S(1)} %get-tuple-element.51.u), channel_id=1, source_target_pairs={{0,1},{2,3},{4,5},{6,7},{8,9},{10,11},{12,13},{14,15},{16,17},{18,... | collective-permute-start | bytes 1572872 | tf_op jit(solution)/shard_map/ppermute | solution.py:243
  85.7 17.3 %collective-permute-start.12 = (f32[512,256]{1,0:T(8,128)S(1)}, f32[512,256]{1,0:T(8,128)S(1)}, u32[]{:S(2)}, u32[]{:S(2)}) collective-permute-start(f32[512,256]{1,0:T(8,128)S(1)} %get-tuple-element.51.u), channel_id=1, source_target_pairs={{1,2},{3,4},{5,6},{7,8},{9,10},{11,12},{13,14},{15,16},{17,18},{19... | collective-permute-start | bytes 1572872 | tf_op jit(solution)/shard_map/ppermute | solution.py:246
  96.5 5.3 %collective-permute-start.16 = (f32[264,256]{1,0:T(8,128)S(1)}, f32[264,256]{1,0:T(8,128)S(1)}, u32[]{:S(2)}, u32[]{:S(2)}) collective-permute-start(f32[264,256]{1,0:T(8,128)S(1)} %get-tuple-element.53.v), channel_id=1, source_target_pairs={{1,2},{3,4},{5,6},{7,8},{9,10},{11,12},{13,14},{17,18},{19,20},{21... | collective-permute-start | bytes 811016 | tf_op jit(solution)/shard_map/ppermute | solution.py:260
  97.8 13.9 %collective-permute-start.15 = (f32[264,256]{1,0:T(8,128)S(1)}, f32[264,256]{1,0:T(8,128)S(1)}, u32[]{:S(2)}, u32[]{:S(2)}) collective-permute-start(f32[264,256]{1,0:T(8,128)S(1)} %get-tuple-element.52.w), channel_id=1, source_target_pairs={{1,2},{3,4},{5,6},{7,8},{9,10},{11,12},{13,14},{15,16},{17,18},{19... | collective-permute-start | bytes 811016 | tf_op jit(solution)/shard_map/ppermute | solution.py:246
  101.7 19.4 %collective-permute-start.17 = (f32[264,256]{1,0:T(8,128)S(1)}, f32[264,256]{1,0:T(8,128)S(1)}, u32[]{:S(2)}, u32[]{:S(2)}) collective-permute-start(f32[264,256]{1,0:T(8,128)S(1)} %collective-permute-done.16.vb), channel_id=1, source_target_pairs={{0,16},{31,15},{32,48},{63,47},{64,80},{95,79},{96,112},{127,111},... | collective-permute-start | bytes 811016 | tf_op jit(solution)/shard_map/ppermute | solution.py:262
  104.2 4.3 %collective-permute-start.13 = (f32[256,256]{1,0:T(8,128)S(1)}, f32[256,256]{1,0:T(8,128)S(1)}, u32[]{:S(2)}, u32[]{:S(2)}) collective-permute-start(f32[256,256]{1,0:T(8,128)S(1)} %get-tuple-element.55), channel_id=1, source_target_pairs={{0,1},{2,3},{4,5},{6,7},{8,9},{10,11},{12,13},{14,15},{16,17},{18,... | collective-permute-start | bytes 786440 | tf_op jit(solution)/shard_map/ppermute | solution.py:243
  106.1 3.6 %collective-permute-start.14 = (f32[256,256]{1,0:T(8,128)S(1)}, f32[256,256]{1,0:T(8,128)S(1)}, u32[]{:S(2)}, u32[]{:S(2)}) collective-permute-start(f32[256,256]{1,0:T(8,128)S(1)} %get-tuple-element.56), channel_id=1, source_target_pairs={{0,1},{2,3},{4,5},{6,7},{8,9},{10,11},{12,13},{14,15},{16,17},{18,... | collective-permute-start | bytes 786440 | tf_op jit(solution)/shard_map/ppermute | solution.py:243
  124.0 14.5 %collective-permute-start.19 = (f32[264,256]{1,0:T(8,128)S(1)}, f32[264,256]{1,0:T(8,128)S(1)}, u32[]{:S(2)}, u32[]{:S(2)}) collective-permute-start(f32[264,256]{1,0:T(8,128)S(1)} %get-tuple-element.63), channel_id=1, source_target_pairs={{32,0},{64,32},{96,64},{128,96},{160,128},{192,160},{224,192},{256... | collective-permute-start | bytes 811016 | tf_op jit(solution)/shard_map/ppermute | solution.py:239
  127.5 11.0 %collective-permute-start.18 = (f32[256,256]{1,0:T(8,128)S(1)}, f32[256,256]{1,0:T(8,128)S(1)}, u32[]{:S(2)}, u32[]{:S(2)}) collective-permute-start(f32[256,256]{1,0:T(8,128)S(1)} %get-tuple-element.62), channel_id=1, source_target_pairs={{0,32},{32,64},{64,96},{96,128},{128,160},{160,192},{192,224},{224... | collective-permute-start | bytes 786440 | tf_op jit(solution)/shard_map/ppermute | solution.py:238

commit v12 on v11

--- a/solution.py
+++ b/solution.py
@@ -87,7 +87,7 @@
     blk, n = up.shape
 
     def body(x, up, down, axh, axl, u, xh, xl):
-        for t, v in enumerate((up[...], x[:blk, :], x[blk:, :], down[...])):
+        for t, v in enumerate((up[...], x[:blk, :], x[blk:, :], down[:blk, :])):
             s = slice(t * blk, (t + 1) * blk)
             xh[s, :], xl[s, :] = split(v)
         left((axh, axl), (xh, xl), u)
@@ -198,7 +198,7 @@
         step, h = sc[0], sc[1]
         lo, hi = slice(0, blk), slice(blk, 2 * blk)
         parts = ((up[...], top, rtop, lo), (x[lo, :], top, rtop, hi))
-        parts += ((x[hi, :], bottom, rbottom, lo), (down[...], bottom, rbottom, hi))
+        parts += ((x[hi, :], bottom, rbottom, lo), (down[:blk, :], bottom, rbottom, hi))
         for t, (v, a, b, s) in enumerate(parts):
             new = soft(v - step * (a[s, :] + b[s, :]), h)
             if t in (1, 2):
@@ -266,7 +266,7 @@
 
     pos = jnp.stack([lax.axis_index("row"), rows, lax.axis_index("col"), cols]).astype(jnp.int32)
     sc = jnp.concatenate([step_size, threshold])
-    up, down = row_swap(x[:blk], x[blk:])
+    up, down = row_swap(x[: blk + 8], x[blk:])
     ax, atx, byf, byt, fb = prepare(fx, bx, fy, by, pos)
     u = apply_left(x, up, down, ax)
     top, bottom, *fb = columns(u, fb, True)

time: 141 us -> 141 us (level)
  starting transfers between devices: 66.1 us -> 62.4 us
  waiting for transfers between devices: 52.7 us -> 56.2 us
    ppermute x3, starting transfers between devices: 16.2 us -> 9.38 us  [row_swap(): from_down = lax.ppermute(to_up, 'row', upward)]
    ppermute x3, waiting for transfers between devices: 17 us -> 20.9 us  [row_swap(): from_up = lax.ppermute(to_down, 'row', downward)]
    ppermute x4, starting transfers between devices: 25.5 us -> 27.1 us  [col_swap(): return lax.ppermute(b, 'col', pairs[1])]
    ppermute x3, starting transfers between devices: 6.83 us -> 8.28 us  [row_swap(): from_up = lax.ppermute(to_down, 'row', downward)]
  transfers between devices with their start and end apart: 20 -> 20, of which waited for: 10 -> 11; matrix products, arithmetic and copies ran while one was open for 0% -> 1% of each run, Pallas kernels for 3% -> 3%
where the time goes in v12:
time: 141 us
  starting transfers between devices  62.4 us (44%)
  waiting for transfers between devices  56.2 us (40%)
  Pallas kernels  14.4 us (10%)
  local copies, waits for them, and re-layouts  5.83 us (4%)
  between operations  1.61 us (1%)
    ppermute x4, starting transfers between devices, col_swap(): return lax.ppermute(b, 'col', pairs[1])  27.1 us
    ppermute x3, waiting for transfers between devices, row_swap(): from_up = lax.ppermute(to_down, 'row', downward)  20.9 us
    pallas_call x10, Pallas kernels, call(): pl.pallas_call(body, out_shape=[jax.ShapeDtypeStruct(s, d) for s, d in ou...  14.4 us
    ppermute x6, starting transfers between devices, chip_swap(): return lax.ppermute(a, 'col', pairs[0])  12.5 us
    ppermute x4, waiting for transfers between devices, col_swap(): return lax.ppermute(b, 'col', pairs[1])  11.8 us
    ppermute x3, starting transfers between devices, row_swap(): from_down = lax.ppermute(to_up, 'row', upward)  9.38 us
    ppermute x2, waiting for transfers between devices, columns(): relayed = lax.ppermute(vb, 'col', second_hop)  9.3 us
    ppermute x3, starting transfers between devices, row_swap(): from_up = lax.ppermute(to_down, 'row', downward)  8.28 us
  transfers between devices with their start and end apart: 20, of which 11 were waited for; matrix products, arithmetic and copies ran while one was open for 1% of the time, Pallas kernels for 3%

profile of v12, /device:TPU:38, one launch (start us, length us, event | category | flops | bytes accessed | tf_op | source)
XLA Modules:
  0.0 140.6 jit_solution(14316261285713558944)
XLA Ops:
  1.0 3.2 %collective-permute-start.1 = (f32[264,256]{1,0:T(8,128)S(1)}, f32[264,256]{1,0:T(8,128)S(1)}, u32[]{:S(2)}, u32[]{:S(2)}) collective-permute-start(f32[264,256]{1,0:T(8,128)S(1)} %slice.7), channel_id=1, source_target_pairs={{32,0},{64,32},{96,64},{128,96},{160,128},{192,160},{224,192},{256... | collective-permute-start | bytes 811016 | tf_op jit(solution)/shard_map/ppermute | solution.py:239
  5.2 2.8 %collective-permute-start = (f32[256,256]{1,0:T(8,128)S(1)}, f32[256,256]{1,0:T(8,128)S(1)}, u32[]{:S(2)}, u32[]{:S(2)}) collective-permute-start(f32[256,256]{1,0:T(8,128)S(1)} %slice.6), channel_id=1, source_target_pairs={{0,32},{32,64},{64,96},{96,128},{128,160},{160,192},{192,224},{224... | collective-permute-start | bytes 786440 | tf_op jit(solution)/shard_map/ppermute | solution.py:238
  8.0 1.4 %copy-done.1 = f32[2,3,256,256]{3,2,1,0:T(8,128)S(1)} copy-done((f32[2,3,256,256]{3,2,1,0:T(8,128)S(1)}, f32[2,3,256,256]{3,2,1,0:T(8,128)}, u32[]{:S(2)}) %copy-start.1) | copy-done | bytes 1572888
  13.2 4.3 %collective-permute-done.up = f32[256,256]{1,0:T(8,128)S(1)} collective-permute-done((f32[256,256]{1,0:T(8,128)S(1)}, f32[256,256]{1,0:T(8,128)S(1)}, u32[]{:S(2)}, u32[]{:S(2)}) %collective-permute-start) | collective-permute-done | bytes 262176 | tf_op jit(solution)/shard_map/ppermute | solution.py:238
  18.4 1.9 %collective-permute-start.2 = (f32[512,256]{1,0:T(8,128)S(1)}, f32[512,256]{1,0:T(8,128)S(1)}, u32[]{:S(2)}, u32[]{:S(2)}) collective-permute-start(f32[512,256]{1,0:T(8,128)S(1)} %shard_map.83.u), channel_id=1, source_target_pairs={{0,1},{2,3},{4,5},{6,7},{8,9},{10,11},{12,13},{14,15},{16,17},{18,... | collective-permute-start | bytes 1572872 | tf_op jit(solution)/shard_map/ppermute | solution.py:243
  20.3 13.3 %collective-permute-start.3 = (f32[512,256]{1,0:T(8,128)S(1)}, f32[512,256]{1,0:T(8,128)S(1)}, u32[]{:S(2)}, u32[]{:S(2)}) collective-permute-start(f32[512,256]{1,0:T(8,128)S(1)} %shard_map.83.u), channel_id=1, source_target_pairs={{1,2},{3,4},{5,6},{7,8},{9,10},{11,12},{13,14},{15,16},{17,18},{19... | collective-permute-start | bytes 1572872 | tf_op jit(solution)/shard_map/ppermute | solution.py:246
  34.2 1.3 collective-permute-start.7
  35.5 5.3 %collective-permute-done.7.vb = f32[392,256]{1,0:T(8,128)S(1)} collective-permute-done((f32[392,256]{1,0:T(8,128)S(1)}, f32[392,256]{1,0:T(8,128)S(1)}, u32[]{:S(2)}, u32[]{:S(2)}) %collective-permute-start.7) | collective-permute-done | bytes 401440 | tf_op jit(solution)/shard_map/ppermute | solution.py:260
  42.2 1.9 %collective-permute-start.6 = (f32[376,256]{1,0:T(8,128)S(1)}, f32[376,256]{1,0:T(8,128)S(1)}, u32[]{:S(2)}, u32[]{:S(2)}) collective-permute-start(f32[376,256]{1,0:T(8,128)S(1)} %get-tuple-element.40.w), channel_id=1, source_target_pairs={{1,2},{3,4},{5,6},{7,8},{9,10},{11,12},{13,14},{15,16},{17,18},{19... | collective-permute-start | bytes 1155080 | tf_op jit(solution)/shard_map/ppermute | solution.py:246
  45.2 1.9 %collective-permute-start.4 = (f32[256,256]{1,0:T(8,128)S(1)}, f32[256,256]{1,0:T(8,128)S(1)}, u32[]{:S(2)}, u32[]{:S(2)}) collective-permute-start(f32[256,256]{1,0:T(8,128)S(1)} %get-tuple-element.45), channel_id=1, source_target_pairs={{0,1},{2,3},{4,5},{6,7},{8,9},{10,11},{12,13},{14,15},{16,17},{18,... | collective-permute-start | bytes 786440 | tf_op jit(solution)/shard_map/ppermute | solution.py:243
  47.2 2.4 %collective-permute-start.5 = (f32[256,256]{1,0:T(8,128)S(1)}, f32[256,256]{1,0:T(8,128)S(1)}, u32[]{:S(2)}, u32[]{:S(2)}) collective-permute-start(f32[256,256]{1,0:T(8,128)S(1)} %get-tuple-element.46), channel_id=1, source_target_pairs={{0,1},{2,3},{4,5},{6,7},{8,9},{10,11},{12,13},{14,15},{16,17},{18,... | collective-permute-start | bytes 786440 | tf_op jit(solution)/shard_map/ppermute | solution.py:243
  50.7 9.7 %collective-permute-done.6.wb = f32[376,256]{1,0:T(8,128)S(1)} collective-permute-done((f32[376,256]{1,0:T(8,128)S(1)}, f32[376,256]{1,0:T(8,128)S(1)}, u32[]{:S(2)}, u32[]{:S(2)}) %collective-permute-start.6) | collective-permute-done | bytes 385056 | tf_op jit(solution)/shard_map/ppermute | solution.py:246
  60.5 3.0 %shard_map.86 = (f32[512,256]{1,0:T(8,128)S(1)}, f32[512,256]{1,0:T(8,128)S(1)}, bf16[256,256]{1,0:T(8,128)(2,1)S(1)}, bf16[256,256]{1,0:T(8,128)(2,1)S(1)}, bf1...) custom-call(f32[512,256]{1,0:T(8,128)S(1)} %get-tuple-element.44.q, f32[256,256]{1,0:T(8,128)S(1)} %collective-permute-done.4.ra, ...), custom_call_target="tpu_custom_call" | custom-call | flops 1006632960 | bytes 4333584 | tf_op jit(solution)/shard_map/pallas_call | solution.py:31
  63.5 3.4 %collective-permute-start.10 = (f32[512,256]{1,0:T(8,128)S(1)}, f32[512,256]{1,0:T(8,128)S(1)}, u32[]{:S(2)}, u32[]{:S(2)}) collective-permute-start(f32[512,256]{1,0:T(8,128)S(1)} %get-tuple-element.49.top), channel_id=1, source_target_pairs={{32,0},{64,32},{96,64},{128,96},{160,128},{192,160},{224,192},{256... | collective-permute-start | bytes 1572872 | tf_op jit(solution)/shard_map/ppermute | solution.py:239
  66.9 2.5 %collective-permute-start.9 = (f32[512,256]{1,0:T(8,128)S(1)}, f32[512,256]{1,0:T(8,128)S(1)}, u32[]{:S(2)}, u32[]{:S(2)}) collective-permute-start(f32[512,256]{1,0:T(8,128)S(1)} %get-tuple-element.50.bottom), channel_id=1, source_target_pairs={{0,32},{32,64},{64,96},{96,128},{128,160},{160,192},{192,224},{224... | collective-permute-start | bytes 1572872 | tf_op jit(solution)/shard_map/ppermute | solution.py:238
  70.7 4.6 %collective-permute-done.10.rbottom = f32[512,256]{1,0:T(8,128)S(1)} collective-permute-done((f32[512,256]{1,0:T(8,128)S(1)}, f32[512,256]{1,0:T(8,128)S(1)}, u32[]{:S(2)}, u32[]{:S(2)}) %collective-permute-start.10) | collective-permute-done | bytes 524320 | tf_op jit(solution)/shard_map/ppermute | solution.py:239
  75.3 8.6 %collective-permute-done.9.rtop = f32[512,256]{1,0:T(8,128)S(1)} collective-permute-done((f32[512,256]{1,0:T(8,128)S(1)}, f32[512,256]{1,0:T(8,128)S(1)}, u32[]{:S(2)}, u32[]{:S(2)}) %collective-permute-start.9) | collective-permute-done | bytes 524320 | tf_op jit(solution)/shard_map/ppermute | solution.py:238
  83.9 1.5 %shard_map.87 = (f32[512,256]{1,0:T(8,128)S(1)}, f32[512,256]{1,0:T(8,128)S(1)}) custom-call(f32[512,256]{1,0:T(8,128)S(1)} %get-tuple-element.49.top, f32[512,256]{1,0:T(8,128)S(1)} %get-tuple-element.50.bottom, f32[512,256]{1,0:T(8,128)S(1)} %collective-permute-done.9.rtop, f32[512,256]{1,0:T(8,128)S(1)} %collective-permute-done.10.rbottom, ...), custom_call_target="tpu_custom_call" | custom-call | flops 603979776 | bytes 4726792 | tf_op jit(solution)/shard_map/pallas_call | solution.py:31
  85.4 1.9 %collective-permute-start.11 = (f32[512,256]{1,0:T(8,128)S(1)}, f32[512,256]{1,0:T(8,128)S(1)}, u32[]{:S(2)}, u32[]{:S(2)}) collective-permute-start(f32[512,256]{1,0:T(8,128)S(1)} %get-tuple-element.51.u), channel_id=1, source_target_pairs={{0,1},{2,3},{4,5},{6,7},{8,9},{10,11},{12,13},{14,15},{16,17},{18,... | collective-permute-start | bytes 1572872 | tf_op jit(solution)/shard_map/ppermute | solution.py:243
  87.3 9.9 %collective-permute-start.12 = (f32[512,256]{1,0:T(8,128)S(1)}, f32[512,256]{1,0:T(8,128)S(1)}, u32[]{:S(2)}, u32[]{:S(2)}) collective-permute-start(f32[512,256]{1,0:T(8,128)S(1)} %get-tuple-element.51.u), channel_id=1, source_target_pairs={{1,2},{3,4},{5,6},{7,8},{9,10},{11,12},{13,14},{15,16},{17,18},{19... | collective-permute-start | bytes 1572872 | tf_op jit(solution)/shard_map/ppermute | solution.py:246
  97.9 1.3 collective-permute-start.16
  99.2 1.9 %collective-permute-start.15 = (f32[264,256]{1,0:T(8,128)S(1)}, f32[264,256]{1,0:T(8,128)S(1)}, u32[]{:S(2)}, u32[]{:S(2)}) collective-permute-start(f32[264,256]{1,0:T(8,128)S(1)} %get-tuple-element.52.w), channel_id=1, source_target_pairs={{1,2},{3,4},{5,6},{7,8},{9,10},{11,12},{13,14},{15,16},{17,18},{19... | collective-permute-start | bytes 811016 | tf_op jit(solution)/shard_map/ppermute | solution.py:246
  101.1 2.0 %collective-permute-done.16.vb = f32[264,256]{1,0:T(8,128)S(1)} collective-permute-done((f32[264,256]{1,0:T(8,128)S(1)}, f32[264,256]{1,0:T(8,128)S(1)}, u32[]{:S(2)}, u32[]{:S(2)}) %collective-permute-start.16) | collective-permute-done | bytes 270368 | tf_op jit(solution)/shard_map/ppermute | solution.py:260
  105.6 1.9 %collective-permute-start.13 = (f32[256,256]{1,0:T(8,128)S(1)}, f32[256,256]{1,0:T(8,128)S(1)}, u32[]{:S(2)}, u32[]{:S(2)}) collective-permute-start(f32[256,256]{1,0:T(8,128)S(1)} %get-tuple-element.55), channel_id=1, source_target_pairs={{0,1},{2,3},{4,5},{6,7},{8,9},{10,11},{12,13},{14,15},{16,17},{18,... | collective-permute-start | bytes 786440 | tf_op jit(solution)/shard_map/ppermute | solution.py:243
  107.5 2.4 %collective-permute-start.14 = (f32[256,256]{1,0:T(8,128)S(1)}, f32[256,256]{1,0:T(8,128)S(1)}, u32[]{:S(2)}, u32[]{:S(2)}) collective-permute-start(f32[256,256]{1,0:T(8,128)S(1)} %get-tuple-element.56), channel_id=1, source_target_pairs={{0,1},{2,3},{4,5},{6,7},{8,9},{10,11},{12,13},{14,15},{16,17},{18,... | collective-permute-start | bytes 786440 | tf_op jit(solution)/shard_map/ppermute | solution.py:243
  111.1 2.0 %collective-permute-done.15.wb = f32[264,256]{1,0:T(8,128)S(1)} collective-permute-done((f32[264,256]{1,0:T(8,128)S(1)}, f32[264,256]{1,0:T(8,128)S(1)}, u32[]{:S(2)}, u32[]{:S(2)}) %collective-permute-start.15) | collective-permute-done | bytes 270368 | tf_op jit(solution)/shard_map/ppermute | solution.py:246
  113.1 9.3 %collective-permute-done.17.relayed = f32[264,256]{1,0:T(8,128)S(1)} collective-permute-done((f32[264,256]{1,0:T(8,128)S(1)}, f32[264,256]{1,0:T(8,128)S(1)}, u32[]{:S(2)}, u32[]{:S(2)}) %collective-permute-start.17) | collective-permute-done | bytes 270368 | tf_op jit(solution)/shard_map/ppermute | solution.py:262
  122.4 2.9 %shard_map.90 = (f32[264,256]{1,0:T(8,128)S(1)}, f32[512,256]{1,0:T(8,128)S(1)}, f32[256,256]{1,0:T(8,128)S(1)}) custom-call(f32[512,256]{1,0:T(8,128)S(1)} %get-tuple-element.54.q, f32[256,256]{1,0:T(8,128)S(1)} %collective-permute-done.13.ra, f32[256,256]{1,0:T(8,128)S(1)} %collective-permute-done.14.ra2, f32[264,256]{1,0:T(8,128)S(1)} %collective-permute-done.15.wb, ...), custom_call_target="tpu_custom_call" | custom-call | flops 1006632960 | bytes 4481040 | tf_op jit(solution)/shard_map/pallas_call | solution.py:31
  125.3 2.8 %collective-permute-start.19 = (f32[264,256]{1,0:T(8,128)S(1)}, f32[264,256]{1,0:T(8,128)S(1)}, u32[]{:S(2)}, u32[]{:S(2)}) collective-permute-start(f32[264,256]{1,0:T(8,128)S(1)} %get-tuple-element.63), channel_id=1, source_target_pairs={{32,0},{64,32},{96,64},{128,96},{160,128},{192,160},{224,192},{256... | collective-permute-start | bytes 811016 | tf_op jit(solution)/shard_map/ppermute | solution.py:239
  128.1 3.1 %collective-permute-start.18 = (f32[256,256]{1,0:T(8,128)S(1)}, f32[256,256]{1,0:T(8,128)S(1)}, u32[]{:S(2)}, u32[]{:S(2)}) collective-permute-start(f32[256,256]{1,0:T(8,128)S(1)} %get-tuple-element.62), channel_id=1, source_target_pairs={{0,32},{32,64},{64,96},{96,128},{128,160},{160,192},{192,224},{224... | collective-permute-start | bytes 786440 | tf_op jit(solution)/shard_map/ppermute | solution.py:238
  131.1 8.0 %collective-permute-done.18.rup = f32[256,256]{1,0:T(8,128)S(1)} collective-permute-done((f32[256,256]{1,0:T(8,128)S(1)}, f32[256,256]{1,0:T(8,128)S(1)}, u32[]{:S(2)}, u32[]{:S(2)}) %collective-permute-start.18) | collective-permute-done | bytes 262176 | tf_op jit(solution)/shard_map/ppermute | solution.py:238
  139.1 1.5 %shard_map.91 = f32[512,256]{1,0:T(8,128)} custom-call(f32[512,256]{1,0:T(8,128)S(1)} %get-tuple-element.61.mid, f32[256,256]{1,0:T(8,128)S(1)} %collective-permute-done.18.rup, f32[264,256]{1,0:T(8,128)S(1)} %collective-permute-done.19.rdown, f32[512,256]{1,0:T(8,128)S(1)} %get-tuple-element.64.x, f32[2]{0:T(128)S(1)} %pad_maximum_fusion.sc), custom_call_target="tpu_custom_call" | custom-call | flops 1048576 | bytes 1581064 | tf_op jit(solution)/shard_map/pallas_call | solution.py:31
  (35 shorter events, 14.9 us)
Async XLA Ops:
  1.0 16.6 %copy-start = (f32[512,256]{1,0:T(8,128)S(1)}, f32[512,256]{1,0:T(8,128)}, u32[]{:S(2)}) copy-start(f32[512,256]{1,0:T(8,128)} %x.3) | copy-start | bytes 1572868
  1.0 16.6 %collective-permute-start.1 = (f32[264,256]{1,0:T(8,128)S(1)}, f32[264,256]{1,0:T(8,128)S(1)}, u32[]{:S(2)}, u32[]{:S(2)}) collective-permute-start(f32[264,256]{1,0:T(8,128)S(1)} %slice.7), channel_id=1, source_target_pairs={{32,0},{64,32},{96,64},{128,96},{160,128},{192,160},{224,192},{256... | collective-permute-start | bytes 811016 | tf_op jit(solution)/shard_map/ppermute | solution.py:239
  5.2 12.4 %collective-permute-start = (f32[256,256]{1,0:T(8,128)S(1)}, f32[256,256]{1,0:T(8,128)S(1)}, u32[]{:S(2)}, u32[]{:S(2)}) collective-permute-start(f32[256,256]{1,0:T(8,128)S(1)} %slice.6), channel_id=1, source_target_pairs={{0,32},{32,64},{64,96},{96,128},{128,160},{160,192},{192,224},{224... | collective-permute-start | bytes 786440 | tf_op jit(solution)/shard_map/ppermute | solution.py:238
  8.0 1.4 %copy-start.1 = (f32[2,3,256,256]{3,2,1,0:T(8,128)S(1)}, f32[2,3,256,256]{3,2,1,0:T(8,128)}, u32[]{:S(2)}) copy-start(f32[2,3,256,256]{3,2,1,0:T(8,128)} %fx.1) | copy-start | bytes 4718596
  9.4 1.1 copy-start.2
  10.6 0.7 copy-start.3
  11.3 0.7 copy-start.4
  17.5 16.1 %copy-start.5 = (f32[512,256]{1,0:T(8,128)S(1)}, f32[512,256]{1,0:T(8,128)}, u32[]{:S(2)}) copy-start(f32[512,256]{1,0:T(8,128)} %obs.3) | copy-start | bytes 1572868
  18.4 15.2 %collective-permute-start.2 = (f32[512,256]{1,0:T(8,128)S(1)}, f32[512,256]{1,0:T(8,128)S(1)}, u32[]{:S(2)}, u32[]{:S(2)}) collective-permute-start(f32[512,256]{1,0:T(8,128)S(1)} %shard_map.83.u), channel_id=1, source_target_pairs={{0,1},{2,3},{4,5},{6,7},{8,9},{10,11},{12,13},{14,15},{16,17},{18,... | collective-permute-start | bytes 1572872 | tf_op jit(solution)/shard_map/ppermute | solution.py:243
  20.3 23.8 %collective-permute-start.3 = (f32[512,256]{1,0:T(8,128)S(1)}, f32[512,256]{1,0:T(8,128)S(1)}, u32[]{:S(2)}, u32[]{:S(2)}) collective-permute-start(f32[512,256]{1,0:T(8,128)S(1)} %shard_map.83.u), channel_id=1, source_target_pairs={{1,2},{3,4},{5,6},{7,8},{9,10},{11,12},{13,14},{15,16},{17,18},{19... | collective-permute-start | bytes 1572872 | tf_op jit(solution)/shard_map/ppermute | solution.py:246
  34.2 6.7 %collective-permute-start.7 = (f32[392,256]{1,0:T(8,128)S(1)}, f32[392,256]{1,0:T(8,128)S(1)}, u32[]{:S(2)}, u32[]{:S(2)}) collective-permute-start(f32[392,256]{1,0:T(8,128)S(1)} %get-tuple-element.41.v), channel_id=1, source_target_pairs={{1,2},{3,4},{5,6},{7,8},{9,10},{11,12},{13,14},{17,18},{19,20},{21... | collective-permute-start | bytes 1204232 | tf_op jit(solution)/shard_map/ppermute | solution.py:260
  40.9 19.6 %collective-permute-start.8 = (f32[392,256]{1,0:T(8,128)S(1)}, f32[392,256]{1,0:T(8,128)S(1)}, u32[]{:S(2)}, u32[]{:S(2)}) collective-permute-start(f32[392,256]{1,0:T(8,128)S(1)} %collective-permute-done.7.vb), channel_id=1, source_target_pairs={{0,16},{31,15},{32,48},{63,47},{64,80},{95,79},{96,112},{127,111},... | collective-permute-start | bytes 1204232 | tf_op jit(solution)/shard_map/ppermute | solution.py:262
  42.2 18.3 %collective-permute-start.6 = (f32[376,256]{1,0:T(8,128)S(1)}, f32[376,256]{1,0:T(8,128)S(1)}, u32[]{:S(2)}, u32[]{:S(2)}) collective-permute-start(f32[376,256]{1,0:T(8,128)S(1)} %get-tuple-element.40.w), channel_id=1, source_target_pairs={{1,2},{3,4},{5,6},{7,8},{9,10},{11,12},{13,14},{15,16},{17,18},{19... | collective-permute-start | bytes 1155080 | tf_op jit(solution)/shard_map/ppermute | solution.py:246
  45.2 4.3 %collective-permute-start.4 = (f32[256,256]{1,0:T(8,128)S(1)}, f32[256,256]{1,0:T(8,128)S(1)}, u32[]{:S(2)}, u32[]{:S(2)}) collective-permute-start(f32[256,256]{1,0:T(8,128)S(1)} %get-tuple-element.45), channel_id=1, source_target_pairs={{0,1},{2,3},{4,5},{6,7},{8,9},{10,11},{12,13},{14,15},{16,17},{18,... | collective-permute-start | bytes 786440 | tf_op jit(solution)/shard_map/ppermute | solution.py:243
  47.2 3.6 %collective-permute-start.5 = (f32[256,256]{1,0:T(8,128)S(1)}, f32[256,256]{1,0:T(8,128)S(1)}, u32[]{:S(2)}, u32[]{:S(2)}) collective-permute-start(f32[256,256]{1,0:T(8,128)S(1)} %get-tuple-element.46), channel_id=1, source_target_pairs={{0,1},{2,3},{4,5},{6,7},{8,9},{10,11},{12,13},{14,15},{16,17},{18,... | collective-permute-start | bytes 786440 | tf_op jit(solution)/shard_map/ppermute | solution.py:243
  63.5 11.8 %collective-permute-start.10 = (f32[512,256]{1,0:T(8,128)S(1)}, f32[512,256]{1,0:T(8,128)S(1)}, u32[]{:S(2)}, u32[]{:S(2)}) collective-permute-start(f32[512,256]{1,0:T(8,128)S(1)} %get-tuple-element.49.top), channel_id=1, source_target_pairs={{32,0},{64,32},{96,64},{128,96},{160,128},{192,160},{224,192},{256... | collective-permute-start | bytes 1572872 | tf_op jit(solution)/shard_map/ppermute | solution.py:239
  66.9 17.0 %collective-permute-start.9 = (f32[512,256]{1,0:T(8,128)S(1)}, f32[512,256]{1,0:T(8,128)S(1)}, u32[]{:S(2)}, u32[]{:S(2)}) collective-permute-start(f32[512,256]{1,0:T(8,128)S(1)} %get-tuple-element.50.bottom), channel_id=1, source_target_pairs={{0,32},{32,64},{64,96},{96,128},{128,160},{160,192},{192,224},{224... | collective-permute-start | bytes 1572872 | tf_op jit(solution)/shard_map/ppermute | solution.py:238
  85.4 11.9 %collective-permute-start.11 = (f32[512,256]{1,0:T(8,128)S(1)}, f32[512,256]{1,0:T(8,128)S(1)}, u32[]{:S(2)}, u32[]{:S(2)}) collective-permute-start(f32[512,256]{1,0:T(8,128)S(1)} %get-tuple-element.51.u), channel_id=1, source_target_pairs={{0,1},{2,3},{4,5},{6,7},{8,9},{10,11},{12,13},{14,15},{16,17},{18,... | collective-permute-start | bytes 1572872 | tf_op jit(solution)/shard_map/ppermute | solution.py:243
  87.3 17.1 %collective-permute-start.12 = (f32[512,256]{1,0:T(8,128)S(1)}, f32[512,256]{1,0:T(8,128)S(1)}, u32[]{:S(2)}, u32[]{:S(2)}) collective-permute-start(f32[512,256]{1,0:T(8,128)S(1)} %get-tuple-element.51.u), channel_id=1, source_target_pairs={{1,2},{3,4},{5,6},{7,8},{9,10},{11,12},{13,14},{15,16},{17,18},{19... | collective-permute-start | bytes 1572872 | tf_op jit(solution)/shard_map/ppermute | solution.py:246
  97.9 5.3 %collective-permute-start.16 = (f32[264,256]{1,0:T(8,128)S(1)}, f32[264,256]{1,0:T(8,128)S(1)}, u32[]{:S(2)}, u32[]{:S(2)}) collective-permute-start(f32[264,256]{1,0:T(8,128)S(1)} %get-tuple-element.53.v), channel_id=1, source_target_pairs={{1,2},{3,4},{5,6},{7,8},{9,10},{11,12},{13,14},{17,18},{19,20},{21... | collective-permute-start | bytes 811016 | tf_op jit(solution)/shard_map/ppermute | solution.py:260
  99.2 13.9 %collective-permute-start.15 = (f32[264,256]{1,0:T(8,128)S(1)}, f32[264,256]{1,0:T(8,128)S(1)}, u32[]{:S(2)}, u32[]{:S(2)}) collective-permute-start(f32[264,256]{1,0:T(8,128)S(1)} %get-tuple-element.52.w), channel_id=1, source_target_pairs={{1,2},{3,4},{5,6},{7,8},{9,10},{11,12},{13,14},{15,16},{17,18},{19... | collective-permute-start | bytes 811016 | tf_op jit(solution)/shard_map/ppermute | solution.py:246
  103.1 19.2 %collective-permute-start.17 = (f32[264,256]{1,0:T(8,128)S(1)}, f32[264,256]{1,0:T(8,128)S(1)}, u32[]{:S(2)}, u32[]{:S(2)}) collective-permute-start(f32[264,256]{1,0:T(8,128)S(1)} %collective-permute-done.16.vb), channel_id=1, source_target_pairs={{0,16},{31,15},{32,48},{63,47},{64,80},{95,79},{96,112},{127,111},... | collective-permute-start | bytes 811016 | tf_op jit(solution)/shard_map/ppermute | solution.py:262
  105.6 4.3 %collective-permute-start.13 = (f32[256,256]{1,0:T(8,128)S(1)}, f32[256,256]{1,0:T(8,128)S(1)}, u32[]{:S(2)}, u32[]{:S(2)}) collective-permute-start(f32[256,256]{1,0:T(8,128)S(1)} %get-tuple-element.55), channel_id=1, source_target_pairs={{0,1},{2,3},{4,5},{6,7},{8,9},{10,11},{12,13},{14,15},{16,17},{18,... | collective-permute-start | bytes 786440 | tf_op jit(solution)/shard_map/ppermute | solution.py:243
  107.5 3.6 %collective-permute-start.14 = (f32[256,256]{1,0:T(8,128)S(1)}, f32[256,256]{1,0:T(8,128)S(1)}, u32[]{:S(2)}, u32[]{:S(2)}) collective-permute-start(f32[256,256]{1,0:T(8,128)S(1)} %get-tuple-element.56), channel_id=1, source_target_pairs={{0,1},{2,3},{4,5},{6,7},{8,9},{10,11},{12,13},{14,15},{16,17},{18,... | collective-permute-start | bytes 786440 | tf_op jit(solution)/shard_map/ppermute | solution.py:243
  125.3 13.8 %collective-permute-start.19 = (f32[264,256]{1,0:T(8,128)S(1)}, f32[264,256]{1,0:T(8,128)S(1)}, u32[]{:S(2)}, u32[]{:S(2)}) collective-permute-start(f32[264,256]{1,0:T(8,128)S(1)} %get-tuple-element.63), channel_id=1, source_target_pairs={{32,0},{64,32},{96,64},{128,96},{160,128},{192,160},{224,192},{256... | collective-permute-start | bytes 811016 | tf_op jit(solution)/shard_map/ppermute | solution.py:239
  128.1 11.0 %collective-permute-start.18 = (f32[256,256]{1,0:T(8,128)S(1)}, f32[256,256]{1,0:T(8,128)S(1)}, u32[]{:S(2)}, u32[]{:S(2)}) collective-permute-start(f32[256,256]{1,0:T(8,128)S(1)} %get-tuple-element.62), channel_id=1, source_target_pairs={{0,32},{32,64},{64,96},{96,128},{128,160},{160,192},{192,224},{224... | collective-permute-start | bytes 786440 | tf_op jit(solution)/shard_map/ppermute | solution.py:238
